TPU v7x, 512 devices: a whole 4x8x8 slice. The times are simulated.
512 devices in a mesh: boxes: 128 (over y, z, core), probe: 4 (over x).
Axes of the slice: x: 4, y: 8, z: 8, core: 2. Of those that a mesh axis runs over, the one named last changes fastest.
Arguments:
- probes: float32 [32, 1048576], P('probe', 'boxes'), may hold values from -0.3 to 0.3
- points: float32 [3, 1048576], P(None, 'boxes'), may hold values from -1 to 1, as said below
- near_list: int32 [4096, 6], P('boxes'), may hold values from -1 to 4095, as said below
- leaf_proxy: float32 [3, 262144], P(None, 'boxes'), may hold values from -1 to 1, as said below
- inner_proxy: float32 [3, 245760], P(None, 'boxes'), may hold values from -1 to 1, as said below
- top_proxy: float32 [3, 16128], replicated, may hold values from -1 to 1, as said below
- far_list: int32 [4096, 3], P('boxes'), may hold values from -1 to 4095, as said below
Outputs:
- kernel_product: float32 [32, 1048576], P('probe', 'boxes')
Inputs may be any that keep to these rules, and one draw needn't show every extreme that they name: `points`: points on the unit sphere, box by box along a curve over it. `leaf_proxy`: proxy points on the unit sphere. `inner_proxy`: proxy points on the unit sphere. `top_proxy`: proxy points on the unit sphere. `near_list`: row b holds b - 1, b, b + 1 (modulo 4096) and those of the three candidates of row b of far_list that are -1 there, in some order, live entries first, then -1; some row is full. `far_list`: in row b, slot 0 holds b - 2, slot 1 holds b + 2, slot 2 holds b + 3 for even b and b - 3 for odd b (all modulo 4096), or -1.
All inputs are finite; a program needn't handle non-finite values.
Results may differ from a plain program's by a relative error of at most 0.00013.
Values sent between devices are 32-bit elements; how exact they have to be, the bound alone decides.
A program may use at most 64 MiB of HBM per device.

v0:
```python
import jax
import jax.numpy as jnp
from jax import lax
from jax.sharding import PartitionSpec as P

BOXES_DEV = 32
P_SIZE = 256
R = 64
W = 3
INNER_DEV = 30


SHARPNESS = 0.05
NUGGET = 1.0
PRECISE = lax.Precision.HIGHEST


def with_halo(array, sides, width):
    for axis, dim in sides:
        size, length = (lax.axis_size(axis), array.shape[dim])
        up = [(i, (i + 1) % size) for i in range(size)]
        down = [(j, i) for i, j in up]
        last = lax.slice_in_dim(array, length - width, length, axis=dim)
        initial = lax.slice_in_dim(array, 0, width, axis=dim)
        before = lax.ppermute(last, axis, up)
        after = lax.ppermute(initial, axis, down)
        array = jnp.concatenate([before, array, after], axis=dim)
    return array


def passed_along(array, axis, by):
    length = lax.axis_size(axis)
    return lax.ppermute(array, axis, [(i, (i + by) % length) for i in range(length)])


def from_partner(array, axis, distance):
    return lax.ppermute(array, axis, [(i, i ^ 1 << distance) for i in range(lax.axis_size(axis))])


def kernel_matrix(left_points, right_points, kernel_scale):
    distance_sq = (left_points[0][..., :, None] - right_points[0][..., None, :]) ** 2
    distance_sq = distance_sq + (left_points[1][..., :, None] - right_points[1][..., None, :]) ** 2
    distance_sq = distance_sq + (left_points[2][..., :, None] - right_points[2][..., None, :]) ** 2
    return 1.0 / (1.0 + kernel_scale * distance_sq)


def interpolation(left_points, right_points, kernel_scale):
    values = kernel_matrix(left_points, right_points, kernel_scale)
    return values / jnp.sum(values, axis=-1, keepdims=True)


def body(probes, points, near_list, leaf_proxy, inner_proxy, top_proxy, far_list):
    groups = lax.axis_size("boxes")
    device = lax.axis_index("boxes")
    boxes_all = BOXES_DEV * groups
    kernel_scale = SHARPNESS * boxes_all
    rows_here = probes.shape[0]
    local_depth = BOXES_DEV.bit_length() - 1
    tree_depth = groups.bit_length() - 1
    live_slot = near_list >= 0
    slot_weight = live_slot.astype(jnp.float32)
    where_in = jnp.where(live_slot, (near_list - device * BOXES_DEV + W + boxes_all) % boxes_all, 0)
    box_points = points.reshape(3, BOXES_DEV, P_SIZE)
    stacked = jnp.concatenate([probes, points], axis=0)
    extended = with_halo(stacked, (("boxes", 1),), W * P_SIZE)
    extended = extended.reshape(rows_here + 3, BOXES_DEV + 2 * W, P_SIZE)

    def near_box(near_inputs):
        slot_index, slot_mask, targets = near_inputs
        near_tiles = jnp.take(extended, slot_index, axis=1)
        near_values = near_tiles[:rows_here] * slot_mask[None, :, None]
        kernel_block = kernel_matrix(near_tiles[rows_here:], targets[:, None, :], kernel_scale)
        return jnp.einsum("qns,nst->qt", near_values, kernel_block, precision=PRECISE)

    near_field = lax.map(near_box, (where_in, slot_weight, jnp.moveaxis(box_points, 1, 0)))
    near_field = jnp.moveaxis(near_field, 0, 1).reshape(rows_here, BOXES_DEV * P_SIZE)
    probe_tiles = probes.reshape(rows_here, BOXES_DEV, P_SIZE)
    leaf_points = leaf_proxy.reshape(3, BOXES_DEV, R)
    leaf_basis = interpolation(box_points, leaf_points, kernel_scale)
    inner_points = inner_proxy.reshape(3, INNER_DEV, R)
    top_points = top_proxy.reshape(3, top_proxy.shape[1] // R, R)

    def node_proxy(height, node_index):
        offset = 2 * groups - 2 * (groups >> height)
        return lax.dynamic_slice_in_dim(top_points, offset + node_index, 1, 1)

    proxies = [leaf_points]
    for height in range(1, local_depth):
        offset = BOXES_DEV - (BOXES_DEV >> height - 1)
        number = BOXES_DEV >> height
        proxies.append(inner_points[:, offset : offset + number, :])
    proxies.append(node_proxy(0, device))
    level_moments = [jnp.einsum("qbp,bpr->qbr", probe_tiles, leaf_basis, precision=PRECISE)]
    transfer_maps = []
    for height in range(local_depth):
        interp_map = interpolation(
            proxies[height], jnp.repeat(proxies[height + 1], 2, axis=1), kernel_scale
        )
        transfer_maps.append(interp_map)
        lifted = jnp.einsum("qnr,nrs->qns", level_moments[-1], interp_map, precision=PRECISE)
        level_moments.append(lifted.reshape(rows_here, -1, 2, R).sum(axis=2))
    pyramid = jnp.concatenate(
        [
            jnp.concatenate(level_moments[:local_depth], axis=1),
            jnp.concatenate([leaf_points, inner_points], axis=1),
        ],
        axis=0,
    )
    pyramid_nodes = pyramid.shape[1]
    spread = with_halo(pyramid, (("boxes", 1),), pyramid_nodes)
    local_couplings = []
    for height in range(local_depth):
        count = BOXES_DEV >> height
        start = 0 if height == 0 else 2 * BOXES_DEV - (BOXES_DEV >> height - 1)
        view = jnp.concatenate(
            [
                spread[:, block * pyramid_nodes + start : block * pyramid_nodes + start + count, :]
                for block in range(3)
            ],
            axis=1,
        )
        if height == 0:
            live_far = far_list >= 0
            slot_ids = [
                jnp.where(
                    live_far[:, slot],
                    (far_list[:, slot] - device * BOXES_DEV + BOXES_DEV + boxes_all) % boxes_all,
                    0,
                )
                for slot in range(3)
            ]
            slot_masks = [live_far[:, slot].astype(jnp.float32)[None, :, None] for slot in range(3)]
        else:
            node = jnp.arange(count, dtype=jnp.int32)
            third = jnp.where(node % 2 == 0, node + 3, node - 3)
            slot_ids = [node - 2 + count, node + 2 + count, third + count]
            slot_masks = [None, None, None]
        coupling = jnp.zeros((rows_here, count, R), jnp.float32)
        for slot in range(3):
            picked = jnp.take(view, slot_ids[slot], axis=1)
            kernel_block = kernel_matrix(picked[rows_here:], proxies[height], kernel_scale)
            source_moment = picked[:rows_here]
            if slot_masks[slot] is not None:
                source_moment = source_moment * slot_masks[slot]
            coupling = coupling + jnp.einsum(
                "qnr,nrs->qns", source_moment, kernel_block, precision=PRECISE
            )
        local_couplings.append(coupling)

    def top_sources(height):
        number = groups >> height
        node = device // 2**height
        third = jnp.where(node % 2 == 0, node + 3, node - 3) % number
        if number > 4:
            return [(node - 2) % number, (node + 2) % number, third]
        return [None, (node + 2) % number, None]

    own_edges = []
    for height in range(tree_depth - 2):
        own_edges.append(
            interpolation(
                node_proxy(height, device // 2**height),
                node_proxy(height + 1, device // 2 ** (height + 1)),
                kernel_scale,
            )
        )
    cousin_moments = []

    def remote(moment, distance):
        return passed_along(moment, "boxes", distance)

    top_moments = [level_moments[local_depth]]
    for height in range(tree_depth - 2):
        lifted = jnp.einsum("qnr,nrs->qns", top_moments[-1], own_edges[height], precision=PRECISE)
        top_moments.append(lifted + from_partner(lifted, "boxes", height))
    for height in range(tree_depth - 1):
        stride = 2**height
        node = device // stride
        moment = top_moments[height]
        if groups >> height > 4:
            third = jnp.where(
                node % 2 == 0, remote(moment, -3 * stride), remote(moment, 3 * stride)
            )
            cousin_moments.append([remote(moment, 2 * stride), remote(moment, -2 * stride), third])
        else:
            cousin_moments.append([None, remote(moment, -2 * stride), None])
    top_couplings = []
    for height in range(tree_depth - 1):
        source_ids = top_sources(height)
        target_points = node_proxy(height, device // 2**height)
        coupling = jnp.zeros((rows_here, 1, R), jnp.float32)
        for slot in range(3):
            if source_ids[slot] is not None:
                kernel_block = kernel_matrix(
                    node_proxy(height, source_ids[slot]), target_points, kernel_scale
                )
                coupling = coupling + jnp.einsum(
                    "qnr,nrs->qns", cousin_moments[height][slot], kernel_block, precision=PRECISE
                )
        top_couplings.append(coupling)
    descent = top_couplings[-1]
    for height in range(tree_depth - 3, -1, -1):
        descent = (
            jnp.einsum("qns,nrs->qnr", descent, own_edges[height], precision=PRECISE)
            + top_couplings[height]
        )
    for height in range(local_depth - 1, -1, -1):
        descent = jnp.einsum(
            "qns,nrs->qnr", jnp.repeat(descent, 2, axis=1), transfer_maps[height], precision=PRECISE
        )
        descent = descent + local_couplings[height]
    far_field = jnp.einsum("qbr,bpr->qbp", descent, leaf_basis, precision=PRECISE).reshape(
        rows_here, BOXES_DEV * P_SIZE
    )
    return near_field + far_field + NUGGET * probes


def solution(mesh):
    in_specs = (
        P("probe", "boxes"),
        P(None, "boxes"),
        P("boxes", None),
        P(None, "boxes"),
        P(None, "boxes"),
        P(),
        P("boxes", None),
    )
    out_specs = P("probe", "boxes")
    return jax.shard_map(body, mesh=mesh, in_specs=in_specs, out_specs=out_specs, check_vma=False)
```

profile of v0, /device:TPU:6, one launch (start us, length us, event | category | flops | bytes accessed | tf_op | source)
XLA Modules:
  0.0 410.5 jit_solution(2084415423867783893)
XLA Ops:
  4.0 3.3 constant_dynamic-update-slice_fusion.6
  8.8 2.6 bitcast_reduce_fusion
  16.7 3.7 collective-permute-start.27
  20.4 11.5 %collective-permute-start.26 = (f32[8,1,64]{2,0,1:T(8,128)}, f32[8,1,64]{2,0,1:T(8,128)}, u32[]{:S(2)}, u32[]{:S(2)}) collective-permute-start(f32[8,1,64]{2,0,1:T(8,128)} %bitcast.174), channel_id=1, source_target_pairs={{0,500},{4,504},{8,508},{12,0},{16,4},{20,8},{24,12},{28,16},{32,2... | collective-permute-start | bytes 6152 | tf_op jit(solution)/shard_map/ppermute | solution.py:33
  31.9 5.1 %collective-permute-start.25 = (f32[8,1,64]{2,0,1:T(8,128)}, f32[8,1,64]{2,0,1:T(8,128)}, u32[]{:S(2)}, u32[]{:S(2)}) collective-permute-start(f32[8,1,64]{2,0,1:T(8,128)} %bitcast.174), channel_id=1, source_target_pairs={{0,504},{4,508},{8,0},{12,4},{16,8},{20,12},{24,16},{28,20},{32,24... | collective-permute-start | bytes 6152 | tf_op jit(solution)/shard_map/ppermute | solution.py:33
  61.3 7.3 %collective-permute-start.29 = (f32[11,62,64]{2,0,1:T(8,128)S(1)}, f32[11,62,64]{2,0,1:T(8,128)S(1)}, u32[]{:S(2)}, u32[]{:S(2)}) collective-permute-start(f32[11,62,64]{2,0,1:T(8,128)S(1)} %maximum_maximum_fusion), channel_id=1, source_target_pairs={{4,0},{8,4},{12,8},{16,12},{20,16},{24,20},{28,24},{32,28},{36,32}... | collective-permute-start | bytes 523784 | tf_op jit(solution)/shard_map/ppermute | solution.py:26
  70.6 9.0 %collective-permute-start.22 = (f32[8,1,64]{2,0,1:T(8,128)S(1)}, f32[8,1,64]{2,0,1:T(8,128)S(1)}, u32[]{:S(2)}, u32[]{:S(2)}) collective-permute-start(f32[8,1,64]{2,0,1:T(8,128)S(1)} %add.2368), channel_id=1, source_target_pairs={{0,488},{4,492},{8,496},{12,500},{16,504},{20,508},{24,0},{28,4},{... | collective-permute-start | bytes 6152 | tf_op jit(solution)/shard_map/ppermute | solution.py:33
  83.7 2.6 collective-permute-done.3
  90.2 10.5 %collective-permute-start.17 = (f32[8,1,64]{2,0,1:T(8,128)S(1)}, f32[8,1,64]{2,0,1:T(8,128)S(1)}, u32[]{:S(2)}, u32[]{:S(2)}) collective-permute-start(f32[8,1,64]{2,0,1:T(8,128)S(1)} %add.2369), channel_id=1, source_target_pairs={{0,480},{4,484},{8,488},{12,492},{16,496},{20,500},{24,504},{28,50... | collective-permute-start | bytes 6152 | tf_op jit(solution)/shard_map/ppermute | solution.py:33
  103.4 4.2 %collective-permute-done.4 = f32[8,1,64]{2,0,1:T(8,128)S(1)} collective-permute-done((f32[8,1,64]{2,0,1:T(8,128)S(1)}, f32[8,1,64]{2,0,1:T(8,128)S(1)}, u32[]{:S(2)}, u32[]{:S(2)}) %collective-permute-start.4) | collective-permute-done | bytes 2080 | tf_op jit(solution)/shard_map/ppermute | solution.py:37
  109.6 3.1 collective-permute-start.15
  112.9 9.7 %collective-permute-start.14 = (f32[8,1,64]{2,0,1:T(8,128)S(1)}, f32[8,1,64]{2,0,1:T(8,128)S(1)}, u32[]{:S(2)}, u32[]{:S(2)}) collective-permute-start(f32[8,1,64]{2,0,1:T(8,128)S(1)} %add.2370), channel_id=1, source_target_pairs={{0,416},{4,420},{8,424},{12,428},{16,432},{20,436},{24,440},{28,44... | collective-permute-start | bytes 6152 | tf_op jit(solution)/shard_map/ppermute | solution.py:33
  125.0 3.1 collective-permute-done.13
  128.1 3.4 collective-permute-start.5
  131.7 5.8 %collective-permute-done.5 = f32[8,1,64]{2,0,1:T(8,128)S(1)} collective-permute-done((f32[8,1,64]{2,0,1:T(8,128)S(1)}, f32[8,1,64]{2,0,1:T(8,128)S(1)}, u32[]{:S(2)}, u32[]{:S(2)}) %collective-permute-start.5) | collective-permute-done | bytes 2080 | tf_op jit(solution)/shard_map/ppermute | solution.py:37
  139.5 3.3 collective-permute-start.11
  142.7 5.6 %collective-permute-start.10 = (f32[8,1,64]{2,0,1:T(8,128)S(1)}, f32[8,1,64]{2,0,1:T(8,128)S(1)}, u32[]{:S(2)}, u32[]{:S(2)}) collective-permute-start(f32[8,1,64]{2,0,1:T(8,128)S(1)} %add.2371), channel_id=1, source_target_pairs={{0,320},{4,324},{8,328},{12,332},{16,336},{20,340},{24,344},{28,34... | collective-permute-start | bytes 6152 | tf_op jit(solution)/shard_map/ppermute | solution.py:33
  148.8 3.0 collective-permute-start.9
  151.9 3.3 collective-permute-start.6
  159.3 5.0 %collective-permute-start.7 = (f32[8,1,64]{2,0,1:T(8,128)S(1)}, f32[8,1,64]{2,0,1:T(8,128)S(1)}, u32[]{:S(2)}, u32[]{:S(2)}) collective-permute-start(f32[8,1,64]{2,0,1:T(8,128)S(1)} %add.2372), channel_id=1, source_target_pairs={{0,256},{4,260},{8,264},{12,268},{16,272},{20,276},{24,280},{28,28... | collective-permute-start | bytes 6152 | tf_op jit(solution)/shard_map/ppermute | solution.py:33
  164.6 4.1 %collective-permute-done.7 = f32[8,1,64]{2,0,1:T(8,128)S(1)} collective-permute-done((f32[8,1,64]{2,0,1:T(8,128)S(1)}, f32[8,1,64]{2,0,1:T(8,128)S(1)}, u32[]{:S(2)}, u32[]{:S(2)}) %collective-permute-start.7) | collective-permute-done | bytes 2080 | tf_op jit(solution)/shard_map/ppermute | solution.py:33
  168.7 4.2 %collective-permute-start.8 = (f32[8,1,64]{2,0,1:T(8,128)S(1)}, f32[8,1,64]{2,0,1:T(8,128)S(1)}, u32[]{:S(2)}, u32[]{:S(2)}) collective-permute-start(f32[8,1,64]{2,0,1:T(8,128)S(1)} %add.2371), channel_id=1, source_target_pairs={{0,128},{4,132},{8,136},{12,140},{16,144},{20,148},{24,152},{28,15... | collective-permute-start | bytes 6152 | tf_op jit(solution)/shard_map/ppermute | solution.py:33
  173.4 2.9 collective-permute-done.8
  176.3 3.3 collective-permute-start.12
  180.1 2.9 collective-permute-done.12
  183.0 2.7 collective-permute-start.16
  186.3 8.3 %collective-permute-done.16 = f32[8,1,64]{2,0,1:T(8,128)S(1)} collective-permute-done((f32[8,1,64]{2,0,1:T(8,128)S(1)}, f32[8,1,64]{2,0,1:T(8,128)S(1)}, u32[]{:S(2)}, u32[]{:S(2)}) %collective-permute-start.16) | collective-permute-done | bytes 2080 | tf_op jit(solution)/shard_map/ppermute | solution.py:33
  197.1 7.1 %collective-permute-done.20 = f32[8,1,64]{2,0,1:T(8,128)S(1)} collective-permute-done((f32[8,1,64]{2,0,1:T(8,128)S(1)}, f32[8,1,64]{2,0,1:T(8,128)S(1)}, u32[]{:S(2)}, u32[]{:S(2)}) %collective-permute-start.20) | collective-permute-done | bytes 2080 | tf_op jit(solution)/shard_map/ppermute | solution.py:33
  208.9 157.3 %while.10 = (s32[]{:T(128)}, f32[32,8,256]{2,1,0:T(8,128)}, s32[32,6]{1,0:T(8,128)}, f32[11,38,256]{2,0,1:T(8,128)S(1)}, f32[32,6]{1,0:T(8,128)}, /*index=5*/f32...) while((s32[]{:T(128)}, f32[32,8,256]{2,1,0:T(8,128)}, s32[32,6]{1,0:T(8,128)}, ...), condition=%wide.region_1.2_spmd, body=%wide.region_0.1_spmd.sunk | while | flops 42104376 | bytes 440149 | solution.py:75
  211.7 2.2 fusion.909
  216.6 2.2 fusion.909
  221.6 2.2 fusion.909
  226.5 2.2 fusion.909
  231.4 2.2 fusion.909
  236.3 2.2 fusion.909
  241.2 2.2 fusion.909
  246.1 2.2 fusion.909
  251.1 2.2 fusion.909
  256.0 2.2 fusion.909
  260.9 2.2 fusion.909
  265.8 2.2 fusion.909
  270.8 2.2 fusion.909
  275.7 2.2 fusion.909
  280.6 2.2 fusion.909
  285.5 2.2 fusion.909
  290.4 2.2 fusion.909
  295.3 2.2 fusion.909
  300.3 2.2 fusion.909
  305.2 2.2 fusion.909
  310.1 2.2 fusion.909
  315.0 2.2 fusion.909
  319.9 2.2 fusion.909
  324.8 2.2 fusion.909
  329.7 2.2 fusion.909
  334.6 2.2 fusion.909
  339.5 2.2 fusion.909
  344.4 2.2 fusion.909
  349.3 2.2 fusion.909
  381.3 2.2 fusion.146
  395.3 2.3 fusion.59
  398.9 2.3 convolution_add_fusion.1
  401.3 2.3 convolution_add_fusion
  403.7 3.2 fusion.17
  407.0 2.7 fusion.16
  (807 shorter events, 188.0 us)
Async XLA Ops:
  0.9 206.7 %copy-start.55 = (f32[2,64]{1,0:T(2,128)}, f32[2,64]{1,0:T(2,128)S(1)}, u32[]{:S(2)}) copy-start(f32[2,64]{1,0:T(2,128)S(1)} %get-tuple-element.205) | copy-start | bytes 1540
  0.9 206.7 %copy-start.57 = (f32[2,64]{1,0:T(2,128)}, f32[2,64]{1,0:T(2,128)S(1)}, u32[]{:S(2)}) copy-start(f32[2,64]{1,0:T(2,128)S(1)} %get-tuple-element.206) | copy-start | bytes 1540
  0.9 206.7 %copy-start.59 = (f32[2,64]{1,0:T(2,128)}, f32[2,64]{1,0:T(2,128)S(1)}, u32[]{:S(2)}) copy-start(f32[2,64]{1,0:T(2,128)S(1)} %get-tuple-element.207) | copy-start | bytes 1540
  14.7 24.4 %copy-start.63 = (f32[2,2,64]{2,1,0:T(2,128)}, f32[2,2,64]{2,1,0:T(2,128)S(1)}, u32[]{:S(2)}) copy-start(f32[2,2,64]{2,1,0:T(2,128)S(1)} %broadcast_in_dim.169) | copy-start | bytes 3076
  14.7 24.4 %copy-start.65 = (f32[2,2,64]{2,1,0:T(2,128)}, f32[2,2,64]{2,1,0:T(2,128)S(1)}, u32[]{:S(2)}) copy-start(f32[2,2,64]{2,1,0:T(2,128)S(1)} %broadcast_in_dim.173) | copy-start | bytes 3076
  15.0 33.2 %copy-start.72 = (s32[32,3]{0,1:T(4,128)S(1)}, s32[32,3]{0,1:T(4,128)}, u32[]{:S(2)}) copy-start(s32[32,3]{0,1:T(4,128)} %param.25) | copy-start | bytes 1156
  15.0 34.4 %copy-start.73 = (s32[32,6]{0,1:T(8,128)S(1)}, s32[32,6]{0,1:T(8,128)}, u32[]{:S(2)}) copy-start(s32[32,6]{0,1:T(8,128)} %param.21) | copy-start | bytes 2308
  15.4 35.3 %copy-start.15 = (f32[3,2048]{1,0:T(4,128)S(1)}, f32[3,2048]{1,0:T(4,128)}, u32[]{:S(2)}) copy-start(f32[3,2048]{1,0:T(4,128)} %param.22) | copy-start | bytes 73732
  16.7 51.9 %collective-permute-start.27 = (f32[8,1,64]{2,0,1:T(8,128)}, f32[8,1,64]{2,0,1:T(8,128)}, u32[]{:S(2)}, u32[]{:S(2)}) collective-permute-start(f32[8,1,64]{2,0,1:T(8,128)} %bitcast.174), channel_id=1, source_target_pairs={{0,12},{4,16},{8,20},{12,24},{16,28},{20,32},{24,36},{28,40},{32,4... | collective-permute-start | bytes 6152 | tf_op jit(solution)/shard_map/ppermute | solution.py:33
  20.4 50.1 %collective-permute-start.26 = (f32[8,1,64]{2,0,1:T(8,128)}, f32[8,1,64]{2,0,1:T(8,128)}, u32[]{:S(2)}, u32[]{:S(2)}) collective-permute-start(f32[8,1,64]{2,0,1:T(8,128)} %bitcast.174), channel_id=1, source_target_pairs={{0,500},{4,504},{8,508},{12,0},{16,4},{20,8},{24,12},{28,16},{32,2... | collective-permute-start | bytes 6152 | tf_op jit(solution)/shard_map/ppermute | solution.py:33
  31.9 48.9 %collective-permute-start.25 = (f32[8,1,64]{2,0,1:T(8,128)}, f32[8,1,64]{2,0,1:T(8,128)}, u32[]{:S(2)}, u32[]{:S(2)}) collective-permute-start(f32[8,1,64]{2,0,1:T(8,128)} %bitcast.174), channel_id=1, source_target_pairs={{0,504},{4,508},{8,0},{12,4},{16,8},{20,12},{24,16},{28,20},{32,24... | collective-permute-start | bytes 6152 | tf_op jit(solution)/shard_map/ppermute | solution.py:33
  37.1 169.6 %collective-permute-start.24 = (f32[8,1,64]{2,0,1:T(8,128)}, f32[8,1,64]{2,0,1:T(8,128)}, u32[]{:S(2)}, u32[]{:S(2)}) collective-permute-start(f32[8,1,64]{2,0,1:T(8,128)} %bitcast.174), channel_id=1, source_target_pairs={{0,8},{4,12},{8,16},{12,20},{16,24},{20,28},{24,32},{28,36},{32,40... | collective-permute-start | bytes 6152 | tf_op jit(solution)/shard_map/ppermute | solution.py:33
  41.7 19.6 %collective-permute-start.2 = (f32[8,1,64]{2,0,1:T(8,128)S(1)}, f32[8,1,64]{2,0,1:T(8,128)S(1)}, u32[]{:S(2)}, u32[]{:S(2)}) collective-permute-start(f32[8,1,64]{2,0,1:T(8,128)S(1)} %convolution_bitcast_fusion.7), channel_id=1, source_target_pairs={{0,4},{4,0},{8,12},{12,8},{16,20},{20,16},{24,28},{28,24},{32,36},... | collective-permute-start | bytes 6152 | tf_op jit(solution)/shard_map/ppermute | solution.py:37
  61.2 39.5 %copy-start.105 = (f32[64]{0:T(128)S(1)}, f32[64]{0:T(128)}, u32[]{:S(2)}) copy-start(f32[64]{0:T(128)} %get-tuple-element.118) | copy-start | bytes 772
  61.2 39.5 %copy-start.106 = (f32[64]{0:T(128)S(1)}, f32[64]{0:T(128)}, u32[]{:S(2)}) copy-start(f32[64]{0:T(128)} %get-tuple-element.119) | copy-start | bytes 772
  61.2 42.0 %copy-start.103 = (f32[64]{0:T(128)S(1)}, f32[64]{0:T(128)}, u32[]{:S(2)}) copy-start(f32[64]{0:T(128)} %get-tuple-element.120) | copy-start | bytes 772
  61.2 42.0 %copy-start.104 = (f32[64]{0:T(128)S(1)}, f32[64]{0:T(128)}, u32[]{:S(2)}) copy-start(f32[64]{0:T(128)} %get-tuple-element.121) | copy-start | bytes 772
  61.2 51.4 %copy-start.101 = (f32[64]{0:T(128)S(1)}, f32[64]{0:T(128)}, u32[]{:S(2)}) copy-start(f32[64]{0:T(128)} %get-tuple-element.126) | copy-start | bytes 772
  61.3 51.4 %copy-start.102 = (f32[64]{0:T(128)S(1)}, f32[64]{0:T(128)}, u32[]{:S(2)}) copy-start(f32[64]{0:T(128)} %get-tuple-element.127) | copy-start | bytes 772
  61.3 304.9 %collective-permute-start.29 = (f32[11,62,64]{2,0,1:T(8,128)S(1)}, f32[11,62,64]{2,0,1:T(8,128)S(1)}, u32[]{:S(2)}, u32[]{:S(2)}) collective-permute-start(f32[11,62,64]{2,0,1:T(8,128)S(1)} %maximum_maximum_fusion), channel_id=1, source_target_pairs={{4,0},{8,4},{12,8},{16,12},{20,16},{24,20},{28,24},{32,28},{36,32}... | collective-permute-start | bytes 523784 | tf_op jit(solution)/shard_map/ppermute | solution.py:26
  68.6 19.6 %collective-permute-start.23 = (f32[8,1,64]{2,0,1:T(8,128)S(1)}, f32[8,1,64]{2,0,1:T(8,128)S(1)}, u32[]{:S(2)}, u32[]{:S(2)}) collective-permute-start(f32[8,1,64]{2,0,1:T(8,128)S(1)} %add.2368), channel_id=1, source_target_pairs={{0,24},{4,28},{8,32},{12,36},{16,40},{20,44},{24,48},{28,52},{32,5... | collective-permute-start | bytes 6152 | tf_op jit(solution)/shard_map/ppermute | solution.py:33
  70.6 19.6 %collective-permute-start.22 = (f32[8,1,64]{2,0,1:T(8,128)S(1)}, f32[8,1,64]{2,0,1:T(8,128)S(1)}, u32[]{:S(2)}, u32[]{:S(2)}) collective-permute-start(f32[8,1,64]{2,0,1:T(8,128)S(1)} %add.2368), channel_id=1, source_target_pairs={{0,488},{4,492},{8,496},{12,500},{16,504},{20,508},{24,0},{28,4},{... | collective-permute-start | bytes 6152 | tf_op jit(solution)/shard_map/ppermute | solution.py:33
  80.6 44.0 %copy-start.99 = (f32[64]{0:T(128)S(1)}, f32[64]{0:T(128)}, u32[]{:S(2)}) copy-start(f32[64]{0:T(128)} %get-tuple-element.124) | copy-start | bytes 772
  80.6 44.0 %copy-start.100 = (f32[64]{0:T(128)S(1)}, f32[64]{0:T(128)}, u32[]{:S(2)}) copy-start(f32[64]{0:T(128)} %get-tuple-element.125) | copy-start | bytes 772
  80.8 5.5 %collective-permute-start.3 = (f32[8,1,64]{2,0,1:T(8,128)S(1)}, f32[8,1,64]{2,0,1:T(8,128)S(1)}, u32[]{:S(2)}, u32[]{:S(2)}) collective-permute-start(f32[8,1,64]{2,0,1:T(8,128)S(1)} %convolution_bitcast_fusion.6), channel_id=1, source_target_pairs={{0,8},{4,12},{8,0},{12,4},{16,24},{20,28},{24,16},{28,20},{32,40},... | collective-permute-start | bytes 6152 | tf_op jit(solution)/shard_map/ppermute | solution.py:37
  83.7 47.8 %copy-start.97 = (f32[64]{0:T(128)S(1)}, f32[64]{0:T(128)}, u32[]{:S(2)}) copy-start(f32[64]{0:T(128)} %get-tuple-element.132) | copy-start | bytes 772
  83.7 47.8 %copy-start.98 = (f32[64]{0:T(128)S(1)}, f32[64]{0:T(128)}, u32[]{:S(2)}) copy-start(f32[64]{0:T(128)} %get-tuple-element.133) | copy-start | bytes 772
  86.3 14.9 %collective-permute-start.21 = (f32[8,1,64]{2,0,1:T(8,128)S(1)}, f32[8,1,64]{2,0,1:T(8,128)S(1)}, u32[]{:S(2)}, u32[]{:S(2)}) collective-permute-start(f32[8,1,64]{2,0,1:T(8,128)S(1)} %add.2368), channel_id=1, source_target_pairs={{0,496},{4,500},{8,504},{12,508},{16,0},{20,4},{24,8},{28,12},{32,... | collective-permute-start | bytes 6152 | tf_op jit(solution)/shard_map/ppermute | solution.py:33
  88.3 24.6 %collective-permute-start.19 = (f32[8,1,64]{2,0,1:T(8,128)S(1)}, f32[8,1,64]{2,0,1:T(8,128)S(1)}, u32[]{:S(2)}, u32[]{:S(2)}) collective-permute-start(f32[8,1,64]{2,0,1:T(8,128)S(1)} %add.2369), channel_id=1, source_target_pairs={{0,48},{4,52},{8,56},{12,60},{16,64},{20,68},{24,72},{28,76},{32,8... | collective-permute-start | bytes 6152 | tf_op jit(solution)/shard_map/ppermute | solution.py:33
  90.2 19.3 %collective-permute-start.17 = (f32[8,1,64]{2,0,1:T(8,128)S(1)}, f32[8,1,64]{2,0,1:T(8,128)S(1)}, u32[]{:S(2)}, u32[]{:S(2)}) collective-permute-start(f32[8,1,64]{2,0,1:T(8,128)S(1)} %add.2369), channel_id=1, source_target_pairs={{0,480},{4,484},{8,488},{12,492},{16,496},{20,500},{24,504},{28,50... | collective-permute-start | bytes 6152 | tf_op jit(solution)/shard_map/ppermute | solution.py:33
  101.0 47.4 %copy-start.95 = (f32[64]{0:T(128)S(1)}, f32[64]{0:T(128)}, u32[]{:S(2)}) copy-start(f32[64]{0:T(128)} %get-tuple-element.130) | copy-start | bytes 772
  101.0 47.4 %copy-start.96 = (f32[64]{0:T(128)S(1)}, f32[64]{0:T(128)}, u32[]{:S(2)}) copy-start(f32[64]{0:T(128)} %get-tuple-element.131) | copy-start | bytes 772
  101.2 6.4 %collective-permute-start.4 = (f32[8,1,64]{2,0,1:T(8,128)S(1)}, f32[8,1,64]{2,0,1:T(8,128)S(1)}, u32[]{:S(2)}, u32[]{:S(2)}) collective-permute-start(f32[8,1,64]{2,0,1:T(8,128)S(1)} %convolution_bitcast_fusion.5), channel_id=1, source_target_pairs={{0,16},{4,20},{8,24},{12,28},{16,0},{20,4},{24,8},{28,12},{32,48},... | collective-permute-start | bytes 6152 | tf_op jit(solution)/shard_map/ppermute | solution.py:37
  103.4 51.8 %copy-start.93 = (f32[64]{0:T(128)S(1)}, f32[64]{0:T(128)}, u32[]{:S(2)}) copy-start(f32[64]{0:T(128)} %get-tuple-element.136) | copy-start | bytes 772
  103.4 51.8 %copy-start.94 = (f32[64]{0:T(128)S(1)}, f32[64]{0:T(128)}, u32[]{:S(2)}) copy-start(f32[64]{0:T(128)} %get-tuple-element.137) | copy-start | bytes 772
  103.4 51.8 %copy-start.115 = (f32[64]{0:T(128)S(1)}, f32[64]{0:T(128)}, u32[]{:S(2)}) copy-start(f32[64]{0:T(128)} %get-tuple-element.173) | copy-start | bytes 772
  107.6 15.0 %collective-permute-start.18 = (f32[8,1,64]{2,0,1:T(8,128)S(1)}, f32[8,1,64]{2,0,1:T(8,128)S(1)}, u32[]{:S(2)}, u32[]{:S(2)}) collective-permute-start(f32[8,1,64]{2,0,1:T(8,128)S(1)} %add.2369), channel_id=1, source_target_pairs={{0,464},{4,468},{8,472},{12,476},{16,480},{20,484},{24,488},{28,49... | collective-permute-start | bytes 6152 | tf_op jit(solution)/shard_map/ppermute | solution.py:33
  109.6 29.9 %collective-permute-start.15 = (f32[8,1,64]{2,0,1:T(8,128)S(1)}, f32[8,1,64]{2,0,1:T(8,128)S(1)}, u32[]{:S(2)}, u32[]{:S(2)}) collective-permute-start(f32[8,1,64]{2,0,1:T(8,128)S(1)} %add.2370), channel_id=1, source_target_pairs={{0,96},{4,100},{8,104},{12,108},{16,112},{20,116},{24,120},{28,124... | collective-permute-start | bytes 6152 | tf_op jit(solution)/shard_map/ppermute | solution.py:33
  112.9 51.5 %copy-start.114 = (f32[64]{0:T(128)S(1)}, f32[64]{0:T(128)}, u32[]{:S(2)}) copy-start(f32[64]{0:T(128)} %get-tuple-element.174) | copy-start | bytes 772
  112.9 29.8 %collective-permute-start.14 = (f32[8,1,64]{2,0,1:T(8,128)S(1)}, f32[8,1,64]{2,0,1:T(8,128)S(1)}, u32[]{:S(2)}, u32[]{:S(2)}) collective-permute-start(f32[8,1,64]{2,0,1:T(8,128)S(1)} %add.2370), channel_id=1, source_target_pairs={{0,416},{4,420},{8,424},{12,428},{16,432},{20,436},{24,440},{28,44... | collective-permute-start | bytes 6152 | tf_op jit(solution)/shard_map/ppermute | solution.py:33
  122.6 5.5 %collective-permute-start.13 = (f32[8,1,64]{2,0,1:T(8,128)S(1)}, f32[8,1,64]{2,0,1:T(8,128)S(1)}, u32[]{:S(2)}, u32[]{:S(2)}) collective-permute-start(f32[8,1,64]{2,0,1:T(8,128)S(1)} %add.2370), channel_id=1, source_target_pairs={{0,448},{4,452},{8,456},{12,460},{16,464},{20,468},{24,472},{28,47... | collective-permute-start | bytes 6152 | tf_op jit(solution)/shard_map/ppermute | solution.py:33
  124.8 48.1 %copy-start.113 = (f32[64]{0:T(128)S(1)}, f32[64]{0:T(128)}, u32[]{:S(2)}) copy-start(f32[64]{0:T(128)} %get-tuple-element.176) | copy-start | bytes 772
  128.1 9.4 %collective-permute-start.5 = (f32[8,1,64]{2,0,1:T(8,128)S(1)}, f32[8,1,64]{2,0,1:T(8,128)S(1)}, u32[]{:S(2)}, u32[]{:S(2)}) collective-permute-start(f32[8,1,64]{2,0,1:T(8,128)S(1)} %convolution_bitcast_fusion.4), channel_id=1, source_target_pairs={{0,32},{4,36},{8,40},{12,44},{16,48},{20,52},{24,56},{28,60},{32,0... | collective-permute-start | bytes 6152 | tf_op jit(solution)/shard_map/ppermute | solution.py:37
  131.7 47.9 %copy-start.112 = (f32[64]{0:T(128)S(1)}, f32[64]{0:T(128)}, u32[]{:S(2)}) copy-start(f32[64]{0:T(128)} %get-tuple-element.175) | copy-start | bytes 772
  137.5 228.7 %collective-permute-start.28 = (f32[11,62,64]{2,0,1:T(8,128)S(1)}, f32[11,62,64]{2,0,1:T(8,128)}, u32[]{:S(2)}, u32[]{:S(2)}) collective-permute-start(f32[11,62,64]{2,0,1:T(8,128)S(1)} %maximum_maximum_fusion), channel_id=1, source_target_pairs={{0,4},{4,8},{8,12},{12,16},{16,20},{20,24},{24,28},{28,32},{32,36}... | collective-permute-start | bytes 523784 | tf_op jit(solution)/shard_map/ppermute | solution.py:25
  139.5 9.4 %collective-permute-start.11 = (f32[8,1,64]{2,0,1:T(8,128)S(1)}, f32[8,1,64]{2,0,1:T(8,128)S(1)}, u32[]{:S(2)}, u32[]{:S(2)}) collective-permute-start(f32[8,1,64]{2,0,1:T(8,128)S(1)} %add.2371), channel_id=1, source_target_pairs={{0,192},{4,196},{8,200},{12,204},{16,208},{20,212},{24,216},{28,22... | collective-permute-start | bytes 6152 | tf_op jit(solution)/shard_map/ppermute | solution.py:33
  142.7 9.1 %collective-permute-start.10 = (f32[8,1,64]{2,0,1:T(8,128)S(1)}, f32[8,1,64]{2,0,1:T(8,128)S(1)}, u32[]{:S(2)}, u32[]{:S(2)}) collective-permute-start(f32[8,1,64]{2,0,1:T(8,128)S(1)} %add.2371), channel_id=1, source_target_pairs={{0,320},{4,324},{8,328},{12,332},{16,336},{20,340},{24,344},{28,34... | collective-permute-start | bytes 6152 | tf_op jit(solution)/shard_map/ppermute | solution.py:33
  148.8 36.9 %copy-start.111 = (f32[64]{0:T(128)S(1)}, f32[64]{0:T(128)}, u32[]{:S(2)}) copy-start(f32[64]{0:T(128)} %get-tuple-element.172) | copy-start | bytes 772
  148.8 10.4 %collective-permute-start.9 = (f32[8,1,64]{2,0,1:T(8,128)S(1)}, f32[8,1,64]{2,0,1:T(8,128)S(1)}, u32[]{:S(2)}, u32[]{:S(2)}) collective-permute-start(f32[8,1,64]{2,0,1:T(8,128)S(1)} %add.2371), channel_id=1, source_target_pairs={{0,384},{4,388},{8,392},{12,396},{16,400},{20,404},{24,408},{28,41... | collective-permute-start | bytes 6152 | tf_op jit(solution)/shard_map/ppermute | solution.py:33
  151.9 5.5 %collective-permute-start.6 = (f32[8,1,64]{2,0,1:T(8,128)S(1)}, f32[8,1,64]{2,0,1:T(8,128)S(1)}, u32[]{:S(2)}, u32[]{:S(2)}) collective-permute-start(f32[8,1,64]{2,0,1:T(8,128)S(1)} %convolution_bitcast_fusion.3), channel_id=1, source_target_pairs={{0,64},{4,68},{8,72},{12,76},{16,80},{20,84},{24,88},{28,92},{32,9... | collective-permute-start | bytes 6152 | tf_op jit(solution)/shard_map/ppermute | solution.py:37
  157.4 51.2 %collective-permute-start = (f32[11,768]{1,0:T(8,128)S(1)}, f32[11,768]{1,0:T(8,128)S(1)}, u32[]{:S(2)}, u32[]{:S(2)}) collective-permute-start(f32[11,768]{1,0:T(8,128)S(1)} %get-tuple-element.110), channel_id=1, source_target_pairs={{0,4},{4,8},{8,12},{12,16},{16,20},{20,24},{24,28},{28,32},{32,36}... | collective-permute-start | bytes 101384 | tf_op jit(solution)/shard_map/ppermute | solution.py:25
  159.3 9.4 %collective-permute-start.7 = (f32[8,1,64]{2,0,1:T(8,128)S(1)}, f32[8,1,64]{2,0,1:T(8,128)S(1)}, u32[]{:S(2)}, u32[]{:S(2)}) collective-permute-start(f32[8,1,64]{2,0,1:T(8,128)S(1)} %add.2372), channel_id=1, source_target_pairs={{0,256},{4,260},{8,264},{12,268},{16,272},{20,276},{24,280},{28,28... | collective-permute-start | bytes 6152 | tf_op jit(solution)/shard_map/ppermute | solution.py:33
  168.7 7.6 %collective-permute-start.8 = (f32[8,1,64]{2,0,1:T(8,128)S(1)}, f32[8,1,64]{2,0,1:T(8,128)S(1)}, u32[]{:S(2)}, u32[]{:S(2)}) collective-permute-start(f32[8,1,64]{2,0,1:T(8,128)S(1)} %add.2371), channel_id=1, source_target_pairs={{0,128},{4,132},{8,136},{12,140},{16,144},{20,148},{24,152},{28,15... | collective-permute-start | bytes 6152 | tf_op jit(solution)/shard_map/ppermute | solution.py:33
  176.3 6.7 %collective-permute-start.12 = (f32[8,1,64]{2,0,1:T(8,128)S(1)}, f32[8,1,64]{2,0,1:T(8,128)S(1)}, u32[]{:S(2)}, u32[]{:S(2)}) collective-permute-start(f32[8,1,64]{2,0,1:T(8,128)S(1)} %add.2370), channel_id=1, source_target_pairs={{0,64},{4,68},{8,72},{12,76},{16,80},{20,84},{24,88},{28,92},{32,9... | collective-permute-start | bytes 6152 | tf_op jit(solution)/shard_map/ppermute | solution.py:33
  183.0 11.5 %collective-permute-start.16 = (f32[8,1,64]{2,0,1:T(8,128)S(1)}, f32[8,1,64]{2,0,1:T(8,128)S(1)}, u32[]{:S(2)}, u32[]{:S(2)}) collective-permute-start(f32[8,1,64]{2,0,1:T(8,128)S(1)} %add.2369), channel_id=1, source_target_pairs={{0,32},{4,36},{8,40},{12,44},{16,48},{20,52},{24,56},{28,60},{32,6... | collective-permute-start | bytes 6152 | tf_op jit(solution)/shard_map/ppermute | solution.py:33
  194.5 9.7 %collective-permute-start.20 = (f32[8,1,64]{2,0,1:T(8,128)S(1)}, f32[8,1,64]{2,0,1:T(8,128)S(1)}, u32[]{:S(2)}, u32[]{:S(2)}) collective-permute-start(f32[8,1,64]{2,0,1:T(8,128)S(1)} %add.2368), channel_id=1, source_target_pairs={{0,16},{4,20},{8,24},{12,28},{16,32},{20,36},{24,40},{28,44},{32,4... | collective-permute-start | bytes 6152 | tf_op jit(solution)/shard_map/ppermute | solution.py:33
  204.2 4.3 %collective-permute-start.1 = (f32[11,768]{1,0:T(8,128)S(1)}, f32[11,768]{1,0:T(8,128)S(1)}, u32[]{:S(2)}, u32[]{:S(2)}) collective-permute-start(f32[11,768]{1,0:T(8,128)S(1)} %get-tuple-element.111), channel_id=1, source_target_pairs={{4,0},{8,4},{12,8},{16,12},{20,16},{24,20},{28,24},{32,28},{36,32}... | collective-permute-start | bytes 101384 | tf_op jit(solution)/shard_map/ppermute | solution.py:26
  208.9 158.1 %copy-start.26 = (f32[11,2,64]{2,0,1:T(8,128)S(1)}, f32[11,2,64]{2,0,1:T(8,128)}, u32[]{:S(2)}) copy-start(f32[11,2,64]{2,0,1:T(8,128)} %slice.1078) | copy-start | bytes 16900
  208.9 158.8 %copy-start.92 = (pred[2]{0:T(512)(128)(4,1)S(1)}, pred[2]{0:T(512)(128)(4,1)}, u32[]{:S(2)}) copy-start(pred[2]{0:T(512)(128)(4,1)} %compare_and_fusion.13) | copy-start | bytes 10
  208.9 160.3 %copy-start.91 = (pred[2]{0:T(512)(128)(4,1)S(1)}, pred[2]{0:T(512)(128)(4,1)}, u32[]{:S(2)}) copy-start(pred[2]{0:T(512)(128)(4,1)} %compare_and_fusion.14) | copy-start | bytes 10
  208.9 160.4 %copy-start.90 = (pred[2]{0:T(512)(128)(4,1)S(1)}, pred[2]{0:T(512)(128)(4,1)}, u32[]{:S(2)}) copy-start(pred[2]{0:T(512)(128)(4,1)} %broadcast_compare_fusion.2) | copy-start | bytes 10
  208.9 160.4 %copy-start.56 = (f32[2,64]{1,0:T(2,128)S(1)}, f32[2,64]{1,0:T(2,128)}, u32[]{:S(2)}) copy-start(f32[2,64]{1,0:T(2,128)} %copy-done.55) | copy-start | bytes 1540
  208.9 160.4 %copy-start.58 = (f32[2,64]{1,0:T(2,128)S(1)}, f32[2,64]{1,0:T(2,128)}, u32[]{:S(2)}) copy-start(f32[2,64]{1,0:T(2,128)} %copy-done.57) | copy-start | bytes 1540
  208.9 160.4 %copy-start.60 = (f32[2,64]{1,0:T(2,128)S(1)}, f32[2,64]{1,0:T(2,128)}, u32[]{:S(2)}) copy-start(f32[2,64]{1,0:T(2,128)} %copy-done.59) | copy-start | bytes 1540
  (88 other events, 407.5 us)
where the time goes:
time: 417 us; the launch traced here: 410 us
  starting transfers between devices  119 us (29%)
  matrix products  111 us (27%)
  other arithmetic  68.3 us (16%)
  local copies, waits for them, and re-layouts  64.7 us (16%)
  waiting for transfers between devices  43 us (10%)
    ppermute x21, starting transfers between devices, passed_along(): lax.ppermute(array, axis, [(i, (i + by) % length) for i in range(length)])  93.3 us
    dot_general x32, matrix products, near_box(): jnp.einsum('qns,nst->qt', near_values, kernel_block, precision=PRECISE)  68.9 us
    ppermute x21, waiting for transfers between devices, passed_along(): lax.ppermute(array, axis, [(i, (i + by) % length) for i in range(length)])  28.5 us
    select_n x64, other arithmetic, near_box(): near_tiles = jnp.take(extended, slot_index, axis=1)  24.4 us
    and x32, other arithmetic, near_box(): near_tiles = jnp.take(extended, slot_index, axis=1)  22.1 us
    mul x32, local copies, waits for them, and re-layouts, near_box(): near_values = near_tiles[:rows_here] * slot_mask[None, :, None]  21.7 us
    gather x32, local copies, waits for them, and re-layouts, near_box(): near_tiles = jnp.take(extended, slot_index, axis=1)  17.8 us
    ppermute x5, waiting for transfers between devices, from_partner(): lax.ppermute(array, axis, [(i, i ^ 1 << distance) for i in range(lax.axis...  14.6 us
  transfers between devices with their start and end apart: 30, of which 10 were waited for; matrix products, arithmetic and copies ran while one was open for 45% of the time, Pallas kernels for 0%

commit v1 on v0

--- a/solution.py
+++ b/solution.py
@@ -26,15 +26,6 @@
         after = lax.ppermute(initial, axis, down)
         array = jnp.concatenate([before, array, after], axis=dim)
     return array
-
-
-def passed_along(array, axis, by):
-    length = lax.axis_size(axis)
-    return lax.ppermute(array, axis, [(i, (i + by) % length) for i in range(length)])
-
-
-def from_partner(array, axis, distance):
-    return lax.ppermute(array, axis, [(i, i ^ 1 << distance) for i in range(lax.axis_size(axis))])
 
 
 def kernel_matrix(left_points, right_points, kernel_scale):
@@ -147,61 +138,47 @@
             )
         local_couplings.append(coupling)
 
-    def top_sources(height):
+    top_levels = tree_depth - 1
+    level_points = []
+    for height in range(top_levels):
+        offset = 2 * groups - 2 * (groups >> height)
+        level_points.append(top_points[:, offset : offset + (groups >> height), :])
+    level_moments_top = [
+        lax.all_gather(level_moments[local_depth], "boxes", axis=1, tiled=True)
+    ]
+    edge_maps = []
+    for height in range(top_levels - 1):
+        interp_map = interpolation(
+            level_points[height], jnp.repeat(level_points[height + 1], 2, axis=1), kernel_scale
+        )
+        edge_maps.append(interp_map)
+        lifted = jnp.einsum("qnr,nrs->qns", level_moments_top[-1], interp_map, precision=PRECISE)
+        level_moments_top.append(lifted.reshape(rows_here, -1, 2, R).sum(axis=2))
+    top_couplings = []
+    for height in range(top_levels):
         number = groups >> height
         node = device // 2**height
         third = jnp.where(node % 2 == 0, node + 3, node - 3) % number
         if number > 4:
-            return [(node - 2) % number, (node + 2) % number, third]
-        return [None, (node + 2) % number, None]
-
-    own_edges = []
-    for height in range(tree_depth - 2):
-        own_edges.append(
-            interpolation(
-                node_proxy(height, device // 2**height),
-                node_proxy(height + 1, device // 2 ** (height + 1)),
-                kernel_scale,
+            source_ids = [(node - 2) % number, (node + 2) % number, third]
+        else:
+            source_ids = [(node + 2) % number]
+        target_points = lax.dynamic_slice_in_dim(level_points[height], node, 1, 1)
+        coupling = jnp.zeros((rows_here, 1, R), jnp.float32)
+        for source in source_ids:
+            kernel_block = kernel_matrix(
+                lax.dynamic_slice_in_dim(level_points[height], source, 1, 1), target_points, kernel_scale
             )
-        )
-    cousin_moments = []
-
-    def remote(moment, distance):
-        return passed_along(moment, "boxes", distance)
-
-    top_moments = [level_moments[local_depth]]
-    for height in range(tree_depth - 2):
-        lifted = jnp.einsum("qnr,nrs->qns", top_moments[-1], own_edges[height], precision=PRECISE)
-        top_moments.append(lifted + from_partner(lifted, "boxes", height))
-    for height in range(tree_depth - 1):
-        stride = 2**height
-        node = device // stride
-        moment = top_moments[height]
-        if groups >> height > 4:
-            third = jnp.where(
-                node % 2 == 0, remote(moment, -3 * stride), remote(moment, 3 * stride)
+            source_moment = lax.dynamic_slice_in_dim(level_moments_top[height], source, 1, 1)
+            coupling = coupling + jnp.einsum(
+                "qnr,nrs->qns", source_moment, kernel_block, precision=PRECISE
             )
-            cousin_moments.append([remote(moment, 2 * stride), remote(moment, -2 * stride), third])
-        else:
-            cousin_moments.append([None, remote(moment, -2 * stride), None])
-    top_couplings = []
-    for height in range(tree_depth - 1):
-        source_ids = top_sources(height)
-        target_points = node_proxy(height, device // 2**height)
-        coupling = jnp.zeros((rows_here, 1, R), jnp.float32)
-        for slot in range(3):
-            if source_ids[slot] is not None:
-                kernel_block = kernel_matrix(
-                    node_proxy(height, source_ids[slot]), target_points, kernel_scale
-                )
-                coupling = coupling + jnp.einsum(
-                    "qnr,nrs->qns", cousin_moments[height][slot], kernel_block, precision=PRECISE
-                )
         top_couplings.append(coupling)
     descent = top_couplings[-1]
-    for height in range(tree_depth - 3, -1, -1):
+    for height in range(top_levels - 2, -1, -1):
+        own_edge = lax.dynamic_slice_in_dim(edge_maps[height], device // 2**height, 1, 0)
         descent = (
-            jnp.einsum("qns,nrs->qnr", descent, own_edges[height], precision=PRECISE)
+            jnp.einsum("qns,nrs->qnr", descent, own_edge, precision=PRECISE)
             + top_couplings[height]
         )
     for height in range(local_depth - 1, -1, -1):

time: 417 us -> 410 us (0.983)
  starting transfers between devices: 119 us -> 24.1 us
  blocking collectives: 0 us -> 47.2 us
  waiting for transfers between devices: 43 us -> 0.01 us
  local copies, waits for them, and re-layouts: 64.7 us -> 95.9 us
  matrix products: 111 us -> 138 us
  other arithmetic: 68.3 us -> 92.4 us
    ppermute x26 -> x0, starting transfers between devices: 106 us -> none  [the longest x21 93.3 us: passed_along(): lax.ppermute(array, axis, [(i, (i + by) % length) for i in range(length)])]
    all_gather x0 -> x1, blocking collectives: none -> 47.2 us  [body(): lax.all_gather(level_moments[local_depth], 'boxes', axis=1, tiled=True)]
    ppermute x26 -> x0, waiting for transfers between devices: 43 us -> none  [the longest x21 28.5 us: passed_along(): lax.ppermute(array, axis, [(i, (i + by) % length) for i in range(length)])]
    slice x37 -> x42, local copies, waits for them, and re-layouts: 1.21 us -> 27.3 us  [kernel_matrix(): right_points[0][..., None, :]]
    dot_general x26 -> x10, matrix products: 8.93 us -> 24.2 us  [the longest x5 20.4 us: body(): jnp.einsum('qnr,nrs->qns', level_moments_top[-1], interp_map, precision=P...]
    div x0 -> x5, other arithmetic: none -> 13.9 us  [interpolation(): return values / jnp.sum(values, axis=-1, keepdims=True)]
    dot_general x15 -> x31, matrix products: 14.2 us -> 26.9 us  [body(): jnp.einsum('qnr,nrs->qns', source_moment, kernel_block, precision=PRECISE)]
    ppermute x2, starting transfers between devices: 9.25 us -> 20.3 us  [with_halo(): after = lax.ppermute(initial, axis, down)]
  transfers between devices with their start and end apart: 30 -> 4, of which waited for: 10 -> 0; matrix products, arithmetic and copies ran while one was open for 45% -> 66% of each run, Pallas kernels for 0% -> 0%
where the time goes in v1:
time: 410 us; the launch traced here: 402 us
  matrix products  138 us (34%)
  local copies, waits for them, and re-layouts  95.9 us (23%)
  other arithmetic  92.4 us (23%)
  blocking collectives  47.2 us (12%)
  starting transfers between devices  24.1 us (6%)
    dot_general x32, matrix products, near_box(): jnp.einsum('qns,nst->qt', near_values, kernel_block, precision=PRECISE)  68.9 us
    all_gather x1, blocking collectives, body(): lax.all_gather(level_moments[local_depth], 'boxes', axis=1, tiled=True)  47.2 us
    slice x42, local copies, waits for them, and re-layouts, kernel_matrix(): right_points[0][..., None, :]  27.3 us
    dot_general x31, matrix products, body(): jnp.einsum('qnr,nrs->qns', source_moment, kernel_block, precision=PRECISE)  26.9 us
    select_n x64, other arithmetic, near_box(): near_tiles = jnp.take(extended, slot_index, axis=1)  24.3 us
    and x32, other arithmetic, near_box(): near_tiles = jnp.take(extended, slot_index, axis=1)  21.9 us
    mul x32, local copies, waits for them, and re-layouts, near_box(): near_values = near_tiles[:rows_here] * slot_mask[None, :, None]  21.8 us
    dot_general x5, matrix products, body(): jnp.einsum('qnr,nrs->qns', level_moments_top[-1], interp_map, precision=P...  20.4 us
  transfers between devices with their start and end apart: 4, of which 0 were waited for; matrix products, arithmetic and copies ran while one was open for 66% of the time, Pallas kernels for 0%

profile of v1, /device:TPU:6, one launch (start us, length us, event | category | flops | bytes accessed | tf_op | source)
XLA Modules:
  0.0 402.4 jit_solution(18085279957621713053)
XLA Ops:
  3.1 1.3 slice_reduce_fusion.2
  5.6 3.8 constant_dynamic-update-slice_fusion.6
  9.6 1.4 divide_reduce_fusion.4
  11.0 2.6 bitcast_reduce_fusion.3
  14.4 1.3 bitcast_reduce_fusion.5
  18.6 13.3 %collective-permute-start.3 = (f32[11,62,64]{2,0,1:T(8,128)S(1)}, f32[11,62,64]{2,0,1:T(8,128)}, u32[]{:S(2)}, u32[]{:S(2)}) collective-permute-start(f32[11,62,64]{2,0,1:T(8,128)S(1)} %maximum_maximum_fusion), channel_id=1, source_target_pairs={{4,0},{8,4},{12,8},{16,12},{20,16},{24,20},{28,24},{32,28},{36,32}... | collective-permute-start | bytes 523784 | tf_op jit(solution)/shard_map/ppermute | solution.py:26
  31.9 1.9 collective-permute-start.2
  34.6 1.9 collective-permute-start
  36.5 7.0 %collective-permute-start.1 = (f32[11,768]{1,0:T(8,128)}, f32[11,768]{1,0:T(8,128)}, u32[]{:S(2)}, u32[]{:S(2)}) collective-permute-start(f32[11,768]{1,0:T(8,128)} %get-tuple-element.106), channel_id=1, source_target_pairs={{4,0},{8,4},{12,8},{16,12},{20,16},{24,20},{28,24},{32,28},{36,32}... | collective-permute-start | bytes 101384 | tf_op jit(solution)/shard_map/ppermute | solution.py:26
  62.4 47.2 %all-gather.1 = f32[128,64,8]{1,2,0:T(8,128)S(1)} all-gather(f32[1,64,8]{1,2,0:T(8,128)S(1)} %convolution_bitcast_fusion.3), channel_id=2, replica_groups=mesh['boxes'=128,'probe'=4] {'boxes'}, dimensions={0}, use_global_device_ids=true | all-gather | bytes 264192 | tf_op jit(solution)/shard_map/all_gather | solution.py:147
  110.2 5.6 %divide_reduce_fusion = f32[128,64]{1,0:T(8,128)S(1)} fusion(f32[128,64]{1,0:T(8,128)S(1)} %bitcast.618, f32[128,64]{1,0:T(8,128)S(1)} %get-tuple-element.123, f32[128,64]{1,0:T(8,128)S(1)} %bitcast.621, f32[128,64]{1,0:T(8,128)S(1)} %get-tuple-element.124, f32[128,64]{1,0:T(8,128)S(1)} %bitcast.615, f32[128,64]{1,0:T(8,128)S(1)} %get-tuple-element.122), kind=kLoop, calls=%fused_computation.49 | loop fusion | flops 6283264 | bytes 229376 | tf_op jit(solution)/shard_map/reduce_sum | solution.py:40
  115.8 6.3 %multiply_divide_fusion = f32[128,64,64]{2,1,0:T(8,128)} fusion(f32[128,64]{1,0:T(8,128)S(1)} %divide_reduce_fusion, f32[128,64]{1,0:T(8,128)S(1)} %bitcast.619, f32[128,64]{1,0:T(8,128)S(1)} %get-tuple-element.123, f32[128,64]{1,0:T(8,128)S(1)} %bitcast.622, f32[128,64]{1,0:T(8,128)S(1)} %get-tuple-element.124, f32[128,64]{1,0:T(8,128)S(1)} %bitcast.616, ...), kind=kLoop, calls=%fused_computation.47 | loop fusion | flops 6291456 | bytes 2326528 | tf_op jit(solution)/shard_map/div | solution.py:40
  122.0 10.2 %bitcast_reduce_fusion = f32[8,64,64]{2,0,1:T(8,128)S(1)} fusion(f32[8,128,64]{2,1,0:T(8,128)S(1)} %reshape.5058, f32[128,64]{1,0:T(8,128)S(1)} %divide_reduce_fusion, f32[128,64]{1,0:T(8,128)S(1)} %bitcast.620, f32[128,64]{1,0:T(8,128)S(1)} %get-tuple-element.123, f32[128,64]{1,0:T(8,128)S(1)} %bitcast.623, f32[128,64]{1,0:T(8,128)S(1)} %get-tuple-element.124, ...), kind=kOutput, calls=%fused_computation.131 | convolution fusion | flops 56655872 | bytes 622592 | tf_op jit(solution)/shard_map/qnr,nrs->qns/dot_general | solution.py:155
  132.4 2.7 divide_reduce_fusion.1
  135.1 3.1 multiply_divide_fusion.1
  138.4 5.1 %bitcast_reduce_fusion.1 = f32[8,32,64]{2,0,1:T(8,128)S(1)} fusion(f32[8,64,64]{2,0,1:T(8,128)S(1)} %bitcast_reduce_fusion, f32[64,64]{1,0:T(8,128)S(1)} %divide_reduce_fusion.1, f32[64,64]{1,0:T(8,128)S(1)} %bitcast.630, f32[64,64]{1,0:T(8,128)S(1)} %copy-done.5, f32[64,64]{1,0:T(8,128)S(1)} %bitcast.633, f32[64,64]{1,0:T(8,128)S(1)} %copy-done.7, ...), kind=kOutput, calls=%fused_computation.189 | convolution fusion | flops 28327936 | bytes 311296 | tf_op jit(solution)/shard_map/qnr,nrs->qns/dot_general | solution.py:155
  143.6 1.4 divide_reduce_fusion.3
  144.9 2.1 multiply_divide_fusion.3
  147.0 2.6 bitcast_reduce_fusion.2
  150.4 1.4 multiply_divide_fusion.7
  151.8 1.3 bitcast_reduce_fusion.4
  153.7 1.2 bitcast_reduce_fusion.6
  175.3 182.3 %while.10 = (s32[]{:T(128)}, f32[32,8,256]{2,1,0:T(8,128)}, s32[32,6]{1,0:T(8,128)}, f32[11,38,256]{2,0,1:T(8,128)S(1)}, f32[32,6]{1,0:T(8,128)}, /*index=5*/f32...) while((s32[]{:T(128)}, f32[32,8,256]{2,1,0:T(8,128)}, s32[32,6]{1,0:T(8,128)}, ...), condition=%wide.region_1.2_spmd, body=%wide.region_0.1_spmd.sunk | while | flops 42104376 | bytes 440149 | solution.py:66
  178.8 2.2 fusion.862
  184.5 2.2 fusion.862
  190.2 2.2 fusion.862
  195.8 2.2 fusion.862
  201.5 2.2 fusion.862
  207.2 2.2 fusion.862
  212.8 2.2 fusion.862
  218.5 2.2 fusion.862
  224.2 2.2 fusion.862
  229.9 2.2 fusion.862
  235.6 2.2 fusion.862
  241.3 2.2 fusion.862
  247.1 2.2 fusion.862
  252.8 2.2 fusion.862
  258.5 2.2 fusion.862
  264.2 2.2 fusion.862
  269.9 2.2 fusion.862
  275.6 2.2 fusion.862
  281.3 2.2 fusion.862
  287.0 2.2 fusion.862
  292.6 2.2 fusion.862
  298.3 2.2 fusion.862
  304.0 2.2 fusion.862
  309.7 2.2 fusion.862
  315.4 2.2 fusion.862
  321.1 2.2 fusion.862
  326.8 2.2 fusion.862
  332.6 2.2 fusion.862
  338.3 2.2 fusion.862
  344.0 2.2 fusion.862
  349.7 2.2 fusion.862
  355.4 2.2 fusion.862
  383.2 1.6 fusion.145
  384.8 1.2 fusion.102
  386.0 1.2 convolution_add_fusion.4
  387.2 2.3 fusion.54
  389.6 2.3 convolution_add_fusion.1
  391.9 2.3 convolution_add_fusion
  394.3 1.2 fusion.19
  395.6 3.2 fusion.17
  398.9 2.7 fusion.16
  (824 shorter events, 186.3 us)
Async XLA Ops:
  0.9 59.6 %copy-start.82 = (f32[2,64]{1,0:T(2,128)}, f32[2,64]{1,0:T(2,128)S(1)}, u32[]{:S(2)}) copy-start(f32[2,64]{1,0:T(2,128)S(1)} %get-tuple-element.194) | copy-start | bytes 1540
  0.9 59.6 %copy-start.84 = (f32[2,64]{1,0:T(2,128)}, f32[2,64]{1,0:T(2,128)S(1)}, u32[]{:S(2)}) copy-start(f32[2,64]{1,0:T(2,128)S(1)} %get-tuple-element.195) | copy-start | bytes 1540
  0.9 59.6 %copy-start.86 = (f32[2,64]{1,0:T(2,128)}, f32[2,64]{1,0:T(2,128)S(1)}, u32[]{:S(2)}) copy-start(f32[2,64]{1,0:T(2,128)S(1)} %get-tuple-element.196) | copy-start | bytes 1540
  0.9 17.1 %copy-start.66 = (f32[4,64]{1,0:T(4,128)}, f32[4,64]{1,0:T(4,128)S(1)}, u32[]{:S(2)}) copy-start(f32[4,64]{1,0:T(4,128)S(1)} %get-tuple-element.197) | copy-start | bytes 3076
  0.9 17.0 %copy-start.68 = (f32[4,64]{1,0:T(4,128)}, f32[4,64]{1,0:T(4,128)S(1)}, u32[]{:S(2)}) copy-start(f32[4,64]{1,0:T(4,128)S(1)} %get-tuple-element.198) | copy-start | bytes 3076
  0.9 17.0 %copy-start.70 = (f32[4,64]{1,0:T(4,128)}, f32[4,64]{1,0:T(4,128)S(1)}, u32[]{:S(2)}) copy-start(f32[4,64]{1,0:T(4,128)S(1)} %get-tuple-element.199) | copy-start | bytes 3076
  0.9 15.2 %copy-start.52 = (f32[8,64]{1,0:T(8,128)}, f32[8,64]{1,0:T(8,128)S(1)}, u32[]{:S(2)}) copy-start(f32[8,64]{1,0:T(8,128)S(1)} %get-tuple-element.200) | copy-start | bytes 6148
  0.9 15.2 %copy-start.54 = (f32[8,64]{1,0:T(8,128)}, f32[8,64]{1,0:T(8,128)S(1)}, u32[]{:S(2)}) copy-start(f32[8,64]{1,0:T(8,128)S(1)} %get-tuple-element.201) | copy-start | bytes 6148
  1.0 15.2 %copy-start.56 = (f32[8,64]{1,0:T(8,128)}, f32[8,64]{1,0:T(8,128)S(1)}, u32[]{:S(2)}) copy-start(f32[8,64]{1,0:T(8,128)S(1)} %get-tuple-element.202) | copy-start | bytes 6148
  1.0 13.4 %copy-start.30 = (f32[16,64]{1,0:T(8,128)}, f32[16,64]{1,0:T(8,128)S(1)}, u32[]{:S(2)}) copy-start(f32[16,64]{1,0:T(8,128)S(1)} %get-tuple-element.203) | copy-start | bytes 12292
  1.0 13.4 %copy-start.32 = (f32[16,64]{1,0:T(8,128)}, f32[16,64]{1,0:T(8,128)S(1)}, u32[]{:S(2)}) copy-start(f32[16,64]{1,0:T(8,128)S(1)} %get-tuple-element.204) | copy-start | bytes 12292
  1.0 13.4 %copy-start.34 = (f32[16,64]{1,0:T(8,128)}, f32[16,64]{1,0:T(8,128)S(1)}, u32[]{:S(2)}) copy-start(f32[16,64]{1,0:T(8,128)S(1)} %get-tuple-element.205) | copy-start | bytes 12292
  2.9 8.0 %copy-start.16 = (f32[32,64]{1,0:T(8,128)}, f32[32,64]{1,0:T(8,128)S(1)}, u32[]{:S(2)}) copy-start(f32[32,64]{1,0:T(8,128)S(1)} %sub.2636) | copy-start | bytes 24580
  3.0 8.0 %copy-start.18 = (f32[32,64]{1,0:T(8,128)}, f32[32,64]{1,0:T(8,128)S(1)}, u32[]{:S(2)}) copy-start(f32[32,64]{1,0:T(8,128)S(1)} %sub.2641) | copy-start | bytes 24580
  3.1 7.9 %copy-start.20 = (f32[32,64]{1,0:T(8,128)}, f32[32,64]{1,0:T(8,128)S(1)}, u32[]{:S(2)}) copy-start(f32[32,64]{1,0:T(8,128)S(1)} %sub.2646) | copy-start | bytes 24580
  15.7 18.2 %copy-start.1 = (f32[8,8192]{1,0:T(8,128)S(1)}, f32[8,8192]{1,0:T(8,128)}, u32[]{:S(2)}) copy-start(f32[8,8192]{1,0:T(8,128)} %param.19) | copy-start | bytes 786436
  15.7 18.2 %copy-start.8 = (f32[3,8192]{1,0:T(4,128)S(1)}, f32[3,8192]{1,0:T(4,128)}, u32[]{:S(2)}) copy-start(f32[3,8192]{1,0:T(4,128)} %param.20) | copy-start | bytes 294916
  17.6 32.0 %copy-start.96 = (s32[32,3]{0,1:T(4,128)S(1)}, s32[32,3]{0,1:T(4,128)}, u32[]{:S(2)}) copy-start(s32[32,3]{0,1:T(4,128)} %param.25) | copy-start | bytes 1156
  17.6 33.2 %copy-start.97 = (s32[32,6]{0,1:T(8,128)S(1)}, s32[32,6]{0,1:T(8,128)}, u32[]{:S(2)}) copy-start(s32[32,6]{0,1:T(8,128)} %param.21) | copy-start | bytes 2308
  17.6 34.5 %copy-start.15 = (f32[3,16128]{1,0:T(4,128)S(1)}, f32[3,16128]{1,0:T(4,128)}, u32[]{:S(2)}) copy-start(f32[3,16128]{1,0:T(4,128)} %param.24) | copy-start | bytes 580612
  17.6 33.9 %copy-start.90 = (f32[2,2,64]{2,1,0:T(2,128)}, f32[2,2,64]{2,1,0:T(2,128)S(1)}, u32[]{:S(2)}) copy-start(f32[2,2,64]{2,1,0:T(2,128)S(1)} %broadcast_in_dim.234) | copy-start | bytes 3076
  17.7 33.8 %copy-start.92 = (f32[2,2,64]{2,1,0:T(2,128)}, f32[2,2,64]{2,1,0:T(2,128)S(1)}, u32[]{:S(2)}) copy-start(f32[2,2,64]{2,1,0:T(2,128)S(1)} %broadcast_in_dim.238) | copy-start | bytes 3076
  17.7 33.8 %copy-start.94 = (f32[2,2,64]{2,1,0:T(2,128)}, f32[2,2,64]{2,1,0:T(2,128)S(1)}, u32[]{:S(2)}) copy-start(f32[2,2,64]{2,1,0:T(2,128)S(1)} %broadcast_in_dim.236) | copy-start | bytes 3076
  18.6 338.9 %collective-permute-start.3 = (f32[11,62,64]{2,0,1:T(8,128)S(1)}, f32[11,62,64]{2,0,1:T(8,128)}, u32[]{:S(2)}, u32[]{:S(2)}) collective-permute-start(f32[11,62,64]{2,0,1:T(8,128)S(1)} %maximum_maximum_fusion), channel_id=1, source_target_pairs={{4,0},{8,4},{12,8},{16,12},{20,16},{24,20},{28,24},{32,28},{36,32}... | collective-permute-start | bytes 523784 | tf_op jit(solution)/shard_map/ppermute | solution.py:26
  31.9 326.4 %collective-permute-start.2 = (f32[11,62,64]{2,0,1:T(8,128)S(1)}, f32[11,62,64]{2,0,1:T(8,128)}, u32[]{:S(2)}, u32[]{:S(2)}) collective-permute-start(f32[11,62,64]{2,0,1:T(8,128)S(1)} %maximum_maximum_fusion), channel_id=1, source_target_pairs={{0,4},{4,8},{8,12},{12,16},{16,20},{20,24},{24,28},{28,32},{32,36}... | collective-permute-start | bytes 523784 | tf_op jit(solution)/shard_map/ppermute | solution.py:25
  34.6 139.5 %collective-permute-start = (f32[11,768]{1,0:T(8,128)}, f32[11,768]{1,0:T(8,128)}, u32[]{:S(2)}, u32[]{:S(2)}) collective-permute-start(f32[11,768]{1,0:T(8,128)} %get-tuple-element.105), channel_id=1, source_target_pairs={{0,4},{4,8},{8,12},{12,16},{16,20},{20,24},{24,28},{28,32},{32,36}... | collective-permute-start | bytes 101384 | tf_op jit(solution)/shard_map/ppermute | solution.py:25
  36.5 137.6 %collective-permute-start.1 = (f32[11,768]{1,0:T(8,128)}, f32[11,768]{1,0:T(8,128)}, u32[]{:S(2)}, u32[]{:S(2)}) collective-permute-start(f32[11,768]{1,0:T(8,128)} %get-tuple-element.106), channel_id=1, source_target_pairs={{4,0},{8,4},{12,8},{16,12},{20,16},{24,20},{28,24},{32,28},{36,32}... | collective-permute-start | bytes 101384 | tf_op jit(solution)/shard_map/ppermute | solution.py:26
  52.3 57.5 %copy-start = (f32[3,252,64]{2,1,0:T(8,128)}, f32[3,252,64]{2,1,0:T(8,128)S(1)}, u32[]{:S(2)}) copy-start(f32[3,252,64]{2,1,0:T(8,128)S(1)} %reshape.4884) | copy-start | bytes 580612
  53.0 9.4 %copy-start.36 = (f32[8,64]{1,0:T(8,128)}, f32[8,64]{1,0:T(8,128)S(1)}, u32[]{:S(2)}) copy-start(f32[8,64]{1,0:T(8,128)S(1)} %get-tuple-element.114) | copy-start | bytes 6148
  53.0 9.4 %copy-start.38 = (f32[8,64]{1,0:T(8,128)}, f32[8,64]{1,0:T(8,128)S(1)}, u32[]{:S(2)}) copy-start(f32[8,64]{1,0:T(8,128)S(1)} %get-tuple-element.115) | copy-start | bytes 6148
  53.6 78.7 %copy-start.9 = (f32[32,64]{1,0:T(8,128)}, f32[32,64]{1,0:T(8,128)S(1)}, u32[]{:S(2)}) copy-start(f32[32,64]{1,0:T(8,128)S(1)} %get-tuple-element.119) | copy-start | bytes 24580
  53.6 78.7 %copy-start.11 = (f32[32,64]{1,0:T(8,128)}, f32[32,64]{1,0:T(8,128)S(1)}, u32[]{:S(2)}) copy-start(f32[32,64]{1,0:T(8,128)S(1)} %get-tuple-element.120) | copy-start | bytes 24580
  53.6 78.8 %copy-start.13 = (f32[32,64]{1,0:T(8,128)}, f32[32,64]{1,0:T(8,128)S(1)}, u32[]{:S(2)}) copy-start(f32[32,64]{1,0:T(8,128)S(1)} %get-tuple-element.121) | copy-start | bytes 24580
  53.6 78.8 %copy-start.4 = (f32[64,64]{1,0:T(8,128)}, f32[64,64]{1,0:T(8,128)S(1)}, u32[]{:S(2)}) copy-start(f32[64,64]{1,0:T(8,128)S(1)} %get-tuple-element.126) | copy-start | bytes 49156
  53.6 78.8 %copy-start.6 = (f32[64,64]{1,0:T(8,128)}, f32[64,64]{1,0:T(8,128)S(1)}, u32[]{:S(2)}) copy-start(f32[64,64]{1,0:T(8,128)S(1)} %get-tuple-element.127) | copy-start | bytes 49156
  110.1 12.0 %copy-start.3 = (f32[8,128,64]{2,1,0:T(8,128)}, f32[8,128,64]{2,1,0:T(8,128)S(1)}, u32[]{:S(2)}) copy-start(f32[8,128,64]{2,1,0:T(8,128)S(1)} %reshape.5058) | copy-start | bytes 786436
  132.3 11.2 %copy-start.132 = (f32[8,64,64]{2,0,1:T(8,128)}, f32[8,64,64]{2,0,1:T(8,128)S(1)}, u32[]{:S(2)}) copy-start(f32[8,64,64]{2,0,1:T(8,128)S(1)} %bitcast_reduce_fusion) | copy-start | bytes 393220
  143.5 6.1 %copy-start.133 = (f32[8,32,64]{2,0,1:T(8,128)}, f32[8,32,64]{2,0,1:T(8,128)S(1)}, u32[]{:S(2)}) copy-start(f32[8,32,64]{2,0,1:T(8,128)S(1)} %bitcast_reduce_fusion.1) | copy-start | bytes 196612
  151.8 6.7 %slice-start = ((f32[3,252,64]{2,1,0:T(8,128)}), f32[3,8,64]{2,1,0:T(8,128)S(1)}, s32[]{:S(2)}) async-start(f32[3,252,64]{2,1,0:T(8,128)} %copy-done), calls=%async_computation | async-start | bytes 24576 | tf_op jit(solution)/shard_map/slice | solution.py:145
  151.8 6.7 %slice-start.2 = ((f32[3,252,64]{2,1,0:T(8,128)}), f32[3,32,64]{2,1,0:T(8,128)S(1)}, s32[]{:S(2)}) async-start(f32[3,252,64]{2,1,0:T(8,128)} %copy-done), calls=%async_computation.2 | async-start | bytes 98304 | tf_op jit(solution)/shard_map/slice | solution.py:145
  153.7 8.6 %slice-start.1 = ((f32[3,252,64]{2,1,0:T(8,128)}), f32[3,16,64]{2,1,0:T(8,128)S(1)}, s32[]{:S(2)}) async-start(f32[3,252,64]{2,1,0:T(8,128)} %copy-done), calls=%async_computation.1 | async-start | bytes 49152 | tf_op jit(solution)/shard_map/slice | solution.py:145
  153.7 8.6 %slice-start.3 = ((f32[3,252,64]{2,1,0:T(8,128)}), f32[3,64,64]{2,1,0:T(8,128)S(1)}, s32[]{:S(2)}) async-start(f32[3,252,64]{2,1,0:T(8,128)} %copy-done), calls=%async_computation.3 | async-start | bytes 196608 | tf_op jit(solution)/shard_map/slice | solution.py:145
  154.9 18.5 %copy-start.83 = (f32[2,64]{1,0:T(2,128)S(1)}, f32[2,64]{1,0:T(2,128)}, u32[]{:S(2)}) copy-start(f32[2,64]{1,0:T(2,128)} %copy-done.82) | copy-start | bytes 1540
  154.9 18.5 %copy-start.85 = (f32[2,64]{1,0:T(2,128)S(1)}, f32[2,64]{1,0:T(2,128)}, u32[]{:S(2)}) copy-start(f32[2,64]{1,0:T(2,128)} %copy-done.84) | copy-start | bytes 1540
  154.9 18.6 %copy-start.87 = (f32[2,64]{1,0:T(2,128)S(1)}, f32[2,64]{1,0:T(2,128)}, u32[]{:S(2)}) copy-start(f32[2,64]{1,0:T(2,128)} %copy-done.86) | copy-start | bytes 1540
  155.0 18.6 %copy-start.107 = (f32[64]{0:T(128)S(1)}, f32[64]{0:T(128)}, u32[]{:S(2)}) copy-start(f32[64]{0:T(128)} %copy-done.106) | copy-start | bytes 772
  155.0 18.6 %copy-start.109 = (f32[64]{0:T(128)S(1)}, f32[64]{0:T(128)}, u32[]{:S(2)}) copy-start(f32[64]{0:T(128)} %copy-done.108) | copy-start | bytes 772
  155.0 18.6 %copy-start.111 = (f32[64]{0:T(128)S(1)}, f32[64]{0:T(128)}, u32[]{:S(2)}) copy-start(f32[64]{0:T(128)} %copy-done.110) | copy-start | bytes 772
  155.0 18.6 %copy-start.113 = (f32[2,64]{1,0:T(2,128)S(1)}, f32[2,64]{1,0:T(2,128)}, u32[]{:S(2)}) copy-start(f32[2,64]{1,0:T(2,128)} %copy-done.112) | copy-start | bytes 1540
  158.6 15.3 %copy-start.126 = (s32[4]{0:T(128)S(1)}, s32[4]{0:T(128)}, u32[]{:S(2)}) copy-start(s32[4]{0:T(128)} %compare_select_fusion.13) | copy-start | bytes 52
  158.6 15.3 %copy-start.127 = (s32[8]{0:T(128)S(1)}, s32[8]{0:T(128)}, u32[]{:S(2)}) copy-start(s32[8]{0:T(128)} %compare_select_fusion.10) | copy-start | bytes 100
  158.6 15.3 %copy-start.105 = (s32[32]{0:T(128)S(1)}, s32[32]{0:T(128)}, u32[]{:S(2)}) copy-start(s32[32]{0:T(128)} %get-tuple-element.257) | copy-start | bytes 388
  158.6 15.3 %copy-start.125 = (s32[16]{0:T(128)S(1)}, s32[16]{0:T(128)}, u32[]{:S(2)}) copy-start(s32[16]{0:T(128)} %compare_select_fusion.7) | copy-start | bytes 196
  175.2 184.5 %copy-start.124 = (pred[2]{0:T(512)(128)(4,1)S(1)}, pred[2]{0:T(512)(128)(4,1)}, u32[]{:S(2)}) copy-start(pred[2]{0:T(512)(128)(4,1)} %get-tuple-element.277) | copy-start | bytes 10
  175.2 185.9 %copy-start.123 = (pred[2]{0:T(512)(128)(4,1)S(1)}, pred[2]{0:T(512)(128)(4,1)}, u32[]{:S(2)}) copy-start(pred[2]{0:T(512)(128)(4,1)} %get-tuple-element.278) | copy-start | bytes 10
  175.2 186.0 %copy-start.122 = (pred[2]{0:T(512)(128)(4,1)S(1)}, pred[2]{0:T(512)(128)(4,1)}, u32[]{:S(2)}) copy-start(pred[2]{0:T(512)(128)(4,1)} %broadcast_compare_fusion.2) | copy-start | bytes 10
  175.3 188.3 %copy-start.121 = (pred[4]{0:T(512)(128)(4,1)S(1)}, pred[4]{0:T(512)(128)(4,1)}, u32[]{:S(2)}) copy-start(pred[4]{0:T(512)(128)(4,1)} %get-tuple-element.275) | copy-start | bytes 16
  175.3 189.6 %copy-start.120 = (pred[4]{0:T(512)(128)(4,1)S(1)}, pred[4]{0:T(512)(128)(4,1)}, u32[]{:S(2)}) copy-start(pred[4]{0:T(512)(128)(4,1)} %get-tuple-element.276) | copy-start | bytes 16
  175.3 189.7 %copy-start.119 = (pred[4]{0:T(512)(128)(4,1)S(1)}, pred[4]{0:T(512)(128)(4,1)}, u32[]{:S(2)}) copy-start(pred[4]{0:T(512)(128)(4,1)} %compare_and_fusion.12) | copy-start | bytes 16
  175.3 192.2 %copy-start.118 = (pred[8]{0:T(512)(128)(4,1)S(1)}, pred[8]{0:T(512)(128)(4,1)}, u32[]{:S(2)}) copy-start(pred[8]{0:T(512)(128)(4,1)} %get-tuple-element.273) | copy-start | bytes 28
  357.5 11.3 %copy-start.117 = (pred[8]{0:T(512)(128)(4,1)S(1)}, pred[8]{0:T(512)(128)(4,1)}, u32[]{:S(2)}) copy-start(pred[8]{0:T(512)(128)(4,1)} %get-tuple-element.274) | copy-start | bytes 28
  357.5 11.4 %copy-start.116 = (pred[8]{0:T(512)(128)(4,1)S(1)}, pred[8]{0:T(512)(128)(4,1)}, u32[]{:S(2)}) copy-start(pred[8]{0:T(512)(128)(4,1)} %compare_and_fusion.9) | copy-start | bytes 28
  357.6 14.0 %copy-start.115 = (pred[16]{0:T(512)(128)(4,1)S(1)}, pred[16]{0:T(512)(128)(4,1)}, u32[]{:S(2)}) copy-start(pred[16]{0:T(512)(128)(4,1)} %get-tuple-element.271) | copy-start | bytes 52
  362.1 10.9 %copy-start.114 = (pred[16]{0:T(512)(128)(4,1)S(1)}, pred[16]{0:T(512)(128)(4,1)}, u32[]{:S(2)}) copy-start(pred[16]{0:T(512)(128)(4,1)} %get-tuple-element.272) | copy-start | bytes 52
  (81 other events, 219.1 us)

commit v2 on v1

--- a/solution.py
+++ b/solution.py
@@ -140,20 +140,31 @@
 
     top_levels = tree_depth - 1
     level_points = []
+    level_offsets = []
     for height in range(top_levels):
         offset = 2 * groups - 2 * (groups >> height)
+        level_offsets.append(offset)
         level_points.append(top_points[:, offset : offset + (groups >> height), :])
-    level_moments_top = [
-        lax.all_gather(level_moments[local_depth], "boxes", axis=1, tiled=True)
-    ]
-    edge_maps = []
+    own_edges = []
     for height in range(top_levels - 1):
-        interp_map = interpolation(
-            level_points[height], jnp.repeat(level_points[height + 1], 2, axis=1), kernel_scale
-        )
-        edge_maps.append(interp_map)
-        lifted = jnp.einsum("qnr,nrs->qns", level_moments_top[-1], interp_map, precision=PRECISE)
-        level_moments_top.append(lifted.reshape(rows_here, -1, 2, R).sum(axis=2))
+        own_edges.append(
+            interpolation(
+                lax.dynamic_slice_in_dim(level_points[height], device // 2**height, 1, 1),
+                lax.dynamic_slice_in_dim(level_points[height + 1], device // 2 ** (height + 1), 1, 1),
+                kernel_scale,
+            )
+        )
+    path_moment = level_moments[local_depth]
+    board = jnp.zeros((rows_here, level_offsets[-1] + 4, R), jnp.float32)
+    for height in range(top_levels):
+        if height > 0:
+            path_moment = jnp.einsum(
+                "qnr,nrs->qns", path_moment, own_edges[height - 1], precision=PRECISE
+            )
+        board = lax.dynamic_update_slice_in_dim(
+            board, path_moment, level_offsets[height] + device // 2**height, 1
+        )
+    board = lax.psum(board, "boxes")
     top_couplings = []
     for height in range(top_levels):
         number = groups >> height
@@ -169,16 +180,15 @@
             kernel_block = kernel_matrix(
                 lax.dynamic_slice_in_dim(level_points[height], source, 1, 1), target_points, kernel_scale
             )
-            source_moment = lax.dynamic_slice_in_dim(level_moments_top[height], source, 1, 1)
+            source_moment = lax.dynamic_slice_in_dim(board, level_offsets[height] + source, 1, 1)
             coupling = coupling + jnp.einsum(
                 "qnr,nrs->qns", source_moment, kernel_block, precision=PRECISE
             )
         top_couplings.append(coupling)
     descent = top_couplings[-1]
     for height in range(top_levels - 2, -1, -1):
-        own_edge = lax.dynamic_slice_in_dim(edge_maps[height], device // 2**height, 1, 0)
         descent = (
-            jnp.einsum("qns,nrs->qnr", descent, own_edge, precision=PRECISE)
+            jnp.einsum("qns,nrs->qnr", descent, own_edges[height], precision=PRECISE)
             + top_couplings[height]
         )
     for height in range(local_depth - 1, -1, -1):

time: 410 us -> 285 us (0.70); the launches traced: 402 us -> 282 us
  other arithmetic: 92.4 us -> 11.5 us
  waiting for transfers between devices: 0.01 us -> 63.8 us
  local copies, waits for them, and re-layouts: 95.9 us -> 46.2 us
  blocking collectives: 47.2 us -> 0 us
  matrix products: 138 us -> 118 us
  between operations: 3.43 us -> 16.9 us
    psum x0 -> x1, waiting for transfers between devices: none -> 63.8 us  [body(): board = lax.psum(board, 'boxes')]
    all_gather x1 -> x0, blocking collectives: 47.2 us -> none  [body(): lax.all_gather(level_moments[local_depth], 'boxes', axis=1, tiled=True)]
    slice x42 -> x38, local copies, waits for them, and re-layouts: 27.3 us -> 2.05 us  [kernel_matrix(): right_points[0][..., None, :]]
    dot_general x10, matrix products: 24.2 us -> 2.45 us  [the longest x5 1.23 us: body(): jnp.einsum('qns,nrs->qnr', descent, own_edges[height], precision=PRECISE)]
    select_n x64, other arithmetic: 24.3 us -> 2.72 us  [near_box(): near_tiles = jnp.take(extended, slot_index, axis=1)]
    mul x32, local copies, waits for them, and re-layouts: 21.8 us -> 0.19 us  [near_box(): near_values = near_tiles[:rows_here] * slot_mask[None, :, None]]
    and x32, other arithmetic: 21.9 us -> 0.56 us  [near_box(): near_tiles = jnp.take(extended, slot_index, axis=1)]
    div x5 -> x0, other arithmetic: 13.9 us -> none  [interpolation(): return values / jnp.sum(values, axis=-1, keepdims=True)]
  transfers between devices with their start and end apart: 4 -> 5, of which waited for: 0 -> 1; matrix products, arithmetic and copies ran while one was open for 66% -> 45% of each run, Pallas kernels for 0% -> 0%
where the time goes in v2:
time: 285 us; the launch traced here: 282 us
  matrix products  118 us (41%)
  waiting for transfers between devices  63.8 us (22%)
  local copies, waits for them, and re-layouts  46.2 us (16%)
  starting transfers between devices  24.2 us (8%)
  between operations  16.9 us (6%)
  other arithmetic  11.5 us (4%)
    dot_general x32, matrix products, near_box(): jnp.einsum('qns,nst->qt', near_values, kernel_block, precision=PRECISE)  68.9 us
    psum x1, waiting for transfers between devices, body(): board = lax.psum(board, 'boxes')  63.8 us
    dot_general x31, matrix products, body(): jnp.einsum('qnr,nrs->qns', source_moment, kernel_block, precision=PRECISE)  28.8 us
    ppermute x2, starting transfers between devices, with_halo(): after = lax.ppermute(initial, axis, down)  20.4 us
    gather x32, local copies, waits for them, and re-layouts, near_box(): near_tiles = jnp.take(extended, slot_index, axis=1)  17.8 us
    gather x15, local copies, waits for them, and re-layouts, body(): picked = jnp.take(view, slot_ids[slot], axis=1)  8.41 us
    dot_general x5, matrix products, body(): jnp.einsum('qns,nrs->qnr', jnp.repeat(descent, 2, axis=1), transfer_maps[...  6.45 us
  transfers between devices with their start and end apart: 5, of which 1 were waited for; matrix products, arithmetic and copies ran while one was open for 45% of the time, Pallas kernels for 0%

profile of v2, /device:TPU:6, one launch (start us, length us, event | category | flops | bytes accessed | tf_op | source)
XLA Modules:
  0.0 282.4 jit_solution(2102276692687929236)
XLA Ops:
  7.6 0.9 slice_reduce_fusion.5
  9.7 1.3 slice_reduce_fusion.2
  11.1 1.1 divide_reduce_fusion
  12.2 3.3 %constant_dynamic-update-slice_fusion.11 = (f32[8,62,64]{2,0,1:T(8,128)S(1)}, f32[8,32,64]{2,0,1:T(8,128)S(1)}) fusion(f32[8,32,256]{2,0,1:T(8,128)S(1)} %bitcast.600, f32[32,256]{1,0:T(8,128)S(1)} %divide_reduce_fusion, f32[32,64]{1,0:T(8,128)S(1)} %sub.3146, f32[32,256]{1,0:T(8,128)S(1)} %sub.3144, f32[32,64]{1,0:T(8,128)S(1)} %sub.3141, ...), kind=kOutput, calls=%fused_computation.883 | convolution fusion | flops 56623104 | bytes 679936 | tf_op jit(solution)/shard_map/qbp,bpr->qbr/dot_general | solution.py:84
  15.6 1.4 divide_reduce_fusion.1
  17.0 2.6 bitcast_reduce_fusion
  20.3 1.3 bitcast_reduce_fusion.1
  23.7 13.4 %collective-permute-start.3 = (f32[11,62,64]{2,0,1:T(8,128)S(1)}, f32[11,62,64]{2,0,1:T(8,128)S(1)}, u32[]{:S(2)}, u32[]{:S(2)}) collective-permute-start(f32[11,62,64]{2,0,1:T(8,128)S(1)} %maximum_maximum_fusion), channel_id=1, source_target_pairs={{4,0},{8,4},{12,8},{16,12},{20,16},{24,20},{28,24},{32,28},{36,32}... | collective-permute-start | bytes 523784 | tf_op jit(solution)/shard_map/ppermute | solution.py:26
  37.2 1.9 collective-permute-start.2
  39.8 1.9 collective-permute-start
  41.7 7.0 %collective-permute-start.1 = (f32[11,768]{1,0:T(8,128)}, f32[11,768]{1,0:T(8,128)}, u32[]{:S(2)}, u32[]{:S(2)}) collective-permute-start(f32[11,768]{1,0:T(8,128)} %get-tuple-element.111), channel_id=1, source_target_pairs={{4,0},{8,4},{12,8},{16,12},{20,16},{24,20},{28,24},{32,28},{36,32}... | collective-permute-start | bytes 101384 | tf_op jit(solution)/shard_map/ppermute | solution.py:26
  55.1 1.0 copy-done
  58.6 93.3 %while.10 = (s32[]{:T(128)}, f32[32,8,256]{2,1,0:T(8,128)}, s32[32,6]{1,0:T(8,128)S(1)}, f32[11,38,256]{2,0,1:T(8,128)S(1)}, f32[32,6]{1,0:T(8,128)S(1)}, /*inde...) while((s32[]{:T(128)}, f32[32,8,256]{2,1,0:T(8,128)}, s32[32,6]{1,0:T(8,128)S(1)}, ...), condition=%wide.region_1.2_spmd, body=%wide.region_0.1_spmd.sunk | while | flops 42104376 | bytes 440149 | solution.py:66
  59.5 2.2 fusion.913
  62.5 2.2 fusion.913
  65.4 2.2 fusion.913
  68.3 2.2 fusion.913
  71.2 2.2 fusion.913
  74.1 2.2 fusion.913
  77.0 2.2 fusion.913
  79.9 2.2 fusion.913
  82.8 2.2 fusion.913
  85.7 2.2 fusion.913
  88.6 2.2 fusion.913
  91.5 2.2 fusion.913
  94.5 2.2 fusion.913
  97.4 2.2 fusion.913
  100.3 2.2 fusion.913
  103.2 2.2 fusion.913
  106.1 2.2 fusion.913
  109.0 2.2 fusion.913
  111.9 2.2 fusion.913
  114.8 2.2 fusion.913
  117.7 2.2 fusion.913
  120.6 2.2 fusion.913
  123.6 2.2 fusion.913
  126.5 2.2 fusion.913
  129.4 2.2 fusion.913
  132.3 2.2 fusion.913
  135.2 2.2 fusion.913
  138.1 2.2 fusion.913
  141.0 2.2 fusion.913
  143.9 2.2 fusion.913
  146.8 2.2 fusion.913
  149.7 2.2 fusion.913
  163.2 0.9 slice.1161
  166.3 1.0 slice.1176
  171.2 1.2 fusion.99
  173.8 1.2 convolution_add_fusion.4
  175.0 2.3 fusion.55
  177.3 2.3 convolution_add_fusion.1
  179.8 2.3 convolution_add_fusion
  182.2 63.8 %all-reduce.2.cloned.1.call-done = f32[8,252,64]{2,0,1:T(8,128)} async-done(((f32[8,252,64]{2,0,1:T(8,128)}), f32[8,252,64]{2,0,1:T(8,128)}) %all-reduce.2.cloned.1.call-update) | async-done | bytes 516112 | tf_op jit(solution)/shard_map/psum | solution.py:167
  247.3 0.9 fusion.262
  250.4 0.9 fusion.258
  252.4 0.9 fusion.33
  254.6 0.9 convolution_add_fusion.16
  255.5 0.9 fusion.31
  258.7 0.9 fusion.29
  260.8 0.9 convolution_add_fusion.12
  265.9 1.6 fusion.142
  267.5 1.2 fusion.19
  268.8 3.2 %fusion.17 = f32[8,32,64]{2,0,1:T(8,128)S(1)} fusion(f32[32,64,8]{1,2,0:T(8,128)S(1)} %convolution_add_fusion, f32[8,32,64]{2,0,1:T(8,128)S(1)} %bitcast.604, f32[32,64]{1,0:T(8,128)S(1)} %copy-done.53, f32[32,64]{1,0:T(8,128)S(1)} %bitcast.610, f32[32,64]{1,0:T(8,128)S(1)} %sub.3146, f32[32,64]{1,0:T(8,128)S(1)} %bitcast.613, f32[32,64]{1,0:T(8,128)S(1)} %sub.3141, ...), kind=kOutput, calls=%fused_computation.56 | convolution fusion | flops 14172160 | bytes 253952 | tf_op jit(solution)/shard_map/qns,nrs->qnr/dot_general | solution.py:195
  272.1 2.7 fusion.16
  (807 shorter events, 67.4 us)
Async XLA Ops:
  6.5 239.5 %all-reduce.2.cloned.1.call-start = ((), (), s32[]{:S(2)}) async-start(), calls=%async_computation | async-start | bytes 2064384 | tf_op jit(solution)/shard_map/psum | solution.py:167
  7.4 42.9 %copy-start.62 = (f32[2,64]{1,0:T(2,128)}, f32[2,64]{1,0:T(2,128)S(1)}, u32[]{:S(2)}) copy-start(f32[2,64]{1,0:T(2,128)S(1)} %get-tuple-element.179) | copy-start | bytes 1540
  7.4 42.9 %copy-start.65 = (f32[2,64]{1,0:T(2,128)}, f32[2,64]{1,0:T(2,128)S(1)}, u32[]{:S(2)}) copy-start(f32[2,64]{1,0:T(2,128)S(1)} %get-tuple-element.180) | copy-start | bytes 1540
  7.5 43.2 %copy-start.60 = (f32[2,64]{1,0:T(2,128)}, f32[2,64]{1,0:T(2,128)S(1)}, u32[]{:S(2)}) copy-start(f32[2,64]{1,0:T(2,128)S(1)} %get-tuple-element.178) | copy-start | bytes 1540
  7.5 15.7 %copy-start.46 = (f32[4,64]{1,0:T(4,128)}, f32[4,64]{1,0:T(4,128)S(1)}, u32[]{:S(2)}) copy-start(f32[4,64]{1,0:T(4,128)S(1)} %get-tuple-element.181) | copy-start | bytes 3076
  7.5 15.7 %copy-start.48 = (f32[4,64]{1,0:T(4,128)}, f32[4,64]{1,0:T(4,128)S(1)}, u32[]{:S(2)}) copy-start(f32[4,64]{1,0:T(4,128)S(1)} %get-tuple-element.182) | copy-start | bytes 3076
  7.5 15.7 %copy-start.50 = (f32[4,64]{1,0:T(4,128)}, f32[4,64]{1,0:T(4,128)S(1)}, u32[]{:S(2)}) copy-start(f32[4,64]{1,0:T(4,128)S(1)} %get-tuple-element.183) | copy-start | bytes 3076
  7.5 14.6 %copy-start.26 = (f32[8,64]{1,0:T(8,128)}, f32[8,64]{1,0:T(8,128)S(1)}, u32[]{:S(2)}) copy-start(f32[8,64]{1,0:T(8,128)S(1)} %get-tuple-element.184) | copy-start | bytes 6148
  7.5 14.6 %copy-start.28 = (f32[8,64]{1,0:T(8,128)}, f32[8,64]{1,0:T(8,128)S(1)}, u32[]{:S(2)}) copy-start(f32[8,64]{1,0:T(8,128)S(1)} %get-tuple-element.185) | copy-start | bytes 6148
  7.5 14.6 %copy-start.30 = (f32[8,64]{1,0:T(8,128)}, f32[8,64]{1,0:T(8,128)S(1)}, u32[]{:S(2)}) copy-start(f32[8,64]{1,0:T(8,128)S(1)} %get-tuple-element.186) | copy-start | bytes 6148
  7.6 12.8 %copy-start.12 = (f32[16,64]{1,0:T(8,128)}, f32[16,64]{1,0:T(8,128)S(1)}, u32[]{:S(2)}) copy-start(f32[16,64]{1,0:T(8,128)S(1)} %get-tuple-element.189) | copy-start | bytes 12292
  22.8 14.3 %copy-start.70 = (f32[2,2,64]{2,1,0:T(2,128)}, f32[2,2,64]{2,1,0:T(2,128)S(1)}, u32[]{:S(2)}) copy-start(f32[2,2,64]{2,1,0:T(2,128)S(1)} %broadcast_in_dim.172) | copy-start | bytes 3076
  22.9 14.3 %copy-start.72 = (f32[2,2,64]{2,1,0:T(2,128)}, f32[2,2,64]{2,1,0:T(2,128)S(1)}, u32[]{:S(2)}) copy-start(f32[2,2,64]{2,1,0:T(2,128)S(1)} %broadcast_in_dim.176) | copy-start | bytes 3076
  22.9 14.3 %copy-start.74 = (f32[2,2,64]{2,1,0:T(2,128)}, f32[2,2,64]{2,1,0:T(2,128)S(1)}, u32[]{:S(2)}) copy-start(f32[2,2,64]{2,1,0:T(2,128)S(1)} %broadcast_in_dim.174) | copy-start | bytes 3076
  23.2 16.0 %copy-start.2 = (f32[3,8192]{1,0:T(4,128)S(1)}, f32[3,8192]{1,0:T(4,128)}, u32[]{:S(2)}) copy-start(f32[3,8192]{1,0:T(4,128)} %param.20) | copy-start | bytes 294916
  23.7 25.5 %copy-start.3 = (f32[3,16128]{1,0:T(4,128)S(1)}, f32[3,16128]{1,0:T(4,128)}, u32[]{:S(2)}) copy-start(f32[3,16128]{1,0:T(4,128)} %param.24) | copy-start | bytes 580612
  23.7 128.2 %collective-permute-start.3 = (f32[11,62,64]{2,0,1:T(8,128)S(1)}, f32[11,62,64]{2,0,1:T(8,128)S(1)}, u32[]{:S(2)}, u32[]{:S(2)}) collective-permute-start(f32[11,62,64]{2,0,1:T(8,128)S(1)} %maximum_maximum_fusion), channel_id=1, source_target_pairs={{4,0},{8,4},{12,8},{16,12},{20,16},{24,20},{28,24},{32,28},{36,32}... | collective-permute-start | bytes 523784 | tf_op jit(solution)/shard_map/ppermute | solution.py:26
  37.2 114.7 %collective-permute-start.2 = (f32[11,62,64]{2,0,1:T(8,128)S(1)}, f32[11,62,64]{2,0,1:T(8,128)}, u32[]{:S(2)}, u32[]{:S(2)}) collective-permute-start(f32[11,62,64]{2,0,1:T(8,128)S(1)} %maximum_maximum_fusion), channel_id=1, source_target_pairs={{0,4},{4,8},{8,12},{12,16},{16,20},{20,24},{24,28},{28,32},{32,36}... | collective-permute-start | bytes 523784 | tf_op jit(solution)/shard_map/ppermute | solution.py:25
  39.8 17.6 %collective-permute-start = (f32[11,768]{1,0:T(8,128)}, f32[11,768]{1,0:T(8,128)}, u32[]{:S(2)}, u32[]{:S(2)}) collective-permute-start(f32[11,768]{1,0:T(8,128)} %get-tuple-element.110), channel_id=1, source_target_pairs={{0,4},{4,8},{8,12},{12,16},{16,20},{20,24},{24,28},{28,32},{32,36}... | collective-permute-start | bytes 101384 | tf_op jit(solution)/shard_map/ppermute | solution.py:25
  41.7 15.7 %collective-permute-start.1 = (f32[11,768]{1,0:T(8,128)}, f32[11,768]{1,0:T(8,128)}, u32[]{:S(2)}, u32[]{:S(2)}) collective-permute-start(f32[11,768]{1,0:T(8,128)} %get-tuple-element.111), channel_id=1, source_target_pairs={{4,0},{8,4},{12,8},{16,12},{20,16},{24,20},{28,24},{32,28},{36,32}... | collective-permute-start | bytes 101384 | tf_op jit(solution)/shard_map/ppermute | solution.py:26
  179.7 66.4 %copy-start.114 = (f32[64]{0:T(128)S(1)}, f32[64]{0:T(128)}, u32[]{:S(2)}) copy-start(f32[64]{0:T(128)} %get-tuple-element.233) | copy-start | bytes 772
  179.7 66.4 %copy-start.115 = (f32[64]{0:T(128)S(1)}, f32[64]{0:T(128)}, u32[]{:S(2)}) copy-start(f32[64]{0:T(128)} %get-tuple-element.234) | copy-start | bytes 772
  179.7 66.4 %copy-start.116 = (f32[64]{0:T(128)S(1)}, f32[64]{0:T(128)}, u32[]{:S(2)}) copy-start(f32[64]{0:T(128)} %get-tuple-element.236) | copy-start | bytes 772
  179.7 67.3 %copy-start.122 = (f32[64]{0:T(128)S(1)}, f32[64]{0:T(128)}, u32[]{:S(2)}) copy-start(f32[64]{0:T(128)} %copy-done.121) | copy-start | bytes 772
  179.7 67.5 %copy-start.109 = (f32[64]{0:T(128)S(1)}, f32[64]{0:T(128)}, u32[]{:S(2)}) copy-start(f32[64]{0:T(128)} %get-tuple-element.224) | copy-start | bytes 772
  179.7 67.5 %copy-start.110 = (f32[64]{0:T(128)S(1)}, f32[64]{0:T(128)}, u32[]{:S(2)}) copy-start(f32[64]{0:T(128)} %get-tuple-element.225) | copy-start | bytes 772
  179.7 67.5 %copy-start.111 = (f32[64]{0:T(128)S(1)}, f32[64]{0:T(128)}, u32[]{:S(2)}) copy-start(f32[64]{0:T(128)} %get-tuple-element.230) | copy-start | bytes 772
  179.7 68.5 %copy-start.106 = (f32[64]{0:T(128)S(1)}, f32[64]{0:T(128)}, u32[]{:S(2)}) copy-start(f32[64]{0:T(128)} %get-tuple-element.222) | copy-start | bytes 772
  179.8 68.5 %copy-start.107 = (f32[64]{0:T(128)S(1)}, f32[64]{0:T(128)}, u32[]{:S(2)}) copy-start(f32[64]{0:T(128)} %get-tuple-element.223) | copy-start | bytes 772
  179.8 68.5 %copy-start.108 = (f32[64]{0:T(128)S(1)}, f32[64]{0:T(128)}, u32[]{:S(2)}) copy-start(f32[64]{0:T(128)} %get-tuple-element.229) | copy-start | bytes 772
  179.8 69.4 %copy-start.103 = (f32[64]{0:T(128)S(1)}, f32[64]{0:T(128)}, u32[]{:S(2)}) copy-start(f32[64]{0:T(128)} %get-tuple-element.220) | copy-start | bytes 772
  179.8 69.4 %copy-start.104 = (f32[64]{0:T(128)S(1)}, f32[64]{0:T(128)}, u32[]{:S(2)}) copy-start(f32[64]{0:T(128)} %get-tuple-element.221) | copy-start | bytes 772
  179.8 69.4 %copy-start.105 = (f32[64]{0:T(128)S(1)}, f32[64]{0:T(128)}, u32[]{:S(2)}) copy-start(f32[64]{0:T(128)} %get-tuple-element.228) | copy-start | bytes 772
  182.1 68.0 %copy-start.120 = (f32[64]{0:T(128)S(1)}, f32[64]{0:T(128)}, u32[]{:S(2)}) copy-start(f32[64]{0:T(128)} %copy-done.119) | copy-start | bytes 772
  182.2 68.3 %copy-start.141 = (f32[64]{0:T(128)S(1)}, f32[64]{0:T(128)}, u32[]{:S(2)}) copy-start(f32[64]{0:T(128)} %get-tuple-element.290) | copy-start | bytes 772
  182.2 68.3 %copy-start.142 = (f32[64]{0:T(128)S(1)}, f32[64]{0:T(128)}, u32[]{:S(2)}) copy-start(f32[64]{0:T(128)} %get-tuple-element.295) | copy-start | bytes 772
  182.2 68.3 %copy-start.143 = (f32[64]{0:T(128)S(1)}, f32[64]{0:T(128)}, u32[]{:S(2)}) copy-start(f32[64]{0:T(128)} %get-tuple-element.296) | copy-start | bytes 772
  182.2 69.2 %copy-start.138 = (f32[64]{0:T(128)S(1)}, f32[64]{0:T(128)}, u32[]{:S(2)}) copy-start(f32[64]{0:T(128)} %get-tuple-element.291) | copy-start | bytes 772
  182.2 69.2 %copy-start.139 = (f32[64]{0:T(128)S(1)}, f32[64]{0:T(128)}, u32[]{:S(2)}) copy-start(f32[64]{0:T(128)} %get-tuple-element.297) | copy-start | bytes 772
  182.2 69.2 %copy-start.140 = (f32[64]{0:T(128)S(1)}, f32[64]{0:T(128)}, u32[]{:S(2)}) copy-start(f32[64]{0:T(128)} %get-tuple-element.298) | copy-start | bytes 772
  182.2 70.1 %copy-start.135 = (f32[64]{0:T(128)S(1)}, f32[64]{0:T(128)}, u32[]{:S(2)}) copy-start(f32[64]{0:T(128)} %get-tuple-element.292) | copy-start | bytes 772
  182.2 70.1 %copy-start.136 = (f32[64]{0:T(128)S(1)}, f32[64]{0:T(128)}, u32[]{:S(2)}) copy-start(f32[64]{0:T(128)} %get-tuple-element.299) | copy-start | bytes 772
  182.2 70.1 %copy-start.137 = (f32[64]{0:T(128)S(1)}, f32[64]{0:T(128)}, u32[]{:S(2)}) copy-start(f32[64]{0:T(128)} %get-tuple-element.300) | copy-start | bytes 772
  247.0 6.3 %copy-start.118 = (f32[64]{0:T(128)S(1)}, f32[64]{0:T(128)}, u32[]{:S(2)}) copy-start(f32[64]{0:T(128)} %copy-done.117) | copy-start | bytes 772
  247.2 6.4 %copy-start.89 = (f32[64]{0:T(128)S(1)}, f32[64]{0:T(128)}, u32[]{:S(2)}) copy-start(f32[64]{0:T(128)} %get-tuple-element.278) | copy-start | bytes 772
  247.2 6.4 %copy-start.90 = (f32[64]{0:T(128)S(1)}, f32[64]{0:T(128)}, u32[]{:S(2)}) copy-start(f32[64]{0:T(128)} %get-tuple-element.283) | copy-start | bytes 772
  247.2 6.4 %copy-start.91 = (f32[64]{0:T(128)S(1)}, f32[64]{0:T(128)}, u32[]{:S(2)}) copy-start(f32[64]{0:T(128)} %get-tuple-element.284) | copy-start | bytes 772
  248.2 6.3 %copy-start.86 = (f32[64]{0:T(128)S(1)}, f32[64]{0:T(128)}, u32[]{:S(2)}) copy-start(f32[64]{0:T(128)} %get-tuple-element.279) | copy-start | bytes 772
  248.2 6.3 %copy-start.87 = (f32[64]{0:T(128)S(1)}, f32[64]{0:T(128)}, u32[]{:S(2)}) copy-start(f32[64]{0:T(128)} %get-tuple-element.285) | copy-start | bytes 772
  248.2 6.4 %copy-start.88 = (f32[64]{0:T(128)S(1)}, f32[64]{0:T(128)}, u32[]{:S(2)}) copy-start(f32[64]{0:T(128)} %get-tuple-element.286) | copy-start | bytes 772
  249.2 6.4 %copy-start.83 = (f32[64]{0:T(128)S(1)}, f32[64]{0:T(128)}, u32[]{:S(2)}) copy-start(f32[64]{0:T(128)} %get-tuple-element.280) | copy-start | bytes 772
  249.2 6.4 %copy-start.84 = (f32[64]{0:T(128)S(1)}, f32[64]{0:T(128)}, u32[]{:S(2)}) copy-start(f32[64]{0:T(128)} %get-tuple-element.287) | copy-start | bytes 772
  249.2 6.4 %copy-start.85 = (f32[64]{0:T(128)S(1)}, f32[64]{0:T(128)}, u32[]{:S(2)}) copy-start(f32[64]{0:T(128)} %get-tuple-element.288) | copy-start | bytes 772
  250.1 6.3 %copy-start.113 = (f32[64]{0:T(128)S(1)}, f32[64]{0:T(128)}, u32[]{:S(2)}) copy-start(f32[64]{0:T(128)} %copy-done.112) | copy-start | bytes 772
  250.4 6.3 %copy-start.98 = (f32[64]{0:T(128)S(1)}, f32[64]{0:T(128)}, u32[]{:S(2)}) copy-start(f32[64]{0:T(128)} %get-tuple-element.302) | copy-start | bytes 772
  250.4 6.4 %copy-start.99 = (f32[64]{0:T(128)S(1)}, f32[64]{0:T(128)}, u32[]{:S(2)}) copy-start(f32[64]{0:T(128)} %get-tuple-element.307) | copy-start | bytes 772
  250.4 6.4 %copy-start.100 = (f32[64]{0:T(128)S(1)}, f32[64]{0:T(128)}, u32[]{:S(2)}) copy-start(f32[64]{0:T(128)} %get-tuple-element.308) | copy-start | bytes 772
  251.4 6.3 %copy-start.95 = (f32[64]{0:T(128)S(1)}, f32[64]{0:T(128)}, u32[]{:S(2)}) copy-start(f32[64]{0:T(128)} %get-tuple-element.303) | copy-start | bytes 772
  251.4 6.3 %copy-start.96 = (f32[64]{0:T(128)S(1)}, f32[64]{0:T(128)}, u32[]{:S(2)}) copy-start(f32[64]{0:T(128)} %get-tuple-element.309) | copy-start | bytes 772
  251.4 6.3 %copy-start.97 = (f32[64]{0:T(128)S(1)}, f32[64]{0:T(128)}, u32[]{:S(2)}) copy-start(f32[64]{0:T(128)} %get-tuple-element.310) | copy-start | bytes 772
  253.3 6.3 %copy-start.102 = (f32[64]{0:T(128)S(1)}, f32[64]{0:T(128)}, u32[]{:S(2)}) copy-start(f32[64]{0:T(128)} %copy-done.101) | copy-start | bytes 772
  253.5 6.3 %copy-start.132 = (f32[64]{0:T(128)S(1)}, f32[64]{0:T(128)}, u32[]{:S(2)}) copy-start(f32[64]{0:T(128)} %get-tuple-element.128) | copy-start | bytes 772
  253.5 6.3 %copy-start.133 = (f32[64]{0:T(128)S(1)}, f32[64]{0:T(128)}, u32[]{:S(2)}) copy-start(f32[64]{0:T(128)} %get-tuple-element.129) | copy-start | bytes 772
  253.5 6.3 %copy-start.134 = (f32[64]{0:T(128)S(1)}, f32[64]{0:T(128)}, u32[]{:S(2)}) copy-start(f32[64]{0:T(128)} %get-tuple-element.134) | copy-start | bytes 772
  (86 other events, 206.1 us)
Sparse Core Ops, SparseCore 0:
  56.2 189.8 all-reduce.1

commit v3 on v1

--- a/solution.py
+++ b/solution.py
@@ -1,6 +1,10 @@
+import functools
+
 import jax
 import jax.numpy as jnp
 from jax import lax
+from jax.experimental import pallas as pl
+from jax.experimental.pallas import tpu as pltpu
 from jax.sharding import PartitionSpec as P
 
 BOXES_DEV = 32
@@ -38,6 +42,54 @@
 def interpolation(left_points, right_points, kernel_scale):
     values = kernel_matrix(left_points, right_points, kernel_scale)
     return values / jnp.sum(values, axis=-1, keepdims=True)
+
+
+def near_kernel(kernel_scale, slots, source_ref, probes_ref, coords_ref, target_ref, out_ref):
+    box = pl.program_id(0)
+    target_x = target_ref[0:1, :]
+    target_y = target_ref[1:2, :]
+    target_z = target_ref[2:3, :]
+    out_ref[...] = jnp.zeros_like(out_ref)
+    for slot in range(slots):
+        source = source_ref[box * slots + slot]
+
+        @pl.when(source >= 0)
+        def _():
+            near = coords_ref[source]
+            distance_sq = (near[:, 0:1] - target_x) ** 2
+            distance_sq = distance_sq + (near[:, 1:2] - target_y) ** 2
+            distance_sq = distance_sq + (near[:, 2:3] - target_z) ** 2
+            kernel_block = 1.0 / (1.0 + kernel_scale * distance_sq)
+            out_ref[...] += jnp.dot(
+                probes_ref[source], kernel_block, precision=PRECISE,
+                preferred_element_type=jnp.float32,
+            )
+
+
+def near_field_call(slot_source, probe_tiles, coord_tiles, points, kernel_scale):
+    tiles, rows, size = probe_tiles.shape
+    boxes = points.shape[1] // size
+    slots = slot_source.shape[0] // boxes
+    return pl.pallas_call(
+        functools.partial(near_kernel, kernel_scale, slots),
+        out_shape=jax.ShapeDtypeStruct((rows, boxes * size), jnp.float32),
+        grid_spec=pltpu.PrefetchScalarGridSpec(
+            num_scalar_prefetch=1,
+            grid=(boxes,),
+            in_specs=[
+                pl.BlockSpec((tiles, rows, size), lambda b, s: (0, 0, 0)),
+                pl.BlockSpec((tiles, size, 3), lambda b, s: (0, 0, 0)),
+                pl.BlockSpec((3, size), lambda b, s: (0, b)),
+            ],
+            out_specs=pl.BlockSpec((rows, size), lambda b, s: (0, b)),
+        ),
+        compiler_params=pltpu.CompilerParams(dimension_semantics=("arbitrary",)),
+        cost_estimate=pl.CostEstimate(
+            flops=boxes * slots * size * size * (2 * rows + 12),
+            transcendentals=0,
+            bytes_accessed=4 * (probe_tiles.size + coord_tiles.size * 43 + 2 * rows * boxes * size),
+        ),
+    )(slot_source, probe_tiles, coord_tiles, points)
 
 
 def body(probes, points, near_list, leaf_proxy, inner_proxy, top_proxy, far_list):
@@ -56,15 +108,14 @@
     extended = with_halo(stacked, (("boxes", 1),), W * P_SIZE)
     extended = extended.reshape(rows_here + 3, BOXES_DEV + 2 * W, P_SIZE)
 
-    def near_box(near_inputs):
-        slot_index, slot_mask, targets = near_inputs
-        near_tiles = jnp.take(extended, slot_index, axis=1)
-        near_values = near_tiles[:rows_here] * slot_mask[None, :, None]
-        kernel_block = kernel_matrix(near_tiles[rows_here:], targets[:, None, :], kernel_scale)
-        return jnp.einsum("qns,nst->qt", near_values, kernel_block, precision=PRECISE)
-
-    near_field = lax.map(near_box, (where_in, slot_weight, jnp.moveaxis(box_points, 1, 0)))
-    near_field = jnp.moveaxis(near_field, 0, 1).reshape(rows_here, BOXES_DEV * P_SIZE)
+    slot_source = jnp.where(live_slot, jnp.clip(where_in, 0, BOXES_DEV + 2 * W - 1), -1)
+    near_field = near_field_call(
+        slot_source.reshape(-1).astype(jnp.int32),
+        jnp.moveaxis(extended[:rows_here], 1, 0),
+        jnp.moveaxis(extended[rows_here:], 0, 2),
+        points,
+        kernel_scale,
+    )
     probe_tiles = probes.reshape(rows_here, BOXES_DEV, P_SIZE)
     leaf_points = leaf_proxy.reshape(3, BOXES_DEV, R)
     leaf_basis = interpolation(box_points, leaf_points, kernel_scale)

time: 410 us -> 300 us (0.73)
  Pallas kernels: 0 us -> 73.4 us
  matrix products: 138 us -> 69.4 us
  local copies, waits for them, and re-layouts: 95.9 us -> 32.2 us
  other arithmetic: 92.4 us -> 45.1 us
    pallas_call x0 -> x1, Pallas kernels: none -> 73.4 us  [near_field_call(): pl.pallas_call(functools.partial(near_kernel, kernel_scale, slots), out_s...]
    dot_general x32 -> x0, matrix products: 68.9 us -> none  [near_box(): jnp.einsum('qns,nst->qt', near_values, kernel_block, precision=PRECISE)]
    slice x42 -> x10, local copies, waits for them, and re-layouts: 27.3 us -> 1.58 us  [kernel_matrix(): right_points[0][..., None, :]]
    select_n x65 -> x1, other arithmetic: 24.9 us -> 0.6 us  [body(): jnp.where(live_slot, jnp.clip(where_in, 0, BOXES_DEV + 2 * W - 1), -1)]
    and x32 -> x0, other arithmetic: 21.9 us -> none  [near_box(): near_tiles = jnp.take(extended, slot_index, axis=1)]
    mul x32 -> x0, local copies, waits for them, and re-layouts: 21.8 us -> none  [near_box(): near_values = near_tiles[:rows_here] * slot_mask[None, :, None]]
    gather x32 -> x0, local copies, waits for them, and re-layouts: 17.8 us -> none  [near_box(): near_tiles = jnp.take(extended, slot_index, axis=1)]
    gather x45 -> x8, other arithmetic: 6.71 us -> 0.65 us
  transfers between devices with their start and end apart: 4 -> 4, of which waited for: 0 -> 0; matrix products, arithmetic and copies ran while one was open for 66% -> 29% of each run, Pallas kernels for 0% -> 25%
where the time goes in v3:
time: 300 us; the launch traced here: 295 us
  Pallas kernels  73.4 us (24%)
  matrix products  69.4 us (23%)
  blocking collectives  47.2 us (16%)
  other arithmetic  45.1 us (15%)
  local copies, waits for them, and re-layouts  32.2 us (11%)
  starting transfers between devices  24.1 us (8%)
  between operations  3.66 us (1%)
    pallas_call x1, Pallas kernels, near_field_call(): pl.pallas_call(functools.partial(near_kernel, kernel_scale, slots), out_s...  73.4 us
    all_gather x1, blocking collectives, body(): lax.all_gather(level_moments[local_depth], 'boxes', axis=1, tiled=True)  47.2 us
    dot_general x31, matrix products, body(): jnp.einsum('qnr,nrs->qns', source_moment, kernel_block, precision=PRECISE)  27 us
    dot_general x5, matrix products, body(): jnp.einsum('qnr,nrs->qns', level_moments_top[-1], interp_map, precision=P...  20.4 us
    ppermute x2, starting transfers between devices, with_halo(): after = lax.ppermute(initial, axis, down)  20.3 us
    reduce_sum x11, other arithmetic, interpolation(): return values / jnp.sum(values, axis=-1, keepdims=True)  14.6 us
    div x5, other arithmetic, interpolation(): return values / jnp.sum(values, axis=-1, keepdims=True)  14 us
    gather x15, local copies, waits for them, and re-layouts, body(): picked = jnp.take(view, slot_ids[slot], axis=1)  8.53 us
  transfers between devices with their start and end apart: 4, of which 0 were waited for; matrix products, arithmetic and copies ran while one was open for 29% of the time, Pallas kernels for 25%

profile of v3, /device:TPU:6, one launch (start us, length us, event | category | flops | bytes accessed | tf_op | source)
XLA Modules:
  0.0 295.1 jit_solution(5684575966444483558)
XLA Ops:
  0.0 0.8 reshape.4838
  1.1 0.9 slice_reduce_fusion.5
  2.0 0.9 reshape.4880
  3.1 1.3 slice_reduce_fusion.2
  4.5 1.1 divide_reduce_fusion.2
  5.6 3.8 %constant_dynamic-update-slice_fusion.6 = (f32[8,62,64]{2,0,1:T(8,128)S(1)}, f32[8,32,64]{2,0,1:T(8,128)S(1)}) fusion(f32[8,32,256]{2,0,1:T(8,128)} %bitcast.568, f32[32,256]{1,0:T(8,128)S(1)} %divide_reduce_fusion.2, f32[32,64]{1,0:T(8,128)S(1)} %sub.2595, f32[32,256]{1,0:T(8,128)S(1)} %sub.2593, f32[32,64]{1,0:T(8,128)S(1)} %sub.2590, ...), kind=kOutput, calls=%fused_computation.828 | convolution fusion | flops 56623104 | bytes 679936 | tf_op jit(solution)/shard_map/qbp,bpr->qbr/dot_general | solution.py:135
  9.6 1.4 divide_reduce_fusion.4
  11.0 2.6 bitcast_reduce_fusion.3
  14.4 1.3 bitcast_reduce_fusion.5
  17.8 13.3 %collective-permute-start.3 = (f32[11,62,64]{2,0,1:T(8,128)S(1)}, f32[11,62,64]{2,0,1:T(8,128)}, u32[]{:S(2)}, u32[]{:S(2)}) collective-permute-start(f32[11,62,64]{2,0,1:T(8,128)S(1)} %maximum_maximum_fusion), channel_id=1, source_target_pairs={{4,0},{8,4},{12,8},{16,12},{20,16},{24,20},{28,24},{32,28},{36,32}... | collective-permute-start | bytes 523784 | tf_op jit(solution)/shard_map/ppermute | solution.py:30
  31.1 1.9 collective-permute-start.2
  33.8 1.9 collective-permute-start
  35.7 7.0 %collective-permute-start.1 = (f32[11,768]{1,0:T(8,128)}, f32[11,768]{1,0:T(8,128)}, u32[]{:S(2)}, u32[]{:S(2)}) collective-permute-start(f32[11,768]{1,0:T(8,128)} %get-tuple-element.26), channel_id=1, source_target_pairs={{4,0},{8,4},{12,8},{16,12},{20,16},{24,20},{28,24},{32,28},{36,32}... | collective-permute-start | bytes 101384 | tf_op jit(solution)/shard_map/ppermute | solution.py:30
  58.5 1.0 multiply_divide_fusion.11
  59.6 47.2 %all-gather.1 = f32[128,64,8]{1,2,0:T(8,128)S(1)} all-gather(f32[1,64,8]{1,2,0:T(8,128)S(1)} %convolution_bitcast_fusion.2), channel_id=2, replica_groups=mesh['boxes'=128,'probe'=4] {'boxes'}, dimensions={0}, use_global_device_ids=true | all-gather | bytes 264192 | tf_op jit(solution)/shard_map/all_gather | solution.py:198
  107.4 5.6 %divide_reduce_fusion = f32[128,64]{1,0:T(8,128)S(1)} fusion(f32[128,64]{1,0:T(8,128)S(1)} %bitcast.572, f32[128,64]{1,0:T(8,128)S(1)} %get-tuple-element.40, f32[128,64]{1,0:T(8,128)S(1)} %bitcast.575, f32[128,64]{1,0:T(8,128)S(1)} %get-tuple-element.41, f32[128,64]{1,0:T(8,128)S(1)} %bitcast.569, f32[128,64]{1,0:T(8,128)S(1)} %get-tuple-element.39), kind=kLoop, calls=%fused_computation.17 | loop fusion | flops 6283264 | bytes 229376 | tf_op jit(solution)/shard_map/reduce_sum | solution.py:44
  113.0 6.3 %multiply_divide_fusion = f32[128,64,64]{2,1,0:T(8,128)} fusion(f32[128,64]{1,0:T(8,128)S(1)} %divide_reduce_fusion, f32[128,64]{1,0:T(8,128)S(1)} %bitcast.573, f32[128,64]{1,0:T(8,128)S(1)} %get-tuple-element.40, f32[128,64]{1,0:T(8,128)S(1)} %bitcast.576, f32[128,64]{1,0:T(8,128)S(1)} %get-tuple-element.41, f32[128,64]{1,0:T(8,128)S(1)} %bitcast.570, ...), kind=kLoop, calls=%fused_computation.15 | loop fusion | flops 6291456 | bytes 2326528 | tf_op jit(solution)/shard_map/div | solution.py:44
  119.3 10.2 %bitcast_reduce_fusion = f32[8,64,64]{2,0,1:T(8,128)S(1)} fusion(f32[8,128,64]{2,1,0:T(8,128)S(1)} %reshape.5006, f32[128,64]{1,0:T(8,128)S(1)} %divide_reduce_fusion, f32[128,64]{1,0:T(8,128)S(1)} %bitcast.574, f32[128,64]{1,0:T(8,128)S(1)} %get-tuple-element.40, f32[128,64]{1,0:T(8,128)S(1)} %bitcast.577, f32[128,64]{1,0:T(8,128)S(1)} %get-tuple-element.41, ...), kind=kOutput, calls=%fused_computation.98 | convolution fusion | flops 56655872 | bytes 622592 | tf_op jit(solution)/shard_map/qnr,nrs->qns/dot_general | solution.py:206
  129.7 2.7 divide_reduce_fusion.1
  132.4 3.1 %multiply_divide_fusion.1 = f32[64,64,64]{2,1,0:T(8,128)S(1)} fusion(f32[64,64]{1,0:T(8,128)S(1)} %divide_reduce_fusion.1, f32[64,64]{1,0:T(8,128)S(1)} %bitcast.582, f32[64,64]{1,0:T(8,128)} %copy-done.6, f32[64,64]{1,0:T(8,128)S(1)} %bitcast.585, f32[64,64]{1,0:T(8,128)} %copy-done.8, f32[64,64]{1,0:T(8,128)S(1)} %bitcast.579, ...), kind=kLoop, calls=%fused_computation.18 | loop fusion | flops 3145728 | bytes 1163264 | tf_op jit(solution)/shard_map/div | solution.py:44
  135.6 5.1 %bitcast_reduce_fusion.1 = f32[8,32,64]{2,0,1:T(8,128)S(1)} fusion(f32[8,64,64]{2,0,1:T(8,128)S(1)} %bitcast_reduce_fusion, f32[64,64]{1,0:T(8,128)S(1)} %divide_reduce_fusion.1, f32[64,64]{1,0:T(8,128)S(1)} %bitcast.583, f32[64,64]{1,0:T(8,128)S(1)} %copy-done.7, f32[64,64]{1,0:T(8,128)S(1)} %bitcast.586, f32[64,64]{1,0:T(8,128)S(1)} %copy-done.9, ...), kind=kOutput, calls=%fused_computation.156 | convolution fusion | flops 28327936 | bytes 311296 | tf_op jit(solution)/shard_map/qnr,nrs->qns/dot_general | solution.py:206
  140.8 1.4 divide_reduce_fusion.3
  142.2 2.1 multiply_divide_fusion.3
  144.3 2.6 bitcast_reduce_fusion.2
  147.6 1.4 multiply_divide_fusion.7
  149.1 1.3 bitcast_reduce_fusion.4
  151.0 1.2 bitcast_reduce_fusion.6
  152.3 0.9 constant_dynamic-slice_fusion.46
  153.2 0.8 fusion.666
  154.0 0.9 convolution_bitcast_fusion.1
  154.9 0.9 fusion.252
  156.0 0.9 fusion.249
  157.0 0.9 convolution_add_fusion.20
  157.9 0.9 fusion.18
  158.8 0.9 fusion.254
  159.9 0.9 fusion.245
  160.8 0.9 convolution_add_fusion.18
  161.7 0.9 fusion.16
  162.6 0.9 fusion.256
  163.6 0.9 fusion.241
  164.5 0.9 convolution_add_fusion.16
  165.4 0.9 fusion.14
  166.5 0.9 fusion.237
  167.4 0.9 convolution_add_fusion.14
  168.4 0.9 fusion.12
  169.3 0.9 fusion.260
  172.4 0.9 pad_maximum_fusion.1
  174.8 3.0 %copy.57 = f32[3,9728]{0,1:T(8,128)} copy(f32[3,9728]{1,0:T(4,128)S(1)} %pad_maximum_fusion.4) | data formatting | bytes 233472 | tf_op jit(solution)/shard_map/slice | solution.py:115
  177.9 73.4 %shard_map.73 = f32[8,8192]{1,0:T(8,128)} custom-call(s32[192]{0:T(256)} %reshape.4837.source_ref, f32[38,8,256]{2,1,0:T(8,128)} %bitcast.566, f32[38,256,3]{2,1,0:T(8,128)} %bitcast.565, f32[3,8192]{1,0:T(4,128)} %target_ref.1), custom_call_target="tpu_custom_call" | custom-call | flops 352321536 | bytes 5855232 | tf_op jit(solution)/shard_map/pallas_call | solution.py:73
  258.4 0.8 slice.1317
  259.3 0.8 slice.1315
  262.1 0.9 slice.1332
  263.0 0.9 slice.1330
  266.1 1.0 slice.1347
  267.1 1.0 slice.1345
  275.9 1.6 fusion.129
  277.5 1.2 fusion.86
  278.7 1.2 convolution_add_fusion.4
  279.9 2.3 fusion.38
  282.3 2.3 convolution_add_fusion.1
  284.6 2.3 convolution_add_fusion
  287.0 1.2 fusion.2
  288.3 3.2 %fusion = f32[8,32,64]{2,0,1:T(8,128)S(1)} fusion(f32[32,64,8]{1,2,0:T(8,128)S(1)} %convolution_add_fusion, f32[8,32,64]{2,0,1:T(8,128)S(1)} %bitcast.597, f32[32,64]{1,0:T(8,128)S(1)} %copy-done.76, f32[32,64]{1,0:T(8,128)S(1)} %bitcast.612, f32[32,64]{1,0:T(8,128)S(1)} %copy-done.22, f32[32,64]{1,0:T(8,128)S(1)} %bitcast.615, ...), kind=kOutput, calls=%fused_computation.28 | convolution fusion | flops 14172160 | bytes 253952 | tf_op jit(solution)/shard_map/qns,nrs->qnr/dot_general | solution.py:236
  291.6 2.7 fusion.37
  (494 shorter events, 43.8 us)
Async XLA Ops:
  0.9 56.9 %copy-start.84 = (f32[2,64]{1,0:T(2,128)}, f32[2,64]{1,0:T(2,128)S(1)}, u32[]{:S(2)}) copy-start(f32[2,64]{1,0:T(2,128)S(1)} %get-tuple-element.111) | copy-start | bytes 1540
  0.9 56.9 %copy-start.86 = (f32[2,64]{1,0:T(2,128)}, f32[2,64]{1,0:T(2,128)S(1)}, u32[]{:S(2)}) copy-start(f32[2,64]{1,0:T(2,128)S(1)} %get-tuple-element.112) | copy-start | bytes 1540
  0.9 56.9 %copy-start.88 = (f32[2,64]{1,0:T(2,128)}, f32[2,64]{1,0:T(2,128)S(1)}, u32[]{:S(2)}) copy-start(f32[2,64]{1,0:T(2,128)S(1)} %get-tuple-element.113) | copy-start | bytes 1540
  0.9 16.3 %copy-start.67 = (f32[4,64]{1,0:T(4,128)}, f32[4,64]{1,0:T(4,128)S(1)}, u32[]{:S(2)}) copy-start(f32[4,64]{1,0:T(4,128)S(1)} %get-tuple-element.114) | copy-start | bytes 3076
  0.9 16.3 %copy-start.69 = (f32[4,64]{1,0:T(4,128)}, f32[4,64]{1,0:T(4,128)S(1)}, u32[]{:S(2)}) copy-start(f32[4,64]{1,0:T(4,128)S(1)} %get-tuple-element.115) | copy-start | bytes 3076
  0.9 16.3 %copy-start.71 = (f32[4,64]{1,0:T(4,128)}, f32[4,64]{1,0:T(4,128)S(1)}, u32[]{:S(2)}) copy-start(f32[4,64]{1,0:T(4,128)S(1)} %get-tuple-element.116) | copy-start | bytes 3076
  0.9 15.2 %copy-start.53 = (f32[8,64]{1,0:T(8,128)}, f32[8,64]{1,0:T(8,128)S(1)}, u32[]{:S(2)}) copy-start(f32[8,64]{1,0:T(8,128)S(1)} %get-tuple-element.117) | copy-start | bytes 6148
  0.9 15.2 %copy-start.55 = (f32[8,64]{1,0:T(8,128)}, f32[8,64]{1,0:T(8,128)S(1)}, u32[]{:S(2)}) copy-start(f32[8,64]{1,0:T(8,128)S(1)} %get-tuple-element.118) | copy-start | bytes 6148
  1.0 15.2 %copy-start.57 = (f32[8,64]{1,0:T(8,128)}, f32[8,64]{1,0:T(8,128)S(1)}, u32[]{:S(2)}) copy-start(f32[8,64]{1,0:T(8,128)S(1)} %get-tuple-element.119) | copy-start | bytes 6148
  1.0 13.4 %copy-start.31 = (f32[16,64]{1,0:T(8,128)}, f32[16,64]{1,0:T(8,128)S(1)}, u32[]{:S(2)}) copy-start(f32[16,64]{1,0:T(8,128)S(1)} %get-tuple-element.120) | copy-start | bytes 12292
  1.0 13.4 %copy-start.33 = (f32[16,64]{1,0:T(8,128)}, f32[16,64]{1,0:T(8,128)S(1)}, u32[]{:S(2)}) copy-start(f32[16,64]{1,0:T(8,128)S(1)} %get-tuple-element.121) | copy-start | bytes 12292
  1.0 13.4 %copy-start.35 = (f32[16,64]{1,0:T(8,128)}, f32[16,64]{1,0:T(8,128)S(1)}, u32[]{:S(2)}) copy-start(f32[16,64]{1,0:T(8,128)S(1)} %get-tuple-element.122) | copy-start | bytes 12292
  15.7 17.4 %copy-start.2 = (f32[8,8192]{1,0:T(8,128)S(1)}, f32[8,8192]{1,0:T(8,128)}, u32[]{:S(2)}) copy-start(f32[8,8192]{1,0:T(8,128)} %param.17) | copy-start | bytes 786436
  15.7 17.4 %copy-start.4 = (f32[3,8192]{1,0:T(4,128)S(1)}, f32[3,8192]{1,0:T(4,128)}, u32[]{:S(2)}) copy-start(f32[3,8192]{1,0:T(4,128)} %target_ref.1) | copy-start | bytes 294916
  15.7 15.3 %copy-start.77 = (f32[4,2,64]{2,1,0:T(2,128)}, f32[4,2,64]{2,1,0:T(2,128)S(1)}, u32[]{:S(2)}) copy-start(f32[4,2,64]{2,1,0:T(2,128)S(1)} %broadcast_in_dim.212) | copy-start | bytes 6148
  15.7 15.3 %copy-start.79 = (f32[4,2,64]{2,1,0:T(2,128)}, f32[4,2,64]{2,1,0:T(2,128)S(1)}, u32[]{:S(2)}) copy-start(f32[4,2,64]{2,1,0:T(2,128)S(1)} %broadcast_in_dim.216) | copy-start | bytes 6148
  15.8 15.3 %copy-start.81 = (f32[4,2,64]{2,1,0:T(2,128)}, f32[4,2,64]{2,1,0:T(2,128)S(1)}, u32[]{:S(2)}) copy-start(f32[4,2,64]{2,1,0:T(2,128)S(1)} %broadcast_in_dim.214) | copy-start | bytes 6148
  16.2 14.9 %copy-start.99 = (f32[8,64]{1,0:T(8,128)}, f32[8,64]{1,0:T(8,128)S(1)}, u32[]{:S(2)}) copy-start(f32[8,64]{1,0:T(8,128)S(1)} %divide_reduce_fusion.8) | copy-start | bytes 6148
  16.9 36.5 %copy-start.16 = (f32[3,16128]{1,0:T(4,128)S(1)}, f32[3,16128]{1,0:T(4,128)}, u32[]{:S(2)}) copy-start(f32[3,16128]{1,0:T(4,128)} %param.22) | copy-start | bytes 580612
  16.9 14.2 %copy-start.92 = (f32[2,2,64]{2,1,0:T(2,128)}, f32[2,2,64]{2,1,0:T(2,128)S(1)}, u32[]{:S(2)}) copy-start(f32[2,2,64]{2,1,0:T(2,128)S(1)} %broadcast_in_dim.218) | copy-start | bytes 3076
  16.9 14.2 %copy-start.94 = (f32[2,2,64]{2,1,0:T(2,128)}, f32[2,2,64]{2,1,0:T(2,128)S(1)}, u32[]{:S(2)}) copy-start(f32[2,2,64]{2,1,0:T(2,128)S(1)} %broadcast_in_dim.222) | copy-start | bytes 3076
  16.9 14.2 %copy-start.96 = (f32[2,2,64]{2,1,0:T(2,128)}, f32[2,2,64]{2,1,0:T(2,128)S(1)}, u32[]{:S(2)}) copy-start(f32[2,2,64]{2,1,0:T(2,128)S(1)} %broadcast_in_dim.220) | copy-start | bytes 3076
  17.2 13.9 %copy-start.105 = (f32[4,64]{1,0:T(4,128)}, f32[4,64]{1,0:T(4,128)S(1)}, u32[]{:S(2)}) copy-start(f32[4,64]{1,0:T(4,128)S(1)} %divide_reduce_fusion.9) | copy-start | bytes 3076
  17.7 37.3 %copy-start.98 = (s32[32,3]{0,1:T(4,128)S(1)}, s32[32,3]{0,1:T(4,128)}, u32[]{:S(2)}) copy-start(s32[32,3]{0,1:T(4,128)} %param.23) | copy-start | bytes 1156
  17.7 38.5 %copy-start.101 = (s32[32,6]{0,1:T(8,128)S(1)}, s32[32,6]{0,1:T(8,128)}, u32[]{:S(2)}) copy-start(s32[32,6]{0,1:T(8,128)} %param.19) | copy-start | bytes 2308
  17.8 233.6 %collective-permute-start.3 = (f32[11,62,64]{2,0,1:T(8,128)S(1)}, f32[11,62,64]{2,0,1:T(8,128)}, u32[]{:S(2)}, u32[]{:S(2)}) collective-permute-start(f32[11,62,64]{2,0,1:T(8,128)S(1)} %maximum_maximum_fusion), channel_id=1, source_target_pairs={{4,0},{8,4},{12,8},{16,12},{20,16},{24,20},{28,24},{32,28},{36,32}... | collective-permute-start | bytes 523784 | tf_op jit(solution)/shard_map/ppermute | solution.py:30
  31.1 221.0 %collective-permute-start.2 = (f32[11,62,64]{2,0,1:T(8,128)S(1)}, f32[11,62,64]{2,0,1:T(8,128)}, u32[]{:S(2)}, u32[]{:S(2)}) collective-permute-start(f32[11,62,64]{2,0,1:T(8,128)S(1)} %maximum_maximum_fusion), channel_id=1, source_target_pairs={{0,4},{4,8},{8,12},{12,16},{16,20},{20,24},{24,28},{28,32},{32,36}... | collective-permute-start | bytes 523784 | tf_op jit(solution)/shard_map/ppermute | solution.py:29
  33.8 138.6 %collective-permute-start = (f32[11,768]{1,0:T(8,128)}, f32[11,768]{1,0:T(8,128)}, u32[]{:S(2)}, u32[]{:S(2)}) collective-permute-start(f32[11,768]{1,0:T(8,128)} %get-tuple-element.25), channel_id=1, source_target_pairs={{0,4},{4,8},{8,12},{12,16},{16,20},{20,24},{24,28},{28,32},{32,36}... | collective-permute-start | bytes 101384 | tf_op jit(solution)/shard_map/ppermute | solution.py:29
  35.7 136.7 %collective-permute-start.1 = (f32[11,768]{1,0:T(8,128)}, f32[11,768]{1,0:T(8,128)}, u32[]{:S(2)}, u32[]{:S(2)}) collective-permute-start(f32[11,768]{1,0:T(8,128)} %get-tuple-element.26), channel_id=1, source_target_pairs={{4,0},{8,4},{12,8},{16,12},{20,16},{24,20},{28,24},{32,28},{36,32}... | collective-permute-start | bytes 101384 | tf_op jit(solution)/shard_map/ppermute | solution.py:30
  53.6 53.5 %copy-start = (f32[3,252,64]{2,1,0:T(8,128)}, f32[3,252,64]{2,1,0:T(8,128)S(1)}, u32[]{:S(2)}) copy-start(f32[3,252,64]{2,1,0:T(8,128)S(1)} %reshape.4839) | copy-start | bytes 580612
  54.9 74.7 %copy-start.10 = (f32[32,64]{1,0:T(8,128)}, f32[32,64]{1,0:T(8,128)S(1)}, u32[]{:S(2)}) copy-start(f32[32,64]{1,0:T(8,128)S(1)} %get-tuple-element.36) | copy-start | bytes 24580
  54.9 74.7 %copy-start.12 = (f32[32,64]{1,0:T(8,128)}, f32[32,64]{1,0:T(8,128)S(1)}, u32[]{:S(2)}) copy-start(f32[32,64]{1,0:T(8,128)S(1)} %get-tuple-element.37) | copy-start | bytes 24580
  54.9 74.7 %copy-start.14 = (f32[32,64]{1,0:T(8,128)}, f32[32,64]{1,0:T(8,128)S(1)}, u32[]{:S(2)}) copy-start(f32[32,64]{1,0:T(8,128)S(1)} %get-tuple-element.38) | copy-start | bytes 24580
  55.0 74.7 %copy-start.6 = (f32[64,64]{1,0:T(8,128)}, f32[64,64]{1,0:T(8,128)S(1)}, u32[]{:S(2)}) copy-start(f32[64,64]{1,0:T(8,128)S(1)} %get-tuple-element.43) | copy-start | bytes 49156
  55.0 74.7 %copy-start.8 = (f32[64,64]{1,0:T(8,128)}, f32[64,64]{1,0:T(8,128)S(1)}, u32[]{:S(2)}) copy-start(f32[64,64]{1,0:T(8,128)S(1)} %get-tuple-element.44) | copy-start | bytes 49156
  152.3 18.7 %copy-start.85 = (f32[2,64]{1,0:T(2,128)S(1)}, f32[2,64]{1,0:T(2,128)}, u32[]{:S(2)}) copy-start(f32[2,64]{1,0:T(2,128)} %copy-done.84) | copy-start | bytes 1540
  152.3 18.7 %copy-start.87 = (f32[2,64]{1,0:T(2,128)S(1)}, f32[2,64]{1,0:T(2,128)}, u32[]{:S(2)}) copy-start(f32[2,64]{1,0:T(2,128)} %copy-done.86) | copy-start | bytes 1540
  152.3 18.7 %copy-start.89 = (f32[2,64]{1,0:T(2,128)S(1)}, f32[2,64]{1,0:T(2,128)}, u32[]{:S(2)}) copy-start(f32[2,64]{1,0:T(2,128)} %copy-done.88) | copy-start | bytes 1540
  152.3 18.7 %copy-start.111 = (f32[64]{0:T(128)S(1)}, f32[64]{0:T(128)}, u32[]{:S(2)}) copy-start(f32[64]{0:T(128)} %copy-done.110) | copy-start | bytes 772
  152.3 18.7 %copy-start.113 = (f32[64]{0:T(128)S(1)}, f32[64]{0:T(128)}, u32[]{:S(2)}) copy-start(f32[64]{0:T(128)} %copy-done.112) | copy-start | bytes 772
  152.3 18.7 %copy-start.115 = (f32[64]{0:T(128)S(1)}, f32[64]{0:T(128)}, u32[]{:S(2)}) copy-start(f32[64]{0:T(128)} %copy-done.114) | copy-start | bytes 772
  152.3 18.7 %copy-start.117 = (f32[2,64]{1,0:T(2,128)S(1)}, f32[2,64]{1,0:T(2,128)}, u32[]{:S(2)}) copy-start(f32[2,64]{1,0:T(2,128)} %copy-done.116) | copy-start | bytes 1540
  155.9 15.4 %copy-start.138 = (s32[16]{0:T(128)S(1)}, s32[16]{0:T(128)}, u32[]{:S(2)}) copy-start(s32[16]{0:T(128)} %compare_select_fusion.5) | copy-start | bytes 196
  155.9 15.4 %copy-start.139 = (s32[16]{0:T(128)S(1)}, s32[16]{0:T(128)}, u32[]{:S(2)}) copy-start(s32[16]{0:T(128)} %compare_select_fusion.4) | copy-start | bytes 196
  155.9 15.4 %copy-start.136 = (s32[8]{0:T(128)S(1)}, s32[8]{0:T(128)}, u32[]{:S(2)}) copy-start(s32[8]{0:T(128)} %compare_select_fusion.7) | copy-start | bytes 100
  155.9 15.4 %copy-start.137 = (s32[8]{0:T(128)S(1)}, s32[8]{0:T(128)}, u32[]{:S(2)}) copy-start(s32[8]{0:T(128)} %compare_select_fusion.6) | copy-start | bytes 100
  156.0 15.4 %copy-start.134 = (s32[4]{0:T(128)S(1)}, s32[4]{0:T(128)}, u32[]{:S(2)}) copy-start(s32[4]{0:T(128)} %compare_select_fusion.9) | copy-start | bytes 52
  156.0 15.4 %copy-start.135 = (s32[8]{0:T(128)S(1)}, s32[8]{0:T(128)}, u32[]{:S(2)}) copy-start(s32[8]{0:T(128)} %compare_select_fusion.8) | copy-start | bytes 100
  156.9 14.5 %copy-start.132 = (s32[4]{0:T(128)S(1)}, s32[4]{0:T(128)}, u32[]{:S(2)}) copy-start(s32[4]{0:T(128)} %compare_select_fusion.11) | copy-start | bytes 52
  156.9 14.5 %copy-start.133 = (s32[4]{0:T(128)S(1)}, s32[4]{0:T(128)}, u32[]{:S(2)}) copy-start(s32[4]{0:T(128)} %compare_select_fusion.10) | copy-start | bytes 52
  156.9 14.6 %copy-start.129 = (s32[2]{0:T(128)S(1)}, s32[2]{0:T(128)}, u32[]{:S(2)}) copy-start(s32[2]{0:T(128)} %compare_select_fusion.13) | copy-start | bytes 28
  156.9 14.6 %copy-start.130 = (s32[2]{0:T(128)S(1)}, s32[2]{0:T(128)}, u32[]{:S(2)}) copy-start(s32[2]{0:T(128)} %compare_select_fusion.12) | copy-start | bytes 28
  156.9 14.6 %copy-start.109 = (s32[32]{0:T(128)S(1)}, s32[32]{0:T(128)}, u32[]{:S(2)}) copy-start(s32[32]{0:T(128)} %get-tuple-element.174) | copy-start | bytes 388
  156.9 14.6 %copy-start.131 = (s32[16]{0:T(128)S(1)}, s32[16]{0:T(128)}, u32[]{:S(2)}) copy-start(s32[16]{0:T(128)} %compare_select_fusion.3) | copy-start | bytes 196
  156.9 14.6 %copy-start.107 = (s32[32]{0:T(128)S(1)}, s32[32]{0:T(128)}, u32[]{:S(2)}) copy-start(s32[32]{0:T(128)} %get-tuple-element.17) | copy-start | bytes 388
  157.0 14.6 %copy-start.108 = (s32[32]{0:T(128)S(1)}, s32[32]{0:T(128)}, u32[]{:S(2)}) copy-start(s32[32]{0:T(128)} %get-tuple-element.172) | copy-start | bytes 388
  177.9 75.5 %copy-start.128 = (pred[2]{0:T(512)(128)(4,1)S(1)}, pred[2]{0:T(512)(128)(4,1)}, u32[]{:S(2)}) copy-start(pred[2]{0:T(512)(128)(4,1)} %get-tuple-element.200) | copy-start | bytes 10
  177.9 76.8 %copy-start.127 = (pred[2]{0:T(512)(128)(4,1)S(1)}, pred[2]{0:T(512)(128)(4,1)}, u32[]{:S(2)}) copy-start(pred[2]{0:T(512)(128)(4,1)} %get-tuple-element.201) | copy-start | bytes 10
  177.9 76.9 %copy-start.125 = (pred[2]{0:T(512)(128)(4,1)S(1)}, pred[2]{0:T(512)(128)(4,1)}, u32[]{:S(2)}) copy-start(pred[2]{0:T(512)(128)(4,1)} %broadcast_compare_fusion.1) | copy-start | bytes 10
  177.9 79.1 %copy-start.126 = (pred[4]{0:T(512)(128)(4,1)S(1)}, pred[4]{0:T(512)(128)(4,1)}, u32[]{:S(2)}) copy-start(pred[4]{0:T(512)(128)(4,1)} %get-tuple-element.198) | copy-start | bytes 16
  177.9 80.3 %copy-start.124 = (pred[4]{0:T(512)(128)(4,1)S(1)}, pred[4]{0:T(512)(128)(4,1)}, u32[]{:S(2)}) copy-start(pred[4]{0:T(512)(128)(4,1)} %get-tuple-element.199) | copy-start | bytes 16
  177.9 80.4 %copy-start.122 = (pred[4]{0:T(512)(128)(4,1)S(1)}, pred[4]{0:T(512)(128)(4,1)}, u32[]{:S(2)}) copy-start(pred[4]{0:T(512)(128)(4,1)} %compare_and_fusion.11) | copy-start | bytes 16
  177.9 82.8 %copy-start.123 = (pred[8]{0:T(512)(128)(4,1)S(1)}, pred[8]{0:T(512)(128)(4,1)}, u32[]{:S(2)}) copy-start(pred[8]{0:T(512)(128)(4,1)} %get-tuple-element.196) | copy-start | bytes 28
  251.4 13.2 %copy-start.120 = (pred[16]{0:T(512)(128)(4,1)S(1)}, pred[16]{0:T(512)(128)(4,1)}, u32[]{:S(2)}) copy-start(pred[16]{0:T(512)(128)(4,1)} %get-tuple-element.194) | copy-start | bytes 52
  (92 other events, 350.7 us)

commit v4 on v3

--- a/solution.py
+++ b/solution.py
@@ -194,21 +194,26 @@
     for height in range(top_levels):
         offset = 2 * groups - 2 * (groups >> height)
         level_points.append(top_points[:, offset : offset + (groups >> height), :])
-    level_moments_top = [
-        lax.all_gather(level_moments[local_depth], "boxes", axis=1, tiled=True)
-    ]
-    edge_maps = []
+    own_edges = []
     for height in range(top_levels - 1):
-        interp_map = interpolation(
-            level_points[height], jnp.repeat(level_points[height + 1], 2, axis=1), kernel_scale
-        )
-        edge_maps.append(interp_map)
-        lifted = jnp.einsum("qnr,nrs->qns", level_moments_top[-1], interp_map, precision=PRECISE)
-        level_moments_top.append(lifted.reshape(rows_here, -1, 2, R).sum(axis=2))
+        own_edges.append(
+            interpolation(
+                lax.dynamic_slice_in_dim(level_points[height], device // 2**height, 1, 1),
+                lax.dynamic_slice_in_dim(level_points[height + 1], device // 2 ** (height + 1), 1, 1),
+                kernel_scale,
+            )
+        )
+    path_moments = [level_moments[local_depth]]
+    for height in range(top_levels - 1):
+        path_moments.append(
+            jnp.einsum("qnr,nrs->qns", path_moments[-1], own_edges[height], precision=PRECISE)
+        )
+    gathered = lax.all_gather(jnp.concatenate(path_moments, axis=1), "boxes", axis=0)
     top_couplings = []
     for height in range(top_levels):
         number = groups >> height
         node = device // 2**height
+        level_sums = gathered[:, :, height, :].reshape(number, 2**height, rows_here, R).sum(axis=1)
         third = jnp.where(node % 2 == 0, node + 3, node - 3) % number
         if number > 4:
             source_ids = [(node - 2) % number, (node + 2) % number, third]
@@ -220,16 +225,15 @@
             kernel_block = kernel_matrix(
                 lax.dynamic_slice_in_dim(level_points[height], source, 1, 1), target_points, kernel_scale
             )
-            source_moment = lax.dynamic_slice_in_dim(level_moments_top[height], source, 1, 1)
+            source_moment = lax.dynamic_index_in_dim(level_sums, source, 0, keepdims=False)
             coupling = coupling + jnp.einsum(
-                "qnr,nrs->qns", source_moment, kernel_block, precision=PRECISE
+                "qnr,nrs->qns", source_moment[:, None, :], kernel_block, precision=PRECISE
             )
         top_couplings.append(coupling)
     descent = top_couplings[-1]
     for height in range(top_levels - 2, -1, -1):
-        own_edge = lax.dynamic_slice_in_dim(edge_maps[height], device // 2**height, 1, 0)
         descent = (
-            jnp.einsum("qns,nrs->qnr", descent, own_edge, precision=PRECISE)
+            jnp.einsum("qns,nrs->qnr", descent, own_edges[height], precision=PRECISE)
             + top_couplings[height]
         )
     for height in range(local_depth - 1, -1, -1):

time: 300 us -> 216 us (0.72)
  the two profiles are of different devices: /device:TPU:6 before, /device:TPU:22 now
where the time goes in v4:
time: 216 us; the launch traced here: 214 us
  Pallas kernels  77.9 us (36%)
  matrix products  52.5 us (24%)
  local copies, waits for them, and re-layouts  33.2 us (15%)
  starting transfers between devices  20.2 us (9%)
  between operations  17.7 us (8%)
  other arithmetic  13 us (6%)
    pallas_call x1, Pallas kernels, near_field_call(): pl.pallas_call(functools.partial(near_kernel, kernel_scale, slots), out_s...  77.9 us
    dot_general x15, matrix products, body(): jnp.einsum('qnr,nrs->qns', source_moment, kernel_block, precision=PRECISE)  18.1 us
    ppermute x2, starting transfers between devices, with_halo(): after = lax.ppermute(initial, axis, down)  16.3 us
    dot_general x16, matrix products, body(): jnp.einsum('qnr,nrs->qns', source_moment[:, None, :], kernel_block, preci...  11.2 us
    slice x16, local copies, waits for them, and re-layouts, kernel_matrix(): left_points[0][..., :, None] - right_points[0][..., None, :]  9.45 us
    gather x15, local copies, waits for them, and re-layouts, body(): picked = jnp.take(view, slot_ids[slot], axis=1)  8.89 us
    dot_general x5, matrix products, body(): jnp.einsum('qns,nrs->qnr', jnp.repeat(descent, 2, axis=1), transfer_maps[...  6.46 us
    dot_general x5, matrix products, body(): jnp.einsum('qnr,nrs->qns', level_moments[-1], interp_map, precision=PRECISE)  5.15 us
  transfers between devices with their start and end apart: 5, of which 0 were waited for; matrix products, arithmetic and copies ran while one was open for 23% of the time, Pallas kernels for 36%

profile of v4, /device:TPU:22, one launch (start us, length us, event | category | flops | bytes accessed | tf_op | source)
XLA Modules:
  0.0 214.5 jit_solution(3368983582325681643)
XLA Ops:
  6.5 0.8 reshape.7477
  7.6 0.9 slice_reduce_fusion.5
  8.5 0.9 reshape.7513
  9.6 1.3 slice_reduce_fusion.2
  11.1 1.1 divide_reduce_fusion
  12.2 3.8 %constant_dynamic-update-slice_fusion.11 = (f32[8,62,64]{2,0,1:T(8,128)S(1)}, f32[8,32,64]{2,0,1:T(8,128)S(1)}) fusion(f32[8,32,256]{2,0,1:T(8,128)} %bitcast.566, f32[32,256]{1,0:T(8,128)S(1)} %divide_reduce_fusion, f32[32,64]{1,0:T(8,128)S(1)} %sub.3089, f32[32,256]{1,0:T(8,128)S(1)} %sub.3087, f32[32,64]{1,0:T(8,128)S(1)} %sub.3084, ...), kind=kOutput, calls=%fused_computation.609 | convolution fusion | flops 56623104 | bytes 679936 | tf_op jit(solution)/shard_map/qbp,bpr->qbr/dot_general | solution.py:135
  16.1 1.4 divide_reduce_fusion.1
  17.5 2.6 %bitcast_reduce_fusion = f32[8,16,64]{2,0,1:T(8,128)S(1)} fusion(f32[8,32,64]{2,0,1:T(8,128)S(1)} %get-tuple-element.179, f32[32,64]{1,0:T(8,128)S(1)} %divide_reduce_fusion.1, f32[32,64]{1,0:T(8,128)S(1)} %bitcast.573, f32[32,64]{1,0:T(8,128)S(1)} %sub.3089, f32[32,64]{1,0:T(8,128)S(1)} %bitcast.576, f32[32,64]{1,0:T(8,128)S(1)} %sub.3084, ...), kind=kOutput, calls=%fused_computation.202 | convolution fusion | flops 14163968 | bytes 155648 | tf_op jit(solution)/shard_map/qnr,nrs->qns/dot_general | solution.py:142
  20.2 0.7 divide_reduce_fusion.2
  20.8 1.3 bitcast_reduce_fusion.1
  22.6 0.6 bitcast_reduce_fusion.2
  24.2 10.4 %collective-permute-start.3 = (f32[11,62,64]{2,0,1:T(8,128)S(1)}, f32[11,62,64]{2,0,1:T(8,128)S(1)}, u32[]{:S(2)}, u32[]{:S(2)}) collective-permute-start(f32[11,62,64]{2,0,1:T(8,128)S(1)} %maximum_maximum_fusion), channel_id=1, source_target_pairs={{4,0},{8,4},{12,8},{16,12},{20,16},{24,20},{28,24},{32,28},{36,32}... | collective-permute-start | bytes 523784 | tf_op jit(solution)/shard_map/ppermute | solution.py:30
  34.6 1.9 collective-permute-start.2
  37.4 0.7 fusion.706
  39.4 0.6 fusion.728
  40.1 0.7 fusion.715
  43.2 1.9 collective-permute-start
  45.2 5.9 %collective-permute-start.1 = (f32[11,768]{1,0:T(8,128)S(1)}, f32[11,768]{1,0:T(8,128)S(1)}, u32[]{:S(2)}, u32[]{:S(2)}) collective-permute-start(f32[11,768]{1,0:T(8,128)S(1)} %get-tuple-element.34), channel_id=1, source_target_pairs={{4,0},{8,4},{12,8},{16,12},{20,16},{24,20},{28,24},{32,28},{36,32}... | collective-permute-start | bytes 101384 | tf_op jit(solution)/shard_map/ppermute | solution.py:30
  55.8 0.7 reshape.7476.source_ref
  56.7 0.8 slice.1104
  57.4 3.0 %copy.49 = f32[3,9728]{0,1:T(8,128)} copy(f32[3,9728]{1,0:T(4,128)S(1)} %pad_maximum_fusion.4) | data formatting | bytes 233472 | tf_op jit(solution)/shard_map/slice | solution.py:115
  60.4 77.9 %shard_map.73 = f32[8,8192]{1,0:T(8,128)} custom-call(s32[192]{0:T(256)} %reshape.7476.source_ref, f32[38,8,256]{2,1,0:T(8,128)} %bitcast.565, f32[38,256,3]{2,1,0:T(8,128)} %bitcast.558, f32[3,8192]{1,0:T(4,128)} %target_ref.1), custom_call_target="tpu_custom_call" | custom-call | flops 352321536 | bytes 5855232 | tf_op jit(solution)/shard_map/pallas_call | solution.py:73
  140.7 0.7 select_bitcast_fusion.14
  141.3 1.4 fusion.874
  151.7 0.6 fusion.863
  152.8 0.7 gather_fusion.9
  154.4 0.6 fusion.865
  155.3 0.7 gather_fusion.14
  156.0 0.7 gather_fusion.13
  156.7 0.7 gather_fusion.12
  157.5 0.7 select_bitcast_fusion.12
  158.2 1.0 fusion.224
  160.3 0.9 convolution_add_fusion.10
  161.3 1.0 convolution_add_fusion.8
  162.9 1.2 convolution_add_fusion.6
  164.6 1.2 fusion.83
  165.8 1.6 convolution_add_fusion.4
  167.4 2.3 %fusion.39 = f32[32,64,8]{1,2,0:T(8,128)S(1)} fusion(f32[32,64]{1,0:T(8,128)S(1)} %sub.3089, f32[32,64]{1,0:T(8,128)S(1)} %bitcast.606, f32[32,64]{1,0:T(8,128)S(1)} %sub.3084, f32[32,64]{1,0:T(8,128)S(1)} %bitcast.607, f32[32,64]{1,0:T(8,128)S(1)} %sub.3079, f32[32,64]{1,0:T(8,128)S(1)} %bitcast.605, f32[11,32,64]{2,0,1:T(8,128)S(1)} %select_bitcast_fusion.2, ...), kind=kOutput, calls=%fused_computation.86 | convolution fusion | flops 14041088 | bytes 295424 | tf_op jit(solution)/shard_map/qnr,nrs->qns/dot_general | solution.py:187
  169.7 2.3 %convolution_add_fusion.1 = f32[32,64,8]{1,2,0:T(8,128)S(1)} fusion(f32[32,64,8]{1,2,0:T(8,128)S(1)} %fusion.39, f32[32,64]{1,0:T(8,128)S(1)} %bitcast.603, f32[32,64]{1,0:T(8,128)S(1)} %bitcast.604, f32[32,64]{1,0:T(8,128)S(1)} %bitcast.602, f32[32,64]{1,0:T(8,128)S(1)} %sub.3089, f32[32,64]{1,0:T(8,128)S(1)} %sub.3084, f32[32,64]{1,0:T(8,128)S(1)} %sub.3079, ...), kind=kOutput, calls=%fused_computation.20 | convolution fusion | flops 14057472 | bytes 426496 | tf_op jit(solution)/shard_map/qnr,nrs->qns/dot_general | solution.py:187
  172.1 2.6 %convolution_add_fusion = f32[32,64,8]{1,2,0:T(8,128)} fusion(f32[32,64,8]{1,2,0:T(8,128)S(1)} %convolution_add_fusion.1, f32[32,64]{1,0:T(8,128)S(1)} %bitcast.600, f32[32,64]{1,0:T(8,128)S(1)} %bitcast.601, f32[32,64]{1,0:T(8,128)S(1)} %bitcast.599, f32[32,64]{1,0:T(8,128)S(1)} %sub.3089, f32[32,64]{1,0:T(8,128)S(1)} %sub.3084, f32[32,64]{1,0:T(8,128)S(1)} %sub.3079, ...), kind=kOutput, calls=%fused_computation.19 | convolution fusion | flops 14057472 | bytes 426496 | tf_op jit(solution)/shard_map/qnr,nrs->qns/dot_general | solution.py:187
  174.7 2.0 fusion.858
  176.7 0.8 reduce_sum.210
  177.8 0.9 convolution_bitcast_fusion.1
  178.7 0.9 fusion.249
  181.0 0.9 fusion.242
  182.0 0.9 convolution_add_fusion.18
  182.9 0.9 fusion.16
  183.8 0.8 fusion.256
  185.0 0.9 convolution_add_fusion.16
  186.1 0.9 fusion.260
  187.0 1.0 fusion.234
  188.1 0.9 convolution_add_fusion.14
  189.0 0.9 fusion.12
  190.0 0.9 fusion.264
  190.9 0.9 fusion.230
  191.8 0.9 convolution_add_fusion.12
  192.7 0.9 fusion.10
  195.1 1.1 fusion.6
  196.3 0.8 fusion.171
  197.8 1.6 fusion.126
  199.6 1.2 fusion.2
  200.9 3.2 %fusion = f32[8,32,64]{2,0,1:T(8,128)S(1)} fusion(f32[32,64,8]{1,2,0:T(8,128)S(1)} %copy-done.197, f32[8,32,64]{2,0,1:T(8,128)S(1)} %bitcast.568, f32[32,64]{1,0:T(8,128)S(1)} %copy-done.58, f32[32,64]{1,0:T(8,128)S(1)} %bitcast.574, f32[32,64]{1,0:T(8,128)S(1)} %copy-done.7, f32[32,64]{1,0:T(8,128)S(1)} %bitcast.577, f32[32,64]{1,0:T(8,128)S(1)} %copy-done.5, ...), kind=kOutput, calls=%fused_computation.22 | convolution fusion | flops 14172160 | bytes 253952 | tf_op jit(solution)/shard_map/qns,nrs->qnr/dot_general | solution.py:240
  204.2 2.7 %fusion.38 = f32[32,256,8]{1,2,0:T(8,128)S(1)} fusion(f32[8,32,64]{2,0,1:T(8,128)S(1)} %fusion, f32[32,256]{1,0:T(8,128)S(1)} %copy-done.43, f32[32,64]{1,0:T(8,128)S(1)} %copy-done.7, f32[32,256]{1,0:T(8,128)S(1)} %copy-done.11, f32[32,64]{1,0:T(8,128)S(1)} %copy-done.5, f32[32,256]{1,0:T(8,128)S(1)} %copy-done.13, f32[32,64]{1,0:T(8,128)S(1)} %sub.3079, ...), kind=kOutput, calls=%fused_computation.85 | convolution fusion | flops 56623104 | bytes 483328 | tf_op jit(solution)/shard_map/qbr,bpr->qbp/dot_general | solution.py:244
  206.9 0.8 add_add_fusion
  (565 shorter events, 28.3 us)
Async XLA Ops:
  6.5 168.1 %all-gather.3.cloned.1.call-start = ((), (), s32[]{:S(2)}) async-start(), calls=%async_computation | async-start | bytes 3170304 | tf_op jit(solution)/shard_map/all_gather | solution.py:211
  7.4 30.9 %copy-start.65 = (f32[2,64]{1,0:T(2,128)}, f32[2,64]{1,0:T(2,128)S(1)}, u32[]{:S(2)}) copy-start(f32[2,64]{1,0:T(2,128)S(1)} %get-tuple-element.101) | copy-start | bytes 1540
  7.4 30.9 %copy-start.68 = (f32[2,64]{1,0:T(2,128)}, f32[2,64]{1,0:T(2,128)S(1)}, u32[]{:S(2)}) copy-start(f32[2,64]{1,0:T(2,128)S(1)} %get-tuple-element.102) | copy-start | bytes 1540
  7.4 30.9 %copy-start.71 = (f32[2,64]{1,0:T(2,128)}, f32[2,64]{1,0:T(2,128)S(1)}, u32[]{:S(2)}) copy-start(f32[2,64]{1,0:T(2,128)S(1)} %get-tuple-element.103) | copy-start | bytes 1540
  7.4 16.2 %copy-start.51 = (f32[4,64]{1,0:T(4,128)}, f32[4,64]{1,0:T(4,128)S(1)}, u32[]{:S(2)}) copy-start(f32[4,64]{1,0:T(4,128)S(1)} %get-tuple-element.105) | copy-start | bytes 3076
  7.4 16.2 %copy-start.54 = (f32[4,64]{1,0:T(4,128)}, f32[4,64]{1,0:T(4,128)S(1)}, u32[]{:S(2)}) copy-start(f32[4,64]{1,0:T(4,128)S(1)} %get-tuple-element.106) | copy-start | bytes 3076
  7.5 153.8 %copy-start.49 = (f32[4,64]{1,0:T(4,128)}, f32[4,64]{1,0:T(4,128)S(1)}, u32[]{:S(2)}) copy-start(f32[4,64]{1,0:T(4,128)S(1)} %get-tuple-element.104) | copy-start | bytes 3076
  7.5 155.4 %copy-start.30 = (f32[8,64]{1,0:T(8,128)}, f32[8,64]{1,0:T(8,128)S(1)}, u32[]{:S(2)}) copy-start(f32[8,64]{1,0:T(8,128)S(1)} %get-tuple-element.107) | copy-start | bytes 6148
  7.5 155.4 %copy-start.32 = (f32[8,64]{1,0:T(8,128)}, f32[8,64]{1,0:T(8,128)S(1)}, u32[]{:S(2)}) copy-start(f32[8,64]{1,0:T(8,128)S(1)} %get-tuple-element.108) | copy-start | bytes 6148
  7.5 155.4 %copy-start.34 = (f32[8,64]{1,0:T(8,128)}, f32[8,64]{1,0:T(8,128)S(1)}, u32[]{:S(2)}) copy-start(f32[8,64]{1,0:T(8,128)S(1)} %get-tuple-element.109) | copy-start | bytes 6148
  7.5 158.3 %copy-start.16 = (f32[16,64]{1,0:T(8,128)}, f32[16,64]{1,0:T(8,128)S(1)}, u32[]{:S(2)}) copy-start(f32[16,64]{1,0:T(8,128)S(1)} %get-tuple-element.110) | copy-start | bytes 12292
  7.5 158.3 %copy-start.18 = (f32[16,64]{1,0:T(8,128)}, f32[16,64]{1,0:T(8,128)S(1)}, u32[]{:S(2)}) copy-start(f32[16,64]{1,0:T(8,128)S(1)} %get-tuple-element.111) | copy-start | bytes 12292
  7.5 158.3 %copy-start.20 = (f32[16,64]{1,0:T(8,128)}, f32[16,64]{1,0:T(8,128)S(1)}, u32[]{:S(2)}) copy-start(f32[16,64]{1,0:T(8,128)S(1)} %get-tuple-element.112) | copy-start | bytes 12292
  9.5 162.6 %copy-start.4 = (f32[32,64]{1,0:T(8,128)}, f32[32,64]{1,0:T(8,128)S(1)}, u32[]{:S(2)}) copy-start(f32[32,64]{1,0:T(8,128)S(1)} %sub.3084) | copy-start | bytes 24580
  9.6 162.5 %copy-start.6 = (f32[32,64]{1,0:T(8,128)}, f32[32,64]{1,0:T(8,128)S(1)}, u32[]{:S(2)}) copy-start(f32[32,64]{1,0:T(8,128)S(1)} %sub.3089) | copy-start | bytes 24580
  22.2 14.8 %copy-start.59 = (f32[4,2,64]{2,1,0:T(2,128)}, f32[4,2,64]{2,1,0:T(2,128)S(1)}, u32[]{:S(2)}) copy-start(f32[4,2,64]{2,1,0:T(2,128)S(1)} %broadcast_in_dim.163) | copy-start | bytes 6148
  22.2 14.8 %copy-start.61 = (f32[4,2,64]{2,1,0:T(2,128)}, f32[4,2,64]{2,1,0:T(2,128)S(1)}, u32[]{:S(2)}) copy-start(f32[4,2,64]{2,1,0:T(2,128)S(1)} %broadcast_in_dim.167) | copy-start | bytes 6148
  22.2 14.8 %copy-start.63 = (f32[4,2,64]{2,1,0:T(2,128)}, f32[4,2,64]{2,1,0:T(2,128)S(1)}, u32[]{:S(2)}) copy-start(f32[4,2,64]{2,1,0:T(2,128)S(1)} %broadcast_in_dim.165) | copy-start | bytes 6148
  22.6 14.4 %copy-start.116 = (f32[8,64]{1,0:T(8,128)}, f32[8,64]{1,0:T(8,128)S(1)}, u32[]{:S(2)}) copy-start(f32[8,64]{1,0:T(8,128)S(1)} %divide_reduce_fusion.3) | copy-start | bytes 6148
  22.6 14.4 %copy-start.3 = (f32[3,16128]{1,0:T(4,128)S(1)}, f32[3,16128]{1,0:T(4,128)}, u32[]{:S(2)}) copy-start(f32[3,16128]{1,0:T(4,128)} %param.22) | copy-start | bytes 580612
  23.3 15.3 %copy-start.76 = (f32[2,2,64]{2,1,0:T(2,128)}, f32[2,2,64]{2,1,0:T(2,128)S(1)}, u32[]{:S(2)}) copy-start(f32[2,2,64]{2,1,0:T(2,128)S(1)} %broadcast_in_dim.169) | copy-start | bytes 3076
  23.3 15.3 %copy-start.78 = (f32[2,2,64]{2,1,0:T(2,128)}, f32[2,2,64]{2,1,0:T(2,128)S(1)}, u32[]{:S(2)}) copy-start(f32[2,2,64]{2,1,0:T(2,128)S(1)} %broadcast_in_dim.173) | copy-start | bytes 3076
  23.4 15.3 %copy-start.80 = (f32[2,2,64]{2,1,0:T(2,128)}, f32[2,2,64]{2,1,0:T(2,128)S(1)}, u32[]{:S(2)}) copy-start(f32[2,2,64]{2,1,0:T(2,128)S(1)} %broadcast_in_dim.171) | copy-start | bytes 3076
  23.7 15.0 %copy-start.131 = (f32[4,64]{1,0:T(4,128)}, f32[4,64]{1,0:T(4,128)S(1)}, u32[]{:S(2)}) copy-start(f32[4,64]{1,0:T(4,128)S(1)} %divide_reduce_fusion.4) | copy-start | bytes 3076
  24.1 19.0 %copy-start.1 = (f32[8,8192]{1,0:T(8,128)S(1)}, f32[8,8192]{1,0:T(8,128)}, u32[]{:S(2)}) copy-start(f32[8,8192]{1,0:T(8,128)} %param.17) | copy-start | bytes 786436
  24.2 114.2 %collective-permute-start.3 = (f32[11,62,64]{2,0,1:T(8,128)S(1)}, f32[11,62,64]{2,0,1:T(8,128)S(1)}, u32[]{:S(2)}, u32[]{:S(2)}) collective-permute-start(f32[11,62,64]{2,0,1:T(8,128)S(1)} %maximum_maximum_fusion), channel_id=1, source_target_pairs={{4,0},{8,4},{12,8},{16,12},{20,16},{24,20},{28,24},{32,28},{36,32}... | collective-permute-start | bytes 523784 | tf_op jit(solution)/shard_map/ppermute | solution.py:30
  34.6 103.8 %collective-permute-start.2 = (f32[11,62,64]{2,0,1:T(8,128)S(1)}, f32[11,62,64]{2,0,1:T(8,128)S(1)}, u32[]{:S(2)}, u32[]{:S(2)}) collective-permute-start(f32[11,62,64]{2,0,1:T(8,128)S(1)} %maximum_maximum_fusion), channel_id=1, source_target_pairs={{0,4},{4,8},{8,12},{12,16},{16,20},{20,24},{24,28},{28,32},{32,36}... | collective-permute-start | bytes 523784 | tf_op jit(solution)/shard_map/ppermute | solution.py:29
  37.0 15.4 %copy-start.91 = (s32[32,3]{0,1:T(4,128)S(1)}, s32[32,3]{0,1:T(4,128)}, u32[]{:S(2)}) copy-start(s32[32,3]{0,1:T(4,128)} %param.23) | copy-start | bytes 1156
  37.0 16.6 %copy-start.118 = (s32[32,6]{0,1:T(8,128)S(1)}, s32[32,6]{0,1:T(8,128)}, u32[]{:S(2)}) copy-start(s32[32,6]{0,1:T(8,128)} %param.19) | copy-start | bytes 2308
  38.1 15.6 %copy-start.149 = (f32[64]{0:T(128)}, f32[64]{0:T(128)S(1)}, u32[]{:S(2)}) copy-start(f32[64]{0:T(128)S(1)} %get-tuple-element.37) | copy-start | bytes 772
  38.1 18.5 %copy-start.92 = (f32[64]{0:T(128)}, f32[64]{0:T(128)S(1)}, u32[]{:S(2)}) copy-start(f32[64]{0:T(128)S(1)} %get-tuple-element.196) | copy-start | bytes 772
  38.1 18.5 %copy-start.94 = (f32[64]{0:T(128)}, f32[64]{0:T(128)S(1)}, u32[]{:S(2)}) copy-start(f32[64]{0:T(128)S(1)} %get-tuple-element.200) | copy-start | bytes 772
  38.1 18.5 %copy-start.96 = (f32[64]{0:T(128)}, f32[64]{0:T(128)S(1)}, u32[]{:S(2)}) copy-start(f32[64]{0:T(128)S(1)} %get-tuple-element.201) | copy-start | bytes 772
  38.1 18.5 %copy-start.145 = (f32[64]{0:T(128)}, f32[64]{0:T(128)S(1)}, u32[]{:S(2)}) copy-start(f32[64]{0:T(128)S(1)} %get-tuple-element.35) | copy-start | bytes 772
  38.1 18.5 %copy-start.147 = (f32[64]{0:T(128)}, f32[64]{0:T(128)S(1)}, u32[]{:S(2)}) copy-start(f32[64]{0:T(128)S(1)} %get-tuple-element.36) | copy-start | bytes 772
  39.3 16.3 %copy-start.104 = (f32[64]{0:T(128)}, f32[64]{0:T(128)S(1)}, u32[]{:S(2)}) copy-start(f32[64]{0:T(128)S(1)} %get-tuple-element.149) | copy-start | bytes 772
  39.3 16.3 %copy-start.106 = (f32[64]{0:T(128)}, f32[64]{0:T(128)S(1)}, u32[]{:S(2)}) copy-start(f32[64]{0:T(128)S(1)} %get-tuple-element.150) | copy-start | bytes 772
  39.4 16.3 %copy-start.108 = (f32[64]{0:T(128)}, f32[64]{0:T(128)S(1)}, u32[]{:S(2)}) copy-start(f32[64]{0:T(128)S(1)} %get-tuple-element.154) | copy-start | bytes 772
  40.0 15.7 %copy-start.102 = (f32[64]{0:T(128)}, f32[64]{0:T(128)S(1)}, u32[]{:S(2)}) copy-start(f32[64]{0:T(128)S(1)} %get-tuple-element.225) | copy-start | bytes 772
  40.0 15.7 %copy-start.133 = (f32[64]{0:T(128)}, f32[64]{0:T(128)S(1)}, u32[]{:S(2)}) copy-start(f32[64]{0:T(128)S(1)} %get-tuple-element.155) | copy-start | bytes 772
  40.0 15.7 %copy-start.134 = (f32[64]{0:T(128)}, f32[64]{0:T(128)S(1)}, u32[]{:S(2)}) copy-start(f32[64]{0:T(128)S(1)} %get-tuple-element.158) | copy-start | bytes 772
  40.0 15.7 %copy-start.135 = (f32[64]{0:T(128)}, f32[64]{0:T(128)S(1)}, u32[]{:S(2)}) copy-start(f32[64]{0:T(128)S(1)} %get-tuple-element.160) | copy-start | bytes 772
  40.0 16.6 %copy-start.98 = (f32[64]{0:T(128)}, f32[64]{0:T(128)S(1)}, u32[]{:S(2)}) copy-start(f32[64]{0:T(128)S(1)} %get-tuple-element.220) | copy-start | bytes 772
  40.1 16.6 %copy-start.100 = (f32[64]{0:T(128)}, f32[64]{0:T(128)S(1)}, u32[]{:S(2)}) copy-start(f32[64]{0:T(128)S(1)} %get-tuple-element.224) | copy-start | bytes 772
  40.8 11.7 %copy-start.151 = (f32[64]{0:T(128)}, f32[64]{0:T(128)S(1)}, u32[]{:S(2)}) copy-start(f32[64]{0:T(128)S(1)} %get-tuple-element.53) | copy-start | bytes 772
  40.8 11.7 %copy-start.153 = (f32[64]{0:T(128)}, f32[64]{0:T(128)S(1)}, u32[]{:S(2)}) copy-start(f32[64]{0:T(128)S(1)} %get-tuple-element.54) | copy-start | bytes 772
  40.8 12.9 %copy-start.155 = (f32[64]{0:T(128)}, f32[64]{0:T(128)S(1)}, u32[]{:S(2)}) copy-start(f32[64]{0:T(128)S(1)} %get-tuple-element.58) | copy-start | bytes 772
  40.8 14.9 %copy-start.114 = (f32[64]{0:T(128)}, f32[64]{0:T(128)S(1)}, u32[]{:S(2)}) copy-start(f32[64]{0:T(128)S(1)} %get-tuple-element.213) | copy-start | bytes 772
  41.2 12.4 %copy-start.174 = (f32[64]{0:T(128)}, f32[64]{0:T(128)S(1)}, u32[]{:S(2)}) copy-start(f32[64]{0:T(128)S(1)} %get-tuple-element.20) | copy-start | bytes 772
  41.3 12.5 %copy-start.184 = (f32[64]{0:T(128)}, f32[64]{0:T(128)S(1)}, u32[]{:S(2)}) copy-start(f32[64]{0:T(128)S(1)} %get-tuple-element.19) | copy-start | bytes 772
  43.2 13.3 %collective-permute-start = (f32[11,768]{1,0:T(8,128)S(1)}, f32[11,768]{1,0:T(8,128)S(1)}, u32[]{:S(2)}, u32[]{:S(2)}) collective-permute-start(f32[11,768]{1,0:T(8,128)S(1)} %get-tuple-element.33), channel_id=1, source_target_pairs={{0,4},{4,8},{8,12},{12,16},{16,20},{20,24},{24,28},{28,32},{32,36}... | collective-permute-start | bytes 101384 | tf_op jit(solution)/shard_map/ppermute | solution.py:29
  45.2 11.4 %collective-permute-start.1 = (f32[11,768]{1,0:T(8,128)S(1)}, f32[11,768]{1,0:T(8,128)S(1)}, u32[]{:S(2)}, u32[]{:S(2)}) collective-permute-start(f32[11,768]{1,0:T(8,128)S(1)} %get-tuple-element.34), channel_id=1, source_target_pairs={{4,0},{8,4},{12,8},{16,12},{20,16},{24,20},{28,24},{32,28},{36,32}... | collective-permute-start | bytes 101384 | tf_op jit(solution)/shard_map/ppermute | solution.py:30
  138.3 13.2 %copy-start.166 = (pred[16]{0:T(512)(128)(4,1)S(1)}, pred[16]{0:T(512)(128)(4,1)}, u32[]{:S(2)}) copy-start(pred[16]{0:T(512)(128)(4,1)} %get-tuple-element.188) | copy-start | bytes 52
  140.1 13.4 %copy-start.47 = (f32[11,2,64]{2,0,1:T(8,128)}, f32[11,2,64]{2,0,1:T(8,128)S(1)}, u32[]{:S(2)}) copy-start(f32[11,2,64]{2,0,1:T(8,128)S(1)} %select_bitcast_fusion.13) | copy-start | bytes 16900
  180.4 13.2 %copy-start.67 = (f32[2,64]{1,0:T(2,128)S(1)}, f32[2,64]{1,0:T(2,128)}, u32[]{:S(2)}) copy-start(f32[2,64]{1,0:T(2,128)} %copy-done.65) | copy-start | bytes 1540
  180.4 13.2 %copy-start.70 = (f32[2,64]{1,0:T(2,128)S(1)}, f32[2,64]{1,0:T(2,128)}, u32[]{:S(2)}) copy-start(f32[2,64]{1,0:T(2,128)} %copy-done.68) | copy-start | bytes 1540
  180.4 13.2 %copy-start.73 = (f32[2,64]{1,0:T(2,128)S(1)}, f32[2,64]{1,0:T(2,128)}, u32[]{:S(2)}) copy-start(f32[2,64]{1,0:T(2,128)} %copy-done.71) | copy-start | bytes 1540
  180.4 13.2 %copy-start.146 = (f32[64]{0:T(128)S(1)}, f32[64]{0:T(128)}, u32[]{:S(2)}) copy-start(f32[64]{0:T(128)} %copy-done.145) | copy-start | bytes 772
  180.4 13.2 %copy-start.148 = (f32[64]{0:T(128)S(1)}, f32[64]{0:T(128)}, u32[]{:S(2)}) copy-start(f32[64]{0:T(128)} %copy-done.147) | copy-start | bytes 772
  180.4 13.2 %copy-start.150 = (f32[64]{0:T(128)S(1)}, f32[64]{0:T(128)}, u32[]{:S(2)}) copy-start(f32[64]{0:T(128)} %copy-done.149) | copy-start | bytes 772
  181.0 13.1 %copy-start.46 = (f32[11,2,64]{2,0,1:T(8,128)S(1)}, f32[11,2,64]{2,0,1:T(8,128)}, u32[]{:S(2)}) copy-start(f32[11,2,64]{2,0,1:T(8,128)} %copy-done.45) | copy-start | bytes 16900
  181.0 12.7 %copy-start.158 = (f32[2,64]{1,0:T(2,128)S(1)}, f32[2,64]{1,0:T(2,128)}, u32[]{:S(2)}) copy-start(f32[2,64]{1,0:T(2,128)} %copy-done.157) | copy-start | bytes 1540
  181.0 13.1 %copy-start.159 = (f32[1,2,64]{2,0,1:T(1,128)S(1)}, f32[1,2,64]{2,0,1:T(1,128)}, u32[]{:S(2)}) copy-start(f32[1,2,64]{2,0,1:T(1,128)} %get-tuple-element.134) | copy-start | bytes 1540
  182.8 11.6 %copy-start.53 = (f32[4,64]{1,0:T(4,128)S(1)}, f32[4,64]{1,0:T(4,128)}, u32[]{:S(2)}) copy-start(f32[4,64]{1,0:T(4,128)} %copy-done.51) | copy-start | bytes 3076
  (139 other events, 692.3 us)
Sparse Core Ops, SparseCore 0:
  43.2 82.0 all-gather.2

commit v5 on v4

--- a/solution.py
+++ b/solution.py
@@ -150,20 +150,13 @@
     )
     pyramid_nodes = pyramid.shape[1]
     spread = with_halo(pyramid, (("boxes", 1),), pyramid_nodes)
-    local_couplings = []
+    index_parts, target_parts, mask_parts = [], [], []
     for height in range(local_depth):
         count = BOXES_DEV >> height
         start = 0 if height == 0 else 2 * BOXES_DEV - (BOXES_DEV >> height - 1)
-        view = jnp.concatenate(
-            [
-                spread[:, block * pyramid_nodes + start : block * pyramid_nodes + start + count, :]
-                for block in range(3)
-            ],
-            axis=1,
-        )
         if height == 0:
             live_far = far_list >= 0
-            slot_ids = [
+            view_ids = [
                 jnp.where(
                     live_far[:, slot],
                     (far_list[:, slot] - device * BOXES_DEV + BOXES_DEV + boxes_all) % boxes_all,
@@ -171,23 +164,26 @@
                 )
                 for slot in range(3)
             ]
-            slot_masks = [live_far[:, slot].astype(jnp.float32)[None, :, None] for slot in range(3)]
+            mask_parts += [live_far[:, slot].astype(jnp.float32) for slot in range(3)]
         else:
             node = jnp.arange(count, dtype=jnp.int32)
             third = jnp.where(node % 2 == 0, node + 3, node - 3)
-            slot_ids = [node - 2 + count, node + 2 + count, third + count]
-            slot_masks = [None, None, None]
-        coupling = jnp.zeros((rows_here, count, R), jnp.float32)
-        for slot in range(3):
-            picked = jnp.take(view, slot_ids[slot], axis=1)
-            kernel_block = kernel_matrix(picked[rows_here:], proxies[height], kernel_scale)
-            source_moment = picked[:rows_here]
-            if slot_masks[slot] is not None:
-                source_moment = source_moment * slot_masks[slot]
-            coupling = coupling + jnp.einsum(
-                "qnr,nrs->qns", source_moment, kernel_block, precision=PRECISE
-            )
-        local_couplings.append(coupling)
+            view_ids = [node - 2 + count, node + 2 + count, third + count]
+            mask_parts += [jnp.ones((count,), jnp.float32)] * 3
+        for view_id in view_ids:
+            index_parts.append(view_id // count * pyramid_nodes + start + view_id % count)
+            target_parts.append(proxies[height])
+    picked = jnp.take(spread, jnp.concatenate(index_parts), axis=1)
+    kernel_block = kernel_matrix(picked[rows_here:], jnp.concatenate(target_parts, axis=1), kernel_scale)
+    source_moment = picked[:rows_here] * jnp.concatenate(mask_parts)[None, :, None]
+    contributions = jnp.einsum("qnr,nrs->qns", source_moment, kernel_block, precision=PRECISE)
+    local_couplings = []
+    first = 0
+    for height in range(local_depth):
+        count = BOXES_DEV >> height
+        part = contributions[:, first : first + 3 * count, :]
+        local_couplings.append(part.reshape(rows_here, 3, count, R).sum(axis=1))
+        first += 3 * count
 
     top_levels = tree_depth - 1
     level_points = []
@@ -209,7 +205,7 @@
             jnp.einsum("qnr,nrs->qns", path_moments[-1], own_edges[height], precision=PRECISE)
         )
     gathered = lax.all_gather(jnp.concatenate(path_moments, axis=1), "boxes", axis=0)
-    top_couplings = []
+    top_moments, top_sources, top_targets, top_slots = [], [], [], []
     for height in range(top_levels):
         number = groups >> height
         node = device // 2**height
@@ -219,17 +215,22 @@
             source_ids = [(node - 2) % number, (node + 2) % number, third]
         else:
             source_ids = [(node + 2) % number]
-        target_points = lax.dynamic_slice_in_dim(level_points[height], node, 1, 1)
-        coupling = jnp.zeros((rows_here, 1, R), jnp.float32)
+        top_slots.append(len(source_ids))
         for source in source_ids:
-            kernel_block = kernel_matrix(
-                lax.dynamic_slice_in_dim(level_points[height], source, 1, 1), target_points, kernel_scale
-            )
-            source_moment = lax.dynamic_index_in_dim(level_sums, source, 0, keepdims=False)
-            coupling = coupling + jnp.einsum(
-                "qnr,nrs->qns", source_moment[:, None, :], kernel_block, precision=PRECISE
-            )
-        top_couplings.append(coupling)
+            top_moments.append(lax.dynamic_index_in_dim(level_sums, source, 0, keepdims=True))
+            top_sources.append(lax.dynamic_slice_in_dim(level_points[height], source, 1, 1))
+            top_targets.append(lax.dynamic_slice_in_dim(level_points[height], node, 1, 1))
+    kernel_block = kernel_matrix(
+        jnp.concatenate(top_sources, axis=1), jnp.concatenate(top_targets, axis=1), kernel_scale
+    )
+    contributions = jnp.einsum(
+        "nqr,nrs->qns", jnp.concatenate(top_moments, axis=0), kernel_block, precision=PRECISE
+    )
+    top_couplings = []
+    first = 0
+    for slots in top_slots:
+        top_couplings.append(contributions[:, first : first + slots, :].sum(axis=1, keepdims=True))
+        first += slots
     descent = top_couplings[-1]
     for height in range(top_levels - 2, -1, -1):
         descent = (

time: 216 us -> 183 us (0.85)
  matrix products: 52.5 us -> 35.7 us
  local copies, waits for them, and re-layouts: 33.2 us -> 20.2 us
    dot_general x16 -> x1, matrix products: 11.2 us -> 1.73 us  [body(): jnp.einsum('nqr,nrs->qns', jnp.concatenate(top_moments, axis=0), kernel_b...]
    dot_general x15 -> x1, matrix products: 18.1 us -> 10.1 us  [body(): jnp.einsum('qnr,nrs->qns', source_moment, kernel_block, precision=PRECISE)]
    slice x16 -> x2, local copies, waits for them, and re-layouts: 9.45 us -> 1.52 us  [kernel_matrix(): left_points[0][..., :, None] - right_points[0][..., None, :]]
    gather x15 -> x1, local copies, waits for them, and re-layouts: 8.89 us -> 1.02 us  [body(): picked = jnp.take(spread, jnp.concatenate(index_parts), axis=1)]
  transfers between devices with their start and end apart: 5 -> 5, of which waited for: 0 -> 0; matrix products, arithmetic and copies ran while one was open for 23% -> 15% of each run, Pallas kernels for 36% -> 43%
where the time goes in v5:
time: 183 us; the launch traced here: 182 us
  Pallas kernels  78.3 us (43%)
  matrix products  35.7 us (20%)
  starting transfers between devices  20.2 us (11%)
  local copies, waits for them, and re-layouts  20.2 us (11%)
  between operations  16.6 us (9%)
  other arithmetic  11.1 us (6%)
    pallas_call x1, Pallas kernels, near_field_call(): pl.pallas_call(functools.partial(near_kernel, kernel_scale, slots), out_s...  78.3 us
    ppermute x2, starting transfers between devices, with_halo(): after = lax.ppermute(initial, axis, down)  16.2 us
    dot_general x1, matrix products, body(): jnp.einsum('qnr,nrs->qns', source_moment, kernel_block, precision=PRECISE)  10.1 us
    dot_general x5, matrix products, body(): jnp.einsum('qns,nrs->qnr', jnp.repeat(descent, 2, axis=1), transfer_maps[...  7.15 us
    dot_general x5, matrix products, body(): jnp.einsum('qnr,nrs->qns', level_moments[-1], interp_map, precision=PRECISE)  5.15 us
    reduce_sum x7, other arithmetic, interpolation(): return values / jnp.sum(values, axis=-1, keepdims=True)  4.31 us
    ppermute x2, starting transfers between devices, with_halo(): before = lax.ppermute(last, axis, up)  3.97 us
    dot_general x1, matrix products, body(): jnp.einsum('qbp,bpr->qbr', probe_tiles, leaf_basis, precision=PRECISE)  3.84 us
  transfers between devices with their start and end apart: 5, of which 0 were waited for; matrix products, arithmetic and copies ran while one was open for 15% of the time, Pallas kernels for 43%

profile of v5, /device:TPU:22, one launch (start us, length us, event | category | flops | bytes accessed | tf_op | source)
XLA Modules:
  0.0 182.1 jit_solution(7002506855509837745)
XLA Ops:
  6.5 0.8 reshape.3408
  7.6 0.9 slice_reduce_fusion.10
  8.5 0.9 reshape.3428
  9.6 1.3 slice_reduce_fusion.2
  11.0 1.1 divide_reduce_fusion
  12.1 3.8 %constant_dynamic-update-slice_fusion.27 = (f32[8,62,64]{2,0,1:T(8,128)S(1)}, f32[8,32,64]{2,0,1:T(8,128)S(1)}) fusion(f32[8,32,256]{2,0,1:T(8,128)} %bitcast.409, f32[32,256]{1,0:T(8,128)S(1)} %divide_reduce_fusion, f32[32,64]{1,0:T(8,128)S(1)} %sub.1273, f32[32,256]{1,0:T(8,128)S(1)} %sub.1271, f32[32,64]{1,0:T(8,128)S(1)} %sub.1268, ...), kind=kOutput, calls=%fused_computation.116 | convolution fusion | flops 56623104 | bytes 679936 | tf_op jit(solution)/shard_map/qbp,bpr->qbr/dot_general | solution.py:135
  16.0 1.4 divide_reduce_fusion.1
  17.4 2.6 %bitcast_reduce_fusion = f32[8,16,64]{2,0,1:T(8,128)S(1)} fusion(f32[8,32,64]{2,0,1:T(8,128)S(1)} %get-tuple-element.116, f32[32,64]{1,0:T(8,128)S(1)} %divide_reduce_fusion.1, f32[32,64]{1,0:T(8,128)S(1)} %bitcast.426, f32[32,64]{1,0:T(8,128)S(1)} %sub.1273, f32[32,64]{1,0:T(8,128)S(1)} %bitcast.423, f32[32,64]{1,0:T(8,128)S(1)} %sub.1268, ...), kind=kOutput, calls=%fused_computation.73 | convolution fusion | flops 14163968 | bytes 155648 | tf_op jit(solution)/shard_map/qnr,nrs->qns/dot_general | solution.py:142
  20.1 0.7 divide_reduce_fusion.2
  20.8 1.3 bitcast_reduce_fusion.1
  22.1 0.4 divide_reduce_fusion.3
  22.6 0.6 bitcast_reduce_fusion.2
  23.3 0.3 divide_reduce_fusion.4
  23.6 0.4 bitcast_reduce_fusion.3
  24.2 2.1 %collective-permute-start.2 = (f32[11,62,64]{2,0,1:T(8,128)S(1)}, f32[11,62,64]{2,0,1:T(8,128)}, u32[]{:S(2)}, u32[]{:S(2)}) collective-permute-start(f32[11,62,64]{2,0,1:T(8,128)S(1)} %maximum_maximum_fusion), channel_id=1, source_target_pairs={{0,4},{4,8},{8,12},{12,16},{16,20},{20,24},{24,28},{28,32},{32,36}... | collective-permute-start | bytes 523784 | tf_op jit(solution)/shard_map/ppermute | solution.py:29
  26.2 10.3 %collective-permute-start.3 = (f32[11,62,64]{2,0,1:T(8,128)S(1)}, f32[11,62,64]{2,0,1:T(8,128)}, u32[]{:S(2)}, u32[]{:S(2)}) collective-permute-start(f32[11,62,64]{2,0,1:T(8,128)S(1)} %maximum_maximum_fusion), channel_id=1, source_target_pairs={{4,0},{8,4},{12,8},{16,12},{20,16},{24,20},{28,24},{32,28},{36,32}... | collective-permute-start | bytes 523784 | tf_op jit(solution)/shard_map/ppermute | solution.py:30
  36.5 0.2 reshape.3409
  37.1 0.2 divide_reduce_fusion.5
  37.3 0.3 constant_dynamic-update-slice_fusion.6
  37.6 0.2 copy-done.109
  38.1 0.4 fusion.53
  38.5 0.2 constant_dynamic-update-slice_fusion.5
  38.7 0.2 constant_dynamic-update-slice_fusion.4
  39.0 0.2 constant_dynamic-update-slice_fusion.3
  39.2 0.2 constant_dynamic-update-slice_fusion.2
  39.5 0.2 fusion.25
  39.7 0.6 copy-done.34
  40.6 1.9 %collective-permute-start = (f32[11,768]{1,0:T(8,128)S(1)}, f32[11,768]{1,0:T(8,128)S(1)}, u32[]{:S(2)}, u32[]{:S(2)}) collective-permute-start(f32[11,768]{1,0:T(8,128)S(1)} %get-tuple-element.30), channel_id=1, source_target_pairs={{0,4},{4,8},{8,12},{12,16},{16,20},{20,24},{24,28},{28,32},{32,36}... | collective-permute-start | bytes 101384 | tf_op jit(solution)/shard_map/ppermute | solution.py:29
  42.5 5.9 %collective-permute-start.1 = (f32[11,768]{1,0:T(8,128)S(1)}, f32[11,768]{1,0:T(8,128)S(1)}, u32[]{:S(2)}, u32[]{:S(2)}) collective-permute-start(f32[11,768]{1,0:T(8,128)S(1)} %get-tuple-element.31), channel_id=1, source_target_pairs={{4,0},{8,4},{12,8},{16,12},{20,16},{24,20},{28,24},{32,28},{36,32}... | collective-permute-start | bytes 101384 | tf_op jit(solution)/shard_map/ppermute | solution.py:30
  49.7 0.6 slice_bitcast_fusion.8
  50.3 0.6 slice_bitcast_fusion.7
  51.2 0.6 compare_and_fusion
  51.8 0.7 slice_bitcast_fusion.2
  52.6 0.6 pad_clamp_fusion
  53.3 0.7 reshape.3407.source_ref
  54.0 0.6 concatenate.116
  54.7 3.0 %copy.81 = f32[3,9728]{0,1:T(8,128)} copy(f32[3,9728]{1,0:T(4,128)S(1)} %pad_maximum_fusion.2) | data formatting | bytes 233472 | tf_op jit(solution)/shard_map/slice | solution.py:115
  57.7 0.7 slice.555
  58.5 78.3 %shard_map.73 = f32[8,8192]{1,0:T(8,128)} custom-call(s32[192]{0:T(256)} %reshape.3407.source_ref, f32[38,8,256]{2,1,0:T(8,128)} %bitcast.408, f32[38,256,3]{2,1,0:T(8,128)} %bitcast.400, f32[3,8192]{1,0:T(4,128)} %target_ref.1), custom_call_target="tpu_custom_call" | custom-call | flops 352321536 | bytes 5855232 | tf_op jit(solution)/shard_map/pallas_call | solution.py:73
  136.8 1.3 pad_maximum_fusion
  138.1 1.0 gather_fusion
  139.2 1.0 select_bitcast_fusion
  140.2 0.2 fusion.217
  140.5 10.1 %fusion.9 = f32[8,186,64]{2,0,1:T(8,128)S(1)} fusion(f32[186,64]{1,0:T(8,128)S(1)} %copy-done.7, f32[186,64]{1,0:T(8,128)S(1)} %bitcast.415, f32[186,64]{1,0:T(8,128)S(1)} %copy-done.8, f32[186,64]{1,0:T(8,128)S(1)} %bitcast.416, f32[186,64]{1,0:T(8,128)S(1)} %copy-done.6, f32[186,64]{1,0:T(8,128)S(1)} %bitcast.417, ...), kind=kOutput, calls=%fused_computation.16 | convolution fusion | flops 81613824 | bytes 1733632 | tf_op jit(solution)/shard_map/qnr,nrs->qns/dot_general | solution.py:179
  150.6 0.6 reduce_sum.310
  151.2 0.6 reduce_sum.311
  151.9 0.6 reduce_sum.313
  152.6 2.8 %fusion.216 = (f32[128,8,1,64]{3,1,0,2:T(8,128)S(1)}, f32[128,8,1,64]{3,1,0,2:T(8,128)S(1)}, f32[128,8,1,64]{3,1,0,2:T(8,128)S(1)}, f32[128,8,1,64]{3,1,0,2:T(8,...) fusion(f32[128,8,6,64]{3,1,0,2:T(8,128)} %bitcast.401), kind=kLoop, calls=%fused_computation.537 | loop fusion | bytes 3145728 | tf_op jit(solution)/shard_map/slice | solution.py:212
  155.5 0.7 constant_dynamic-update-slice_fusion.22
  156.1 0.7 constant_dynamic-update-slice_fusion.21
  156.8 0.7 constant_dynamic-update-slice_fusion.20
  158.2 1.7 convolution_bitcast_fusion.3
  160.1 0.2 fusion.24
  160.4 1.0 fusion.22
  161.5 0.8 fusion.20
  162.3 0.8 fusion.18
  163.2 0.9 fusion.16
  164.2 1.0 fusion.14
  165.3 0.5 fusion.13
  165.8 0.8 fusion.12
  166.8 1.6 fusion.11
  168.5 3.2 %fusion.10 = f32[8,32,64]{2,0,1:T(8,128)S(1)} fusion(f32[8,32,64]{2,0,1:T(8,128)S(1)} %reduce_sum.314, f32[8,32,64]{2,0,1:T(8,128)S(1)} %bitcast.414, f32[32,64]{1,0:T(8,128)S(1)} %copy-done.42, f32[32,64]{1,0:T(8,128)S(1)} %bitcast.427, f32[32,64]{1,0:T(8,128)S(1)} %sub.1273, f32[32,64]{1,0:T(8,128)S(1)} %bitcast.424, f32[32,64]{1,0:T(8,128)S(1)} %sub.1268, ...), kind=kOutput, calls=%fused_computation.19 | convolution fusion | flops 14172160 | bytes 253952 | tf_op jit(solution)/shard_map/qns,nrs->qnr/dot_general | solution.py:241
  171.7 2.7 %fusion.26 = f32[32,256,8]{1,2,0:T(8,128)S(1)} fusion(f32[8,32,64]{2,0,1:T(8,128)S(1)} %fusion.10, f32[32,256]{1,0:T(8,128)S(1)} %copy-done.33, f32[32,64]{1,0:T(8,128)S(1)} %sub.1273, f32[32,256]{1,0:T(8,128)S(1)} %copy-done.5, f32[32,64]{1,0:T(8,128)S(1)} %sub.1268, f32[32,256]{1,0:T(8,128)S(1)} %sub.1266, f32[32,64]{1,0:T(8,128)S(1)} %sub.1263, ...), kind=kOutput, calls=%fused_computation.48 | convolution fusion | flops 56623104 | bytes 483328 | tf_op jit(solution)/shard_map/qbr,bpr->qbp/dot_general | solution.py:245
  174.5 0.8 add_add_fusion
  (358 shorter events, 2.7 us)
Async XLA Ops:
  6.5 146.0 %all-gather.3.cloned.1.call-start = ((), (), s32[]{:S(2)}) async-start(), calls=%async_computation | async-start | bytes 3170304 | tf_op jit(solution)/shard_map/all_gather | solution.py:207
  7.4 13.3 %copy-start.9 = (f32[16,64]{1,0:T(8,128)}, f32[16,64]{1,0:T(8,128)S(1)}, u32[]{:S(2)}) copy-start(f32[16,64]{1,0:T(8,128)S(1)} %get-tuple-element.68) | copy-start | bytes 12292
  7.4 13.3 %copy-start.11 = (f32[16,64]{1,0:T(8,128)}, f32[16,64]{1,0:T(8,128)S(1)}, u32[]{:S(2)}) copy-start(f32[16,64]{1,0:T(8,128)S(1)} %get-tuple-element.69) | copy-start | bytes 12292
  7.4 13.3 %copy-start.13 = (f32[16,64]{1,0:T(8,128)}, f32[16,64]{1,0:T(8,128)S(1)}, u32[]{:S(2)}) copy-start(f32[16,64]{1,0:T(8,128)S(1)} %get-tuple-element.70) | copy-start | bytes 12292
  7.4 15.1 %copy-start.22 = (f32[8,64]{1,0:T(8,128)}, f32[8,64]{1,0:T(8,128)S(1)}, u32[]{:S(2)}) copy-start(f32[8,64]{1,0:T(8,128)S(1)} %get-tuple-element.66) | copy-start | bytes 6148
  7.4 15.1 %copy-start.24 = (f32[8,64]{1,0:T(8,128)}, f32[8,64]{1,0:T(8,128)S(1)}, u32[]{:S(2)}) copy-start(f32[8,64]{1,0:T(8,128)S(1)} %get-tuple-element.67) | copy-start | bytes 6148
  7.5 16.1 %copy-start.35 = (f32[4,64]{1,0:T(4,128)}, f32[4,64]{1,0:T(4,128)S(1)}, u32[]{:S(2)}) copy-start(f32[4,64]{1,0:T(4,128)S(1)} %get-tuple-element.62) | copy-start | bytes 3076
  7.5 16.1 %copy-start.37 = (f32[4,64]{1,0:T(4,128)}, f32[4,64]{1,0:T(4,128)S(1)}, u32[]{:S(2)}) copy-start(f32[4,64]{1,0:T(4,128)S(1)} %get-tuple-element.63) | copy-start | bytes 3076
  7.5 16.1 %copy-start.39 = (f32[4,64]{1,0:T(4,128)}, f32[4,64]{1,0:T(4,128)S(1)}, u32[]{:S(2)}) copy-start(f32[4,64]{1,0:T(4,128)S(1)} %get-tuple-element.64) | copy-start | bytes 3076
  7.5 29.8 %copy-start.51 = (f32[2,64]{1,0:T(2,128)}, f32[2,64]{1,0:T(2,128)S(1)}, u32[]{:S(2)}) copy-start(f32[2,64]{1,0:T(2,128)S(1)} %get-tuple-element.59) | copy-start | bytes 1540
  7.5 29.8 %copy-start.53 = (f32[2,64]{1,0:T(2,128)}, f32[2,64]{1,0:T(2,128)S(1)}, u32[]{:S(2)}) copy-start(f32[2,64]{1,0:T(2,128)S(1)} %get-tuple-element.60) | copy-start | bytes 1540
  7.5 29.8 %copy-start.55 = (f32[2,64]{1,0:T(2,128)}, f32[2,64]{1,0:T(2,128)S(1)}, u32[]{:S(2)}) copy-start(f32[2,64]{1,0:T(2,128)S(1)} %get-tuple-element.61) | copy-start | bytes 1540
  22.0 14.5 %copy-start.3 = (f32[3,16128]{1,0:T(4,128)S(1)}, f32[3,16128]{1,0:T(4,128)}, u32[]{:S(2)}) copy-start(f32[3,16128]{1,0:T(4,128)} %param.12) | copy-start | bytes 580612
  22.1 14.7 %copy-start.43 = (f32[4,2,64]{2,1,0:T(2,128)}, f32[4,2,64]{2,1,0:T(2,128)S(1)}, u32[]{:S(2)}) copy-start(f32[4,2,64]{2,1,0:T(2,128)S(1)} %broadcast_in_dim.126) | copy-start | bytes 6148
  22.1 14.7 %copy-start.45 = (f32[4,2,64]{2,1,0:T(2,128)}, f32[4,2,64]{2,1,0:T(2,128)S(1)}, u32[]{:S(2)}) copy-start(f32[4,2,64]{2,1,0:T(2,128)S(1)} %broadcast_in_dim.128) | copy-start | bytes 6148
  22.1 14.7 %copy-start.47 = (f32[4,2,64]{2,1,0:T(2,128)}, f32[4,2,64]{2,1,0:T(2,128)S(1)}, u32[]{:S(2)}) copy-start(f32[4,2,64]{2,1,0:T(2,128)S(1)} %broadcast_in_dim.130) | copy-start | bytes 6148
  22.6 14.2 %copy-start.91 = (f32[8,64]{1,0:T(8,128)}, f32[8,64]{1,0:T(8,128)S(1)}, u32[]{:S(2)}) copy-start(f32[8,64]{1,0:T(8,128)S(1)} %divide_reduce_fusion.3) | copy-start | bytes 6148
  23.3 13.5 %copy-start.59 = (f32[2,2,64]{2,1,0:T(2,128)}, f32[2,2,64]{2,1,0:T(2,128)S(1)}, u32[]{:S(2)}) copy-start(f32[2,2,64]{2,1,0:T(2,128)S(1)} %broadcast_in_dim.132) | copy-start | bytes 3076
  23.3 13.5 %copy-start.61 = (f32[2,2,64]{2,1,0:T(2,128)}, f32[2,2,64]{2,1,0:T(2,128)S(1)}, u32[]{:S(2)}) copy-start(f32[2,2,64]{2,1,0:T(2,128)S(1)} %broadcast_in_dim.134) | copy-start | bytes 3076
  23.3 13.5 %copy-start.63 = (f32[2,2,64]{2,1,0:T(2,128)}, f32[2,2,64]{2,1,0:T(2,128)S(1)}, u32[]{:S(2)}) copy-start(f32[2,2,64]{2,1,0:T(2,128)S(1)} %broadcast_in_dim.136) | copy-start | bytes 3076
  23.6 14.2 %copy-start.94 = (f32[4,64]{1,0:T(4,128)}, f32[4,64]{1,0:T(4,128)S(1)}, u32[]{:S(2)}) copy-start(f32[4,64]{1,0:T(4,128)S(1)} %divide_reduce_fusion.4) | copy-start | bytes 3076
  24.1 16.2 %copy-start.1 = (f32[8,8192]{1,0:T(8,128)S(1)}, f32[8,8192]{1,0:T(8,128)}, u32[]{:S(2)}) copy-start(f32[8,8192]{1,0:T(8,128)} %param.7) | copy-start | bytes 786436
  24.2 16.3 %copy-start.2 = (f32[3,8192]{1,0:T(4,128)S(1)}, f32[3,8192]{1,0:T(4,128)}, u32[]{:S(2)}) copy-start(f32[3,8192]{1,0:T(4,128)} %target_ref.1) | copy-start | bytes 294916
  24.2 112.6 %collective-permute-start.2 = (f32[11,62,64]{2,0,1:T(8,128)S(1)}, f32[11,62,64]{2,0,1:T(8,128)}, u32[]{:S(2)}, u32[]{:S(2)}) collective-permute-start(f32[11,62,64]{2,0,1:T(8,128)S(1)} %maximum_maximum_fusion), channel_id=1, source_target_pairs={{0,4},{4,8},{8,12},{12,16},{16,20},{20,24},{24,28},{28,32},{32,36}... | collective-permute-start | bytes 523784 | tf_op jit(solution)/shard_map/ppermute | solution.py:29
  26.2 110.6 %collective-permute-start.3 = (f32[11,62,64]{2,0,1:T(8,128)S(1)}, f32[11,62,64]{2,0,1:T(8,128)}, u32[]{:S(2)}, u32[]{:S(2)}) collective-permute-start(f32[11,62,64]{2,0,1:T(8,128)S(1)} %maximum_maximum_fusion), channel_id=1, source_target_pairs={{4,0},{8,4},{12,8},{16,12},{20,16},{24,20},{28,24},{32,28},{36,32}... | collective-permute-start | bytes 523784 | tf_op jit(solution)/shard_map/ppermute | solution.py:30
  36.9 12.1 %copy-start.50 = (s32[32,3]{0,1:T(4,128)S(1)}, s32[32,3]{0,1:T(4,128)}, u32[]{:S(2)}) copy-start(s32[32,3]{0,1:T(4,128)} %param.13) | copy-start | bytes 1156
  37.0 12.2 %copy-start.98 = (f32[64]{0:T(128)}, f32[64]{0:T(128)S(1)}, u32[]{:S(2)}) copy-start(f32[64]{0:T(128)S(1)} %get-tuple-element.134) | copy-start | bytes 772
  37.1 12.2 %copy-start.99 = (f32[64]{0:T(128)}, f32[64]{0:T(128)S(1)}, u32[]{:S(2)}) copy-start(f32[64]{0:T(128)S(1)} %get-tuple-element.135) | copy-start | bytes 772
  38.0 11.3 %copy-start.67 = (f32[64]{0:T(128)}, f32[64]{0:T(128)S(1)}, u32[]{:S(2)}) copy-start(f32[64]{0:T(128)S(1)} %get-tuple-element.49) | copy-start | bytes 772
  38.0 11.2 %copy-start.100 = (f32[64]{0:T(128)}, f32[64]{0:T(128)S(1)}, u32[]{:S(2)}) copy-start(f32[64]{0:T(128)S(1)} %get-tuple-element.93) | copy-start | bytes 772
  38.0 11.4 %copy-start.102 = (f32[64]{0:T(128)}, f32[64]{0:T(128)S(1)}, u32[]{:S(2)}) copy-start(f32[64]{0:T(128)S(1)} %get-tuple-element.94) | copy-start | bytes 772
  38.0 11.4 %copy-start.104 = (f32[64]{0:T(128)}, f32[64]{0:T(128)S(1)}, u32[]{:S(2)}) copy-start(f32[64]{0:T(128)S(1)} %get-tuple-element.95) | copy-start | bytes 772
  38.4 10.6 %copy-start.114 = (f32[64]{0:T(128)}, f32[64]{0:T(128)S(1)}, u32[]{:S(2)}) copy-start(f32[64]{0:T(128)S(1)} %get-tuple-element.16) | copy-start | bytes 772
  38.4 10.6 %copy-start.115 = (f32[64]{0:T(128)}, f32[64]{0:T(128)S(1)}, u32[]{:S(2)}) copy-start(f32[64]{0:T(128)S(1)} %get-tuple-element.20) | copy-start | bytes 772
  38.4 11.0 %copy-start.111 = (f32[64]{0:T(128)}, f32[64]{0:T(128)S(1)}, u32[]{:S(2)}) copy-start(f32[64]{0:T(128)S(1)} %get-tuple-element.19) | copy-start | bytes 772
  38.5 11.0 %copy-start.112 = (f32[64]{0:T(128)}, f32[64]{0:T(128)S(1)}, u32[]{:S(2)}) copy-start(f32[64]{0:T(128)S(1)} %get-tuple-element.18) | copy-start | bytes 772
  38.5 11.0 %copy-start.113 = (f32[64]{0:T(128)}, f32[64]{0:T(128)S(1)}, u32[]{:S(2)}) copy-start(f32[64]{0:T(128)S(1)} %get-tuple-element.17) | copy-start | bytes 772
  39.0 13.6 %copy-start.93 = (s32[32,6]{0,1:T(8,128)S(1)}, s32[32,6]{0,1:T(8,128)}, u32[]{:S(2)}) copy-start(s32[32,6]{0,1:T(8,128)} %param.9) | copy-start | bytes 2308
  40.6 14.0 %collective-permute-start = (f32[11,768]{1,0:T(8,128)S(1)}, f32[11,768]{1,0:T(8,128)S(1)}, u32[]{:S(2)}, u32[]{:S(2)}) collective-permute-start(f32[11,768]{1,0:T(8,128)S(1)} %get-tuple-element.30), channel_id=1, source_target_pairs={{0,4},{4,8},{8,12},{12,16},{16,20},{20,24},{24,28},{28,32},{32,36}... | collective-permute-start | bytes 101384 | tf_op jit(solution)/shard_map/ppermute | solution.py:29
  42.5 12.1 %collective-permute-start.1 = (f32[11,768]{1,0:T(8,128)S(1)}, f32[11,768]{1,0:T(8,128)S(1)}, u32[]{:S(2)}, u32[]{:S(2)}) collective-permute-start(f32[11,768]{1,0:T(8,128)S(1)} %get-tuple-element.31), channel_id=1, source_target_pairs={{4,0},{8,4},{12,8},{16,12},{20,16},{24,20},{28,24},{32,28},{36,32}... | collective-permute-start | bytes 101384 | tf_op jit(solution)/shard_map/ppermute | solution.py:30
  158.1 6.0 %copy-start.52 = (f32[2,64]{1,0:T(2,128)S(1)}, f32[2,64]{1,0:T(2,128)}, u32[]{:S(2)}) copy-start(f32[2,64]{1,0:T(2,128)} %copy-done.51) | copy-start | bytes 1540
  158.1 6.0 %copy-start.54 = (f32[2,64]{1,0:T(2,128)S(1)}, f32[2,64]{1,0:T(2,128)}, u32[]{:S(2)}) copy-start(f32[2,64]{1,0:T(2,128)} %copy-done.53) | copy-start | bytes 1540
  158.1 6.0 %copy-start.56 = (f32[2,64]{1,0:T(2,128)S(1)}, f32[2,64]{1,0:T(2,128)}, u32[]{:S(2)}) copy-start(f32[2,64]{1,0:T(2,128)} %copy-done.55) | copy-start | bytes 1540
  158.1 6.0 %copy-start.66 = (f32[8,2,64]{2,0,1:T(8,128)S(1)}, f32[8,2,64]{2,0,1:T(8,128)}, u32[]{:S(2)}) copy-start(f32[8,2,64]{2,0,1:T(8,128)} %reduce_sum.310) | copy-start | bytes 12292
  158.1 7.1 %copy-start.36 = (f32[4,64]{1,0:T(4,128)S(1)}, f32[4,64]{1,0:T(4,128)}, u32[]{:S(2)}) copy-start(f32[4,64]{1,0:T(4,128)} %copy-done.35) | copy-start | bytes 3076
  158.1 7.1 %copy-start.38 = (f32[4,64]{1,0:T(4,128)S(1)}, f32[4,64]{1,0:T(4,128)}, u32[]{:S(2)}) copy-start(f32[4,64]{1,0:T(4,128)} %copy-done.37) | copy-start | bytes 3076
  158.1 7.1 %copy-start.40 = (f32[4,64]{1,0:T(4,128)S(1)}, f32[4,64]{1,0:T(4,128)}, u32[]{:S(2)}) copy-start(f32[4,64]{1,0:T(4,128)} %copy-done.39) | copy-start | bytes 3076
  158.1 7.1 %copy-start.49 = (f32[8,4,64]{2,0,1:T(8,128)S(1)}, f32[8,4,64]{2,0,1:T(8,128)}, u32[]{:S(2)}) copy-start(f32[8,4,64]{2,0,1:T(8,128)} %reduce_sum.311) | copy-start | bytes 24580
  158.1 7.1 %copy-start.60 = (f32[2,2,64]{2,1,0:T(2,128)S(1)}, f32[2,2,64]{2,1,0:T(2,128)}, u32[]{:S(2)}) copy-start(f32[2,2,64]{2,1,0:T(2,128)} %copy-done.59) | copy-start | bytes 3076
  158.2 7.1 %copy-start.62 = (f32[2,2,64]{2,1,0:T(2,128)S(1)}, f32[2,2,64]{2,1,0:T(2,128)}, u32[]{:S(2)}) copy-start(f32[2,2,64]{2,1,0:T(2,128)} %copy-done.61) | copy-start | bytes 3076
  158.2 7.1 %copy-start.64 = (f32[2,2,64]{2,1,0:T(2,128)S(1)}, f32[2,2,64]{2,1,0:T(2,128)}, u32[]{:S(2)}) copy-start(f32[2,2,64]{2,1,0:T(2,128)} %copy-done.63) | copy-start | bytes 3076
  158.2 7.1 %copy-start.95 = (f32[4,64]{1,0:T(4,128)S(1)}, f32[4,64]{1,0:T(4,128)}, u32[]{:S(2)}) copy-start(f32[4,64]{1,0:T(4,128)} %copy-done.94) | copy-start | bytes 3076
  159.9 5.9 %copy-start.23 = (f32[8,64]{1,0:T(8,128)S(1)}, f32[8,64]{1,0:T(8,128)}, u32[]{:S(2)}) copy-start(f32[8,64]{1,0:T(8,128)} %copy-done.22) | copy-start | bytes 6148
  159.9 5.9 %copy-start.25 = (f32[8,64]{1,0:T(8,128)S(1)}, f32[8,64]{1,0:T(8,128)}, u32[]{:S(2)}) copy-start(f32[8,64]{1,0:T(8,128)} %copy-done.24) | copy-start | bytes 6148
  159.9 5.9 %copy-start.44 = (f32[4,2,64]{2,1,0:T(2,128)S(1)}, f32[4,2,64]{2,1,0:T(2,128)}, u32[]{:S(2)}) copy-start(f32[4,2,64]{2,1,0:T(2,128)} %copy-done.43) | copy-start | bytes 6148
  159.9 5.9 %copy-start.46 = (f32[4,2,64]{2,1,0:T(2,128)S(1)}, f32[4,2,64]{2,1,0:T(2,128)}, u32[]{:S(2)}) copy-start(f32[4,2,64]{2,1,0:T(2,128)} %copy-done.45) | copy-start | bytes 6148
  160.3 6.3 %copy-start.10 = (f32[16,64]{1,0:T(8,128)S(1)}, f32[16,64]{1,0:T(8,128)}, u32[]{:S(2)}) copy-start(f32[16,64]{1,0:T(8,128)} %copy-done.9) | copy-start | bytes 12292
  160.4 6.3 %copy-start.12 = (f32[16,64]{1,0:T(8,128)S(1)}, f32[16,64]{1,0:T(8,128)}, u32[]{:S(2)}) copy-start(f32[16,64]{1,0:T(8,128)} %copy-done.11) | copy-start | bytes 12292
  160.4 6.3 %copy-start.14 = (f32[16,64]{1,0:T(8,128)S(1)}, f32[16,64]{1,0:T(8,128)}, u32[]{:S(2)}) copy-start(f32[16,64]{1,0:T(8,128)} %copy-done.13) | copy-start | bytes 12292
  160.4 6.3 %copy-start.21 = (f32[8,16,64]{2,0,1:T(8,128)S(1)}, f32[8,16,64]{2,0,1:T(8,128)}, u32[]{:S(2)}) copy-start(f32[8,16,64]{2,0,1:T(8,128)} %reduce_sum.313) | copy-start | bytes 98308
  160.4 6.3 %copy-start.27 = (f32[8,2,64]{2,1,0:T(2,128)S(1)}, f32[8,2,64]{2,1,0:T(2,128)}, u32[]{:S(2)}) copy-start(f32[8,2,64]{2,1,0:T(2,128)} %copy-done.26) | copy-start | bytes 12292
  160.4 6.3 %copy-start.29 = (f32[8,2,64]{2,1,0:T(2,128)S(1)}, f32[8,2,64]{2,1,0:T(2,128)}, u32[]{:S(2)}) copy-start(f32[8,2,64]{2,1,0:T(2,128)} %copy-done.28) | copy-start | bytes 12292
  160.4 6.3 %copy-start.31 = (f32[8,2,64]{2,1,0:T(2,128)S(1)}, f32[8,2,64]{2,1,0:T(2,128)}, u32[]{:S(2)}) copy-start(f32[8,2,64]{2,1,0:T(2,128)} %copy-done.30) | copy-start | bytes 12292
  160.4 6.3 %copy-start.58 = (f32[16,64]{1,0:T(8,128)S(1)}, f32[16,64]{1,0:T(8,128)}, u32[]{:S(2)}) copy-start(f32[16,64]{1,0:T(8,128)} %copy-done.57) | copy-start | bytes 12292
  (58 other events, 157.5 us)
Sparse Core Ops, SparseCore 0:
  40.5 81.4 all-gather.2

commit v6 on v5

--- a/solution.py
+++ b/solution.py
@@ -17,20 +17,59 @@
 SHARPNESS = 0.05
 NUGGET = 1.0
 PRECISE = lax.Precision.HIGHEST
-
-
-def with_halo(array, sides, width):
-    for axis, dim in sides:
-        size, length = (lax.axis_size(axis), array.shape[dim])
-        up = [(i, (i + 1) % size) for i in range(size)]
-        down = [(j, i) for i, j in up]
-        last = lax.slice_in_dim(array, length - width, length, axis=dim)
-        initial = lax.slice_in_dim(array, 0, width, axis=dim)
-        before = lax.ppermute(last, axis, up)
-        after = lax.ppermute(initial, axis, down)
-        array = jnp.concatenate([before, array, after], axis=dim)
-    return array
-
+MESH = pl.DeviceIdType.MESH
+
+
+def halo_kernel(to_right, to_left, from_left, from_right, left_slot, right_slot, send_sems, recv_sems):
+    me = lax.axis_index("boxes")
+    size = lax.axis_size("boxes")
+    probe = lax.axis_index("probe")
+    right = lax.rem(me + 1, size)
+    left = lax.rem(me + size - 1, size)
+    barrier = pltpu.get_barrier_semaphore()
+    for neighbour in (left, right):
+        pl.semaphore_signal(barrier, inc=1, device_id=(neighbour, probe), device_id_type=MESH)
+    pl.semaphore_wait(barrier, 2)
+    rightward = pltpu.make_async_remote_copy(
+        src_ref=to_right,
+        dst_ref=left_slot,
+        send_sem=send_sems.at[0],
+        recv_sem=recv_sems.at[0],
+        device_id=(right, probe),
+        device_id_type=MESH,
+    )
+    leftward = pltpu.make_async_remote_copy(
+        src_ref=to_left,
+        dst_ref=right_slot,
+        send_sem=send_sems.at[1],
+        recv_sem=recv_sems.at[1],
+        device_id=(left, probe),
+        device_id_type=MESH,
+    )
+    rightward.start()
+    leftward.start()
+    rightward.wait()
+    leftward.wait()
+    from_left[...] = left_slot[...]
+    from_right[...] = right_slot[...]
+
+
+def exchange_halo(to_right, to_left):
+    shape = jax.ShapeDtypeStruct(to_right.shape, to_right.dtype)
+    vmem = pl.BlockSpec(memory_space=pltpu.VMEM)
+    return pl.pallas_call(
+        halo_kernel,
+        out_shape=(shape, shape),
+        in_specs=[vmem, vmem],
+        out_specs=(vmem, vmem),
+        scratch_shapes=[
+            pltpu.VMEM(to_right.shape, to_right.dtype),
+            pltpu.VMEM(to_right.shape, to_right.dtype),
+            pltpu.SemaphoreType.DMA((2,)),
+            pltpu.SemaphoreType.DMA((2,)),
+        ],
+        compiler_params=pltpu.CompilerParams(collective_id=0, has_side_effects=True),
+    )(to_right, to_left)
 
 def kernel_matrix(left_points, right_points, kernel_scale):
     distance_sq = (left_points[0][..., :, None] - right_points[0][..., None, :]) ** 2
@@ -104,18 +143,6 @@
     slot_weight = live_slot.astype(jnp.float32)
     where_in = jnp.where(live_slot, (near_list - device * BOXES_DEV + W + boxes_all) % boxes_all, 0)
     box_points = points.reshape(3, BOXES_DEV, P_SIZE)
-    stacked = jnp.concatenate([probes, points], axis=0)
-    extended = with_halo(stacked, (("boxes", 1),), W * P_SIZE)
-    extended = extended.reshape(rows_here + 3, BOXES_DEV + 2 * W, P_SIZE)
-
-    slot_source = jnp.where(live_slot, jnp.clip(where_in, 0, BOXES_DEV + 2 * W - 1), -1)
-    near_field = near_field_call(
-        slot_source.reshape(-1).astype(jnp.int32),
-        jnp.moveaxis(extended[:rows_here], 1, 0),
-        jnp.moveaxis(extended[rows_here:], 0, 2),
-        points,
-        kernel_scale,
-    )
     probe_tiles = probes.reshape(rows_here, BOXES_DEV, P_SIZE)
     leaf_points = leaf_proxy.reshape(3, BOXES_DEV, R)
     leaf_basis = interpolation(box_points, leaf_points, kernel_scale)
@@ -149,7 +176,31 @@
         axis=0,
     )
     pyramid_nodes = pyramid.shape[1]
-    spread = with_halo(pyramid, (("boxes", 1),), pyramid_nodes)
+    stacked = jnp.concatenate([probes, points], axis=0)
+    width = W * P_SIZE
+    flat_pyramid = pyramid.reshape(rows_here + 3, -1)
+    from_left, from_right = exchange_halo(
+        jnp.concatenate([stacked[:, -width:], flat_pyramid], axis=1),
+        jnp.concatenate([stacked[:, :width], flat_pyramid], axis=1),
+    )
+    extended = jnp.concatenate([from_left[:, :width], stacked, from_right[:, :width]], axis=1)
+    extended = extended.reshape(rows_here + 3, BOXES_DEV + 2 * W, P_SIZE)
+    spread = jnp.concatenate(
+        [
+            from_left[:, width:].reshape(pyramid.shape),
+            pyramid,
+            from_right[:, width:].reshape(pyramid.shape),
+        ],
+        axis=1,
+    )
+    slot_source = jnp.where(live_slot, jnp.clip(where_in, 0, BOXES_DEV + 2 * W - 1), -1)
+    near_field = near_field_call(
+        slot_source.reshape(-1).astype(jnp.int32),
+        jnp.moveaxis(extended[:rows_here], 1, 0),
+        jnp.moveaxis(extended[rows_here:], 0, 2),
+        points,
+        kernel_scale,
+    )
     index_parts, target_parts, mask_parts = [], [], []
     for height in range(local_depth):
         count = BOXES_DEV >> height

time: 183 us -> 185 us (1.011)
  the two profiles are of different devices: /device:TPU:22 before, /device:TPU:28 now
where the time goes in v6:
time: 185 us; the launch traced here: 184 us
  Pallas kernels  92.3 us (50%)
  matrix products  35.1 us (19%)
  local copies, waits for them, and re-layouts  27.1 us (15%)
  between operations  16.8 us (9%)
  other arithmetic  12.3 us (7%)
    pallas_call x1, Pallas kernels, near_field_call(): pl.pallas_call(functools.partial(near_kernel, kernel_scale, slots), out_s...  76.2 us
    pallas_call x1, Pallas kernels, exchange_halo(): pl.pallas_call(halo_kernel, out_shape=(shape, shape), in_specs=[vmem, vme...  16.1 us
    dot_general x1, matrix products, body(): jnp.einsum('qnr,nrs->qns', source_moment, kernel_block, precision=PRECISE)  10 us
    dot_general x5, matrix products, body(): jnp.einsum('qns,nrs->qnr', jnp.repeat(descent, 2, axis=1), transfer_maps[...  7.14 us
    unnamed x301, local copies, waits for them, and re-layouts  5.64 us
    dot_general x5, matrix products, body(): jnp.einsum('qnr,nrs->qns', level_moments[-1], interp_map, precision=PRECISE)  5.15 us
    reduce_sum x7, other arithmetic, interpolation(): return values / jnp.sum(values, axis=-1, keepdims=True)  4.31 us
    dot_general x5, matrix products, body(): jnp.einsum('qns,nrs->qnr', descent, own_edges[height], precision=PRECISE)  3.86 us
  transfers between devices with their start and end apart: 1, of which 0 were waited for; matrix products, arithmetic and copies ran while one was open for 17% of the time, Pallas kernels for 50%

profile of v6, /device:TPU:28, one launch (start us, length us, event | category | flops | bytes accessed | tf_op | source)
XLA Modules:
  0.0 183.6 jit_solution(9378460202459409998)
XLA Ops:
  6.5 1.2 reshape.3425
  7.9 0.9 reshape.3418
  9.0 0.9 slice_reduce_fusion.10
  10.1 1.3 slice_reduce_fusion.2
  11.6 1.1 divide_reduce_fusion
  12.7 3.3 %constant_dynamic-update-slice_fusion.6 = (f32[8,62,64]{2,0,1:T(8,128)S(1)}, f32[8,32,64]{2,0,1:T(8,128)S(1)}) fusion(f32[8,32,256]{2,0,1:T(8,128)S(1)} %bitcast.409, f32[32,256]{1,0:T(8,128)S(1)} %divide_reduce_fusion, f32[32,64]{1,0:T(8,128)S(1)} %sub.1273, f32[32,256]{1,0:T(8,128)S(1)} %sub.1271, f32[32,64]{1,0:T(8,128)S(1)} %sub.1268, ...), kind=kOutput, calls=%fused_computation.97 | convolution fusion | flops 56623104 | bytes 679936 | tf_op jit(solution)/shard_map/qbp,bpr->qbr/dot_general | solution.py:162
  16.1 1.4 divide_reduce_fusion.1
  17.5 2.6 %bitcast_reduce_fusion = f32[8,16,64]{2,0,1:T(8,128)S(1)} fusion(f32[8,32,64]{2,0,1:T(8,128)S(1)} %get-tuple-element.122, f32[32,64]{1,0:T(8,128)S(1)} %divide_reduce_fusion.1, f32[32,64]{1,0:T(8,128)S(1)} %bitcast.426, f32[32,64]{1,0:T(8,128)S(1)} %sub.1273, f32[32,64]{1,0:T(8,128)S(1)} %bitcast.423, f32[32,64]{1,0:T(8,128)S(1)} %sub.1268, ...), kind=kOutput, calls=%fused_computation.75 | convolution fusion | flops 14163968 | bytes 155648 | tf_op jit(solution)/shard_map/qnr,nrs->qns/dot_general | solution.py:169
  20.2 0.7 divide_reduce_fusion.2
  20.9 1.3 bitcast_reduce_fusion.1
  22.3 0.4 divide_reduce_fusion.3
  22.8 0.6 copy-done.112
  23.4 0.6 bitcast_reduce_fusion.2
  24.2 0.3 divide_reduce_fusion.4
  24.5 0.4 bitcast_reduce_fusion.3
  25.5 0.6 copy-done.133
  26.1 0.3 constant_dynamic-update-slice_fusion.11
  26.6 0.4 fusion.53
  27.2 0.2 constant_dynamic-update-slice_fusion.9
  27.5 0.2 constant_dynamic-update-slice_fusion.8
  28.2 0.6 copy-done.53
  30.0 0.6 slice.613
  30.6 0.6 slice.615
  31.2 0.6 bitcast_convert_fusion
  31.8 0.6 copy-done.5
  33.0 1.0 pad_maximum_fusion.2
  33.9 16.1 %shard_map.73 = (f32[11,4736]{1,0:T(8,128)}, f32[11,4736]{1,0:T(8,128)}) custom-call(f32[11,4736]{1,0:T(8,128)} %get-tuple-element.43.to_right, f32[11,4736]{1,0:T(8,128)} %get-tuple-element.42.to_left), custom_call_target="tpu_custom_call" | custom-call | tf_op jit(solution)/shard_map/pallas_call | solution.py:60
  50.1 1.0 slice.546
  52.1 0.6 compare_and_fusion
  52.7 1.1 pad_maximum_fusion
  53.8 0.9 gather_fusion
  54.8 0.3 select_bitcast_fusion
  55.7 10.0 %fusion.9 = f32[8,186,64]{2,0,1:T(8,128)S(1)} fusion(f32[186,64]{1,0:T(8,128)S(1)} %get-tuple-element.40, f32[186,64]{1,0:T(8,128)S(1)} %bitcast.415, f32[186,64]{1,0:T(8,128)S(1)} %get-tuple-element.41, f32[186,64]{1,0:T(8,128)S(1)} %bitcast.416, f32[186,64]{1,0:T(8,128)S(1)} %get-tuple-element.39, f32[186,64]{1,0:T(8,128)S(1)} %bitcast.417, ...), kind=kOutput, calls=%fused_computation.16 | convolution fusion | flops 81613824 | bytes 1733632 | tf_op jit(solution)/shard_map/qnr,nrs->qns/dot_general | solution.py:230
  65.9 0.9 slice.474
  66.7 0.8 slice.475
  67.5 0.6 reduce_sum.310
  68.1 0.6 reduce_sum.311
  68.8 0.6 reduce_sum.313
  69.4 0.7 reduce_sum.314
  70.1 3.1 %copy.95 = f32[3,9728]{0,1:T(8,128)} copy(f32[3,9728]{1,0:T(4,128)S(1)} %pad_maximum_fusion.4) | data formatting | bytes 233472 | tf_op jit(solution)/shard_map/slice | solution.py:200
  73.2 0.7 slice.583
  74.1 0.7 reshape.3416.source_ref
  74.8 1.0 constant_dynamic-slice_fusion.40
  75.8 0.9 constant_dynamic-slice_fusion.46
  76.8 76.2 %shard_map.74 = f32[8,8192]{1,0:T(8,128)} custom-call(s32[192]{0:T(256)} %reshape.3416.source_ref, f32[38,8,256]{2,1,0:T(8,128)} %bitcast.408, f32[38,256,3]{2,1,0:T(8,128)} %bitcast.400, f32[3,8192]{1,0:T(4,128)} %target_ref.1), custom_call_target="tpu_custom_call" | custom-call | flops 352321536 | bytes 5855232 | tf_op jit(solution)/shard_map/pallas_call | solution.py:112
  153.0 0.6 slice_bitcast_fusion.8
  153.6 0.6 slice_bitcast_fusion.7
  154.2 2.0 %fusion.216 = (f32[128,8,1,64]{3,1,0,2:T(8,128)S(1)}, f32[128,8,1,64]{3,1,0,2:T(8,128)S(1)}, f32[128,8,1,64]{3,1,0,2:T(8,128)S(1)}, f32[128,8,1,64]{3,1,0,2:T(8,...) fusion(f32[128,8,6,64]{3,1,0,2:T(8,128)} %bitcast.401), kind=kLoop, calls=%fused_computation.539 | loop fusion | bytes 3145728 | tf_op jit(solution)/shard_map/slice | solution.py:263
  156.3 0.8 reduce_sum.300
  157.0 0.7 constant_dynamic-update-slice_fusion.24
  157.7 0.7 constant_dynamic-update-slice_fusion.23
  158.4 0.7 constant_dynamic-update-slice_fusion.22
  159.7 1.6 convolution_bitcast_fusion.3
  161.9 0.9 fusion.22
  162.8 0.9 fusion.20
  163.8 0.9 fusion.18
  164.7 0.9 fusion.16
  165.7 1.0 fusion.14
  166.8 0.5 fusion.13
  167.3 0.8 fusion.12
  168.3 1.6 fusion.11
  170.0 3.2 %fusion.10 = f32[8,32,64]{2,0,1:T(8,128)S(1)} fusion(f32[8,32,64]{2,0,1:T(8,128)S(1)} %copy-done.13, f32[8,32,64]{2,0,1:T(8,128)S(1)} %bitcast.414, f32[32,64]{1,0:T(8,128)S(1)} %copy-done.63, f32[32,64]{1,0:T(8,128)S(1)} %bitcast.427, f32[32,64]{1,0:T(8,128)S(1)} %copy-done.12, f32[32,64]{1,0:T(8,128)S(1)} %bitcast.424, f32[32,64]{1,0:T(8,128)S(1)} %copy-done.10, ...), kind=kOutput, calls=%fused_computation.19 | convolution fusion | flops 14172160 | bytes 253952 | tf_op jit(solution)/shard_map/qns,nrs->qnr/dot_general | solution.py:292
  173.3 2.7 %fusion.26 = f32[32,256,8]{1,2,0:T(8,128)S(1)} fusion(f32[8,32,64]{2,0,1:T(8,128)S(1)} %fusion.10, f32[32,256]{1,0:T(8,128)S(1)} %copy-done.48, f32[32,64]{1,0:T(8,128)S(1)} %copy-done.12, f32[32,256]{1,0:T(8,128)S(1)} %copy-done.19, f32[32,64]{1,0:T(8,128)S(1)} %copy-done.10, f32[32,256]{1,0:T(8,128)S(1)} %copy-done.17, f32[32,64]{1,0:T(8,128)S(1)} %sub.1263, ...), kind=kOutput, calls=%fused_computation.48 | convolution fusion | flops 56623104 | bytes 483328 | tf_op jit(solution)/shard_map/qbr,bpr->qbp/dot_general | solution.py:296
  176.1 0.7 add_add_fusion
  (415 shorter events, 5.7 us)
Async XLA Ops:
  6.5 6.1 %copy-start.4 = (f32[8,8192]{1,0:T(8,128)S(1)}, f32[8,8192]{1,0:T(8,128)}, u32[]{:S(2)}) copy-start(f32[8,8192]{1,0:T(8,128)} %param.7) | copy-start | bytes 786436
  6.5 147.7 %all-gather.3.cloned.1.call-start = ((), (), s32[]{:S(2)}) async-start(), calls=%async_computation | async-start | bytes 3170304 | tf_op jit(solution)/shard_map/all_gather | solution.py:258
  7.8 17.1 %copy-start.49 = (f32[3,8,64]{2,1,0:T(8,128)}, f32[3,8,64]{2,1,0:T(8,128)S(1)}, u32[]{:S(2)}) copy-start(f32[3,8,64]{2,1,0:T(8,128)S(1)} %slice.588) | copy-start | bytes 18436
  7.8 18.6 %copy-start.54 = (f32[3,4,64]{2,1,0:T(4,128)}, f32[3,4,64]{2,1,0:T(4,128)S(1)}, u32[]{:S(2)}) copy-start(f32[3,4,64]{2,1,0:T(4,128)S(1)} %slice.589) | copy-start | bytes 9220
  7.8 18.6 %copy-start.26 = (f32[3,32,64]{2,1,0:T(8,128)}, f32[3,32,64]{2,1,0:T(8,128)S(1)}, u32[]{:S(2)}) copy-start(f32[3,32,64]{2,1,0:T(8,128)S(1)} %slice.586) | copy-start | bytes 73732
  7.8 18.6 %copy-start.34 = (f32[3,16,64]{2,1,0:T(8,128)}, f32[3,16,64]{2,1,0:T(8,128)S(1)}, u32[]{:S(2)}) copy-start(f32[3,16,64]{2,1,0:T(8,128)S(1)} %slice.587) | copy-start | bytes 36868
  7.9 17.0 %copy-start.8 = (f32[3,128,64]{2,1,0:T(8,128)}, f32[3,128,64]{2,1,0:T(8,128)S(1)}, u32[]{:S(2)}) copy-start(f32[3,128,64]{2,1,0:T(8,128)S(1)} %slice.584) | copy-start | bytes 294916
  7.9 18.5 %copy-start.20 = (f32[3,64,64]{2,1,0:T(8,128)}, f32[3,64,64]{2,1,0:T(8,128)S(1)}, u32[]{:S(2)}) copy-start(f32[3,64,64]{2,1,0:T(8,128)S(1)} %slice.585) | copy-start | bytes 147460
  8.8 21.8 %copy-start.2 = (f32[3,30,64]{2,1,0:T(8,128)}, f32[3,30,64]{2,1,0:T(8,128)S(1)}, u32[]{:S(2)}) copy-start(f32[3,30,64]{2,1,0:T(8,128)S(1)} %reshape.3418) | copy-start | bytes 69124
  8.8 12.1 %copy-start.22 = (f32[16,64]{1,0:T(8,128)}, f32[16,64]{1,0:T(8,128)S(1)}, u32[]{:S(2)}) copy-start(f32[16,64]{1,0:T(8,128)S(1)} %get-tuple-element.75) | copy-start | bytes 12292
  8.8 12.1 %copy-start.24 = (f32[16,64]{1,0:T(8,128)}, f32[16,64]{1,0:T(8,128)S(1)}, u32[]{:S(2)}) copy-start(f32[16,64]{1,0:T(8,128)S(1)} %get-tuple-element.76) | copy-start | bytes 12292
  8.8 13.8 %copy-start.35 = (f32[8,64]{1,0:T(8,128)}, f32[8,64]{1,0:T(8,128)S(1)}, u32[]{:S(2)}) copy-start(f32[8,64]{1,0:T(8,128)S(1)} %get-tuple-element.71) | copy-start | bytes 6148
  8.8 13.8 %copy-start.37 = (f32[8,64]{1,0:T(8,128)}, f32[8,64]{1,0:T(8,128)S(1)}, u32[]{:S(2)}) copy-start(f32[8,64]{1,0:T(8,128)S(1)} %get-tuple-element.72) | copy-start | bytes 6148
  8.8 13.8 %copy-start.39 = (f32[8,64]{1,0:T(8,128)}, f32[8,64]{1,0:T(8,128)S(1)}, u32[]{:S(2)}) copy-start(f32[8,64]{1,0:T(8,128)S(1)} %get-tuple-element.73) | copy-start | bytes 6148
  8.9 15.6 %copy-start.56 = (f32[4,64]{1,0:T(4,128)}, f32[4,64]{1,0:T(4,128)S(1)}, u32[]{:S(2)}) copy-start(f32[4,64]{1,0:T(4,128)S(1)} %get-tuple-element.68) | copy-start | bytes 3076
  8.9 15.6 %copy-start.58 = (f32[4,64]{1,0:T(4,128)}, f32[4,64]{1,0:T(4,128)S(1)}, u32[]{:S(2)}) copy-start(f32[4,64]{1,0:T(4,128)S(1)} %get-tuple-element.69) | copy-start | bytes 3076
  8.9 15.6 %copy-start.60 = (f32[4,64]{1,0:T(4,128)}, f32[4,64]{1,0:T(4,128)S(1)}, u32[]{:S(2)}) copy-start(f32[4,64]{1,0:T(4,128)S(1)} %get-tuple-element.70) | copy-start | bytes 3076
  8.9 16.3 %copy-start.72 = (f32[2,64]{1,0:T(2,128)}, f32[2,64]{1,0:T(2,128)S(1)}, u32[]{:S(2)}) copy-start(f32[2,64]{1,0:T(2,128)S(1)} %get-tuple-element.65) | copy-start | bytes 1540
  8.9 16.3 %copy-start.74 = (f32[2,64]{1,0:T(2,128)}, f32[2,64]{1,0:T(2,128)S(1)}, u32[]{:S(2)}) copy-start(f32[2,64]{1,0:T(2,128)S(1)} %get-tuple-element.66) | copy-start | bytes 1540
  8.9 16.3 %copy-start.76 = (f32[2,64]{1,0:T(2,128)}, f32[2,64]{1,0:T(2,128)S(1)}, u32[]{:S(2)}) copy-start(f32[2,64]{1,0:T(2,128)S(1)} %get-tuple-element.67) | copy-start | bytes 1540
  10.1 7.4 %copy-start.9 = (f32[32,64]{1,0:T(8,128)}, f32[32,64]{1,0:T(8,128)S(1)}, u32[]{:S(2)}) copy-start(f32[32,64]{1,0:T(8,128)S(1)} %sub.1268) | copy-start | bytes 24580
  10.1 7.4 %copy-start.11 = (f32[32,64]{1,0:T(8,128)}, f32[32,64]{1,0:T(8,128)S(1)}, u32[]{:S(2)}) copy-start(f32[32,64]{1,0:T(8,128)S(1)} %sub.1273) | copy-start | bytes 24580
  24.1 5.4 %copy-start.21 = (f32[3,2048]{1,0:T(4,128)S(1)}, f32[3,2048]{1,0:T(4,128)}, u32[]{:S(2)}) copy-start(f32[3,2048]{1,0:T(4,128)} %param.10) | copy-start | bytes 73732
  24.1 5.7 %copy-start.71 = (s32[32,3]{0,1:T(4,128)S(1)}, s32[32,3]{0,1:T(4,128)}, u32[]{:S(2)}) copy-start(s32[32,3]{0,1:T(4,128)} %param.13) | copy-start | bytes 1156
  24.1 5.9 %copy-start.80 = (f32[2,2,64]{2,1,0:T(2,128)}, f32[2,2,64]{2,1,0:T(2,128)S(1)}, u32[]{:S(2)}) copy-start(f32[2,2,64]{2,1,0:T(2,128)S(1)} %broadcast_in_dim.132) | copy-start | bytes 3076
  24.1 5.8 %copy-start.82 = (f32[2,2,64]{2,1,0:T(2,128)}, f32[2,2,64]{2,1,0:T(2,128)S(1)}, u32[]{:S(2)}) copy-start(f32[2,2,64]{2,1,0:T(2,128)S(1)} %broadcast_in_dim.134) | copy-start | bytes 3076
  24.1 5.8 %copy-start.84 = (f32[2,2,64]{2,1,0:T(2,128)}, f32[2,2,64]{2,1,0:T(2,128)S(1)}, u32[]{:S(2)}) copy-start(f32[2,2,64]{2,1,0:T(2,128)S(1)} %broadcast_in_dim.136) | copy-start | bytes 3076
  24.4 5.0 %copy-start.115 = (f32[4,64]{1,0:T(4,128)}, f32[4,64]{1,0:T(4,128)S(1)}, u32[]{:S(2)}) copy-start(f32[4,64]{1,0:T(4,128)S(1)} %divide_reduce_fusion.4) | copy-start | bytes 3076
  26.5 6.1 %copy-start.88 = (f32[64]{0:T(128)}, f32[64]{0:T(128)S(1)}, u32[]{:S(2)}) copy-start(f32[64]{0:T(128)S(1)} %get-tuple-element.55) | copy-start | bytes 772
  26.5 6.1 %copy-start.90 = (f32[64]{0:T(128)}, f32[64]{0:T(128)S(1)}, u32[]{:S(2)}) copy-start(f32[64]{0:T(128)S(1)} %get-tuple-element.56) | copy-start | bytes 772
  26.5 6.1 %copy-start.92 = (f32[64]{0:T(128)}, f32[64]{0:T(128)S(1)}, u32[]{:S(2)}) copy-start(f32[64]{0:T(128)S(1)} %get-tuple-element.57) | copy-start | bytes 772
  27.0 5.6 %copy-start.135 = (f32[64]{0:T(128)}, f32[64]{0:T(128)S(1)}, u32[]{:S(2)}) copy-start(f32[64]{0:T(128)S(1)} %get-tuple-element.23) | copy-start | bytes 772
  27.0 5.6 %copy-start.136 = (f32[64]{0:T(128)}, f32[64]{0:T(128)S(1)}, u32[]{:S(2)}) copy-start(f32[64]{0:T(128)S(1)} %get-tuple-element.22) | copy-start | bytes 772
  27.0 5.6 %copy-start.138 = (f32[64]{0:T(128)}, f32[64]{0:T(128)S(1)}, u32[]{:S(2)}) copy-start(f32[64]{0:T(128)S(1)} %get-tuple-element.20) | copy-start | bytes 772
  27.0 5.6 %copy-start.139 = (f32[64]{0:T(128)}, f32[64]{0:T(128)S(1)}, u32[]{:S(2)}) copy-start(f32[64]{0:T(128)S(1)} %get-tuple-element.24) | copy-start | bytes 772
  32.9 18.6 %copy-start = (f32[11,8192]{1,0:T(8,128)}, f32[11,8192]{1,0:T(8,128)S(1)}, u32[]{:S(2)}) copy-start(f32[11,8192]{1,0:T(8,128)S(1)} %constant_dynamic-update-slice_fusion) | copy-start | bytes 1081348
  70.1 4.6 %copy-start.50 = (f32[3,8,64]{2,1,0:T(8,128)S(1)}, f32[3,8,64]{2,1,0:T(8,128)}, u32[]{:S(2)}) copy-start(f32[3,8,64]{2,1,0:T(8,128)} %copy-done.49) | copy-start | bytes 18436
  159.6 5.1 %copy-start.118 = (f32[64]{0:T(128)S(1)}, f32[64]{0:T(128)}, u32[]{:S(2)}) copy-start(f32[64]{0:T(128)} %copy-done.117) | copy-start | bytes 772
  159.6 6.0 %copy-start.73 = (f32[2,64]{1,0:T(2,128)S(1)}, f32[2,64]{1,0:T(2,128)}, u32[]{:S(2)}) copy-start(f32[2,64]{1,0:T(2,128)} %copy-done.72) | copy-start | bytes 1540
  159.6 6.0 %copy-start.75 = (f32[2,64]{1,0:T(2,128)S(1)}, f32[2,64]{1,0:T(2,128)}, u32[]{:S(2)}) copy-start(f32[2,64]{1,0:T(2,128)} %copy-done.74) | copy-start | bytes 1540
  159.6 6.0 %copy-start.77 = (f32[2,64]{1,0:T(2,128)S(1)}, f32[2,64]{1,0:T(2,128)}, u32[]{:S(2)}) copy-start(f32[2,64]{1,0:T(2,128)} %copy-done.76) | copy-start | bytes 1540
  159.7 6.0 %copy-start.86 = (f32[8,2,64]{2,0,1:T(8,128)S(1)}, f32[8,2,64]{2,0,1:T(8,128)}, u32[]{:S(2)}) copy-start(f32[8,2,64]{2,0,1:T(8,128)} %reduce_sum.310) | copy-start | bytes 12292
  159.7 7.0 %copy-start.57 = (f32[4,64]{1,0:T(4,128)S(1)}, f32[4,64]{1,0:T(4,128)}, u32[]{:S(2)}) copy-start(f32[4,64]{1,0:T(4,128)} %copy-done.56) | copy-start | bytes 3076
  159.7 7.0 %copy-start.59 = (f32[4,64]{1,0:T(4,128)S(1)}, f32[4,64]{1,0:T(4,128)}, u32[]{:S(2)}) copy-start(f32[4,64]{1,0:T(4,128)} %copy-done.58) | copy-start | bytes 3076
  159.7 7.0 %copy-start.61 = (f32[4,64]{1,0:T(4,128)S(1)}, f32[4,64]{1,0:T(4,128)}, u32[]{:S(2)}) copy-start(f32[4,64]{1,0:T(4,128)} %copy-done.60) | copy-start | bytes 3076
  159.7 7.0 %copy-start.70 = (f32[8,4,64]{2,0,1:T(8,128)S(1)}, f32[8,4,64]{2,0,1:T(8,128)}, u32[]{:S(2)}) copy-start(f32[8,4,64]{2,0,1:T(8,128)} %reduce_sum.311) | copy-start | bytes 24580
  159.7 7.0 %copy-start.81 = (f32[2,2,64]{2,1,0:T(2,128)S(1)}, f32[2,2,64]{2,1,0:T(2,128)}, u32[]{:S(2)}) copy-start(f32[2,2,64]{2,1,0:T(2,128)} %copy-done.80) | copy-start | bytes 3076
  159.7 7.0 %copy-start.83 = (f32[2,2,64]{2,1,0:T(2,128)S(1)}, f32[2,2,64]{2,1,0:T(2,128)}, u32[]{:S(2)}) copy-start(f32[2,2,64]{2,1,0:T(2,128)} %copy-done.82) | copy-start | bytes 3076
  159.7 7.0 %copy-start.85 = (f32[2,2,64]{2,1,0:T(2,128)S(1)}, f32[2,2,64]{2,1,0:T(2,128)}, u32[]{:S(2)}) copy-start(f32[2,2,64]{2,1,0:T(2,128)} %copy-done.84) | copy-start | bytes 3076
  159.7 7.0 %copy-start.116 = (f32[4,64]{1,0:T(4,128)S(1)}, f32[4,64]{1,0:T(4,128)}, u32[]{:S(2)}) copy-start(f32[4,64]{1,0:T(4,128)} %copy-done.115) | copy-start | bytes 3076
  161.4 5.9 %copy-start.36 = (f32[8,64]{1,0:T(8,128)S(1)}, f32[8,64]{1,0:T(8,128)}, u32[]{:S(2)}) copy-start(f32[8,64]{1,0:T(8,128)} %copy-done.35) | copy-start | bytes 6148
  161.4 5.9 %copy-start.38 = (f32[8,64]{1,0:T(8,128)S(1)}, f32[8,64]{1,0:T(8,128)}, u32[]{:S(2)}) copy-start(f32[8,64]{1,0:T(8,128)} %copy-done.37) | copy-start | bytes 6148
  161.4 5.9 %copy-start.40 = (f32[8,64]{1,0:T(8,128)S(1)}, f32[8,64]{1,0:T(8,128)}, u32[]{:S(2)}) copy-start(f32[8,64]{1,0:T(8,128)} %copy-done.39) | copy-start | bytes 6148
  161.4 5.9 %copy-start.65 = (f32[4,2,64]{2,1,0:T(2,128)S(1)}, f32[4,2,64]{2,1,0:T(2,128)}, u32[]{:S(2)}) copy-start(f32[4,2,64]{2,1,0:T(2,128)} %copy-done.64) | copy-start | bytes 6148
  161.4 5.9 %copy-start.67 = (f32[4,2,64]{2,1,0:T(2,128)S(1)}, f32[4,2,64]{2,1,0:T(2,128)}, u32[]{:S(2)}) copy-start(f32[4,2,64]{2,1,0:T(2,128)} %copy-done.66) | copy-start | bytes 6148
  161.4 5.9 %copy-start.69 = (f32[4,2,64]{2,1,0:T(2,128)S(1)}, f32[4,2,64]{2,1,0:T(2,128)}, u32[]{:S(2)}) copy-start(f32[4,2,64]{2,1,0:T(2,128)} %copy-done.68) | copy-start | bytes 6148
  161.5 5.9 %copy-start.113 = (f32[8,64]{1,0:T(8,128)S(1)}, f32[8,64]{1,0:T(8,128)}, u32[]{:S(2)}) copy-start(f32[8,64]{1,0:T(8,128)} %copy-done.112) | copy-start | bytes 6148
  161.8 6.4 %copy-start.23 = (f32[16,64]{1,0:T(8,128)S(1)}, f32[16,64]{1,0:T(8,128)}, u32[]{:S(2)}) copy-start(f32[16,64]{1,0:T(8,128)} %copy-done.22) | copy-start | bytes 12292
  161.8 6.4 %copy-start.25 = (f32[16,64]{1,0:T(8,128)S(1)}, f32[16,64]{1,0:T(8,128)}, u32[]{:S(2)}) copy-start(f32[16,64]{1,0:T(8,128)} %copy-done.24) | copy-start | bytes 12292
  161.9 6.4 %copy-start.33 = (f32[8,16,64]{2,0,1:T(8,128)S(1)}, f32[8,16,64]{2,0,1:T(8,128)}, u32[]{:S(2)}) copy-start(f32[8,16,64]{2,0,1:T(8,128)} %reduce_sum.313) | copy-start | bytes 98308
  161.9 6.4 %copy-start.42 = (f32[8,2,64]{2,1,0:T(2,128)S(1)}, f32[8,2,64]{2,1,0:T(2,128)}, u32[]{:S(2)}) copy-start(f32[8,2,64]{2,1,0:T(2,128)} %copy-done.41) | copy-start | bytes 12292
  161.9 6.4 %copy-start.44 = (f32[8,2,64]{2,1,0:T(2,128)S(1)}, f32[8,2,64]{2,1,0:T(2,128)}, u32[]{:S(2)}) copy-start(f32[8,2,64]{2,1,0:T(2,128)} %copy-done.43) | copy-start | bytes 12292
  161.9 6.4 %copy-start.46 = (f32[8,2,64]{2,1,0:T(2,128)S(1)}, f32[8,2,64]{2,1,0:T(2,128)}, u32[]{:S(2)}) copy-start(f32[8,2,64]{2,1,0:T(2,128)} %copy-done.45) | copy-start | bytes 12292
  161.9 6.4 %copy-start.79 = (f32[16,64]{1,0:T(8,128)S(1)}, f32[16,64]{1,0:T(8,128)}, u32[]{:S(2)}) copy-start(f32[16,64]{1,0:T(8,128)} %copy-done.78) | copy-start | bytes 12292
  (83 other events, 206.8 us)
Sparse Core Ops, SparseCore 0:
  29.0 86.3 all-gather.2

commit v7 on v6

--- a/solution.py
+++ b/solution.py
@@ -100,7 +100,7 @@
             distance_sq = distance_sq + (near[:, 2:3] - target_z) ** 2
             kernel_block = 1.0 / (1.0 + kernel_scale * distance_sq)
             out_ref[...] += jnp.dot(
-                probes_ref[source], kernel_block, precision=PRECISE,
+                probes_ref[source], kernel_block, precision=lax.Precision.HIGH,
                 preferred_element_type=jnp.float32,
             )
 

time: 185 us -> 182 us (0.984)
  the two profiles are of different devices: /device:TPU:28 before, /device:TPU:16 now
where the time goes in v7:
time: 182 us; the launch traced here: 181 us
  Pallas kernels  89.5 us (49%)
  matrix products  35.1 us (19%)
  local copies, waits for them, and re-layouts  27.1 us (15%)
  between operations  16.8 us (9%)
  other arithmetic  12.3 us (7%)
    pallas_call x1, Pallas kernels, near_field_call(): pl.pallas_call(functools.partial(near_kernel, kernel_scale, slots), out_s...  73.3 us
    pallas_call x1, Pallas kernels, exchange_halo(): pl.pallas_call(halo_kernel, out_shape=(shape, shape), in_specs=[vmem, vme...  16.1 us
    dot_general x1, matrix products, body(): jnp.einsum('qnr,nrs->qns', source_moment, kernel_block, precision=PRECISE)  10 us
    dot_general x5, matrix products, body(): jnp.einsum('qns,nrs->qnr', jnp.repeat(descent, 2, axis=1), transfer_maps[...  7.14 us
    unnamed x301, local copies, waits for them, and re-layouts  5.65 us
    dot_general x5, matrix products, body(): jnp.einsum('qnr,nrs->qns', level_moments[-1], interp_map, precision=PRECISE)  5.15 us
    reduce_sum x7, other arithmetic, interpolation(): return values / jnp.sum(values, axis=-1, keepdims=True)  4.31 us
    dot_general x5, matrix products, body(): jnp.einsum('qns,nrs->qnr', descent, own_edges[height], precision=PRECISE)  3.86 us
  transfers between devices with their start and end apart: 1, of which 0 were waited for; matrix products, arithmetic and copies ran while one was open for 17% of the time, Pallas kernels for 49%

profile of v7, /device:TPU:16, one launch (start us, length us, event | category | flops | bytes accessed | tf_op | source)
XLA Modules:
  0.0 180.8 jit_solution(11916088645480974506)
XLA Ops:
  6.5 1.2 reshape.3425
  7.9 0.9 reshape.3418
  9.0 0.9 slice_reduce_fusion.10
  10.1 1.3 slice_reduce_fusion.2
  11.6 1.1 divide_reduce_fusion
  12.7 3.3 %constant_dynamic-update-slice_fusion.6 = (f32[8,62,64]{2,0,1:T(8,128)S(1)}, f32[8,32,64]{2,0,1:T(8,128)S(1)}) fusion(f32[8,32,256]{2,0,1:T(8,128)S(1)} %bitcast.409, f32[32,256]{1,0:T(8,128)S(1)} %divide_reduce_fusion, f32[32,64]{1,0:T(8,128)S(1)} %sub.1273, f32[32,256]{1,0:T(8,128)S(1)} %sub.1271, f32[32,64]{1,0:T(8,128)S(1)} %sub.1268, ...), kind=kOutput, calls=%fused_computation.97 | convolution fusion | flops 56623104 | bytes 679936 | tf_op jit(solution)/shard_map/qbp,bpr->qbr/dot_general | solution.py:162
  16.1 1.4 divide_reduce_fusion.1
  17.5 2.6 %bitcast_reduce_fusion = f32[8,16,64]{2,0,1:T(8,128)S(1)} fusion(f32[8,32,64]{2,0,1:T(8,128)S(1)} %get-tuple-element.122, f32[32,64]{1,0:T(8,128)S(1)} %divide_reduce_fusion.1, f32[32,64]{1,0:T(8,128)S(1)} %bitcast.426, f32[32,64]{1,0:T(8,128)S(1)} %sub.1273, f32[32,64]{1,0:T(8,128)S(1)} %bitcast.423, f32[32,64]{1,0:T(8,128)S(1)} %sub.1268, ...), kind=kOutput, calls=%fused_computation.75 | convolution fusion | flops 14163968 | bytes 155648 | tf_op jit(solution)/shard_map/qnr,nrs->qns/dot_general | solution.py:169
  20.2 0.7 divide_reduce_fusion.2
  20.9 1.3 bitcast_reduce_fusion.1
  22.3 0.4 divide_reduce_fusion.3
  22.8 0.6 copy-done.112
  23.4 0.6 bitcast_reduce_fusion.2
  24.2 0.3 divide_reduce_fusion.4
  24.5 0.4 bitcast_reduce_fusion.3
  25.5 0.6 copy-done.133
  26.1 0.3 constant_dynamic-update-slice_fusion.11
  26.6 0.4 fusion.53
  27.2 0.2 constant_dynamic-update-slice_fusion.9
  27.5 0.2 constant_dynamic-update-slice_fusion.8
  28.2 0.6 copy-done.53
  30.0 0.6 slice.613
  30.6 0.6 slice.615
  31.2 0.6 bitcast_convert_fusion
  31.8 0.6 copy-done.5
  33.0 1.0 pad_maximum_fusion.2
  33.9 16.1 %shard_map.73 = (f32[11,4736]{1,0:T(8,128)}, f32[11,4736]{1,0:T(8,128)}) custom-call(f32[11,4736]{1,0:T(8,128)} %get-tuple-element.43.to_right, f32[11,4736]{1,0:T(8,128)} %get-tuple-element.42.to_left), custom_call_target="tpu_custom_call" | custom-call | tf_op jit(solution)/shard_map/pallas_call | solution.py:60
  50.1 1.0 slice.546
  52.1 0.6 compare_and_fusion
  52.7 1.1 pad_maximum_fusion
  53.8 0.9 gather_fusion
  54.8 0.3 select_bitcast_fusion
  55.7 10.0 %fusion.9 = f32[8,186,64]{2,0,1:T(8,128)S(1)} fusion(f32[186,64]{1,0:T(8,128)S(1)} %get-tuple-element.40, f32[186,64]{1,0:T(8,128)S(1)} %bitcast.415, f32[186,64]{1,0:T(8,128)S(1)} %get-tuple-element.41, f32[186,64]{1,0:T(8,128)S(1)} %bitcast.416, f32[186,64]{1,0:T(8,128)S(1)} %get-tuple-element.39, f32[186,64]{1,0:T(8,128)S(1)} %bitcast.417, ...), kind=kOutput, calls=%fused_computation.16 | convolution fusion | flops 81613824 | bytes 1733632 | tf_op jit(solution)/shard_map/qnr,nrs->qns/dot_general | solution.py:230
  65.9 0.9 slice.474
  66.7 0.8 slice.475
  67.5 0.6 reduce_sum.310
  68.1 0.6 reduce_sum.311
  68.8 0.6 reduce_sum.313
  69.4 0.7 reduce_sum.314
  70.1 3.1 %copy.95 = f32[3,9728]{0,1:T(8,128)} copy(f32[3,9728]{1,0:T(4,128)S(1)} %pad_maximum_fusion.4) | data formatting | bytes 233472 | tf_op jit(solution)/shard_map/slice | solution.py:200
  73.2 0.7 slice.583
  74.1 0.7 reshape.3416.source_ref
  74.8 0.9 constant_dynamic-slice_fusion.40
  75.7 0.9 constant_dynamic-slice_fusion.46
  76.8 73.3 %shard_map.74 = f32[8,8192]{1,0:T(8,128)} custom-call(s32[192]{0:T(256)} %reshape.3416.source_ref, f32[38,8,256]{2,1,0:T(8,128)} %bitcast.408, f32[38,256,3]{2,1,0:T(8,128)} %bitcast.400, f32[3,8192]{1,0:T(4,128)} %target_ref.1), custom_call_target="tpu_custom_call" | custom-call | flops 352321536 | bytes 5855232 | tf_op jit(solution)/shard_map/pallas_call | solution.py:112
  150.1 0.6 slice_bitcast_fusion.8
  150.7 0.6 slice_bitcast_fusion.7
  151.3 2.0 %fusion.216 = (f32[128,8,1,64]{3,1,0,2:T(8,128)S(1)}, f32[128,8,1,64]{3,1,0,2:T(8,128)S(1)}, f32[128,8,1,64]{3,1,0,2:T(8,128)S(1)}, f32[128,8,1,64]{3,1,0,2:T(8,...) fusion(f32[128,8,6,64]{3,1,0,2:T(8,128)} %bitcast.401), kind=kLoop, calls=%fused_computation.539 | loop fusion | bytes 3145728 | tf_op jit(solution)/shard_map/slice | solution.py:263
  153.4 0.8 reduce_sum.300
  154.1 0.7 constant_dynamic-update-slice_fusion.24
  154.8 0.7 constant_dynamic-update-slice_fusion.23
  155.5 0.7 constant_dynamic-update-slice_fusion.22
  156.9 1.6 convolution_bitcast_fusion.3
  159.0 0.9 fusion.22
  160.0 0.9 fusion.20
  160.9 0.9 fusion.18
  161.8 0.9 fusion.16
  162.8 1.0 fusion.14
  163.9 0.5 fusion.13
  164.5 0.8 fusion.12
  165.4 1.6 fusion.11
  167.2 3.2 %fusion.10 = f32[8,32,64]{2,0,1:T(8,128)S(1)} fusion(f32[8,32,64]{2,0,1:T(8,128)S(1)} %copy-done.13, f32[8,32,64]{2,0,1:T(8,128)S(1)} %bitcast.414, f32[32,64]{1,0:T(8,128)S(1)} %copy-done.63, f32[32,64]{1,0:T(8,128)S(1)} %bitcast.427, f32[32,64]{1,0:T(8,128)S(1)} %copy-done.12, f32[32,64]{1,0:T(8,128)S(1)} %bitcast.424, f32[32,64]{1,0:T(8,128)S(1)} %copy-done.10, ...), kind=kOutput, calls=%fused_computation.19 | convolution fusion | flops 14172160 | bytes 253952 | tf_op jit(solution)/shard_map/qns,nrs->qnr/dot_general | solution.py:292
  170.4 2.7 %fusion.26 = f32[32,256,8]{1,2,0:T(8,128)S(1)} fusion(f32[8,32,64]{2,0,1:T(8,128)S(1)} %fusion.10, f32[32,256]{1,0:T(8,128)S(1)} %copy-done.48, f32[32,64]{1,0:T(8,128)S(1)} %copy-done.12, f32[32,256]{1,0:T(8,128)S(1)} %copy-done.19, f32[32,64]{1,0:T(8,128)S(1)} %copy-done.10, f32[32,256]{1,0:T(8,128)S(1)} %copy-done.17, f32[32,64]{1,0:T(8,128)S(1)} %sub.1263, ...), kind=kOutput, calls=%fused_computation.48 | convolution fusion | flops 56623104 | bytes 483328 | tf_op jit(solution)/shard_map/qbr,bpr->qbp/dot_general | solution.py:296
  173.2 0.7 add_add_fusion
  (415 shorter events, 5.7 us)
Async XLA Ops:
  6.5 6.1 %copy-start.4 = (f32[8,8192]{1,0:T(8,128)S(1)}, f32[8,8192]{1,0:T(8,128)}, u32[]{:S(2)}) copy-start(f32[8,8192]{1,0:T(8,128)} %param.7) | copy-start | bytes 786436
  6.5 144.8 %all-gather.3.cloned.1.call-start = ((), (), s32[]{:S(2)}) async-start(), calls=%async_computation | async-start | bytes 3170304 | tf_op jit(solution)/shard_map/all_gather | solution.py:258
  7.8 17.1 %copy-start.49 = (f32[3,8,64]{2,1,0:T(8,128)}, f32[3,8,64]{2,1,0:T(8,128)S(1)}, u32[]{:S(2)}) copy-start(f32[3,8,64]{2,1,0:T(8,128)S(1)} %slice.588) | copy-start | bytes 18436
  7.8 18.6 %copy-start.54 = (f32[3,4,64]{2,1,0:T(4,128)}, f32[3,4,64]{2,1,0:T(4,128)S(1)}, u32[]{:S(2)}) copy-start(f32[3,4,64]{2,1,0:T(4,128)S(1)} %slice.589) | copy-start | bytes 9220
  7.8 18.6 %copy-start.26 = (f32[3,32,64]{2,1,0:T(8,128)}, f32[3,32,64]{2,1,0:T(8,128)S(1)}, u32[]{:S(2)}) copy-start(f32[3,32,64]{2,1,0:T(8,128)S(1)} %slice.586) | copy-start | bytes 73732
  7.8 18.6 %copy-start.34 = (f32[3,16,64]{2,1,0:T(8,128)}, f32[3,16,64]{2,1,0:T(8,128)S(1)}, u32[]{:S(2)}) copy-start(f32[3,16,64]{2,1,0:T(8,128)S(1)} %slice.587) | copy-start | bytes 36868
  7.9 17.0 %copy-start.8 = (f32[3,128,64]{2,1,0:T(8,128)}, f32[3,128,64]{2,1,0:T(8,128)S(1)}, u32[]{:S(2)}) copy-start(f32[3,128,64]{2,1,0:T(8,128)S(1)} %slice.584) | copy-start | bytes 294916
  7.9 18.5 %copy-start.20 = (f32[3,64,64]{2,1,0:T(8,128)}, f32[3,64,64]{2,1,0:T(8,128)S(1)}, u32[]{:S(2)}) copy-start(f32[3,64,64]{2,1,0:T(8,128)S(1)} %slice.585) | copy-start | bytes 147460
  8.8 21.8 %copy-start.2 = (f32[3,30,64]{2,1,0:T(8,128)}, f32[3,30,64]{2,1,0:T(8,128)S(1)}, u32[]{:S(2)}) copy-start(f32[3,30,64]{2,1,0:T(8,128)S(1)} %reshape.3418) | copy-start | bytes 69124
  8.8 12.1 %copy-start.22 = (f32[16,64]{1,0:T(8,128)}, f32[16,64]{1,0:T(8,128)S(1)}, u32[]{:S(2)}) copy-start(f32[16,64]{1,0:T(8,128)S(1)} %get-tuple-element.75) | copy-start | bytes 12292
  8.8 12.1 %copy-start.24 = (f32[16,64]{1,0:T(8,128)}, f32[16,64]{1,0:T(8,128)S(1)}, u32[]{:S(2)}) copy-start(f32[16,64]{1,0:T(8,128)S(1)} %get-tuple-element.76) | copy-start | bytes 12292
  8.8 13.8 %copy-start.35 = (f32[8,64]{1,0:T(8,128)}, f32[8,64]{1,0:T(8,128)S(1)}, u32[]{:S(2)}) copy-start(f32[8,64]{1,0:T(8,128)S(1)} %get-tuple-element.71) | copy-start | bytes 6148
  8.8 13.8 %copy-start.37 = (f32[8,64]{1,0:T(8,128)}, f32[8,64]{1,0:T(8,128)S(1)}, u32[]{:S(2)}) copy-start(f32[8,64]{1,0:T(8,128)S(1)} %get-tuple-element.72) | copy-start | bytes 6148
  8.8 13.8 %copy-start.39 = (f32[8,64]{1,0:T(8,128)}, f32[8,64]{1,0:T(8,128)S(1)}, u32[]{:S(2)}) copy-start(f32[8,64]{1,0:T(8,128)S(1)} %get-tuple-element.73) | copy-start | bytes 6148
  8.9 15.6 %copy-start.56 = (f32[4,64]{1,0:T(4,128)}, f32[4,64]{1,0:T(4,128)S(1)}, u32[]{:S(2)}) copy-start(f32[4,64]{1,0:T(4,128)S(1)} %get-tuple-element.68) | copy-start | bytes 3076
  8.9 15.6 %copy-start.58 = (f32[4,64]{1,0:T(4,128)}, f32[4,64]{1,0:T(4,128)S(1)}, u32[]{:S(2)}) copy-start(f32[4,64]{1,0:T(4,128)S(1)} %get-tuple-element.69) | copy-start | bytes 3076
  8.9 15.6 %copy-start.60 = (f32[4,64]{1,0:T(4,128)}, f32[4,64]{1,0:T(4,128)S(1)}, u32[]{:S(2)}) copy-start(f32[4,64]{1,0:T(4,128)S(1)} %get-tuple-element.70) | copy-start | bytes 3076
  8.9 16.3 %copy-start.72 = (f32[2,64]{1,0:T(2,128)}, f32[2,64]{1,0:T(2,128)S(1)}, u32[]{:S(2)}) copy-start(f32[2,64]{1,0:T(2,128)S(1)} %get-tuple-element.65) | copy-start | bytes 1540
  8.9 16.3 %copy-start.74 = (f32[2,64]{1,0:T(2,128)}, f32[2,64]{1,0:T(2,128)S(1)}, u32[]{:S(2)}) copy-start(f32[2,64]{1,0:T(2,128)S(1)} %get-tuple-element.66) | copy-start | bytes 1540
  8.9 16.3 %copy-start.76 = (f32[2,64]{1,0:T(2,128)}, f32[2,64]{1,0:T(2,128)S(1)}, u32[]{:S(2)}) copy-start(f32[2,64]{1,0:T(2,128)S(1)} %get-tuple-element.67) | copy-start | bytes 1540
  10.1 7.4 %copy-start.9 = (f32[32,64]{1,0:T(8,128)}, f32[32,64]{1,0:T(8,128)S(1)}, u32[]{:S(2)}) copy-start(f32[32,64]{1,0:T(8,128)S(1)} %sub.1268) | copy-start | bytes 24580
  10.1 7.4 %copy-start.11 = (f32[32,64]{1,0:T(8,128)}, f32[32,64]{1,0:T(8,128)S(1)}, u32[]{:S(2)}) copy-start(f32[32,64]{1,0:T(8,128)S(1)} %sub.1273) | copy-start | bytes 24580
  24.1 5.4 %copy-start.21 = (f32[3,2048]{1,0:T(4,128)S(1)}, f32[3,2048]{1,0:T(4,128)}, u32[]{:S(2)}) copy-start(f32[3,2048]{1,0:T(4,128)} %param.10) | copy-start | bytes 73732
  24.1 5.7 %copy-start.71 = (s32[32,3]{0,1:T(4,128)S(1)}, s32[32,3]{0,1:T(4,128)}, u32[]{:S(2)}) copy-start(s32[32,3]{0,1:T(4,128)} %param.13) | copy-start | bytes 1156
  24.1 5.9 %copy-start.80 = (f32[2,2,64]{2,1,0:T(2,128)}, f32[2,2,64]{2,1,0:T(2,128)S(1)}, u32[]{:S(2)}) copy-start(f32[2,2,64]{2,1,0:T(2,128)S(1)} %broadcast_in_dim.132) | copy-start | bytes 3076
  24.1 5.8 %copy-start.82 = (f32[2,2,64]{2,1,0:T(2,128)}, f32[2,2,64]{2,1,0:T(2,128)S(1)}, u32[]{:S(2)}) copy-start(f32[2,2,64]{2,1,0:T(2,128)S(1)} %broadcast_in_dim.134) | copy-start | bytes 3076
  24.1 5.8 %copy-start.84 = (f32[2,2,64]{2,1,0:T(2,128)}, f32[2,2,64]{2,1,0:T(2,128)S(1)}, u32[]{:S(2)}) copy-start(f32[2,2,64]{2,1,0:T(2,128)S(1)} %broadcast_in_dim.136) | copy-start | bytes 3076
  24.4 5.0 %copy-start.115 = (f32[4,64]{1,0:T(4,128)}, f32[4,64]{1,0:T(4,128)S(1)}, u32[]{:S(2)}) copy-start(f32[4,64]{1,0:T(4,128)S(1)} %divide_reduce_fusion.4) | copy-start | bytes 3076
  26.5 6.1 %copy-start.88 = (f32[64]{0:T(128)}, f32[64]{0:T(128)S(1)}, u32[]{:S(2)}) copy-start(f32[64]{0:T(128)S(1)} %get-tuple-element.55) | copy-start | bytes 772
  26.5 6.1 %copy-start.90 = (f32[64]{0:T(128)}, f32[64]{0:T(128)S(1)}, u32[]{:S(2)}) copy-start(f32[64]{0:T(128)S(1)} %get-tuple-element.56) | copy-start | bytes 772
  26.5 6.1 %copy-start.92 = (f32[64]{0:T(128)}, f32[64]{0:T(128)S(1)}, u32[]{:S(2)}) copy-start(f32[64]{0:T(128)S(1)} %get-tuple-element.57) | copy-start | bytes 772
  27.0 5.6 %copy-start.135 = (f32[64]{0:T(128)}, f32[64]{0:T(128)S(1)}, u32[]{:S(2)}) copy-start(f32[64]{0:T(128)S(1)} %get-tuple-element.23) | copy-start | bytes 772
  27.0 5.6 %copy-start.136 = (f32[64]{0:T(128)}, f32[64]{0:T(128)S(1)}, u32[]{:S(2)}) copy-start(f32[64]{0:T(128)S(1)} %get-tuple-element.22) | copy-start | bytes 772
  27.0 5.6 %copy-start.138 = (f32[64]{0:T(128)}, f32[64]{0:T(128)S(1)}, u32[]{:S(2)}) copy-start(f32[64]{0:T(128)S(1)} %get-tuple-element.20) | copy-start | bytes 772
  27.0 5.6 %copy-start.139 = (f32[64]{0:T(128)}, f32[64]{0:T(128)S(1)}, u32[]{:S(2)}) copy-start(f32[64]{0:T(128)S(1)} %get-tuple-element.24) | copy-start | bytes 772
  32.9 18.6 %copy-start = (f32[11,8192]{1,0:T(8,128)}, f32[11,8192]{1,0:T(8,128)S(1)}, u32[]{:S(2)}) copy-start(f32[11,8192]{1,0:T(8,128)S(1)} %constant_dynamic-update-slice_fusion) | copy-start | bytes 1081348
  70.1 4.6 %copy-start.50 = (f32[3,8,64]{2,1,0:T(8,128)S(1)}, f32[3,8,64]{2,1,0:T(8,128)}, u32[]{:S(2)}) copy-start(f32[3,8,64]{2,1,0:T(8,128)} %copy-done.49) | copy-start | bytes 18436
  156.7 5.1 %copy-start.118 = (f32[64]{0:T(128)S(1)}, f32[64]{0:T(128)}, u32[]{:S(2)}) copy-start(f32[64]{0:T(128)} %copy-done.117) | copy-start | bytes 772
  156.7 6.0 %copy-start.73 = (f32[2,64]{1,0:T(2,128)S(1)}, f32[2,64]{1,0:T(2,128)}, u32[]{:S(2)}) copy-start(f32[2,64]{1,0:T(2,128)} %copy-done.72) | copy-start | bytes 1540
  156.8 6.0 %copy-start.75 = (f32[2,64]{1,0:T(2,128)S(1)}, f32[2,64]{1,0:T(2,128)}, u32[]{:S(2)}) copy-start(f32[2,64]{1,0:T(2,128)} %copy-done.74) | copy-start | bytes 1540
  156.8 6.0 %copy-start.77 = (f32[2,64]{1,0:T(2,128)S(1)}, f32[2,64]{1,0:T(2,128)}, u32[]{:S(2)}) copy-start(f32[2,64]{1,0:T(2,128)} %copy-done.76) | copy-start | bytes 1540
  156.8 6.0 %copy-start.86 = (f32[8,2,64]{2,0,1:T(8,128)S(1)}, f32[8,2,64]{2,0,1:T(8,128)}, u32[]{:S(2)}) copy-start(f32[8,2,64]{2,0,1:T(8,128)} %reduce_sum.310) | copy-start | bytes 12292
  156.8 7.0 %copy-start.57 = (f32[4,64]{1,0:T(4,128)S(1)}, f32[4,64]{1,0:T(4,128)}, u32[]{:S(2)}) copy-start(f32[4,64]{1,0:T(4,128)} %copy-done.56) | copy-start | bytes 3076
  156.8 7.0 %copy-start.59 = (f32[4,64]{1,0:T(4,128)S(1)}, f32[4,64]{1,0:T(4,128)}, u32[]{:S(2)}) copy-start(f32[4,64]{1,0:T(4,128)} %copy-done.58) | copy-start | bytes 3076
  156.8 7.0 %copy-start.61 = (f32[4,64]{1,0:T(4,128)S(1)}, f32[4,64]{1,0:T(4,128)}, u32[]{:S(2)}) copy-start(f32[4,64]{1,0:T(4,128)} %copy-done.60) | copy-start | bytes 3076
  156.8 7.0 %copy-start.70 = (f32[8,4,64]{2,0,1:T(8,128)S(1)}, f32[8,4,64]{2,0,1:T(8,128)}, u32[]{:S(2)}) copy-start(f32[8,4,64]{2,0,1:T(8,128)} %reduce_sum.311) | copy-start | bytes 24580
  156.8 7.0 %copy-start.81 = (f32[2,2,64]{2,1,0:T(2,128)S(1)}, f32[2,2,64]{2,1,0:T(2,128)}, u32[]{:S(2)}) copy-start(f32[2,2,64]{2,1,0:T(2,128)} %copy-done.80) | copy-start | bytes 3076
  156.8 7.0 %copy-start.83 = (f32[2,2,64]{2,1,0:T(2,128)S(1)}, f32[2,2,64]{2,1,0:T(2,128)}, u32[]{:S(2)}) copy-start(f32[2,2,64]{2,1,0:T(2,128)} %copy-done.82) | copy-start | bytes 3076
  156.8 7.0 %copy-start.85 = (f32[2,2,64]{2,1,0:T(2,128)S(1)}, f32[2,2,64]{2,1,0:T(2,128)}, u32[]{:S(2)}) copy-start(f32[2,2,64]{2,1,0:T(2,128)} %copy-done.84) | copy-start | bytes 3076
  156.9 7.0 %copy-start.116 = (f32[4,64]{1,0:T(4,128)S(1)}, f32[4,64]{1,0:T(4,128)}, u32[]{:S(2)}) copy-start(f32[4,64]{1,0:T(4,128)} %copy-done.115) | copy-start | bytes 3076
  158.5 5.9 %copy-start.36 = (f32[8,64]{1,0:T(8,128)S(1)}, f32[8,64]{1,0:T(8,128)}, u32[]{:S(2)}) copy-start(f32[8,64]{1,0:T(8,128)} %copy-done.35) | copy-start | bytes 6148
  158.5 5.9 %copy-start.38 = (f32[8,64]{1,0:T(8,128)S(1)}, f32[8,64]{1,0:T(8,128)}, u32[]{:S(2)}) copy-start(f32[8,64]{1,0:T(8,128)} %copy-done.37) | copy-start | bytes 6148
  158.5 5.9 %copy-start.40 = (f32[8,64]{1,0:T(8,128)S(1)}, f32[8,64]{1,0:T(8,128)}, u32[]{:S(2)}) copy-start(f32[8,64]{1,0:T(8,128)} %copy-done.39) | copy-start | bytes 6148
  158.5 5.9 %copy-start.65 = (f32[4,2,64]{2,1,0:T(2,128)S(1)}, f32[4,2,64]{2,1,0:T(2,128)}, u32[]{:S(2)}) copy-start(f32[4,2,64]{2,1,0:T(2,128)} %copy-done.64) | copy-start | bytes 6148
  158.6 5.9 %copy-start.67 = (f32[4,2,64]{2,1,0:T(2,128)S(1)}, f32[4,2,64]{2,1,0:T(2,128)}, u32[]{:S(2)}) copy-start(f32[4,2,64]{2,1,0:T(2,128)} %copy-done.66) | copy-start | bytes 6148
  158.6 5.9 %copy-start.69 = (f32[4,2,64]{2,1,0:T(2,128)S(1)}, f32[4,2,64]{2,1,0:T(2,128)}, u32[]{:S(2)}) copy-start(f32[4,2,64]{2,1,0:T(2,128)} %copy-done.68) | copy-start | bytes 6148
  158.6 5.9 %copy-start.113 = (f32[8,64]{1,0:T(8,128)S(1)}, f32[8,64]{1,0:T(8,128)}, u32[]{:S(2)}) copy-start(f32[8,64]{1,0:T(8,128)} %copy-done.112) | copy-start | bytes 6148
  159.0 6.4 %copy-start.23 = (f32[16,64]{1,0:T(8,128)S(1)}, f32[16,64]{1,0:T(8,128)}, u32[]{:S(2)}) copy-start(f32[16,64]{1,0:T(8,128)} %copy-done.22) | copy-start | bytes 12292
  159.0 6.4 %copy-start.25 = (f32[16,64]{1,0:T(8,128)S(1)}, f32[16,64]{1,0:T(8,128)}, u32[]{:S(2)}) copy-start(f32[16,64]{1,0:T(8,128)} %copy-done.24) | copy-start | bytes 12292
  159.0 6.4 %copy-start.33 = (f32[8,16,64]{2,0,1:T(8,128)S(1)}, f32[8,16,64]{2,0,1:T(8,128)}, u32[]{:S(2)}) copy-start(f32[8,16,64]{2,0,1:T(8,128)} %reduce_sum.313) | copy-start | bytes 98308
  159.0 6.4 %copy-start.42 = (f32[8,2,64]{2,1,0:T(2,128)S(1)}, f32[8,2,64]{2,1,0:T(2,128)}, u32[]{:S(2)}) copy-start(f32[8,2,64]{2,1,0:T(2,128)} %copy-done.41) | copy-start | bytes 12292
  159.0 6.4 %copy-start.44 = (f32[8,2,64]{2,1,0:T(2,128)S(1)}, f32[8,2,64]{2,1,0:T(2,128)}, u32[]{:S(2)}) copy-start(f32[8,2,64]{2,1,0:T(2,128)} %copy-done.43) | copy-start | bytes 12292
  159.0 6.4 %copy-start.46 = (f32[8,2,64]{2,1,0:T(2,128)S(1)}, f32[8,2,64]{2,1,0:T(2,128)}, u32[]{:S(2)}) copy-start(f32[8,2,64]{2,1,0:T(2,128)} %copy-done.45) | copy-start | bytes 12292
  159.0 6.4 %copy-start.79 = (f32[16,64]{1,0:T(8,128)S(1)}, f32[16,64]{1,0:T(8,128)}, u32[]{:S(2)}) copy-start(f32[16,64]{1,0:T(8,128)} %copy-done.78) | copy-start | bytes 12292
  (83 other events, 206.8 us)
Sparse Core Ops, SparseCore 0:
  29.0 86.8 all-gather.2

commit v8 on v7

--- a/solution.py
+++ b/solution.py
@@ -83,22 +83,24 @@
     return values / jnp.sum(values, axis=-1, keepdims=True)
 
 
-def near_kernel(kernel_scale, slots, source_ref, probes_ref, coords_ref, target_ref, out_ref):
+def near_kernel(kernel_scale, slots, source_ref, probes_ref, coords_ref, target_ref, shift_ref,
+                shift_col_ref, out_ref):
     box = pl.program_id(0)
-    target_x = target_ref[0:1, :]
-    target_y = target_ref[1:2, :]
-    target_z = target_ref[2:3, :]
+    target = target_ref[...] - shift_col_ref[0]
+    target_term = kernel_scale * jnp.sum(target * target, axis=0, keepdims=True)
+    target_cross = (-2.0 * kernel_scale) * target
     out_ref[...] = jnp.zeros_like(out_ref)
     for slot in range(slots):
         source = source_ref[box * slots + slot]
 
         @pl.when(source >= 0)
         def _():
-            near = coords_ref[source]
-            distance_sq = (near[:, 0:1] - target_x) ** 2
-            distance_sq = distance_sq + (near[:, 1:2] - target_y) ** 2
-            distance_sq = distance_sq + (near[:, 2:3] - target_z) ** 2
-            kernel_block = 1.0 / (1.0 + kernel_scale * distance_sq)
+            near = coords_ref[source] - shift_ref[0]
+            near_term = 1.0 + kernel_scale * jnp.sum(near * near, axis=1, keepdims=True)
+            cross = jnp.dot(
+                near, target_cross, precision=PRECISE, preferred_element_type=jnp.float32
+            )
+            kernel_block = 1.0 / ((cross + near_term) + target_term)
             out_ref[...] += jnp.dot(
                 probes_ref[source], kernel_block, precision=lax.Precision.HIGH,
                 preferred_element_type=jnp.float32,
@@ -109,6 +111,10 @@
     tiles, rows, size = probe_tiles.shape
     boxes = points.shape[1] // size
     slots = slot_source.shape[0] // boxes
+    lanes = 8
+    coords = jnp.pad(coord_tiles, ((0, 0), (0, 0), (0, lanes - 3)))
+    targets = jnp.pad(points, ((0, lanes - 3), (0, 0)))
+    shift = jnp.pad(points.reshape(3, boxes, size)[:, :, 0].T, ((0, 0), (0, lanes - 3)))
     return pl.pallas_call(
         functools.partial(near_kernel, kernel_scale, slots),
         out_shape=jax.ShapeDtypeStruct((rows, boxes * size), jnp.float32),
@@ -117,18 +123,20 @@
             grid=(boxes,),
             in_specs=[
                 pl.BlockSpec((tiles, rows, size), lambda b, s: (0, 0, 0)),
-                pl.BlockSpec((tiles, size, 3), lambda b, s: (0, 0, 0)),
-                pl.BlockSpec((3, size), lambda b, s: (0, b)),
+                pl.BlockSpec((tiles, size, lanes), lambda b, s: (0, 0, 0)),
+                pl.BlockSpec((lanes, size), lambda b, s: (0, b)),
+                pl.BlockSpec((1, 1, lanes), lambda b, s: (b, 0, 0)),
+                pl.BlockSpec((1, lanes, 1), lambda b, s: (b, 0, 0)),
             ],
             out_specs=pl.BlockSpec((rows, size), lambda b, s: (0, b)),
         ),
         compiler_params=pltpu.CompilerParams(dimension_semantics=("arbitrary",)),
         cost_estimate=pl.CostEstimate(
-            flops=boxes * slots * size * size * (2 * rows + 12),
+            flops=boxes * slots * size * size * (2 * rows + 2 * lanes + 4),
             transcendentals=0,
-            bytes_accessed=4 * (probe_tiles.size + coord_tiles.size * 43 + 2 * rows * boxes * size),
+            bytes_accessed=4 * (probe_tiles.size + coords.size + 2 * rows * boxes * size),
         ),
-    )(slot_source, probe_tiles, coord_tiles, points)
+    )(slot_source, probe_tiles, coords, targets, shift[:, None, :], shift[:, :, None])
 
 
 def body(probes, points, near_list, leaf_proxy, inner_proxy, top_proxy, far_list):

time: 182 us -> 220 us (1.21)
  the two profiles are of different devices: /device:TPU:16 before, /device:TPU:189 now
where the time goes in v8:
time: 220 us; the launch traced here: 219 us
  Pallas kernels  123 us (56%)
  matrix products  35 us (16%)
  local copies, waits for them, and re-layouts  32 us (15%)
  between operations  16.7 us (8%)
  other arithmetic  12.2 us (6%)
    pallas_call x1, Pallas kernels, near_field_call(): pl.pallas_call(functools.partial(near_kernel, kernel_scale, slots), out_s...  114 us
    dot_general x1, matrix products, body(): jnp.einsum('qnr,nrs->qns', source_moment, kernel_block, precision=PRECISE)  10 us
    pallas_call x1, Pallas kernels, exchange_halo(): pl.pallas_call(halo_kernel, out_shape=(shape, shape), in_specs=[vmem, vme...  9.79 us
    dot_general x5, matrix products, body(): jnp.einsum('qns,nrs->qnr', jnp.repeat(descent, 2, axis=1), transfer_maps[...  7.76 us
    pad x1, local copies, waits for them, and re-layouts, near_field_call(): coords = jnp.pad(coord_tiles, ((0, 0), (0, 0), (0, lanes - 3)))  5.24 us
    dot_general x5, matrix products, body(): jnp.einsum('qnr,nrs->qns', level_moments[-1], interp_map, precision=PRECISE)  5.15 us
  transfers between devices with their start and end apart: 1, of which 0 were waited for; matrix products, arithmetic and copies ran while one was open for 18% of the time, Pallas kernels for 56%

profile of v8, /device:TPU:189, one launch (start us, length us, event | category | flops | bytes accessed | tf_op | source)
XLA Modules:
  0.0 219.5 jit_solution(7470713069203143134)
XLA Ops:
  6.5 1.2 reshape.3429
  7.9 0.9 reshape.3421
  9.0 0.9 slice_reduce_fusion.10
  10.2 1.3 slice_reduce_fusion.2
  11.6 1.1 divide_reduce_fusion
  12.7 3.3 %constant_dynamic-update-slice_fusion.6 = (f32[8,62,64]{2,0,1:T(8,128)S(1)}, f32[8,32,64]{2,0,1:T(8,128)S(1)}) fusion(f32[8,32,256]{2,0,1:T(8,128)S(1)} %bitcast.419, f32[32,256]{1,0:T(8,128)S(1)} %divide_reduce_fusion, f32[32,64]{1,0:T(8,128)S(1)} %sub.1273, f32[32,256]{1,0:T(8,128)S(1)} %sub.1271, f32[32,64]{1,0:T(8,128)S(1)} %sub.1268, ...), kind=kOutput, calls=%fused_computation.98 | convolution fusion | flops 56623104 | bytes 679936 | tf_op jit(solution)/shard_map/qbp,bpr->qbr/dot_general | solution.py:170
  16.1 1.4 divide_reduce_fusion.1
  17.4 2.6 %bitcast_reduce_fusion = f32[8,16,64]{2,0,1:T(8,128)S(1)} fusion(f32[8,32,64]{2,0,1:T(8,128)S(1)} %get-tuple-element.124, f32[32,64]{1,0:T(8,128)S(1)} %divide_reduce_fusion.1, f32[32,64]{1,0:T(8,128)S(1)} %bitcast.438, f32[32,64]{1,0:T(8,128)S(1)} %sub.1273, f32[32,64]{1,0:T(8,128)S(1)} %bitcast.435, f32[32,64]{1,0:T(8,128)S(1)} %sub.1268, ...), kind=kOutput, calls=%fused_computation.75 | convolution fusion | flops 14163968 | bytes 155648 | tf_op jit(solution)/shard_map/qnr,nrs->qns/dot_general | solution.py:177
  20.1 0.7 divide_reduce_fusion.2
  20.8 1.3 bitcast_reduce_fusion.1
  22.2 0.4 divide_reduce_fusion.3
  22.8 0.6 copy-done.106
  23.3 0.6 bitcast_reduce_fusion.2
  24.1 0.3 divide_reduce_fusion.4
  24.4 0.4 bitcast_reduce_fusion.3
  25.2 0.5 copy-done.125
  25.8 0.3 constant_dynamic-update-slice_fusion.11
  26.3 0.4 fusion.53
  26.9 0.2 constant_dynamic-update-slice_fusion.9
  27.2 0.2 constant_dynamic-update-slice_fusion.8
  27.9 0.6 copy-done.46
  29.6 0.6 slice.618
  30.2 0.6 bitcast_convert_fusion
  30.9 0.6 copy-done.7
  32.1 0.9 pad_maximum_fusion.2
  33.0 9.8 %shard_map.73 = (f32[11,4736]{1,0:T(8,128)}, f32[11,4736]{1,0:T(8,128)}) custom-call(f32[11,4736]{1,0:T(8,128)} %get-tuple-element.43.to_right, f32[11,4736]{1,0:T(8,128)} %get-tuple-element.42.to_left), custom_call_target="tpu_custom_call" | custom-call | tf_op jit(solution)/shard_map/pallas_call | solution.py:60
  42.8 1.0 slice.550
  44.9 0.6 compare_and_fusion
  45.4 1.1 pad_maximum_fusion
  46.5 0.9 gather_fusion
  47.5 0.3 select_bitcast_fusion
  48.5 10.0 %fusion.9 = f32[8,186,64]{2,0,1:T(8,128)S(1)} fusion(f32[186,64]{1,0:T(8,128)S(1)} %get-tuple-element.40, f32[186,64]{1,0:T(8,128)S(1)} %bitcast.426, f32[186,64]{1,0:T(8,128)S(1)} %get-tuple-element.41, f32[186,64]{1,0:T(8,128)S(1)} %bitcast.427, f32[186,64]{1,0:T(8,128)S(1)} %get-tuple-element.39, f32[186,64]{1,0:T(8,128)S(1)} %bitcast.428, ...), kind=kOutput, calls=%fused_computation.16 | convolution fusion | flops 81613824 | bytes 1733632 | tf_op jit(solution)/shard_map/qnr,nrs->qns/dot_general | solution.py:238
  58.6 0.9 slice.477
  59.5 0.8 slice.478
  60.3 0.7 pad.13.target_ref
  61.0 0.6 reduce_sum.310
  61.6 0.6 reduce_sum.311
  62.2 0.6 reduce_sum.312
  62.8 0.6 reduce_sum.313
  63.5 0.7 reduce_sum.314
  64.2 3.1 %copy.114 = f32[3,9728]{0,1:T(8,128)} copy(f32[3,9728]{1,0:T(4,128)S(1)} %pad_maximum_fusion.4) | data formatting | bytes 233472 | tf_op jit(solution)/shard_map/slice | solution.py:208
  67.3 5.2 %pad.12.coords_ref = f32[38,256,8]{2,1,0:T(8,128)} pad(f32[38,256,3]{2,1,0:T(8,128)} %bitcast.409, f32[]{:T(128)} %constant.604.clone.1), padding=0_0x0_0x0_5 | pad | bytes 428036 | tf_op jit(solution)/shard_map/jit(_pad)/pad | solution.py:115
  72.6 0.8 slice.587
  73.4 0.6 reshape.3419.source_ref
  74.3 0.6 pad_bitcast_fusion
  74.9 0.9 copy.118.shift_col_ref
  75.8 0.9 constant_dynamic-slice_fusion.40
  76.7 1.0 constant_dynamic-slice_fusion.46
  77.8 113.7 %shard_map.74 = f32[8,8192]{1,0:T(8,128)} custom-call(s32[192]{0:T(256)} %reshape.3419.source_ref, f32[38,8,256]{2,1,0:T(8,128)} %bitcast.418, f32[38,256,8]{2,1,0:T(8,128)} %pad.12.coords_ref, f32[8,8192]{1,0:T(8,128)} %pad.13.target_ref, f32[32,1,8]{2,1,0:T(1,128)} %bitcast.430, f32[32,8,1]{2,1,0:T(8,128)} %copy.118.shift_col_ref), custom_call_target="tpu_custom_call" | custom-call | flops 452984832 | bytes 1146880 | tf_op jit(solution)/shard_map/pallas_call | solution.py:118
  191.5 0.6 slice_bitcast_fusion.8
  192.2 0.6 slice_bitcast_fusion.7
  192.8 2.0 fusion.216
  195.7 0.9 convolution_bitcast_fusion.3
  197.2 0.9 fusion.22
  198.1 0.9 fusion.20
  199.0 0.9 fusion.18
  199.9 1.0 fusion.16
  200.9 1.0 fusion.14
  202.0 1.2 fusion.13
  203.2 0.8 fusion.12
  204.1 1.6 fusion.11
  205.9 3.2 %fusion.10 = f32[8,32,64]{2,0,1:T(8,128)S(1)} fusion(f32[8,32,64]{2,0,1:T(8,128)S(1)} %copy-done.10, f32[8,32,64]{2,0,1:T(8,128)S(1)} %bitcast.425, f32[32,64]{1,0:T(8,128)S(1)} %copy-done.56, f32[32,64]{1,0:T(8,128)S(1)} %bitcast.439, f32[32,64]{1,0:T(8,128)S(1)} %sub.1273, f32[32,64]{1,0:T(8,128)S(1)} %bitcast.436, f32[32,64]{1,0:T(8,128)S(1)} %sub.1268, ...), kind=kOutput, calls=%fused_computation.19 | convolution fusion | flops 14172160 | bytes 253952 | tf_op jit(solution)/shard_map/qns,nrs->qnr/dot_general | solution.py:300
  209.1 2.7 %fusion.26 = f32[32,256,8]{1,2,0:T(8,128)S(1)} fusion(f32[8,32,64]{2,0,1:T(8,128)S(1)} %fusion.10, f32[32,256]{1,0:T(8,128)S(1)} %copy-done.41, f32[32,64]{1,0:T(8,128)S(1)} %sub.1273, f32[32,256]{1,0:T(8,128)S(1)} %sub.1271, f32[32,64]{1,0:T(8,128)S(1)} %sub.1268, f32[32,256]{1,0:T(8,128)S(1)} %sub.1266, f32[32,64]{1,0:T(8,128)S(1)} %sub.1263, ...), kind=kOutput, calls=%fused_computation.48 | convolution fusion | flops 56623104 | bytes 483328 | tf_op jit(solution)/shard_map/qbr,bpr->qbp/dot_general | solution.py:304
  211.9 0.7 add_add_fusion
  (407 shorter events, 5.8 us)
Async XLA Ops:
  6.5 6.1 %copy-start.5 = (f32[8,8192]{1,0:T(8,128)S(1)}, f32[8,8192]{1,0:T(8,128)}, u32[]{:S(2)}) copy-start(f32[8,8192]{1,0:T(8,128)} %param.7) | copy-start | bytes 786436
  6.5 186.2 %all-gather.3.cloned.1.call-start = ((), (), s32[]{:S(2)}) async-start(), calls=%async_computation | async-start | bytes 3170304 | tf_op jit(solution)/shard_map/all_gather | solution.py:266
  7.8 17.0 %copy-start.43 = (f32[3,8,64]{2,1,0:T(8,128)}, f32[3,8,64]{2,1,0:T(8,128)S(1)}, u32[]{:S(2)}) copy-start(f32[3,8,64]{2,1,0:T(8,128)S(1)} %slice.593) | copy-start | bytes 18436
  7.8 18.3 %copy-start.47 = (f32[3,4,64]{2,1,0:T(4,128)}, f32[3,4,64]{2,1,0:T(4,128)S(1)}, u32[]{:S(2)}) copy-start(f32[3,4,64]{2,1,0:T(4,128)S(1)} %slice.594) | copy-start | bytes 9220
  7.8 18.2 %copy-start.19 = (f32[3,32,64]{2,1,0:T(8,128)}, f32[3,32,64]{2,1,0:T(8,128)S(1)}, u32[]{:S(2)}) copy-start(f32[3,32,64]{2,1,0:T(8,128)S(1)} %slice.591) | copy-start | bytes 73732
  7.8 18.3 %copy-start.27 = (f32[3,16,64]{2,1,0:T(8,128)}, f32[3,16,64]{2,1,0:T(8,128)S(1)}, u32[]{:S(2)}) copy-start(f32[3,16,64]{2,1,0:T(8,128)S(1)} %slice.592) | copy-start | bytes 36868
  7.9 17.0 %copy-start.9 = (f32[3,128,64]{2,1,0:T(8,128)}, f32[3,128,64]{2,1,0:T(8,128)S(1)}, u32[]{:S(2)}) copy-start(f32[3,128,64]{2,1,0:T(8,128)S(1)} %slice.589) | copy-start | bytes 294916
  7.9 18.1 %copy-start.11 = (f32[3,64,64]{2,1,0:T(8,128)}, f32[3,64,64]{2,1,0:T(8,128)S(1)}, u32[]{:S(2)}) copy-start(f32[3,64,64]{2,1,0:T(8,128)S(1)} %slice.590) | copy-start | bytes 147460
  8.8 21.4 %copy-start.3 = (f32[3,30,64]{2,1,0:T(8,128)}, f32[3,30,64]{2,1,0:T(8,128)S(1)}, u32[]{:S(2)}) copy-start(f32[3,30,64]{2,1,0:T(8,128)S(1)} %reshape.3421) | copy-start | bytes 69124
  8.8 12.0 %copy-start.13 = (f32[16,64]{1,0:T(8,128)}, f32[16,64]{1,0:T(8,128)S(1)}, u32[]{:S(2)}) copy-start(f32[16,64]{1,0:T(8,128)S(1)} %get-tuple-element.74) | copy-start | bytes 12292
  8.8 12.0 %copy-start.15 = (f32[16,64]{1,0:T(8,128)}, f32[16,64]{1,0:T(8,128)S(1)}, u32[]{:S(2)}) copy-start(f32[16,64]{1,0:T(8,128)S(1)} %get-tuple-element.75) | copy-start | bytes 12292
  8.8 12.0 %copy-start.17 = (f32[16,64]{1,0:T(8,128)}, f32[16,64]{1,0:T(8,128)S(1)}, u32[]{:S(2)}) copy-start(f32[16,64]{1,0:T(8,128)S(1)} %get-tuple-element.76) | copy-start | bytes 12292
  8.8 13.8 %copy-start.28 = (f32[8,64]{1,0:T(8,128)}, f32[8,64]{1,0:T(8,128)S(1)}, u32[]{:S(2)}) copy-start(f32[8,64]{1,0:T(8,128)S(1)} %get-tuple-element.71) | copy-start | bytes 6148
  8.8 13.8 %copy-start.30 = (f32[8,64]{1,0:T(8,128)}, f32[8,64]{1,0:T(8,128)S(1)}, u32[]{:S(2)}) copy-start(f32[8,64]{1,0:T(8,128)S(1)} %get-tuple-element.72) | copy-start | bytes 6148
  8.9 13.8 %copy-start.32 = (f32[8,64]{1,0:T(8,128)}, f32[8,64]{1,0:T(8,128)S(1)}, u32[]{:S(2)}) copy-start(f32[8,64]{1,0:T(8,128)S(1)} %get-tuple-element.73) | copy-start | bytes 6148
  8.9 15.5 %copy-start.49 = (f32[4,64]{1,0:T(4,128)}, f32[4,64]{1,0:T(4,128)S(1)}, u32[]{:S(2)}) copy-start(f32[4,64]{1,0:T(4,128)S(1)} %get-tuple-element.68) | copy-start | bytes 3076
  8.9 15.5 %copy-start.51 = (f32[4,64]{1,0:T(4,128)}, f32[4,64]{1,0:T(4,128)S(1)}, u32[]{:S(2)}) copy-start(f32[4,64]{1,0:T(4,128)S(1)} %get-tuple-element.69) | copy-start | bytes 3076
  8.9 15.5 %copy-start.53 = (f32[4,64]{1,0:T(4,128)}, f32[4,64]{1,0:T(4,128)S(1)}, u32[]{:S(2)}) copy-start(f32[4,64]{1,0:T(4,128)S(1)} %get-tuple-element.70) | copy-start | bytes 3076
  8.9 16.3 %copy-start.65 = (f32[2,64]{1,0:T(2,128)}, f32[2,64]{1,0:T(2,128)S(1)}, u32[]{:S(2)}) copy-start(f32[2,64]{1,0:T(2,128)S(1)} %get-tuple-element.65) | copy-start | bytes 1540
  8.9 16.3 %copy-start.67 = (f32[2,64]{1,0:T(2,128)}, f32[2,64]{1,0:T(2,128)S(1)}, u32[]{:S(2)}) copy-start(f32[2,64]{1,0:T(2,128)S(1)} %get-tuple-element.66) | copy-start | bytes 1540
  8.9 16.3 %copy-start.69 = (f32[2,64]{1,0:T(2,128)}, f32[2,64]{1,0:T(2,128)S(1)}, u32[]{:S(2)}) copy-start(f32[2,64]{1,0:T(2,128)S(1)} %get-tuple-element.67) | copy-start | bytes 1540
  22.1 5.5 %copy-start.57 = (f32[4,2,64]{2,1,0:T(2,128)}, f32[4,2,64]{2,1,0:T(2,128)S(1)}, u32[]{:S(2)}) copy-start(f32[4,2,64]{2,1,0:T(2,128)S(1)} %broadcast_in_dim.132) | copy-start | bytes 6148
  22.2 5.5 %copy-start.59 = (f32[4,2,64]{2,1,0:T(2,128)}, f32[4,2,64]{2,1,0:T(2,128)S(1)}, u32[]{:S(2)}) copy-start(f32[4,2,64]{2,1,0:T(2,128)S(1)} %broadcast_in_dim.134) | copy-start | bytes 6148
  24.0 5.4 %copy-start.64 = (s32[32,3]{0,1:T(4,128)S(1)}, s32[32,3]{0,1:T(4,128)}, u32[]{:S(2)}) copy-start(s32[32,3]{0,1:T(4,128)} %param.13) | copy-start | bytes 1156
  24.8 6.7 %copy-start.92 = (f32[64]{0:T(128)}, f32[64]{0:T(128)S(1)}, u32[]{:S(2)}) copy-start(f32[64]{0:T(128)S(1)} %get-tuple-element.96) | copy-start | bytes 772
  24.9 6.7 %copy-start.94 = (f32[64]{0:T(128)}, f32[64]{0:T(128)S(1)}, u32[]{:S(2)}) copy-start(f32[64]{0:T(128)S(1)} %get-tuple-element.97) | copy-start | bytes 772
  24.9 6.7 %copy-start.96 = (f32[64]{0:T(128)}, f32[64]{0:T(128)S(1)}, u32[]{:S(2)}) copy-start(f32[64]{0:T(128)S(1)} %get-tuple-element.98) | copy-start | bytes 772
  26.1 5.5 %copy-start.86 = (f32[64]{0:T(128)}, f32[64]{0:T(128)S(1)}, u32[]{:S(2)}) copy-start(f32[64]{0:T(128)S(1)} %get-tuple-element.55) | copy-start | bytes 772
  26.1 5.5 %copy-start.88 = (f32[64]{0:T(128)}, f32[64]{0:T(128)S(1)}, u32[]{:S(2)}) copy-start(f32[64]{0:T(128)S(1)} %get-tuple-element.56) | copy-start | bytes 772
  26.2 5.5 %copy-start.90 = (f32[64]{0:T(128)}, f32[64]{0:T(128)S(1)}, u32[]{:S(2)}) copy-start(f32[64]{0:T(128)S(1)} %get-tuple-element.57) | copy-start | bytes 772
  26.2 5.5 %copy-start.98 = (f32[64]{0:T(128)}, f32[64]{0:T(128)S(1)}, u32[]{:S(2)}) copy-start(f32[64]{0:T(128)S(1)} %get-tuple-element.144) | copy-start | bytes 772
  26.2 5.5 %copy-start.100 = (f32[64]{0:T(128)}, f32[64]{0:T(128)S(1)}, u32[]{:S(2)}) copy-start(f32[64]{0:T(128)S(1)} %get-tuple-element.145) | copy-start | bytes 772
  26.2 5.5 %copy-start.102 = (f32[64]{0:T(128)}, f32[64]{0:T(128)S(1)}, u32[]{:S(2)}) copy-start(f32[64]{0:T(128)S(1)} %get-tuple-element.146) | copy-start | bytes 772
  26.7 5.1 %copy-start.128 = (f32[64]{0:T(128)}, f32[64]{0:T(128)S(1)}, u32[]{:S(2)}) copy-start(f32[64]{0:T(128)S(1)} %get-tuple-element.22) | copy-start | bytes 772
  32.0 12.2 %copy-start = (f32[11,8192]{1,0:T(8,128)}, f32[11,8192]{1,0:T(8,128)S(1)}, u32[]{:S(2)}) copy-start(f32[11,8192]{1,0:T(8,128)S(1)} %constant_dynamic-update-slice_fusion) | copy-start | bytes 1081348
  58.5 5.6 %copy-start.1 = (f32[11,8192]{1,0:T(8,128)S(1)}, f32[11,8192]{1,0:T(8,128)}, u32[]{:S(2)}) copy-start(f32[11,8192]{1,0:T(8,128)} %copy-done) | copy-start | bytes 1081348
  67.3 6.1 %copy-start.108 = (s32[32,6]{0,1:T(8,128)S(1)}, s32[32,6]{0,1:T(8,128)}, u32[]{:S(2)}) copy-start(s32[32,6]{0,1:T(8,128)} %param.9) | copy-start | bytes 2308
  195.6 5.2 %copy-start.66 = (f32[2,64]{1,0:T(2,128)S(1)}, f32[2,64]{1,0:T(2,128)}, u32[]{:S(2)}) copy-start(f32[2,64]{1,0:T(2,128)} %copy-done.65) | copy-start | bytes 1540
  195.6 5.2 %copy-start.68 = (f32[2,64]{1,0:T(2,128)S(1)}, f32[2,64]{1,0:T(2,128)}, u32[]{:S(2)}) copy-start(f32[2,64]{1,0:T(2,128)} %copy-done.67) | copy-start | bytes 1540
  195.6 5.3 %copy-start.70 = (f32[2,64]{1,0:T(2,128)S(1)}, f32[2,64]{1,0:T(2,128)}, u32[]{:S(2)}) copy-start(f32[2,64]{1,0:T(2,128)} %copy-done.69) | copy-start | bytes 1540
  195.6 5.3 %copy-start.79 = (f32[8,2,64]{2,0,1:T(8,128)S(1)}, f32[8,2,64]{2,0,1:T(8,128)}, u32[]{:S(2)}) copy-start(f32[8,2,64]{2,0,1:T(8,128)} %reduce_sum.310) | copy-start | bytes 12292
  195.7 6.2 %copy-start.50 = (f32[4,64]{1,0:T(4,128)S(1)}, f32[4,64]{1,0:T(4,128)}, u32[]{:S(2)}) copy-start(f32[4,64]{1,0:T(4,128)} %copy-done.49) | copy-start | bytes 3076
  195.7 6.2 %copy-start.52 = (f32[4,64]{1,0:T(4,128)S(1)}, f32[4,64]{1,0:T(4,128)}, u32[]{:S(2)}) copy-start(f32[4,64]{1,0:T(4,128)} %copy-done.51) | copy-start | bytes 3076
  195.7 6.2 %copy-start.54 = (f32[4,64]{1,0:T(4,128)S(1)}, f32[4,64]{1,0:T(4,128)}, u32[]{:S(2)}) copy-start(f32[4,64]{1,0:T(4,128)} %copy-done.53) | copy-start | bytes 3076
  195.7 6.2 %copy-start.63 = (f32[8,4,64]{2,0,1:T(8,128)S(1)}, f32[8,4,64]{2,0,1:T(8,128)}, u32[]{:S(2)}) copy-start(f32[8,4,64]{2,0,1:T(8,128)} %reduce_sum.311) | copy-start | bytes 24580
  195.7 6.2 %copy-start.74 = (f32[2,2,64]{2,1,0:T(2,128)S(1)}, f32[2,2,64]{2,1,0:T(2,128)}, u32[]{:S(2)}) copy-start(f32[2,2,64]{2,1,0:T(2,128)} %copy-done.73) | copy-start | bytes 3076
  195.7 6.2 %copy-start.76 = (f32[2,2,64]{2,1,0:T(2,128)S(1)}, f32[2,2,64]{2,1,0:T(2,128)}, u32[]{:S(2)}) copy-start(f32[2,2,64]{2,1,0:T(2,128)} %copy-done.75) | copy-start | bytes 3076
  195.7 6.2 %copy-start.78 = (f32[2,2,64]{2,1,0:T(2,128)S(1)}, f32[2,2,64]{2,1,0:T(2,128)}, u32[]{:S(2)}) copy-start(f32[2,2,64]{2,1,0:T(2,128)} %copy-done.77) | copy-start | bytes 3076
  196.7 6.5 %copy-start.29 = (f32[8,64]{1,0:T(8,128)S(1)}, f32[8,64]{1,0:T(8,128)}, u32[]{:S(2)}) copy-start(f32[8,64]{1,0:T(8,128)} %copy-done.28) | copy-start | bytes 6148
  196.7 6.5 %copy-start.31 = (f32[8,64]{1,0:T(8,128)S(1)}, f32[8,64]{1,0:T(8,128)}, u32[]{:S(2)}) copy-start(f32[8,64]{1,0:T(8,128)} %copy-done.30) | copy-start | bytes 6148
  196.7 6.5 %copy-start.33 = (f32[8,64]{1,0:T(8,128)S(1)}, f32[8,64]{1,0:T(8,128)}, u32[]{:S(2)}) copy-start(f32[8,64]{1,0:T(8,128)} %copy-done.32) | copy-start | bytes 6148
  196.7 6.5 %copy-start.42 = (f32[8,8,64]{2,0,1:T(8,128)S(1)}, f32[8,8,64]{2,0,1:T(8,128)}, u32[]{:S(2)}) copy-start(f32[8,8,64]{2,0,1:T(8,128)} %reduce_sum.312) | copy-start | bytes 49156
  196.7 6.5 %copy-start.58 = (f32[4,2,64]{2,1,0:T(2,128)S(1)}, f32[4,2,64]{2,1,0:T(2,128)}, u32[]{:S(2)}) copy-start(f32[4,2,64]{2,1,0:T(2,128)} %copy-done.57) | copy-start | bytes 6148
  196.7 6.5 %copy-start.60 = (f32[4,2,64]{2,1,0:T(2,128)S(1)}, f32[4,2,64]{2,1,0:T(2,128)}, u32[]{:S(2)}) copy-start(f32[4,2,64]{2,1,0:T(2,128)} %copy-done.59) | copy-start | bytes 6148
  196.7 6.5 %copy-start.62 = (f32[4,2,64]{2,1,0:T(2,128)S(1)}, f32[4,2,64]{2,1,0:T(2,128)}, u32[]{:S(2)}) copy-start(f32[4,2,64]{2,1,0:T(2,128)} %copy-done.61) | copy-start | bytes 6148
  196.7 6.5 %copy-start.107 = (f32[8,64]{1,0:T(8,128)S(1)}, f32[8,64]{1,0:T(8,128)}, u32[]{:S(2)}) copy-start(f32[8,64]{1,0:T(8,128)} %copy-done.106) | copy-start | bytes 6148
  197.1 7.0 %copy-start.14 = (f32[16,64]{1,0:T(8,128)S(1)}, f32[16,64]{1,0:T(8,128)}, u32[]{:S(2)}) copy-start(f32[16,64]{1,0:T(8,128)} %copy-done.13) | copy-start | bytes 12292
  197.1 7.0 %copy-start.16 = (f32[16,64]{1,0:T(8,128)S(1)}, f32[16,64]{1,0:T(8,128)}, u32[]{:S(2)}) copy-start(f32[16,64]{1,0:T(8,128)} %copy-done.15) | copy-start | bytes 12292
  197.1 7.0 %copy-start.18 = (f32[16,64]{1,0:T(8,128)S(1)}, f32[16,64]{1,0:T(8,128)}, u32[]{:S(2)}) copy-start(f32[16,64]{1,0:T(8,128)} %copy-done.17) | copy-start | bytes 12292
  197.1 7.0 %copy-start.26 = (f32[8,16,64]{2,0,1:T(8,128)S(1)}, f32[8,16,64]{2,0,1:T(8,128)}, u32[]{:S(2)}) copy-start(f32[8,16,64]{2,0,1:T(8,128)} %reduce_sum.313) | copy-start | bytes 98308
  197.1 7.0 %copy-start.35 = (f32[8,2,64]{2,1,0:T(2,128)S(1)}, f32[8,2,64]{2,1,0:T(2,128)}, u32[]{:S(2)}) copy-start(f32[8,2,64]{2,1,0:T(2,128)} %copy-done.34) | copy-start | bytes 12292
  197.1 7.0 %copy-start.37 = (f32[8,2,64]{2,1,0:T(2,128)S(1)}, f32[8,2,64]{2,1,0:T(2,128)}, u32[]{:S(2)}) copy-start(f32[8,2,64]{2,1,0:T(2,128)} %copy-done.36) | copy-start | bytes 12292
  197.1 7.0 %copy-start.39 = (f32[8,2,64]{2,1,0:T(2,128)S(1)}, f32[8,2,64]{2,1,0:T(2,128)}, u32[]{:S(2)}) copy-start(f32[8,2,64]{2,1,0:T(2,128)} %copy-done.38) | copy-start | bytes 12292
  197.1 7.0 %copy-start.72 = (f32[16,64]{1,0:T(8,128)S(1)}, f32[16,64]{1,0:T(8,128)}, u32[]{:S(2)}) copy-start(f32[16,64]{1,0:T(8,128)} %copy-done.71) | copy-start | bytes 12292
  (75 other events, 164.1 us)
Sparse Core Ops, SparseCore 0:
  28.7 84.4 all-gather.2

commit v9 on v7

--- a/solution.py
+++ b/solution.py
@@ -85,9 +85,10 @@
 
 def near_kernel(kernel_scale, slots, source_ref, probes_ref, coords_ref, target_ref, out_ref):
     box = pl.program_id(0)
-    target_x = target_ref[0:1, :]
-    target_y = target_ref[1:2, :]
-    target_z = target_ref[2:3, :]
+    size = target_ref.shape[0]
+    target_x = jnp.broadcast_to(target_ref[:, 0:1], (size, size))
+    target_y = jnp.broadcast_to(target_ref[:, 1:2], (size, size))
+    target_z = jnp.broadcast_to(target_ref[:, 2:3], (size, size))
     out_ref[...] = jnp.zeros_like(out_ref)
     for slot in range(slots):
         source = source_ref[box * slots + slot]
@@ -95,13 +96,13 @@
         @pl.when(source >= 0)
         def _():
             near = coords_ref[source]
-            distance_sq = (near[:, 0:1] - target_x) ** 2
-            distance_sq = distance_sq + (near[:, 1:2] - target_y) ** 2
-            distance_sq = distance_sq + (near[:, 2:3] - target_z) ** 2
+            distance_sq = (near[0:1, :] - target_x) ** 2
+            distance_sq = distance_sq + (near[1:2, :] - target_y) ** 2
+            distance_sq = distance_sq + (near[2:3, :] - target_z) ** 2
             kernel_block = 1.0 / (1.0 + kernel_scale * distance_sq)
-            out_ref[...] += jnp.dot(
-                probes_ref[source], kernel_block, precision=lax.Precision.HIGH,
-                preferred_element_type=jnp.float32,
+            out_ref[...] += lax.dot_general(
+                probes_ref[source], kernel_block, (((1,), (1,)), ((), ())),
+                precision=lax.Precision.HIGH, preferred_element_type=jnp.float32,
             )
 
 
@@ -117,8 +118,8 @@
             grid=(boxes,),
             in_specs=[
                 pl.BlockSpec((tiles, rows, size), lambda b, s: (0, 0, 0)),
-                pl.BlockSpec((tiles, size, 3), lambda b, s: (0, 0, 0)),
-                pl.BlockSpec((3, size), lambda b, s: (0, b)),
+                pl.BlockSpec((tiles, 3, size), lambda b, s: (0, 0, 0)),
+                pl.BlockSpec((size, 3), lambda b, s: (b, 0)),
             ],
             out_specs=pl.BlockSpec((rows, size), lambda b, s: (0, b)),
         ),
@@ -126,9 +127,9 @@
         cost_estimate=pl.CostEstimate(
             flops=boxes * slots * size * size * (2 * rows + 12),
             transcendentals=0,
-            bytes_accessed=4 * (probe_tiles.size + coord_tiles.size * 43 + 2 * rows * boxes * size),
+            bytes_accessed=4 * (probe_tiles.size + coord_tiles.size + 2 * rows * boxes * size),
         ),
-    )(slot_source, probe_tiles, coord_tiles, points)
+    )(slot_source, probe_tiles, coord_tiles, points.T)
 
 
 def body(probes, points, near_list, leaf_proxy, inner_proxy, top_proxy, far_list):
@@ -197,7 +198,7 @@
     near_field = near_field_call(
         slot_source.reshape(-1).astype(jnp.int32),
         jnp.moveaxis(extended[:rows_here], 1, 0),
-        jnp.moveaxis(extended[rows_here:], 0, 2),
+        jnp.moveaxis(extended[rows_here:], 0, 1),
         points,
         kernel_scale,
     )

time: 182 us -> 171 us (0.940)
  the two profiles are of different devices: /device:TPU:16 before, /device:TPU:46 now
where the time goes in v9:
time: 171 us; the launch traced here: 170 us
  Pallas kernels  78.3 us (46%)
  matrix products  35.1 us (21%)
  local copies, waits for them, and re-layouts  26.6 us (16%)
  between operations  16.8 us (10%)
  other arithmetic  13 us (8%)
    pallas_call x1, Pallas kernels, near_field_call(): pl.pallas_call(functools.partial(near_kernel, kernel_scale, slots), out_s...  61.3 us
    pallas_call x1, Pallas kernels, exchange_halo(): pl.pallas_call(halo_kernel, out_shape=(shape, shape), in_specs=[vmem, vme...  17.1 us
    dot_general x1, matrix products, body(): jnp.einsum('qnr,nrs->qns', source_moment, kernel_block, precision=PRECISE)  10 us
    unnamed x304, local copies, waits for them, and re-layouts  8.33 us
    dot_general x5, matrix products, body(): jnp.einsum('qns,nrs->qnr', jnp.repeat(descent, 2, axis=1), transfer_maps[...  7.16 us
    dot_general x5, matrix products, body(): jnp.einsum('qnr,nrs->qns', level_moments[-1], interp_map, precision=PRECISE)  5.15 us
    reduce_sum x7, other arithmetic, interpolation(): return values / jnp.sum(values, axis=-1, keepdims=True)  4.31 us
    dot_general x5, matrix products, body(): jnp.einsum('qns,nrs->qnr', descent, own_edges[height], precision=PRECISE)  3.84 us
  transfers between devices with their start and end apart: 1, of which 0 were waited for; matrix products, arithmetic and copies ran while one was open for 18% of the time, Pallas kernels for 46%

profile of v9, /device:TPU:46, one launch (start us, length us, event | category | flops | bytes accessed | tf_op | source)
XLA Modules:
  0.0 169.8 jit_solution(14013262866880317456)
XLA Ops:
  6.5 1.2 reshape.3425
  7.9 0.9 reshape.3418
  9.0 0.9 slice_reduce_fusion.10
  10.1 1.3 slice_reduce_fusion.2
  11.6 1.1 divide_reduce_fusion
  12.7 3.3 %constant_dynamic-update-slice_fusion.6 = (f32[8,62,64]{2,0,1:T(8,128)S(1)}, f32[8,32,64]{2,0,1:T(8,128)S(1)}) fusion(f32[8,32,256]{2,0,1:T(8,128)S(1)} %bitcast.410, f32[32,256]{1,0:T(8,128)S(1)} %divide_reduce_fusion, f32[32,64]{1,0:T(8,128)S(1)} %sub.1273, f32[32,256]{1,0:T(8,128)S(1)} %sub.1271, f32[32,64]{1,0:T(8,128)S(1)} %sub.1268, ...), kind=kOutput, calls=%fused_computation.97 | convolution fusion | flops 56623104 | bytes 679936 | tf_op jit(solution)/shard_map/qbp,bpr->qbr/dot_general | solution.py:163
  16.1 1.4 divide_reduce_fusion.1
  17.5 2.6 %bitcast_reduce_fusion = f32[8,16,64]{2,0,1:T(8,128)S(1)} fusion(f32[8,32,64]{2,0,1:T(8,128)S(1)} %get-tuple-element.122, f32[32,64]{1,0:T(8,128)S(1)} %divide_reduce_fusion.1, f32[32,64]{1,0:T(8,128)S(1)} %bitcast.428, f32[32,64]{1,0:T(8,128)S(1)} %sub.1273, f32[32,64]{1,0:T(8,128)S(1)} %bitcast.425, f32[32,64]{1,0:T(8,128)S(1)} %sub.1268, ...), kind=kOutput, calls=%fused_computation.75 | convolution fusion | flops 14163968 | bytes 155648 | tf_op jit(solution)/shard_map/qnr,nrs->qns/dot_general | solution.py:170
  20.2 0.7 divide_reduce_fusion.2
  20.9 1.3 bitcast_reduce_fusion.1
  22.3 0.4 divide_reduce_fusion.3
  22.8 0.6 copy-done.113
  23.4 0.6 bitcast_reduce_fusion.2
  24.2 0.3 divide_reduce_fusion.4
  24.5 0.4 bitcast_reduce_fusion.3
  25.6 0.5 copy-done.134
  26.1 0.3 constant_dynamic-update-slice_fusion.11
  26.6 0.4 fusion.53
  27.3 0.2 constant_dynamic-update-slice_fusion.9
  28.2 0.6 copy-done.54
  30.0 0.6 slice.613
  30.6 0.6 slice.615
  31.2 0.6 bitcast_convert_fusion
  31.9 0.6 copy-done.5
  33.0 1.0 pad_maximum_fusion.2
  34.0 17.1 %shard_map.73 = (f32[11,4736]{1,0:T(8,128)}, f32[11,4736]{1,0:T(8,128)}) custom-call(f32[11,4736]{1,0:T(8,128)} %get-tuple-element.43.to_right, f32[11,4736]{1,0:T(8,128)} %get-tuple-element.42.to_left), custom_call_target="tpu_custom_call" | custom-call | tf_op jit(solution)/shard_map/pallas_call | solution.py:60
  51.0 1.0 slice.546
  53.1 0.5 compare_and_fusion
  53.6 1.1 pad_maximum_fusion
  54.7 0.9 gather_fusion
  55.7 0.3 select_bitcast_fusion
  56.7 10.0 %fusion.9 = f32[8,186,64]{2,0,1:T(8,128)S(1)} fusion(f32[186,64]{1,0:T(8,128)S(1)} %get-tuple-element.40, f32[186,64]{1,0:T(8,128)S(1)} %bitcast.417, f32[186,64]{1,0:T(8,128)S(1)} %get-tuple-element.41, f32[186,64]{1,0:T(8,128)S(1)} %bitcast.418, f32[186,64]{1,0:T(8,128)S(1)} %get-tuple-element.39, f32[186,64]{1,0:T(8,128)S(1)} %bitcast.419, ...), kind=kOutput, calls=%fused_computation.16 | convolution fusion | flops 81613824 | bytes 1733632 | tf_op jit(solution)/shard_map/qnr,nrs->qns/dot_general | solution.py:231
  66.8 0.8 slice.474
  67.6 0.8 slice.475
  68.4 2.7 %copy.95 = f32[3,8192]{0,1:T(8,128)} copy(f32[3,8192]{1,0:T(4,128)S(1)} %copy-done.7) | data formatting | bytes 196608 | tf_op args[1]
  71.1 0.6 reduce_sum.310
  71.7 0.6 reduce_sum.311
  72.4 0.7 reduce_sum.313
  73.0 0.7 reduce_sum.314
  73.8 0.7 slice.583
  74.6 0.6 reshape.3416.source_ref
  75.3 1.0 constant_dynamic-slice_fusion.40
  76.2 0.9 constant_dynamic-slice_fusion.46
  77.3 0.7 pad_maximum_fusion.4
  78.0 61.3 %shard_map.74 = f32[8,8192]{1,0:T(8,128)} custom-call(s32[192]{0:T(256)} %reshape.3416.source_ref, f32[38,8,256]{2,1,0:T(8,128)} %bitcast.409, f32[38,3,256]{2,1,0:T(4,128)} %bitcast.412, f32[8192,3]{1,0:T(8,128)} %bitcast.401), custom_call_target="tpu_custom_call" | custom-call | flops 352321536 | bytes 952320 | tf_op jit(solution)/shard_map/pallas_call | solution.py:113
  139.2 0.6 slice_bitcast_fusion.8
  139.8 0.6 slice_bitcast_fusion.7
  140.4 2.0 %fusion.216 = (f32[128,8,1,64]{3,1,0,2:T(8,128)S(1)}, f32[128,8,1,64]{3,1,0,2:T(8,128)S(1)}, f32[128,8,1,64]{3,1,0,2:T(8,128)S(1)}, f32[128,8,1,64]{3,1,0,2:T(8,...) fusion(f32[128,8,6,64]{3,1,0,2:T(8,128)} %bitcast.402), kind=kLoop, calls=%fused_computation.539 | loop fusion | bytes 3145728 | tf_op jit(solution)/shard_map/slice | solution.py:264
  142.5 0.7 reduce_sum.300
  143.2 0.7 constant_dynamic-update-slice_fusion.24
  143.9 0.7 constant_dynamic-update-slice_fusion.23
  144.6 0.7 constant_dynamic-update-slice_fusion.22
  145.9 1.6 convolution_bitcast_fusion.3
  148.1 0.9 fusion.22
  149.0 0.8 fusion.20
  149.9 0.9 fusion.18
  150.8 1.0 fusion.16
  151.8 1.0 fusion.14
  153.0 0.5 fusion.13
  153.5 0.8 fusion.12
  154.5 1.6 fusion.11
  156.2 3.2 %fusion.10 = f32[8,32,64]{2,0,1:T(8,128)S(1)} fusion(f32[8,32,64]{2,0,1:T(8,128)S(1)} %copy-done.14, f32[8,32,64]{2,0,1:T(8,128)S(1)} %bitcast.416, f32[32,64]{1,0:T(8,128)S(1)} %copy-done.64, f32[32,64]{1,0:T(8,128)S(1)} %bitcast.429, f32[32,64]{1,0:T(8,128)S(1)} %copy-done.13, f32[32,64]{1,0:T(8,128)S(1)} %bitcast.426, f32[32,64]{1,0:T(8,128)S(1)} %copy-done.11, ...), kind=kOutput, calls=%fused_computation.19 | convolution fusion | flops 14172160 | bytes 253952 | tf_op jit(solution)/shard_map/qns,nrs->qnr/dot_general | solution.py:293
  159.5 2.7 %fusion.26 = f32[32,256,8]{1,2,0:T(8,128)S(1)} fusion(f32[8,32,64]{2,0,1:T(8,128)S(1)} %fusion.10, f32[32,256]{1,0:T(8,128)S(1)} %copy-done.49, f32[32,64]{1,0:T(8,128)S(1)} %copy-done.13, f32[32,256]{1,0:T(8,128)S(1)} %copy-done.20, f32[32,64]{1,0:T(8,128)S(1)} %copy-done.11, f32[32,256]{1,0:T(8,128)S(1)} %copy-done.18, f32[32,64]{1,0:T(8,128)S(1)} %sub.1263, ...), kind=kOutput, calls=%fused_computation.48 | convolution fusion | flops 56623104 | bytes 483328 | tf_op jit(solution)/shard_map/qbr,bpr->qbp/dot_general | solution.py:297
  162.2 0.7 add_add_fusion
  (417 shorter events, 6.0 us)
Async XLA Ops:
  6.5 6.1 %copy-start.3 = (f32[8,8192]{1,0:T(8,128)S(1)}, f32[8,8192]{1,0:T(8,128)}, u32[]{:S(2)}) copy-start(f32[8,8192]{1,0:T(8,128)} %param.7) | copy-start | bytes 786436
  6.5 133.9 %all-gather.3.cloned.1.call-start = ((), (), s32[]{:S(2)}) async-start(), calls=%async_computation | async-start | bytes 3170304 | tf_op jit(solution)/shard_map/all_gather | solution.py:259
  7.8 17.1 %copy-start.50 = (f32[3,8,64]{2,1,0:T(8,128)}, f32[3,8,64]{2,1,0:T(8,128)S(1)}, u32[]{:S(2)}) copy-start(f32[3,8,64]{2,1,0:T(8,128)S(1)} %slice.588) | copy-start | bytes 18436
  7.8 18.6 %copy-start.55 = (f32[3,4,64]{2,1,0:T(4,128)}, f32[3,4,64]{2,1,0:T(4,128)S(1)}, u32[]{:S(2)}) copy-start(f32[3,4,64]{2,1,0:T(4,128)S(1)} %slice.589) | copy-start | bytes 9220
  7.8 18.6 %copy-start.27 = (f32[3,32,64]{2,1,0:T(8,128)}, f32[3,32,64]{2,1,0:T(8,128)S(1)}, u32[]{:S(2)}) copy-start(f32[3,32,64]{2,1,0:T(8,128)S(1)} %slice.586) | copy-start | bytes 73732
  7.8 18.6 %copy-start.35 = (f32[3,16,64]{2,1,0:T(8,128)}, f32[3,16,64]{2,1,0:T(8,128)S(1)}, u32[]{:S(2)}) copy-start(f32[3,16,64]{2,1,0:T(8,128)S(1)} %slice.587) | copy-start | bytes 36868
  7.9 17.0 %copy-start.9 = (f32[3,128,64]{2,1,0:T(8,128)}, f32[3,128,64]{2,1,0:T(8,128)S(1)}, u32[]{:S(2)}) copy-start(f32[3,128,64]{2,1,0:T(8,128)S(1)} %slice.584) | copy-start | bytes 294916
  7.9 18.5 %copy-start.21 = (f32[3,64,64]{2,1,0:T(8,128)}, f32[3,64,64]{2,1,0:T(8,128)S(1)}, u32[]{:S(2)}) copy-start(f32[3,64,64]{2,1,0:T(8,128)S(1)} %slice.585) | copy-start | bytes 147460
  8.8 21.8 %copy-start.2 = (f32[3,30,64]{2,1,0:T(8,128)}, f32[3,30,64]{2,1,0:T(8,128)S(1)}, u32[]{:S(2)}) copy-start(f32[3,30,64]{2,1,0:T(8,128)S(1)} %reshape.3418) | copy-start | bytes 69124
  8.8 12.1 %copy-start.23 = (f32[16,64]{1,0:T(8,128)}, f32[16,64]{1,0:T(8,128)S(1)}, u32[]{:S(2)}) copy-start(f32[16,64]{1,0:T(8,128)S(1)} %get-tuple-element.75) | copy-start | bytes 12292
  8.8 12.1 %copy-start.25 = (f32[16,64]{1,0:T(8,128)}, f32[16,64]{1,0:T(8,128)S(1)}, u32[]{:S(2)}) copy-start(f32[16,64]{1,0:T(8,128)S(1)} %get-tuple-element.76) | copy-start | bytes 12292
  8.8 13.8 %copy-start.36 = (f32[8,64]{1,0:T(8,128)}, f32[8,64]{1,0:T(8,128)S(1)}, u32[]{:S(2)}) copy-start(f32[8,64]{1,0:T(8,128)S(1)} %get-tuple-element.71) | copy-start | bytes 6148
  8.8 13.8 %copy-start.38 = (f32[8,64]{1,0:T(8,128)}, f32[8,64]{1,0:T(8,128)S(1)}, u32[]{:S(2)}) copy-start(f32[8,64]{1,0:T(8,128)S(1)} %get-tuple-element.72) | copy-start | bytes 6148
  8.8 13.8 %copy-start.40 = (f32[8,64]{1,0:T(8,128)}, f32[8,64]{1,0:T(8,128)S(1)}, u32[]{:S(2)}) copy-start(f32[8,64]{1,0:T(8,128)S(1)} %get-tuple-element.73) | copy-start | bytes 6148
  8.9 15.6 %copy-start.57 = (f32[4,64]{1,0:T(4,128)}, f32[4,64]{1,0:T(4,128)S(1)}, u32[]{:S(2)}) copy-start(f32[4,64]{1,0:T(4,128)S(1)} %get-tuple-element.68) | copy-start | bytes 3076
  8.9 15.6 %copy-start.59 = (f32[4,64]{1,0:T(4,128)}, f32[4,64]{1,0:T(4,128)S(1)}, u32[]{:S(2)}) copy-start(f32[4,64]{1,0:T(4,128)S(1)} %get-tuple-element.69) | copy-start | bytes 3076
  8.9 15.6 %copy-start.61 = (f32[4,64]{1,0:T(4,128)}, f32[4,64]{1,0:T(4,128)S(1)}, u32[]{:S(2)}) copy-start(f32[4,64]{1,0:T(4,128)S(1)} %get-tuple-element.70) | copy-start | bytes 3076
  8.9 16.3 %copy-start.73 = (f32[2,64]{1,0:T(2,128)}, f32[2,64]{1,0:T(2,128)S(1)}, u32[]{:S(2)}) copy-start(f32[2,64]{1,0:T(2,128)S(1)} %get-tuple-element.65) | copy-start | bytes 1540
  8.9 16.3 %copy-start.75 = (f32[2,64]{1,0:T(2,128)}, f32[2,64]{1,0:T(2,128)S(1)}, u32[]{:S(2)}) copy-start(f32[2,64]{1,0:T(2,128)S(1)} %get-tuple-element.66) | copy-start | bytes 1540
  8.9 16.3 %copy-start.77 = (f32[2,64]{1,0:T(2,128)}, f32[2,64]{1,0:T(2,128)S(1)}, u32[]{:S(2)}) copy-start(f32[2,64]{1,0:T(2,128)S(1)} %get-tuple-element.67) | copy-start | bytes 1540
  10.1 7.4 %copy-start.10 = (f32[32,64]{1,0:T(8,128)}, f32[32,64]{1,0:T(8,128)S(1)}, u32[]{:S(2)}) copy-start(f32[32,64]{1,0:T(8,128)S(1)} %sub.1268) | copy-start | bytes 24580
  10.1 7.4 %copy-start.12 = (f32[32,64]{1,0:T(8,128)}, f32[32,64]{1,0:T(8,128)S(1)}, u32[]{:S(2)}) copy-start(f32[32,64]{1,0:T(8,128)S(1)} %sub.1273) | copy-start | bytes 24580
  24.1 5.4 %copy-start.22 = (f32[3,2048]{1,0:T(4,128)S(1)}, f32[3,2048]{1,0:T(4,128)}, u32[]{:S(2)}) copy-start(f32[3,2048]{1,0:T(4,128)} %param.10) | copy-start | bytes 73732
  24.1 5.7 %copy-start.72 = (s32[32,3]{0,1:T(4,128)S(1)}, s32[32,3]{0,1:T(4,128)}, u32[]{:S(2)}) copy-start(s32[32,3]{0,1:T(4,128)} %param.13) | copy-start | bytes 1156
  24.1 5.8 %copy-start.81 = (f32[2,2,64]{2,1,0:T(2,128)}, f32[2,2,64]{2,1,0:T(2,128)S(1)}, u32[]{:S(2)}) copy-start(f32[2,2,64]{2,1,0:T(2,128)S(1)} %broadcast_in_dim.132) | copy-start | bytes 3076
  24.1 5.8 %copy-start.83 = (f32[2,2,64]{2,1,0:T(2,128)}, f32[2,2,64]{2,1,0:T(2,128)S(1)}, u32[]{:S(2)}) copy-start(f32[2,2,64]{2,1,0:T(2,128)S(1)} %broadcast_in_dim.134) | copy-start | bytes 3076
  24.2 5.8 %copy-start.85 = (f32[2,2,64]{2,1,0:T(2,128)}, f32[2,2,64]{2,1,0:T(2,128)S(1)}, u32[]{:S(2)}) copy-start(f32[2,2,64]{2,1,0:T(2,128)S(1)} %broadcast_in_dim.136) | copy-start | bytes 3076
  26.5 6.1 %copy-start.89 = (f32[64]{0:T(128)}, f32[64]{0:T(128)S(1)}, u32[]{:S(2)}) copy-start(f32[64]{0:T(128)S(1)} %get-tuple-element.55) | copy-start | bytes 772
  26.5 6.1 %copy-start.91 = (f32[64]{0:T(128)}, f32[64]{0:T(128)S(1)}, u32[]{:S(2)}) copy-start(f32[64]{0:T(128)S(1)} %get-tuple-element.56) | copy-start | bytes 772
  26.5 6.1 %copy-start.93 = (f32[64]{0:T(128)}, f32[64]{0:T(128)S(1)}, u32[]{:S(2)}) copy-start(f32[64]{0:T(128)S(1)} %get-tuple-element.57) | copy-start | bytes 772
  27.0 5.6 %copy-start.136 = (f32[64]{0:T(128)}, f32[64]{0:T(128)S(1)}, u32[]{:S(2)}) copy-start(f32[64]{0:T(128)S(1)} %get-tuple-element.23) | copy-start | bytes 772
  27.0 5.6 %copy-start.137 = (f32[64]{0:T(128)}, f32[64]{0:T(128)S(1)}, u32[]{:S(2)}) copy-start(f32[64]{0:T(128)S(1)} %get-tuple-element.22) | copy-start | bytes 772
  27.0 5.6 %copy-start.139 = (f32[64]{0:T(128)}, f32[64]{0:T(128)S(1)}, u32[]{:S(2)}) copy-start(f32[64]{0:T(128)S(1)} %get-tuple-element.20) | copy-start | bytes 772
  27.0 5.6 %copy-start.140 = (f32[64]{0:T(128)}, f32[64]{0:T(128)S(1)}, u32[]{:S(2)}) copy-start(f32[64]{0:T(128)S(1)} %get-tuple-element.24) | copy-start | bytes 772
  33.0 19.5 %copy-start = (f32[11,8192]{1,0:T(8,128)}, f32[11,8192]{1,0:T(8,128)S(1)}, u32[]{:S(2)}) copy-start(f32[11,8192]{1,0:T(8,128)S(1)} %constant_dynamic-update-slice_fusion) | copy-start | bytes 1081348
  56.7 11.8 %copy-start.7 = (f32[3,8192]{1,0:T(4,128)S(1)}, f32[3,8192]{1,0:T(4,128)}, u32[]{:S(2)}) copy-start(f32[3,8192]{1,0:T(4,128)} %param.8) | copy-start | bytes 294916
  68.4 5.3 %copy-start.1 = (f32[11,8192]{1,0:T(8,128)S(1)}, f32[11,8192]{1,0:T(8,128)}, u32[]{:S(2)}) copy-start(f32[11,8192]{1,0:T(8,128)} %copy-done) | copy-start | bytes 1081348
  145.8 5.0 %copy-start.119 = (f32[64]{0:T(128)S(1)}, f32[64]{0:T(128)}, u32[]{:S(2)}) copy-start(f32[64]{0:T(128)} %copy-done.118) | copy-start | bytes 772
  145.8 6.0 %copy-start.74 = (f32[2,64]{1,0:T(2,128)S(1)}, f32[2,64]{1,0:T(2,128)}, u32[]{:S(2)}) copy-start(f32[2,64]{1,0:T(2,128)} %copy-done.73) | copy-start | bytes 1540
  145.8 6.0 %copy-start.76 = (f32[2,64]{1,0:T(2,128)S(1)}, f32[2,64]{1,0:T(2,128)}, u32[]{:S(2)}) copy-start(f32[2,64]{1,0:T(2,128)} %copy-done.75) | copy-start | bytes 1540
  145.8 6.0 %copy-start.78 = (f32[2,64]{1,0:T(2,128)S(1)}, f32[2,64]{1,0:T(2,128)}, u32[]{:S(2)}) copy-start(f32[2,64]{1,0:T(2,128)} %copy-done.77) | copy-start | bytes 1540
  145.8 6.0 %copy-start.87 = (f32[8,2,64]{2,0,1:T(8,128)S(1)}, f32[8,2,64]{2,0,1:T(8,128)}, u32[]{:S(2)}) copy-start(f32[8,2,64]{2,0,1:T(8,128)} %reduce_sum.310) | copy-start | bytes 12292
  145.9 7.0 %copy-start.58 = (f32[4,64]{1,0:T(4,128)S(1)}, f32[4,64]{1,0:T(4,128)}, u32[]{:S(2)}) copy-start(f32[4,64]{1,0:T(4,128)} %copy-done.57) | copy-start | bytes 3076
  145.9 7.0 %copy-start.60 = (f32[4,64]{1,0:T(4,128)S(1)}, f32[4,64]{1,0:T(4,128)}, u32[]{:S(2)}) copy-start(f32[4,64]{1,0:T(4,128)} %copy-done.59) | copy-start | bytes 3076
  145.9 7.0 %copy-start.62 = (f32[4,64]{1,0:T(4,128)S(1)}, f32[4,64]{1,0:T(4,128)}, u32[]{:S(2)}) copy-start(f32[4,64]{1,0:T(4,128)} %copy-done.61) | copy-start | bytes 3076
  145.9 7.0 %copy-start.71 = (f32[8,4,64]{2,0,1:T(8,128)S(1)}, f32[8,4,64]{2,0,1:T(8,128)}, u32[]{:S(2)}) copy-start(f32[8,4,64]{2,0,1:T(8,128)} %reduce_sum.311) | copy-start | bytes 24580
  145.9 7.0 %copy-start.82 = (f32[2,2,64]{2,1,0:T(2,128)S(1)}, f32[2,2,64]{2,1,0:T(2,128)}, u32[]{:S(2)}) copy-start(f32[2,2,64]{2,1,0:T(2,128)} %copy-done.81) | copy-start | bytes 3076
  145.9 7.0 %copy-start.84 = (f32[2,2,64]{2,1,0:T(2,128)S(1)}, f32[2,2,64]{2,1,0:T(2,128)}, u32[]{:S(2)}) copy-start(f32[2,2,64]{2,1,0:T(2,128)} %copy-done.83) | copy-start | bytes 3076
  145.9 7.0 %copy-start.86 = (f32[2,2,64]{2,1,0:T(2,128)S(1)}, f32[2,2,64]{2,1,0:T(2,128)}, u32[]{:S(2)}) copy-start(f32[2,2,64]{2,1,0:T(2,128)} %copy-done.85) | copy-start | bytes 3076
  145.9 7.0 %copy-start.117 = (f32[4,64]{1,0:T(4,128)S(1)}, f32[4,64]{1,0:T(4,128)}, u32[]{:S(2)}) copy-start(f32[4,64]{1,0:T(4,128)} %copy-done.116) | copy-start | bytes 3076
  147.6 5.9 %copy-start.37 = (f32[8,64]{1,0:T(8,128)S(1)}, f32[8,64]{1,0:T(8,128)}, u32[]{:S(2)}) copy-start(f32[8,64]{1,0:T(8,128)} %copy-done.36) | copy-start | bytes 6148
  147.6 5.9 %copy-start.39 = (f32[8,64]{1,0:T(8,128)S(1)}, f32[8,64]{1,0:T(8,128)}, u32[]{:S(2)}) copy-start(f32[8,64]{1,0:T(8,128)} %copy-done.38) | copy-start | bytes 6148
  147.6 5.9 %copy-start.41 = (f32[8,64]{1,0:T(8,128)S(1)}, f32[8,64]{1,0:T(8,128)}, u32[]{:S(2)}) copy-start(f32[8,64]{1,0:T(8,128)} %copy-done.40) | copy-start | bytes 6148
  147.6 5.9 %copy-start.66 = (f32[4,2,64]{2,1,0:T(2,128)S(1)}, f32[4,2,64]{2,1,0:T(2,128)}, u32[]{:S(2)}) copy-start(f32[4,2,64]{2,1,0:T(2,128)} %copy-done.65) | copy-start | bytes 6148
  147.6 5.9 %copy-start.68 = (f32[4,2,64]{2,1,0:T(2,128)S(1)}, f32[4,2,64]{2,1,0:T(2,128)}, u32[]{:S(2)}) copy-start(f32[4,2,64]{2,1,0:T(2,128)} %copy-done.67) | copy-start | bytes 6148
  147.6 5.9 %copy-start.70 = (f32[4,2,64]{2,1,0:T(2,128)S(1)}, f32[4,2,64]{2,1,0:T(2,128)}, u32[]{:S(2)}) copy-start(f32[4,2,64]{2,1,0:T(2,128)} %copy-done.69) | copy-start | bytes 6148
  147.6 5.9 %copy-start.114 = (f32[8,64]{1,0:T(8,128)S(1)}, f32[8,64]{1,0:T(8,128)}, u32[]{:S(2)}) copy-start(f32[8,64]{1,0:T(8,128)} %copy-done.113) | copy-start | bytes 6148
  148.0 6.4 %copy-start.24 = (f32[16,64]{1,0:T(8,128)S(1)}, f32[16,64]{1,0:T(8,128)}, u32[]{:S(2)}) copy-start(f32[16,64]{1,0:T(8,128)} %copy-done.23) | copy-start | bytes 12292
  148.0 6.4 %copy-start.26 = (f32[16,64]{1,0:T(8,128)S(1)}, f32[16,64]{1,0:T(8,128)}, u32[]{:S(2)}) copy-start(f32[16,64]{1,0:T(8,128)} %copy-done.25) | copy-start | bytes 12292
  148.0 6.4 %copy-start.34 = (f32[8,16,64]{2,0,1:T(8,128)S(1)}, f32[8,16,64]{2,0,1:T(8,128)}, u32[]{:S(2)}) copy-start(f32[8,16,64]{2,0,1:T(8,128)} %reduce_sum.313) | copy-start | bytes 98308
  148.1 6.4 %copy-start.43 = (f32[8,2,64]{2,1,0:T(2,128)S(1)}, f32[8,2,64]{2,1,0:T(2,128)}, u32[]{:S(2)}) copy-start(f32[8,2,64]{2,1,0:T(2,128)} %copy-done.42) | copy-start | bytes 12292
  148.1 6.4 %copy-start.45 = (f32[8,2,64]{2,1,0:T(2,128)S(1)}, f32[8,2,64]{2,1,0:T(2,128)}, u32[]{:S(2)}) copy-start(f32[8,2,64]{2,1,0:T(2,128)} %copy-done.44) | copy-start | bytes 12292
  148.1 6.4 %copy-start.47 = (f32[8,2,64]{2,1,0:T(2,128)S(1)}, f32[8,2,64]{2,1,0:T(2,128)}, u32[]{:S(2)}) copy-start(f32[8,2,64]{2,1,0:T(2,128)} %copy-done.46) | copy-start | bytes 12292
  148.1 6.4 %copy-start.80 = (f32[16,64]{1,0:T(8,128)S(1)}, f32[16,64]{1,0:T(8,128)}, u32[]{:S(2)}) copy-start(f32[16,64]{1,0:T(8,128)} %copy-done.79) | copy-start | bytes 12292
  (84 other events, 210.6 us)
Sparse Core Ops, SparseCore 0:
  29.0 84.9 all-gather.2

commit v10 on v9

--- a/solution.py
+++ b/solution.py
@@ -99,7 +99,7 @@
             distance_sq = (near[0:1, :] - target_x) ** 2
             distance_sq = distance_sq + (near[1:2, :] - target_y) ** 2
             distance_sq = distance_sq + (near[2:3, :] - target_z) ** 2
-            kernel_block = 1.0 / (1.0 + kernel_scale * distance_sq)
+            kernel_block = 1.0 / (1.0 + distance_sq)
             out_ref[...] += lax.dot_general(
                 probes_ref[source], kernel_block, (((1,), (1,)), ((), ())),
                 precision=lax.Precision.HIGH, preferred_element_type=jnp.float32,
@@ -110,6 +110,7 @@
     tiles, rows, size = probe_tiles.shape
     boxes = points.shape[1] // size
     slots = slot_source.shape[0] // boxes
+    stretch = kernel_scale**0.5
     return pl.pallas_call(
         functools.partial(near_kernel, kernel_scale, slots),
         out_shape=jax.ShapeDtypeStruct((rows, boxes * size), jnp.float32),
@@ -129,7 +130,7 @@
             transcendentals=0,
             bytes_accessed=4 * (probe_tiles.size + coord_tiles.size + 2 * rows * boxes * size),
         ),
-    )(slot_source, probe_tiles, coord_tiles, points.T)
+    )(slot_source, probe_tiles, coord_tiles * stretch, points.T * stretch)
 
 
 def body(probes, points, near_list, leaf_proxy, inner_proxy, top_proxy, far_list):

time: 171 us -> 166 us (0.971)
  the two profiles are of different devices: /device:TPU:46 before, /device:TPU:53 now
where the time goes in v10:
time: 166 us; the launch traced here: 165 us
  Pallas kernels  72.5 us (44%)
  matrix products  35 us (21%)
  local copies, waits for them, and re-layouts  26.9 us (16%)
  between operations  16.7 us (10%)
  other arithmetic  13.7 us (8%)
    pallas_call x1, Pallas kernels, near_field_call(): pl.pallas_call(functools.partial(near_kernel, kernel_scale, slots), out_s...  58.9 us
    pallas_call x1, Pallas kernels, exchange_halo(): pl.pallas_call(halo_kernel, out_shape=(shape, shape), in_specs=[vmem, vme...  13.6 us
    dot_general x1, matrix products, body(): jnp.einsum('qnr,nrs->qns', source_moment, kernel_block, precision=PRECISE)  10 us
    dot_general x5, matrix products, body(): jnp.einsum('qns,nrs->qnr', jnp.repeat(descent, 2, axis=1), transfer_maps[...  7.14 us
    unnamed x303, local copies, waits for them, and re-layouts  5.67 us
    dot_general x5, matrix products, body(): jnp.einsum('qnr,nrs->qns', level_moments[-1], interp_map, precision=PRECISE)  5.15 us
    reduce_sum x7, other arithmetic, interpolation(): return values / jnp.sum(values, axis=-1, keepdims=True)  4.31 us
    dot_general x5, matrix products, body(): jnp.einsum('qns,nrs->qnr', descent, own_edges[height], precision=PRECISE)  3.82 us
  transfers between devices with their start and end apart: 1, of which 0 were waited for; matrix products, arithmetic and copies ran while one was open for 19% of the time, Pallas kernels for 44%

profile of v10, /device:TPU:53, one launch (start us, length us, event | category | flops | bytes accessed | tf_op | source)
XLA Modules:
  0.0 164.9 jit_solution(11103686390418212460)
XLA Ops:
  6.5 1.2 reshape.3427
  7.9 0.9 reshape.3420
  9.0 0.9 slice_reduce_fusion.10
  10.1 1.3 slice_reduce_fusion.2
  11.6 1.1 divide_reduce_fusion
  12.7 3.3 %constant_dynamic-update-slice_fusion.6 = (f32[8,62,64]{2,0,1:T(8,128)S(1)}, f32[8,32,64]{2,0,1:T(8,128)S(1)}) fusion(f32[8,32,256]{2,0,1:T(8,128)S(1)} %bitcast.410, f32[32,256]{1,0:T(8,128)S(1)} %divide_reduce_fusion, f32[32,64]{1,0:T(8,128)S(1)} %sub.1273, f32[32,256]{1,0:T(8,128)S(1)} %sub.1271, f32[32,64]{1,0:T(8,128)S(1)} %sub.1268, ...), kind=kOutput, calls=%fused_computation.98 | convolution fusion | flops 56623104 | bytes 679936 | tf_op jit(solution)/shard_map/qbp,bpr->qbr/dot_general | solution.py:164
  16.1 1.4 divide_reduce_fusion.1
  17.5 2.6 %bitcast_reduce_fusion = f32[8,16,64]{2,0,1:T(8,128)S(1)} fusion(f32[8,32,64]{2,0,1:T(8,128)S(1)} %get-tuple-element.124, f32[32,64]{1,0:T(8,128)S(1)} %divide_reduce_fusion.1, f32[32,64]{1,0:T(8,128)S(1)} %bitcast.428, f32[32,64]{1,0:T(8,128)S(1)} %sub.1273, f32[32,64]{1,0:T(8,128)S(1)} %bitcast.425, f32[32,64]{1,0:T(8,128)S(1)} %sub.1268, ...), kind=kOutput, calls=%fused_computation.75 | convolution fusion | flops 14163968 | bytes 155648 | tf_op jit(solution)/shard_map/qnr,nrs->qns/dot_general | solution.py:171
  20.2 0.7 divide_reduce_fusion.2
  20.9 1.3 bitcast_reduce_fusion.1
  22.3 0.4 divide_reduce_fusion.3
  22.8 0.6 copy-done.113
  23.4 0.6 bitcast_reduce_fusion.2
  24.5 0.4 bitcast_reduce_fusion.3
  25.3 0.3 copy-done.131
  25.6 0.6 copy-done.134
  26.1 0.3 constant_dynamic-update-slice_fusion.11
  26.6 0.4 fusion.53
  28.3 0.6 copy-done.54
  30.0 0.6 slice.610
  30.6 0.6 slice.612
  31.2 0.6 bitcast_convert_fusion
  31.9 0.6 copy-done.5
  32.9 0.7 broadcast_multiply_fusion
  33.6 0.9 pad_maximum_fusion.2
  34.6 13.6 %shard_map.73 = (f32[11,4736]{1,0:T(8,128)}, f32[11,4736]{1,0:T(8,128)}) custom-call(f32[11,4736]{1,0:T(8,128)} %get-tuple-element.43.to_right, f32[11,4736]{1,0:T(8,128)} %get-tuple-element.42.to_left), custom_call_target="tpu_custom_call" | custom-call | tf_op jit(solution)/shard_map/pallas_call | solution.py:60
  48.3 1.0 slice.543
  50.3 0.5 compare_and_fusion
  50.8 1.1 pad_maximum_fusion
  51.9 0.9 gather_fusion
  52.9 0.3 select_bitcast_fusion
  53.9 10.0 %fusion.9 = f32[8,186,64]{2,0,1:T(8,128)S(1)} fusion(f32[186,64]{1,0:T(8,128)S(1)} %get-tuple-element.40, f32[186,64]{1,0:T(8,128)S(1)} %bitcast.417, f32[186,64]{1,0:T(8,128)S(1)} %get-tuple-element.41, f32[186,64]{1,0:T(8,128)S(1)} %bitcast.418, f32[186,64]{1,0:T(8,128)S(1)} %get-tuple-element.39, f32[186,64]{1,0:T(8,128)S(1)} %bitcast.419, ...), kind=kOutput, calls=%fused_computation.16 | convolution fusion | flops 81613824 | bytes 1733632 | tf_op jit(solution)/shard_map/qnr,nrs->qns/dot_general | solution.py:232
  64.1 0.9 slice.472
  65.0 0.8 slice.473
  65.8 0.6 reduce_sum.310
  66.4 0.6 reduce_sum.311
  67.0 0.6 reduce_sum.313
  67.6 0.7 reduce_sum.314
  68.4 0.8 slice.580
  69.2 0.6 reshape.3418.source_ref
  69.9 2.9 %copy.100 = f32[3,8192]{0,1:T(8,128)} copy(f32[3,8192]{1,0:T(4,128)S(1)} %copy-done.6) | data formatting | bytes 196608 | tf_op jit(solution)/shard_map/mul | solution.py:133
  72.8 0.9 constant_dynamic-slice_fusion.40
  73.7 0.9 constant_dynamic-slice_fusion.46
  74.7 0.7 maximum_multiply_fusion
  75.4 58.9 %shard_map.74 = f32[8,8192]{1,0:T(8,128)} custom-call(s32[192]{0:T(256)} %reshape.3418.source_ref, f32[38,8,256]{2,1,0:T(8,128)} %bitcast.409, f32[38,3,256]{2,1,0:T(4,128)} %bitcast.412, f32[8192,3]{1,0:T(8,128)} %bitcast.401), custom_call_target="tpu_custom_call" | custom-call | flops 352321536 | bytes 952320 | tf_op jit(solution)/shard_map/pallas_call | solution.py:114
  134.3 0.6 slice_bitcast_fusion.8
  134.9 0.6 slice_bitcast_fusion.7
  135.5 2.0 %fusion.216 = (f32[128,8,1,64]{3,1,0,2:T(8,128)S(1)}, f32[128,8,1,64]{3,1,0,2:T(8,128)S(1)}, f32[128,8,1,64]{3,1,0,2:T(8,128)S(1)}, f32[128,8,1,64]{3,1,0,2:T(8,...) fusion(f32[128,8,6,64]{3,1,0,2:T(8,128)} %bitcast.402), kind=kLoop, calls=%fused_computation.540 | loop fusion | bytes 3145728 | tf_op jit(solution)/shard_map/slice | solution.py:265
  137.6 0.8 reduce_sum.300
  138.3 0.7 constant_dynamic-update-slice_fusion.24
  139.0 0.7 constant_dynamic-update-slice_fusion.23
  139.7 0.7 constant_dynamic-update-slice_fusion.22
  141.0 1.6 convolution_bitcast_fusion.3
  143.2 1.0 fusion.22
  144.2 0.9 fusion.20
  145.1 0.8 fusion.18
  145.9 0.9 fusion.16
  146.9 1.0 fusion.14
  148.0 0.5 fusion.13
  148.6 0.8 fusion.12
  149.5 1.6 fusion.11
  151.3 3.2 %fusion.10 = f32[8,32,64]{2,0,1:T(8,128)S(1)} fusion(f32[8,32,64]{2,0,1:T(8,128)S(1)} %copy-done.14, f32[8,32,64]{2,0,1:T(8,128)S(1)} %bitcast.416, f32[32,64]{1,0:T(8,128)S(1)} %copy-done.64, f32[32,64]{1,0:T(8,128)S(1)} %bitcast.429, f32[32,64]{1,0:T(8,128)S(1)} %copy-done.13, f32[32,64]{1,0:T(8,128)S(1)} %bitcast.426, f32[32,64]{1,0:T(8,128)S(1)} %copy-done.11, ...), kind=kOutput, calls=%fused_computation.19 | convolution fusion | flops 14172160 | bytes 253952 | tf_op jit(solution)/shard_map/qns,nrs->qnr/dot_general | solution.py:294
  154.6 2.7 %fusion.26 = f32[32,256,8]{1,2,0:T(8,128)S(1)} fusion(f32[8,32,64]{2,0,1:T(8,128)S(1)} %fusion.10, f32[32,256]{1,0:T(8,128)S(1)} %copy-done.49, f32[32,64]{1,0:T(8,128)S(1)} %copy-done.13, f32[32,256]{1,0:T(8,128)S(1)} %copy-done.20, f32[32,64]{1,0:T(8,128)S(1)} %copy-done.11, f32[32,256]{1,0:T(8,128)S(1)} %copy-done.18, f32[32,64]{1,0:T(8,128)S(1)} %sub.1263, ...), kind=kOutput, calls=%fused_computation.48 | convolution fusion | flops 56623104 | bytes 483328 | tf_op jit(solution)/shard_map/qbr,bpr->qbp/dot_general | solution.py:298
  157.3 0.7 add_add_fusion
  (417 shorter events, 6.2 us)
Async XLA Ops:
  6.5 6.1 %copy-start.3 = (f32[8,8192]{1,0:T(8,128)S(1)}, f32[8,8192]{1,0:T(8,128)}, u32[]{:S(2)}) copy-start(f32[8,8192]{1,0:T(8,128)} %param.7) | copy-start | bytes 786436
  6.5 129.0 %all-gather.3.cloned.1.call-start = ((), (), s32[]{:S(2)}) async-start(), calls=%async_computation | async-start | bytes 3170304 | tf_op jit(solution)/shard_map/all_gather | solution.py:260
  7.8 17.1 %copy-start.50 = (f32[3,8,64]{2,1,0:T(8,128)}, f32[3,8,64]{2,1,0:T(8,128)S(1)}, u32[]{:S(2)}) copy-start(f32[3,8,64]{2,1,0:T(8,128)S(1)} %slice.585) | copy-start | bytes 18436
  7.8 18.7 %copy-start.55 = (f32[3,4,64]{2,1,0:T(4,128)}, f32[3,4,64]{2,1,0:T(4,128)S(1)}, u32[]{:S(2)}) copy-start(f32[3,4,64]{2,1,0:T(4,128)S(1)} %slice.586) | copy-start | bytes 9220
  7.8 18.6 %copy-start.27 = (f32[3,32,64]{2,1,0:T(8,128)}, f32[3,32,64]{2,1,0:T(8,128)S(1)}, u32[]{:S(2)}) copy-start(f32[3,32,64]{2,1,0:T(8,128)S(1)} %slice.583) | copy-start | bytes 73732
  7.8 18.6 %copy-start.35 = (f32[3,16,64]{2,1,0:T(8,128)}, f32[3,16,64]{2,1,0:T(8,128)S(1)}, u32[]{:S(2)}) copy-start(f32[3,16,64]{2,1,0:T(8,128)S(1)} %slice.584) | copy-start | bytes 36868
  7.9 17.0 %copy-start.9 = (f32[3,128,64]{2,1,0:T(8,128)}, f32[3,128,64]{2,1,0:T(8,128)S(1)}, u32[]{:S(2)}) copy-start(f32[3,128,64]{2,1,0:T(8,128)S(1)} %slice.581) | copy-start | bytes 294916
  7.9 18.5 %copy-start.21 = (f32[3,64,64]{2,1,0:T(8,128)}, f32[3,64,64]{2,1,0:T(8,128)S(1)}, u32[]{:S(2)}) copy-start(f32[3,64,64]{2,1,0:T(8,128)S(1)} %slice.582) | copy-start | bytes 147460
  8.8 21.8 %copy-start.2 = (f32[3,30,64]{2,1,0:T(8,128)}, f32[3,30,64]{2,1,0:T(8,128)S(1)}, u32[]{:S(2)}) copy-start(f32[3,30,64]{2,1,0:T(8,128)S(1)} %reshape.3420) | copy-start | bytes 69124
  8.8 12.1 %copy-start.23 = (f32[16,64]{1,0:T(8,128)}, f32[16,64]{1,0:T(8,128)S(1)}, u32[]{:S(2)}) copy-start(f32[16,64]{1,0:T(8,128)S(1)} %get-tuple-element.77) | copy-start | bytes 12292
  8.8 12.1 %copy-start.25 = (f32[16,64]{1,0:T(8,128)}, f32[16,64]{1,0:T(8,128)S(1)}, u32[]{:S(2)}) copy-start(f32[16,64]{1,0:T(8,128)S(1)} %get-tuple-element.78) | copy-start | bytes 12292
  8.8 13.8 %copy-start.36 = (f32[8,64]{1,0:T(8,128)}, f32[8,64]{1,0:T(8,128)S(1)}, u32[]{:S(2)}) copy-start(f32[8,64]{1,0:T(8,128)S(1)} %get-tuple-element.73) | copy-start | bytes 6148
  8.8 13.8 %copy-start.38 = (f32[8,64]{1,0:T(8,128)}, f32[8,64]{1,0:T(8,128)S(1)}, u32[]{:S(2)}) copy-start(f32[8,64]{1,0:T(8,128)S(1)} %get-tuple-element.74) | copy-start | bytes 6148
  8.8 13.8 %copy-start.40 = (f32[8,64]{1,0:T(8,128)}, f32[8,64]{1,0:T(8,128)S(1)}, u32[]{:S(2)}) copy-start(f32[8,64]{1,0:T(8,128)S(1)} %get-tuple-element.75) | copy-start | bytes 6148
  8.9 15.6 %copy-start.57 = (f32[4,64]{1,0:T(4,128)}, f32[4,64]{1,0:T(4,128)S(1)}, u32[]{:S(2)}) copy-start(f32[4,64]{1,0:T(4,128)S(1)} %get-tuple-element.70) | copy-start | bytes 3076
  8.9 15.6 %copy-start.59 = (f32[4,64]{1,0:T(4,128)}, f32[4,64]{1,0:T(4,128)S(1)}, u32[]{:S(2)}) copy-start(f32[4,64]{1,0:T(4,128)S(1)} %get-tuple-element.71) | copy-start | bytes 3076
  8.9 15.6 %copy-start.61 = (f32[4,64]{1,0:T(4,128)}, f32[4,64]{1,0:T(4,128)S(1)}, u32[]{:S(2)}) copy-start(f32[4,64]{1,0:T(4,128)S(1)} %get-tuple-element.72) | copy-start | bytes 3076
  8.9 16.3 %copy-start.73 = (f32[2,64]{1,0:T(2,128)}, f32[2,64]{1,0:T(2,128)S(1)}, u32[]{:S(2)}) copy-start(f32[2,64]{1,0:T(2,128)S(1)} %get-tuple-element.67) | copy-start | bytes 1540
  8.9 16.3 %copy-start.75 = (f32[2,64]{1,0:T(2,128)}, f32[2,64]{1,0:T(2,128)S(1)}, u32[]{:S(2)}) copy-start(f32[2,64]{1,0:T(2,128)S(1)} %get-tuple-element.68) | copy-start | bytes 1540
  8.9 16.3 %copy-start.77 = (f32[2,64]{1,0:T(2,128)}, f32[2,64]{1,0:T(2,128)S(1)}, u32[]{:S(2)}) copy-start(f32[2,64]{1,0:T(2,128)S(1)} %get-tuple-element.69) | copy-start | bytes 1540
  10.1 7.4 %copy-start.10 = (f32[32,64]{1,0:T(8,128)}, f32[32,64]{1,0:T(8,128)S(1)}, u32[]{:S(2)}) copy-start(f32[32,64]{1,0:T(8,128)S(1)} %sub.1268) | copy-start | bytes 24580
  10.1 7.4 %copy-start.12 = (f32[32,64]{1,0:T(8,128)}, f32[32,64]{1,0:T(8,128)S(1)}, u32[]{:S(2)}) copy-start(f32[32,64]{1,0:T(8,128)S(1)} %sub.1273) | copy-start | bytes 24580
  24.1 5.5 %copy-start.22 = (f32[3,2048]{1,0:T(4,128)S(1)}, f32[3,2048]{1,0:T(4,128)}, u32[]{:S(2)}) copy-start(f32[3,2048]{1,0:T(4,128)} %param.10) | copy-start | bytes 73732
  24.1 5.7 %copy-start.72 = (s32[32,3]{0,1:T(4,128)S(1)}, s32[32,3]{0,1:T(4,128)}, u32[]{:S(2)}) copy-start(s32[32,3]{0,1:T(4,128)} %param.13) | copy-start | bytes 1156
  24.1 5.9 %copy-start.81 = (f32[2,2,64]{2,1,0:T(2,128)}, f32[2,2,64]{2,1,0:T(2,128)S(1)}, u32[]{:S(2)}) copy-start(f32[2,2,64]{2,1,0:T(2,128)S(1)} %broadcast_in_dim.132) | copy-start | bytes 3076
  24.1 5.9 %copy-start.83 = (f32[2,2,64]{2,1,0:T(2,128)}, f32[2,2,64]{2,1,0:T(2,128)S(1)}, u32[]{:S(2)}) copy-start(f32[2,2,64]{2,1,0:T(2,128)S(1)} %broadcast_in_dim.134) | copy-start | bytes 3076
  24.2 5.9 %copy-start.85 = (f32[2,2,64]{2,1,0:T(2,128)}, f32[2,2,64]{2,1,0:T(2,128)S(1)}, u32[]{:S(2)}) copy-start(f32[2,2,64]{2,1,0:T(2,128)S(1)} %broadcast_in_dim.136) | copy-start | bytes 3076
  26.5 6.1 %copy-start.89 = (f32[64]{0:T(128)}, f32[64]{0:T(128)S(1)}, u32[]{:S(2)}) copy-start(f32[64]{0:T(128)S(1)} %get-tuple-element.57) | copy-start | bytes 772
  26.5 6.1 %copy-start.91 = (f32[64]{0:T(128)}, f32[64]{0:T(128)S(1)}, u32[]{:S(2)}) copy-start(f32[64]{0:T(128)S(1)} %get-tuple-element.58) | copy-start | bytes 772
  26.5 6.1 %copy-start.93 = (f32[64]{0:T(128)}, f32[64]{0:T(128)S(1)}, u32[]{:S(2)}) copy-start(f32[64]{0:T(128)S(1)} %get-tuple-element.59) | copy-start | bytes 772
  27.0 5.6 %copy-start.136 = (f32[64]{0:T(128)}, f32[64]{0:T(128)S(1)}, u32[]{:S(2)}) copy-start(f32[64]{0:T(128)S(1)} %get-tuple-element.23) | copy-start | bytes 772
  27.0 5.6 %copy-start.137 = (f32[64]{0:T(128)}, f32[64]{0:T(128)S(1)}, u32[]{:S(2)}) copy-start(f32[64]{0:T(128)S(1)} %get-tuple-element.22) | copy-start | bytes 772
  27.0 5.6 %copy-start.139 = (f32[64]{0:T(128)}, f32[64]{0:T(128)S(1)}, u32[]{:S(2)}) copy-start(f32[64]{0:T(128)S(1)} %get-tuple-element.20) | copy-start | bytes 772
  27.0 5.6 %copy-start.140 = (f32[64]{0:T(128)}, f32[64]{0:T(128)S(1)}, u32[]{:S(2)}) copy-start(f32[64]{0:T(128)S(1)} %get-tuple-element.24) | copy-start | bytes 772
  33.6 16.1 %copy-start = (f32[11,8192]{1,0:T(8,128)}, f32[11,8192]{1,0:T(8,128)S(1)}, u32[]{:S(2)}) copy-start(f32[11,8192]{1,0:T(8,128)S(1)} %get-tuple-element.52) | copy-start | bytes 1081348
  64.0 5.1 %copy-start.115 = (s32[32,6]{0,1:T(8,128)S(1)}, s32[32,6]{0,1:T(8,128)}, u32[]{:S(2)}) copy-start(s32[32,6]{0,1:T(8,128)} %param.9) | copy-start | bytes 2308
  64.0 5.8 %copy-start.6 = (f32[3,8192]{1,0:T(4,128)S(1)}, f32[3,8192]{1,0:T(4,128)}, u32[]{:S(2)}) copy-start(f32[3,8192]{1,0:T(4,128)} %get-tuple-element.51) | copy-start | bytes 294916
  140.9 5.0 %copy-start.119 = (f32[64]{0:T(128)S(1)}, f32[64]{0:T(128)}, u32[]{:S(2)}) copy-start(f32[64]{0:T(128)} %copy-done.118) | copy-start | bytes 772
  140.9 5.9 %copy-start.74 = (f32[2,64]{1,0:T(2,128)S(1)}, f32[2,64]{1,0:T(2,128)}, u32[]{:S(2)}) copy-start(f32[2,64]{1,0:T(2,128)} %copy-done.73) | copy-start | bytes 1540
  140.9 6.0 %copy-start.76 = (f32[2,64]{1,0:T(2,128)S(1)}, f32[2,64]{1,0:T(2,128)}, u32[]{:S(2)}) copy-start(f32[2,64]{1,0:T(2,128)} %copy-done.75) | copy-start | bytes 1540
  140.9 6.0 %copy-start.78 = (f32[2,64]{1,0:T(2,128)S(1)}, f32[2,64]{1,0:T(2,128)}, u32[]{:S(2)}) copy-start(f32[2,64]{1,0:T(2,128)} %copy-done.77) | copy-start | bytes 1540
  140.9 6.0 %copy-start.87 = (f32[8,2,64]{2,0,1:T(8,128)S(1)}, f32[8,2,64]{2,0,1:T(8,128)}, u32[]{:S(2)}) copy-start(f32[8,2,64]{2,0,1:T(8,128)} %reduce_sum.310) | copy-start | bytes 12292
  141.0 7.0 %copy-start.58 = (f32[4,64]{1,0:T(4,128)S(1)}, f32[4,64]{1,0:T(4,128)}, u32[]{:S(2)}) copy-start(f32[4,64]{1,0:T(4,128)} %copy-done.57) | copy-start | bytes 3076
  141.0 7.0 %copy-start.60 = (f32[4,64]{1,0:T(4,128)S(1)}, f32[4,64]{1,0:T(4,128)}, u32[]{:S(2)}) copy-start(f32[4,64]{1,0:T(4,128)} %copy-done.59) | copy-start | bytes 3076
  141.0 7.0 %copy-start.62 = (f32[4,64]{1,0:T(4,128)S(1)}, f32[4,64]{1,0:T(4,128)}, u32[]{:S(2)}) copy-start(f32[4,64]{1,0:T(4,128)} %copy-done.61) | copy-start | bytes 3076
  141.0 7.0 %copy-start.71 = (f32[8,4,64]{2,0,1:T(8,128)S(1)}, f32[8,4,64]{2,0,1:T(8,128)}, u32[]{:S(2)}) copy-start(f32[8,4,64]{2,0,1:T(8,128)} %reduce_sum.311) | copy-start | bytes 24580
  141.0 7.0 %copy-start.82 = (f32[2,2,64]{2,1,0:T(2,128)S(1)}, f32[2,2,64]{2,1,0:T(2,128)}, u32[]{:S(2)}) copy-start(f32[2,2,64]{2,1,0:T(2,128)} %copy-done.81) | copy-start | bytes 3076
  141.0 7.0 %copy-start.84 = (f32[2,2,64]{2,1,0:T(2,128)S(1)}, f32[2,2,64]{2,1,0:T(2,128)}, u32[]{:S(2)}) copy-start(f32[2,2,64]{2,1,0:T(2,128)} %copy-done.83) | copy-start | bytes 3076
  141.0 7.0 %copy-start.86 = (f32[2,2,64]{2,1,0:T(2,128)S(1)}, f32[2,2,64]{2,1,0:T(2,128)}, u32[]{:S(2)}) copy-start(f32[2,2,64]{2,1,0:T(2,128)} %copy-done.85) | copy-start | bytes 3076
  141.0 7.0 %copy-start.117 = (f32[4,64]{1,0:T(4,128)S(1)}, f32[4,64]{1,0:T(4,128)}, u32[]{:S(2)}) copy-start(f32[4,64]{1,0:T(4,128)} %copy-done.116) | copy-start | bytes 3076
  142.7 5.8 %copy-start.37 = (f32[8,64]{1,0:T(8,128)S(1)}, f32[8,64]{1,0:T(8,128)}, u32[]{:S(2)}) copy-start(f32[8,64]{1,0:T(8,128)} %copy-done.36) | copy-start | bytes 6148
  142.7 5.8 %copy-start.39 = (f32[8,64]{1,0:T(8,128)S(1)}, f32[8,64]{1,0:T(8,128)}, u32[]{:S(2)}) copy-start(f32[8,64]{1,0:T(8,128)} %copy-done.38) | copy-start | bytes 6148
  142.7 5.8 %copy-start.41 = (f32[8,64]{1,0:T(8,128)S(1)}, f32[8,64]{1,0:T(8,128)}, u32[]{:S(2)}) copy-start(f32[8,64]{1,0:T(8,128)} %copy-done.40) | copy-start | bytes 6148
  142.7 5.8 %copy-start.66 = (f32[4,2,64]{2,1,0:T(2,128)S(1)}, f32[4,2,64]{2,1,0:T(2,128)}, u32[]{:S(2)}) copy-start(f32[4,2,64]{2,1,0:T(2,128)} %copy-done.65) | copy-start | bytes 6148
  142.7 5.8 %copy-start.68 = (f32[4,2,64]{2,1,0:T(2,128)S(1)}, f32[4,2,64]{2,1,0:T(2,128)}, u32[]{:S(2)}) copy-start(f32[4,2,64]{2,1,0:T(2,128)} %copy-done.67) | copy-start | bytes 6148
  142.7 5.8 %copy-start.70 = (f32[4,2,64]{2,1,0:T(2,128)S(1)}, f32[4,2,64]{2,1,0:T(2,128)}, u32[]{:S(2)}) copy-start(f32[4,2,64]{2,1,0:T(2,128)} %copy-done.69) | copy-start | bytes 6148
  142.7 5.8 %copy-start.114 = (f32[8,64]{1,0:T(8,128)S(1)}, f32[8,64]{1,0:T(8,128)}, u32[]{:S(2)}) copy-start(f32[8,64]{1,0:T(8,128)} %copy-done.113) | copy-start | bytes 6148
  143.1 6.3 %copy-start.24 = (f32[16,64]{1,0:T(8,128)S(1)}, f32[16,64]{1,0:T(8,128)}, u32[]{:S(2)}) copy-start(f32[16,64]{1,0:T(8,128)} %copy-done.23) | copy-start | bytes 12292
  143.1 6.3 %copy-start.26 = (f32[16,64]{1,0:T(8,128)S(1)}, f32[16,64]{1,0:T(8,128)}, u32[]{:S(2)}) copy-start(f32[16,64]{1,0:T(8,128)} %copy-done.25) | copy-start | bytes 12292
  143.1 6.3 %copy-start.34 = (f32[8,16,64]{2,0,1:T(8,128)S(1)}, f32[8,16,64]{2,0,1:T(8,128)}, u32[]{:S(2)}) copy-start(f32[8,16,64]{2,0,1:T(8,128)} %reduce_sum.313) | copy-start | bytes 98308
  143.1 6.3 %copy-start.43 = (f32[8,2,64]{2,1,0:T(2,128)S(1)}, f32[8,2,64]{2,1,0:T(2,128)}, u32[]{:S(2)}) copy-start(f32[8,2,64]{2,1,0:T(2,128)} %copy-done.42) | copy-start | bytes 12292
  143.2 6.3 %copy-start.45 = (f32[8,2,64]{2,1,0:T(2,128)S(1)}, f32[8,2,64]{2,1,0:T(2,128)}, u32[]{:S(2)}) copy-start(f32[8,2,64]{2,1,0:T(2,128)} %copy-done.44) | copy-start | bytes 12292
  143.2 6.3 %copy-start.47 = (f32[8,2,64]{2,1,0:T(2,128)S(1)}, f32[8,2,64]{2,1,0:T(2,128)}, u32[]{:S(2)}) copy-start(f32[8,2,64]{2,1,0:T(2,128)} %copy-done.46) | copy-start | bytes 12292
  143.2 6.3 %copy-start.80 = (f32[16,64]{1,0:T(8,128)S(1)}, f32[16,64]{1,0:T(8,128)}, u32[]{:S(2)}) copy-start(f32[16,64]{1,0:T(8,128)} %copy-done.79) | copy-start | bytes 12292
  (84 other events, 210.1 us)
Sparse Core Ops, SparseCore 0:
  29.0 86.3 all-gather.2

commit v11 on v10

--- a/solution.py
+++ b/solution.py
@@ -83,27 +83,52 @@
     return values / jnp.sum(values, axis=-1, keepdims=True)
 
 
-def near_kernel(kernel_scale, slots, source_ref, probes_ref, coords_ref, target_ref, out_ref):
+def near_kernel(slots, halo, source_ref, probes_ref, coords_ref, target_ref, out_ref):
     box = pl.program_id(0)
+    boxes = pl.num_programs(0)
     size = target_ref.shape[0]
     target_x = jnp.broadcast_to(target_ref[:, 0:1], (size, size))
     target_y = jnp.broadcast_to(target_ref[:, 1:2], (size, size))
     target_z = jnp.broadcast_to(target_ref[:, 2:3], (size, size))
-    out_ref[...] = jnp.zeros_like(out_ref)
+    here = box + halo
+    columns = pl.ds(pl.multiple_of(box * size, size), size)
+
+    def block(tile):
+        near = coords_ref[tile]
+        distance_sq = (near[0:1, :] - target_x) ** 2
+        distance_sq = distance_sq + (near[1:2, :] - target_y) ** 2
+        distance_sq = distance_sq + (near[2:3, :] - target_z) ** 2
+        return 1.0 / (1.0 + distance_sq)
+
+    def gather_into(tile, kernel_block):
+        out_ref[:, columns] += lax.dot_general(
+            probes_ref[tile], kernel_block, (((1,), (1,)), ((), ())),
+            precision=lax.Precision.HIGH, preferred_element_type=jnp.float32,
+        )
+
+    @pl.when(box == 0)
+    def _():
+        out_ref[...] = jnp.zeros_like(out_ref)
+        gather_into(here - 1, block(here - 1))
+
+    gather_into(here, block(here))
+    pair_block = block(here + 1)
+    gather_into(here + 1, pair_block)
+
+    @pl.when(box < boxes - 1)
+    def _():
+        following = pl.ds(pl.multiple_of((box + 1) * size, size), size)
+        out_ref[:, following] += jnp.dot(
+            probes_ref[here], pair_block, precision=lax.Precision.HIGH,
+            preferred_element_type=jnp.float32,
+        )
+
     for slot in range(slots):
         source = source_ref[box * slots + slot]
 
-        @pl.when(source >= 0)
+        @pl.when((source >= 0) & (source != here - 1) & (source != here) & (source != here + 1))
         def _():
-            near = coords_ref[source]
-            distance_sq = (near[0:1, :] - target_x) ** 2
-            distance_sq = distance_sq + (near[1:2, :] - target_y) ** 2
-            distance_sq = distance_sq + (near[2:3, :] - target_z) ** 2
-            kernel_block = 1.0 / (1.0 + distance_sq)
-            out_ref[...] += lax.dot_general(
-                probes_ref[source], kernel_block, (((1,), (1,)), ((), ())),
-                precision=lax.Precision.HIGH, preferred_element_type=jnp.float32,
-            )
+            gather_into(source, block(source))
 
 
 def near_field_call(slot_source, probe_tiles, coord_tiles, points, kernel_scale):
@@ -112,7 +137,7 @@
     slots = slot_source.shape[0] // boxes
     stretch = kernel_scale**0.5
     return pl.pallas_call(
-        functools.partial(near_kernel, kernel_scale, slots),
+        functools.partial(near_kernel, slots, W),
         out_shape=jax.ShapeDtypeStruct((rows, boxes * size), jnp.float32),
         grid_spec=pltpu.PrefetchScalarGridSpec(
             num_scalar_prefetch=1,
@@ -122,7 +147,7 @@
                 pl.BlockSpec((tiles, 3, size), lambda b, s: (0, 0, 0)),
                 pl.BlockSpec((size, 3), lambda b, s: (b, 0)),
             ],
-            out_specs=pl.BlockSpec((rows, size), lambda b, s: (0, b)),
+            out_specs=pl.BlockSpec((rows, boxes * size), lambda b, s: (0, 0)),
         ),
         compiler_params=pltpu.CompilerParams(dimension_semantics=("arbitrary",)),
         cost_estimate=pl.CostEstimate(

time: 166 us -> 161 us (0.970)
  the two profiles are of different devices: /device:TPU:53 before, /device:TPU:14 now
where the time goes in v11:
time: 161 us; the launch traced here: 160 us
  Pallas kernels  67.3 us (42%)
  matrix products  35 us (22%)
  local copies, waits for them, and re-layouts  27 us (17%)
  between operations  16.7 us (10%)
  other arithmetic  13.7 us (9%)
    pallas_call x1, Pallas kernels, near_field_call(): pl.pallas_call(functools.partial(near_kernel, slots, W), out_shape=jax.Sh...  51.1 us
    pallas_call x1, Pallas kernels, exchange_halo(): pl.pallas_call(halo_kernel, out_shape=(shape, shape), in_specs=[vmem, vme...  16.2 us
    dot_general x1, matrix products, body(): jnp.einsum('qnr,nrs->qns', source_moment, kernel_block, precision=PRECISE)  10 us
    dot_general x5, matrix products, body(): jnp.einsum('qns,nrs->qnr', jnp.repeat(descent, 2, axis=1), transfer_maps[...  7.14 us
    unnamed x303, local copies, waits for them, and re-layouts  5.69 us
    dot_general x5, matrix products, body(): jnp.einsum('qnr,nrs->qns', level_moments[-1], interp_map, precision=PRECISE)  5.15 us
    reduce_sum x7, other arithmetic, interpolation(): return values / jnp.sum(values, axis=-1, keepdims=True)  4.31 us
    dot_general x5, matrix products, body(): jnp.einsum('qns,nrs->qnr', descent, own_edges[height], precision=PRECISE)  3.82 us
  transfers between devices with their start and end apart: 1, of which 0 were waited for; matrix products, arithmetic and copies ran while one was open for 20% of the time, Pallas kernels for 42%

profile of v11, /device:TPU:14, one launch (start us, length us, event | category | flops | bytes accessed | tf_op | source)
XLA Modules:
  0.0 159.8 jit_solution(14973908419855169559)
XLA Ops:
  6.5 1.2 reshape.3427
  7.9 0.9 reshape.3420
  9.0 0.9 slice_reduce_fusion.10
  10.1 1.3 slice_reduce_fusion.2
  11.6 1.1 divide_reduce_fusion
  12.7 3.3 %constant_dynamic-update-slice_fusion.6 = (f32[8,62,64]{2,0,1:T(8,128)S(1)}, f32[8,32,64]{2,0,1:T(8,128)S(1)}) fusion(f32[8,32,256]{2,0,1:T(8,128)S(1)} %bitcast.410, f32[32,256]{1,0:T(8,128)S(1)} %divide_reduce_fusion, f32[32,64]{1,0:T(8,128)S(1)} %sub.1273, f32[32,256]{1,0:T(8,128)S(1)} %sub.1271, f32[32,64]{1,0:T(8,128)S(1)} %sub.1268, ...), kind=kOutput, calls=%fused_computation.98 | convolution fusion | flops 56623104 | bytes 679936 | tf_op jit(solution)/shard_map/qbp,bpr->qbr/dot_general | solution.py:189
  16.1 1.4 divide_reduce_fusion.1
  17.5 2.6 %bitcast_reduce_fusion = f32[8,16,64]{2,0,1:T(8,128)S(1)} fusion(f32[8,32,64]{2,0,1:T(8,128)S(1)} %get-tuple-element.124, f32[32,64]{1,0:T(8,128)S(1)} %divide_reduce_fusion.1, f32[32,64]{1,0:T(8,128)S(1)} %bitcast.428, f32[32,64]{1,0:T(8,128)S(1)} %sub.1273, f32[32,64]{1,0:T(8,128)S(1)} %bitcast.425, f32[32,64]{1,0:T(8,128)S(1)} %sub.1268, ...), kind=kOutput, calls=%fused_computation.75 | convolution fusion | flops 14163968 | bytes 155648 | tf_op jit(solution)/shard_map/qnr,nrs->qns/dot_general | solution.py:196
  20.2 0.7 divide_reduce_fusion.2
  20.9 1.3 bitcast_reduce_fusion.1
  22.3 0.4 divide_reduce_fusion.3
  22.8 0.6 copy-done.113
  23.4 0.6 bitcast_reduce_fusion.2
  24.5 0.4 bitcast_reduce_fusion.3
  25.3 0.3 copy-done.131
  25.6 0.6 copy-done.134
  26.1 0.3 constant_dynamic-update-slice_fusion.11
  26.6 0.4 fusion.53
  28.3 0.6 copy-done.54
  30.0 0.6 slice.610
  30.6 0.6 slice.612
  31.2 0.6 bitcast_convert_fusion
  31.9 0.6 copy-done.5
  32.9 0.7 broadcast_multiply_fusion
  33.6 0.9 pad_maximum_fusion.2
  34.6 16.2 %shard_map.73 = (f32[11,4736]{1,0:T(8,128)}, f32[11,4736]{1,0:T(8,128)}) custom-call(f32[11,4736]{1,0:T(8,128)} %get-tuple-element.43.to_right, f32[11,4736]{1,0:T(8,128)} %get-tuple-element.42.to_left), custom_call_target="tpu_custom_call" | custom-call | tf_op jit(solution)/shard_map/pallas_call | solution.py:60
  50.8 1.0 slice.543
  52.8 0.5 compare_and_fusion
  53.3 1.1 pad_maximum_fusion
  54.4 0.9 gather_fusion
  55.4 0.3 select_bitcast_fusion
  56.4 10.0 %fusion.9 = f32[8,186,64]{2,0,1:T(8,128)S(1)} fusion(f32[186,64]{1,0:T(8,128)S(1)} %get-tuple-element.40, f32[186,64]{1,0:T(8,128)S(1)} %bitcast.417, f32[186,64]{1,0:T(8,128)S(1)} %get-tuple-element.41, f32[186,64]{1,0:T(8,128)S(1)} %bitcast.418, f32[186,64]{1,0:T(8,128)S(1)} %get-tuple-element.39, f32[186,64]{1,0:T(8,128)S(1)} %bitcast.419, ...), kind=kOutput, calls=%fused_computation.16 | convolution fusion | flops 81613824 | bytes 1733632 | tf_op jit(solution)/shard_map/qnr,nrs->qns/dot_general | solution.py:257
  66.6 0.9 slice.472
  67.5 0.8 slice.473
  68.3 0.6 reduce_sum.310
  68.9 0.6 reduce_sum.311
  69.5 0.6 reduce_sum.313
  70.1 0.7 reduce_sum.314
  70.9 0.8 slice.580
  71.7 0.6 reshape.3418.source_ref
  72.4 2.9 %copy.100 = f32[3,8192]{0,1:T(8,128)} copy(f32[3,8192]{1,0:T(4,128)S(1)} %copy-done.6) | data formatting | bytes 196608 | tf_op jit(solution)/shard_map/mul | solution.py:158
  75.3 1.0 constant_dynamic-slice_fusion.40
  76.3 0.9 constant_dynamic-slice_fusion.46
  77.3 0.7 maximum_multiply_fusion
  78.0 51.1 %shard_map.74 = f32[8,8192]{1,0:T(8,128)} custom-call(s32[192]{0:T(256)} %reshape.3418.source_ref, f32[38,8,256]{2,1,0:T(8,128)} %bitcast.409, f32[38,3,256]{2,1,0:T(4,128)} %bitcast.412, f32[8192,3]{1,0:T(8,128)} %bitcast.401), custom_call_target="tpu_custom_call" | custom-call | flops 352321536 | bytes 952320 | tf_op jit(solution)/shard_map/pallas_call | solution.py:139
  129.2 0.6 slice_bitcast_fusion.8
  129.8 0.6 slice_bitcast_fusion.7
  130.4 2.0 %fusion.216 = (f32[128,8,1,64]{3,1,0,2:T(8,128)S(1)}, f32[128,8,1,64]{3,1,0,2:T(8,128)S(1)}, f32[128,8,1,64]{3,1,0,2:T(8,128)S(1)}, f32[128,8,1,64]{3,1,0,2:T(8,...) fusion(f32[128,8,6,64]{3,1,0,2:T(8,128)} %bitcast.402), kind=kLoop, calls=%fused_computation.540 | loop fusion | bytes 3145728 | tf_op jit(solution)/shard_map/slice | solution.py:290
  132.4 0.8 reduce_sum.300
  133.2 0.7 constant_dynamic-update-slice_fusion.24
  133.9 0.7 constant_dynamic-update-slice_fusion.23
  134.6 0.7 constant_dynamic-update-slice_fusion.22
  135.9 1.6 %convolution_bitcast_fusion.3 = f32[8,16,64]{2,0,1:T(8,128)S(1)} fusion(f32[16,8,64]{2,1,0:T(8,128)S(1)} %constant_dynamic-update-slice_fusion.12, f32[16,64]{1,0:T(8,128)} %get-tuple-element.83, f32[16,64]{1,0:T(8,128)S(1)} %get-tuple-element.80, f32[16,64]{1,0:T(8,128)} %get-tuple-element.84, f32[16,64]{1,0:T(8,128)S(1)} %copy-done.88, ...), kind=kOutput, calls=%fused_computation.21 | convolution fusion | flops 7012352 | bytes 90112 | tf_op jit(solution)/shard_map/nqr,nrs->qns/dot_general | solution.py:304
  138.1 1.0 fusion.22
  139.1 0.9 fusion.20
  140.0 0.8 fusion.18
  140.8 0.9 fusion.16
  141.8 1.0 fusion.14
  142.9 0.5 fusion.13
  143.5 0.8 fusion.12
  144.4 1.6 %fusion.11 = f32[8,16,64]{2,0,1:T(8,128)S(1)} fusion(f32[8,16,64]{2,0,1:T(8,128)S(1)} %copy-done.34, f32[8,16,64]{2,0,1:T(8,128)S(1)} %bitcast.430, f32[16,64]{1,0:T(8,128)S(1)} %copy-done.80, f32[16,64]{1,0:T(8,128)S(1)} %bitcast.439, f32[16,64]{1,0:T(8,128)S(1)} %copy-done.24, f32[16,64]{1,0:T(8,128)S(1)} %bitcast.436, f32[16,64]{1,0:T(8,128)S(1)} %copy-done.26, ...), kind=kOutput, calls=%fused_computation.22 | convolution fusion | flops 7086080 | bytes 126976 | tf_op jit(solution)/shard_map/qns,nrs->qnr/dot_general | solution.py:319
  146.2 3.2 %fusion.10 = f32[8,32,64]{2,0,1:T(8,128)S(1)} fusion(f32[8,32,64]{2,0,1:T(8,128)S(1)} %copy-done.14, f32[8,32,64]{2,0,1:T(8,128)S(1)} %bitcast.416, f32[32,64]{1,0:T(8,128)S(1)} %copy-done.64, f32[32,64]{1,0:T(8,128)S(1)} %bitcast.429, f32[32,64]{1,0:T(8,128)S(1)} %copy-done.13, f32[32,64]{1,0:T(8,128)S(1)} %bitcast.426, f32[32,64]{1,0:T(8,128)S(1)} %copy-done.11, ...), kind=kOutput, calls=%fused_computation.19 | convolution fusion | flops 14172160 | bytes 253952 | tf_op jit(solution)/shard_map/qns,nrs->qnr/dot_general | solution.py:319
  149.5 2.7 %fusion.26 = f32[32,256,8]{1,2,0:T(8,128)S(1)} fusion(f32[8,32,64]{2,0,1:T(8,128)S(1)} %fusion.10, f32[32,256]{1,0:T(8,128)S(1)} %copy-done.49, f32[32,64]{1,0:T(8,128)S(1)} %copy-done.13, f32[32,256]{1,0:T(8,128)S(1)} %copy-done.20, f32[32,64]{1,0:T(8,128)S(1)} %copy-done.11, f32[32,256]{1,0:T(8,128)S(1)} %copy-done.18, f32[32,64]{1,0:T(8,128)S(1)} %sub.1263, ...), kind=kOutput, calls=%fused_computation.48 | convolution fusion | flops 56623104 | bytes 483328 | tf_op jit(solution)/shard_map/qbr,bpr->qbp/dot_general | solution.py:323
  152.2 0.7 add_add_fusion
  (417 shorter events, 6.2 us)
Async XLA Ops:
  6.5 6.1 %copy-start.3 = (f32[8,8192]{1,0:T(8,128)S(1)}, f32[8,8192]{1,0:T(8,128)}, u32[]{:S(2)}) copy-start(f32[8,8192]{1,0:T(8,128)} %param.7) | copy-start | bytes 786436
  6.5 123.8 %all-gather.3.cloned.1.call-start = ((), (), s32[]{:S(2)}) async-start(), calls=%async_computation | async-start | bytes 3170304 | tf_op jit(solution)/shard_map/all_gather | solution.py:285
  7.8 17.1 %copy-start.50 = (f32[3,8,64]{2,1,0:T(8,128)}, f32[3,8,64]{2,1,0:T(8,128)S(1)}, u32[]{:S(2)}) copy-start(f32[3,8,64]{2,1,0:T(8,128)S(1)} %slice.585) | copy-start | bytes 18436
  7.8 18.7 %copy-start.55 = (f32[3,4,64]{2,1,0:T(4,128)}, f32[3,4,64]{2,1,0:T(4,128)S(1)}, u32[]{:S(2)}) copy-start(f32[3,4,64]{2,1,0:T(4,128)S(1)} %slice.586) | copy-start | bytes 9220
  7.8 18.6 %copy-start.27 = (f32[3,32,64]{2,1,0:T(8,128)}, f32[3,32,64]{2,1,0:T(8,128)S(1)}, u32[]{:S(2)}) copy-start(f32[3,32,64]{2,1,0:T(8,128)S(1)} %slice.583) | copy-start | bytes 73732
  7.8 18.6 %copy-start.35 = (f32[3,16,64]{2,1,0:T(8,128)}, f32[3,16,64]{2,1,0:T(8,128)S(1)}, u32[]{:S(2)}) copy-start(f32[3,16,64]{2,1,0:T(8,128)S(1)} %slice.584) | copy-start | bytes 36868
  7.9 17.0 %copy-start.9 = (f32[3,128,64]{2,1,0:T(8,128)}, f32[3,128,64]{2,1,0:T(8,128)S(1)}, u32[]{:S(2)}) copy-start(f32[3,128,64]{2,1,0:T(8,128)S(1)} %slice.581) | copy-start | bytes 294916
  7.9 18.5 %copy-start.21 = (f32[3,64,64]{2,1,0:T(8,128)}, f32[3,64,64]{2,1,0:T(8,128)S(1)}, u32[]{:S(2)}) copy-start(f32[3,64,64]{2,1,0:T(8,128)S(1)} %slice.582) | copy-start | bytes 147460
  8.8 21.8 %copy-start.2 = (f32[3,30,64]{2,1,0:T(8,128)}, f32[3,30,64]{2,1,0:T(8,128)S(1)}, u32[]{:S(2)}) copy-start(f32[3,30,64]{2,1,0:T(8,128)S(1)} %reshape.3420) | copy-start | bytes 69124
  8.8 12.1 %copy-start.23 = (f32[16,64]{1,0:T(8,128)}, f32[16,64]{1,0:T(8,128)S(1)}, u32[]{:S(2)}) copy-start(f32[16,64]{1,0:T(8,128)S(1)} %get-tuple-element.77) | copy-start | bytes 12292
  8.8 12.1 %copy-start.25 = (f32[16,64]{1,0:T(8,128)}, f32[16,64]{1,0:T(8,128)S(1)}, u32[]{:S(2)}) copy-start(f32[16,64]{1,0:T(8,128)S(1)} %get-tuple-element.78) | copy-start | bytes 12292
  8.8 13.8 %copy-start.36 = (f32[8,64]{1,0:T(8,128)}, f32[8,64]{1,0:T(8,128)S(1)}, u32[]{:S(2)}) copy-start(f32[8,64]{1,0:T(8,128)S(1)} %get-tuple-element.73) | copy-start | bytes 6148
  8.8 13.8 %copy-start.38 = (f32[8,64]{1,0:T(8,128)}, f32[8,64]{1,0:T(8,128)S(1)}, u32[]{:S(2)}) copy-start(f32[8,64]{1,0:T(8,128)S(1)} %get-tuple-element.74) | copy-start | bytes 6148
  8.8 13.8 %copy-start.40 = (f32[8,64]{1,0:T(8,128)}, f32[8,64]{1,0:T(8,128)S(1)}, u32[]{:S(2)}) copy-start(f32[8,64]{1,0:T(8,128)S(1)} %get-tuple-element.75) | copy-start | bytes 6148
  8.9 15.6 %copy-start.57 = (f32[4,64]{1,0:T(4,128)}, f32[4,64]{1,0:T(4,128)S(1)}, u32[]{:S(2)}) copy-start(f32[4,64]{1,0:T(4,128)S(1)} %get-tuple-element.70) | copy-start | bytes 3076
  8.9 15.6 %copy-start.59 = (f32[4,64]{1,0:T(4,128)}, f32[4,64]{1,0:T(4,128)S(1)}, u32[]{:S(2)}) copy-start(f32[4,64]{1,0:T(4,128)S(1)} %get-tuple-element.71) | copy-start | bytes 3076
  8.9 15.6 %copy-start.61 = (f32[4,64]{1,0:T(4,128)}, f32[4,64]{1,0:T(4,128)S(1)}, u32[]{:S(2)}) copy-start(f32[4,64]{1,0:T(4,128)S(1)} %get-tuple-element.72) | copy-start | bytes 3076
  8.9 16.3 %copy-start.73 = (f32[2,64]{1,0:T(2,128)}, f32[2,64]{1,0:T(2,128)S(1)}, u32[]{:S(2)}) copy-start(f32[2,64]{1,0:T(2,128)S(1)} %get-tuple-element.67) | copy-start | bytes 1540
  8.9 16.3 %copy-start.75 = (f32[2,64]{1,0:T(2,128)}, f32[2,64]{1,0:T(2,128)S(1)}, u32[]{:S(2)}) copy-start(f32[2,64]{1,0:T(2,128)S(1)} %get-tuple-element.68) | copy-start | bytes 1540
  8.9 16.3 %copy-start.77 = (f32[2,64]{1,0:T(2,128)}, f32[2,64]{1,0:T(2,128)S(1)}, u32[]{:S(2)}) copy-start(f32[2,64]{1,0:T(2,128)S(1)} %get-tuple-element.69) | copy-start | bytes 1540
  10.1 7.4 %copy-start.10 = (f32[32,64]{1,0:T(8,128)}, f32[32,64]{1,0:T(8,128)S(1)}, u32[]{:S(2)}) copy-start(f32[32,64]{1,0:T(8,128)S(1)} %sub.1268) | copy-start | bytes 24580
  10.1 7.4 %copy-start.12 = (f32[32,64]{1,0:T(8,128)}, f32[32,64]{1,0:T(8,128)S(1)}, u32[]{:S(2)}) copy-start(f32[32,64]{1,0:T(8,128)S(1)} %sub.1273) | copy-start | bytes 24580
  24.1 5.5 %copy-start.22 = (f32[3,2048]{1,0:T(4,128)S(1)}, f32[3,2048]{1,0:T(4,128)}, u32[]{:S(2)}) copy-start(f32[3,2048]{1,0:T(4,128)} %param.10) | copy-start | bytes 73732
  24.1 5.7 %copy-start.72 = (s32[32,3]{0,1:T(4,128)S(1)}, s32[32,3]{0,1:T(4,128)}, u32[]{:S(2)}) copy-start(s32[32,3]{0,1:T(4,128)} %param.13) | copy-start | bytes 1156
  24.1 5.9 %copy-start.81 = (f32[2,2,64]{2,1,0:T(2,128)}, f32[2,2,64]{2,1,0:T(2,128)S(1)}, u32[]{:S(2)}) copy-start(f32[2,2,64]{2,1,0:T(2,128)S(1)} %broadcast_in_dim.132) | copy-start | bytes 3076
  24.1 5.9 %copy-start.83 = (f32[2,2,64]{2,1,0:T(2,128)}, f32[2,2,64]{2,1,0:T(2,128)S(1)}, u32[]{:S(2)}) copy-start(f32[2,2,64]{2,1,0:T(2,128)S(1)} %broadcast_in_dim.134) | copy-start | bytes 3076
  24.2 5.9 %copy-start.85 = (f32[2,2,64]{2,1,0:T(2,128)}, f32[2,2,64]{2,1,0:T(2,128)S(1)}, u32[]{:S(2)}) copy-start(f32[2,2,64]{2,1,0:T(2,128)S(1)} %broadcast_in_dim.136) | copy-start | bytes 3076
  26.5 6.1 %copy-start.89 = (f32[64]{0:T(128)}, f32[64]{0:T(128)S(1)}, u32[]{:S(2)}) copy-start(f32[64]{0:T(128)S(1)} %get-tuple-element.57) | copy-start | bytes 772
  26.5 6.1 %copy-start.91 = (f32[64]{0:T(128)}, f32[64]{0:T(128)S(1)}, u32[]{:S(2)}) copy-start(f32[64]{0:T(128)S(1)} %get-tuple-element.58) | copy-start | bytes 772
  26.5 6.1 %copy-start.93 = (f32[64]{0:T(128)}, f32[64]{0:T(128)S(1)}, u32[]{:S(2)}) copy-start(f32[64]{0:T(128)S(1)} %get-tuple-element.59) | copy-start | bytes 772
  27.0 5.6 %copy-start.136 = (f32[64]{0:T(128)}, f32[64]{0:T(128)S(1)}, u32[]{:S(2)}) copy-start(f32[64]{0:T(128)S(1)} %get-tuple-element.23) | copy-start | bytes 772
  27.0 5.6 %copy-start.137 = (f32[64]{0:T(128)}, f32[64]{0:T(128)S(1)}, u32[]{:S(2)}) copy-start(f32[64]{0:T(128)S(1)} %get-tuple-element.22) | copy-start | bytes 772
  27.0 5.6 %copy-start.139 = (f32[64]{0:T(128)}, f32[64]{0:T(128)S(1)}, u32[]{:S(2)}) copy-start(f32[64]{0:T(128)S(1)} %get-tuple-element.20) | copy-start | bytes 772
  27.0 5.6 %copy-start.140 = (f32[64]{0:T(128)}, f32[64]{0:T(128)S(1)}, u32[]{:S(2)}) copy-start(f32[64]{0:T(128)S(1)} %get-tuple-element.24) | copy-start | bytes 772
  33.6 18.6 %copy-start = (f32[11,8192]{1,0:T(8,128)}, f32[11,8192]{1,0:T(8,128)S(1)}, u32[]{:S(2)}) copy-start(f32[11,8192]{1,0:T(8,128)S(1)} %get-tuple-element.52) | copy-start | bytes 1081348
  66.5 5.1 %copy-start.115 = (s32[32,6]{0,1:T(8,128)S(1)}, s32[32,6]{0,1:T(8,128)}, u32[]{:S(2)}) copy-start(s32[32,6]{0,1:T(8,128)} %param.9) | copy-start | bytes 2308
  66.5 5.8 %copy-start.6 = (f32[3,8192]{1,0:T(4,128)S(1)}, f32[3,8192]{1,0:T(4,128)}, u32[]{:S(2)}) copy-start(f32[3,8192]{1,0:T(4,128)} %get-tuple-element.51) | copy-start | bytes 294916
  135.8 5.0 %copy-start.119 = (f32[64]{0:T(128)S(1)}, f32[64]{0:T(128)}, u32[]{:S(2)}) copy-start(f32[64]{0:T(128)} %copy-done.118) | copy-start | bytes 772
  135.8 5.9 %copy-start.74 = (f32[2,64]{1,0:T(2,128)S(1)}, f32[2,64]{1,0:T(2,128)}, u32[]{:S(2)}) copy-start(f32[2,64]{1,0:T(2,128)} %copy-done.73) | copy-start | bytes 1540
  135.8 6.0 %copy-start.76 = (f32[2,64]{1,0:T(2,128)S(1)}, f32[2,64]{1,0:T(2,128)}, u32[]{:S(2)}) copy-start(f32[2,64]{1,0:T(2,128)} %copy-done.75) | copy-start | bytes 1540
  135.8 6.0 %copy-start.78 = (f32[2,64]{1,0:T(2,128)S(1)}, f32[2,64]{1,0:T(2,128)}, u32[]{:S(2)}) copy-start(f32[2,64]{1,0:T(2,128)} %copy-done.77) | copy-start | bytes 1540
  135.8 6.0 %copy-start.87 = (f32[8,2,64]{2,0,1:T(8,128)S(1)}, f32[8,2,64]{2,0,1:T(8,128)}, u32[]{:S(2)}) copy-start(f32[8,2,64]{2,0,1:T(8,128)} %reduce_sum.310) | copy-start | bytes 12292
  135.8 7.0 %copy-start.58 = (f32[4,64]{1,0:T(4,128)S(1)}, f32[4,64]{1,0:T(4,128)}, u32[]{:S(2)}) copy-start(f32[4,64]{1,0:T(4,128)} %copy-done.57) | copy-start | bytes 3076
  135.9 7.0 %copy-start.60 = (f32[4,64]{1,0:T(4,128)S(1)}, f32[4,64]{1,0:T(4,128)}, u32[]{:S(2)}) copy-start(f32[4,64]{1,0:T(4,128)} %copy-done.59) | copy-start | bytes 3076
  135.9 7.0 %copy-start.62 = (f32[4,64]{1,0:T(4,128)S(1)}, f32[4,64]{1,0:T(4,128)}, u32[]{:S(2)}) copy-start(f32[4,64]{1,0:T(4,128)} %copy-done.61) | copy-start | bytes 3076
  135.9 7.0 %copy-start.71 = (f32[8,4,64]{2,0,1:T(8,128)S(1)}, f32[8,4,64]{2,0,1:T(8,128)}, u32[]{:S(2)}) copy-start(f32[8,4,64]{2,0,1:T(8,128)} %reduce_sum.311) | copy-start | bytes 24580
  135.9 7.0 %copy-start.82 = (f32[2,2,64]{2,1,0:T(2,128)S(1)}, f32[2,2,64]{2,1,0:T(2,128)}, u32[]{:S(2)}) copy-start(f32[2,2,64]{2,1,0:T(2,128)} %copy-done.81) | copy-start | bytes 3076
  135.9 7.0 %copy-start.84 = (f32[2,2,64]{2,1,0:T(2,128)S(1)}, f32[2,2,64]{2,1,0:T(2,128)}, u32[]{:S(2)}) copy-start(f32[2,2,64]{2,1,0:T(2,128)} %copy-done.83) | copy-start | bytes 3076
  135.9 7.0 %copy-start.86 = (f32[2,2,64]{2,1,0:T(2,128)S(1)}, f32[2,2,64]{2,1,0:T(2,128)}, u32[]{:S(2)}) copy-start(f32[2,2,64]{2,1,0:T(2,128)} %copy-done.85) | copy-start | bytes 3076
  135.9 7.0 %copy-start.117 = (f32[4,64]{1,0:T(4,128)S(1)}, f32[4,64]{1,0:T(4,128)}, u32[]{:S(2)}) copy-start(f32[4,64]{1,0:T(4,128)} %copy-done.116) | copy-start | bytes 3076
  137.6 5.8 %copy-start.37 = (f32[8,64]{1,0:T(8,128)S(1)}, f32[8,64]{1,0:T(8,128)}, u32[]{:S(2)}) copy-start(f32[8,64]{1,0:T(8,128)} %copy-done.36) | copy-start | bytes 6148
  137.6 5.8 %copy-start.39 = (f32[8,64]{1,0:T(8,128)S(1)}, f32[8,64]{1,0:T(8,128)}, u32[]{:S(2)}) copy-start(f32[8,64]{1,0:T(8,128)} %copy-done.38) | copy-start | bytes 6148
  137.6 5.8 %copy-start.41 = (f32[8,64]{1,0:T(8,128)S(1)}, f32[8,64]{1,0:T(8,128)}, u32[]{:S(2)}) copy-start(f32[8,64]{1,0:T(8,128)} %copy-done.40) | copy-start | bytes 6148
  137.6 5.8 %copy-start.66 = (f32[4,2,64]{2,1,0:T(2,128)S(1)}, f32[4,2,64]{2,1,0:T(2,128)}, u32[]{:S(2)}) copy-start(f32[4,2,64]{2,1,0:T(2,128)} %copy-done.65) | copy-start | bytes 6148
  137.6 5.8 %copy-start.68 = (f32[4,2,64]{2,1,0:T(2,128)S(1)}, f32[4,2,64]{2,1,0:T(2,128)}, u32[]{:S(2)}) copy-start(f32[4,2,64]{2,1,0:T(2,128)} %copy-done.67) | copy-start | bytes 6148
  137.6 5.8 %copy-start.70 = (f32[4,2,64]{2,1,0:T(2,128)S(1)}, f32[4,2,64]{2,1,0:T(2,128)}, u32[]{:S(2)}) copy-start(f32[4,2,64]{2,1,0:T(2,128)} %copy-done.69) | copy-start | bytes 6148
  137.6 5.8 %copy-start.114 = (f32[8,64]{1,0:T(8,128)S(1)}, f32[8,64]{1,0:T(8,128)}, u32[]{:S(2)}) copy-start(f32[8,64]{1,0:T(8,128)} %copy-done.113) | copy-start | bytes 6148
  138.0 6.3 %copy-start.24 = (f32[16,64]{1,0:T(8,128)S(1)}, f32[16,64]{1,0:T(8,128)}, u32[]{:S(2)}) copy-start(f32[16,64]{1,0:T(8,128)} %copy-done.23) | copy-start | bytes 12292
  138.0 6.3 %copy-start.26 = (f32[16,64]{1,0:T(8,128)S(1)}, f32[16,64]{1,0:T(8,128)}, u32[]{:S(2)}) copy-start(f32[16,64]{1,0:T(8,128)} %copy-done.25) | copy-start | bytes 12292
  138.0 6.3 %copy-start.34 = (f32[8,16,64]{2,0,1:T(8,128)S(1)}, f32[8,16,64]{2,0,1:T(8,128)}, u32[]{:S(2)}) copy-start(f32[8,16,64]{2,0,1:T(8,128)} %reduce_sum.313) | copy-start | bytes 98308
  138.0 6.3 %copy-start.43 = (f32[8,2,64]{2,1,0:T(2,128)S(1)}, f32[8,2,64]{2,1,0:T(2,128)}, u32[]{:S(2)}) copy-start(f32[8,2,64]{2,1,0:T(2,128)} %copy-done.42) | copy-start | bytes 12292
  138.0 6.3 %copy-start.45 = (f32[8,2,64]{2,1,0:T(2,128)S(1)}, f32[8,2,64]{2,1,0:T(2,128)}, u32[]{:S(2)}) copy-start(f32[8,2,64]{2,1,0:T(2,128)} %copy-done.44) | copy-start | bytes 12292
  138.1 6.3 %copy-start.47 = (f32[8,2,64]{2,1,0:T(2,128)S(1)}, f32[8,2,64]{2,1,0:T(2,128)}, u32[]{:S(2)}) copy-start(f32[8,2,64]{2,1,0:T(2,128)} %copy-done.46) | copy-start | bytes 12292
  138.1 6.3 %copy-start.80 = (f32[16,64]{1,0:T(8,128)S(1)}, f32[16,64]{1,0:T(8,128)}, u32[]{:S(2)}) copy-start(f32[16,64]{1,0:T(8,128)} %copy-done.79) | copy-start | bytes 12292
  (84 other events, 210.2 us)
Sparse Core Ops, SparseCore 0:
  29.0 87.6 all-gather.2

commit v12 on v11

--- a/solution.py
+++ b/solution.py
@@ -123,10 +123,44 @@
             preferred_element_type=jnp.float32,
         )
 
+    def lists(row, tile):
+        found = source_ref[row * slots] == tile
+        for k in range(1, slots):
+            found = found | (source_ref[row * slots + k] == tile)
+        return found
+
+    even = lax.rem(box, 2) == 0
+    shared = []
+    for step, allowed in ((2, True), (3, even)):
+        partner = jnp.minimum(box + step, boxes - 1)
+        shared.append(
+            allowed & (box + step < boxes) & lists(box, here + step) & lists(partner, here)
+        )
+    skipped = []
+    for step, allowed in ((2, True), (3, jnp.logical_not(even))):
+        partner = jnp.maximum(box - step, 0)
+        skipped.append(
+            allowed & (box - step >= 0) & lists(box, here - step) & lists(partner, here)
+        )
+    for step, flag in zip((2, 3), shared):
+
+        @pl.when(flag)
+        def _():
+            kernel_block = block(here + step)
+            gather_into(here + step, kernel_block)
+            later = pl.ds(pl.multiple_of((box + step) * size, size), size)
+            out_ref[:, later] += jnp.dot(
+                probes_ref[here], kernel_block, precision=lax.Precision.HIGH,
+                preferred_element_type=jnp.float32,
+            )
+
     for slot in range(slots):
         source = source_ref[box * slots + slot]
-
-        @pl.when((source >= 0) & (source != here - 1) & (source != here) & (source != here + 1))
+        done = (source == here - 1) | (source == here) | (source == here + 1)
+        done = done | ((source == here + 2) & shared[0]) | ((source == here + 3) & shared[1])
+        done = done | ((source == here - 2) & skipped[0]) | ((source == here - 3) & skipped[1])
+
+        @pl.when((source >= 0) & jnp.logical_not(done))
         def _():
             gather_into(source, block(source))
 

time: 161 us -> 157 us (0.975)
  the two profiles are of different devices: /device:TPU:14 before, /device:TPU:6 now
where the time goes in v12:
time: 157 us; the launch traced here: 156 us
  Pallas kernels  63.2 us (40%)
  matrix products  35 us (22%)
  local copies, waits for them, and re-layouts  26.9 us (17%)
  between operations  16.7 us (11%)
  other arithmetic  13.7 us (9%)
    pallas_call x1, Pallas kernels, near_field_call(): pl.pallas_call(functools.partial(near_kernel, slots, W), out_shape=jax.Sh...  44.1 us
    pallas_call x1, Pallas kernels, exchange_halo(): pl.pallas_call(halo_kernel, out_shape=(shape, shape), in_specs=[vmem, vme...  19.2 us
    dot_general x1, matrix products, body(): jnp.einsum('qnr,nrs->qns', source_moment, kernel_block, precision=PRECISE)  10 us
    dot_general x5, matrix products, body(): jnp.einsum('qns,nrs->qnr', jnp.repeat(descent, 2, axis=1), transfer_maps[...  7.14 us
    unnamed x303, local copies, waits for them, and re-layouts  5.67 us
    dot_general x5, matrix products, body(): jnp.einsum('qnr,nrs->qns', level_moments[-1], interp_map, precision=PRECISE)  5.15 us
    reduce_sum x7, other arithmetic, interpolation(): return values / jnp.sum(values, axis=-1, keepdims=True)  4.31 us
    dot_general x5, matrix products, body(): jnp.einsum('qns,nrs->qnr', descent, own_edges[height], precision=PRECISE)  3.82 us
  transfers between devices with their start and end apart: 1, of which 0 were waited for; matrix products, arithmetic and copies ran while one was open for 20% of the time, Pallas kernels for 41%

profile of v12, /device:TPU:6, one launch (start us, length us, event | category | flops | bytes accessed | tf_op | source)
XLA Modules:
  0.0 155.6 jit_solution(2264607878745069980)
XLA Ops:
  6.5 1.2 reshape.3427
  7.9 0.9 reshape.3420
  9.0 0.9 slice_reduce_fusion.10
  10.1 1.3 slice_reduce_fusion.2
  11.6 1.1 divide_reduce_fusion
  12.7 3.3 %constant_dynamic-update-slice_fusion.6 = (f32[8,62,64]{2,0,1:T(8,128)S(1)}, f32[8,32,64]{2,0,1:T(8,128)S(1)}) fusion(f32[8,32,256]{2,0,1:T(8,128)S(1)} %bitcast.410, f32[32,256]{1,0:T(8,128)S(1)} %divide_reduce_fusion, f32[32,64]{1,0:T(8,128)S(1)} %sub.1273, f32[32,256]{1,0:T(8,128)S(1)} %sub.1271, f32[32,64]{1,0:T(8,128)S(1)} %sub.1268, ...), kind=kOutput, calls=%fused_computation.98 | convolution fusion | flops 56623104 | bytes 679936 | tf_op jit(solution)/shard_map/qbp,bpr->qbr/dot_general | solution.py:223
  16.1 1.4 divide_reduce_fusion.1
  17.5 2.6 %bitcast_reduce_fusion = f32[8,16,64]{2,0,1:T(8,128)S(1)} fusion(f32[8,32,64]{2,0,1:T(8,128)S(1)} %get-tuple-element.124, f32[32,64]{1,0:T(8,128)S(1)} %divide_reduce_fusion.1, f32[32,64]{1,0:T(8,128)S(1)} %bitcast.428, f32[32,64]{1,0:T(8,128)S(1)} %sub.1273, f32[32,64]{1,0:T(8,128)S(1)} %bitcast.425, f32[32,64]{1,0:T(8,128)S(1)} %sub.1268, ...), kind=kOutput, calls=%fused_computation.75 | convolution fusion | flops 14163968 | bytes 155648 | tf_op jit(solution)/shard_map/qnr,nrs->qns/dot_general | solution.py:230
  20.2 0.7 divide_reduce_fusion.2
  20.9 1.3 bitcast_reduce_fusion.1
  22.3 0.4 divide_reduce_fusion.3
  22.8 0.6 copy-done.113
  23.4 0.6 bitcast_reduce_fusion.2
  24.5 0.4 bitcast_reduce_fusion.3
  25.3 0.3 copy-done.131
  25.6 0.6 copy-done.134
  26.1 0.3 constant_dynamic-update-slice_fusion.11
  26.6 0.4 fusion.53
  28.3 0.6 copy-done.54
  30.0 0.6 slice.610
  30.6 0.6 slice.612
  31.2 0.6 bitcast_convert_fusion
  31.9 0.6 copy-done.5
  32.9 0.7 broadcast_multiply_fusion
  33.6 0.9 pad_maximum_fusion.2
  34.6 19.2 %shard_map.73 = (f32[11,4736]{1,0:T(8,128)}, f32[11,4736]{1,0:T(8,128)}) custom-call(f32[11,4736]{1,0:T(8,128)} %get-tuple-element.43.to_right, f32[11,4736]{1,0:T(8,128)} %get-tuple-element.42.to_left), custom_call_target="tpu_custom_call" | custom-call | tf_op jit(solution)/shard_map/pallas_call | solution.py:60
  53.8 1.0 slice.543
  55.8 0.5 compare_and_fusion
  56.4 1.1 pad_maximum_fusion
  57.4 0.9 gather_fusion
  58.4 0.3 select_bitcast_fusion
  59.4 10.0 %fusion.9 = f32[8,186,64]{2,0,1:T(8,128)S(1)} fusion(f32[186,64]{1,0:T(8,128)S(1)} %get-tuple-element.40, f32[186,64]{1,0:T(8,128)S(1)} %bitcast.417, f32[186,64]{1,0:T(8,128)S(1)} %get-tuple-element.41, f32[186,64]{1,0:T(8,128)S(1)} %bitcast.418, f32[186,64]{1,0:T(8,128)S(1)} %get-tuple-element.39, f32[186,64]{1,0:T(8,128)S(1)} %bitcast.419, ...), kind=kOutput, calls=%fused_computation.16 | convolution fusion | flops 81613824 | bytes 1733632 | tf_op jit(solution)/shard_map/qnr,nrs->qns/dot_general | solution.py:291
  69.6 0.9 slice.472
  70.5 0.8 slice.473
  71.3 0.6 reduce_sum.310
  71.9 0.6 reduce_sum.311
  72.5 0.6 reduce_sum.313
  73.2 0.7 reduce_sum.314
  73.9 0.8 slice.580
  74.8 0.6 reshape.3418.source_ref
  75.4 2.9 %copy.100 = f32[3,8192]{0,1:T(8,128)} copy(f32[3,8192]{1,0:T(4,128)S(1)} %copy-done.6) | data formatting | bytes 196608 | tf_op jit(solution)/shard_map/mul | solution.py:192
  78.3 0.9 constant_dynamic-slice_fusion.40
  79.2 0.9 constant_dynamic-slice_fusion.46
  80.3 0.7 maximum_multiply_fusion
  81.0 44.1 %shard_map.74 = f32[8,8192]{1,0:T(8,128)} custom-call(s32[192]{0:T(256)} %reshape.3418.source_ref, f32[38,8,256]{2,1,0:T(8,128)} %bitcast.409, f32[38,3,256]{2,1,0:T(4,128)} %bitcast.412, f32[8192,3]{1,0:T(8,128)} %bitcast.401), custom_call_target="tpu_custom_call" | custom-call | flops 352321536 | bytes 952320 | tf_op jit(solution)/shard_map/pallas_call | solution.py:173
  125.0 0.6 slice_bitcast_fusion.8
  125.6 0.6 slice_bitcast_fusion.7
  126.2 2.0 %fusion.216 = (f32[128,8,1,64]{3,1,0,2:T(8,128)S(1)}, f32[128,8,1,64]{3,1,0,2:T(8,128)S(1)}, f32[128,8,1,64]{3,1,0,2:T(8,128)S(1)}, f32[128,8,1,64]{3,1,0,2:T(8,...) fusion(f32[128,8,6,64]{3,1,0,2:T(8,128)} %bitcast.402), kind=kLoop, calls=%fused_computation.540 | loop fusion | bytes 3145728 | tf_op jit(solution)/shard_map/slice | solution.py:324
  128.3 0.8 reduce_sum.300
  129.1 0.7 constant_dynamic-update-slice_fusion.24
  129.7 0.7 constant_dynamic-update-slice_fusion.23
  130.4 0.7 constant_dynamic-update-slice_fusion.22
  131.8 1.6 %convolution_bitcast_fusion.3 = f32[8,16,64]{2,0,1:T(8,128)S(1)} fusion(f32[16,8,64]{2,1,0:T(8,128)S(1)} %constant_dynamic-update-slice_fusion.12, f32[16,64]{1,0:T(8,128)} %get-tuple-element.83, f32[16,64]{1,0:T(8,128)S(1)} %get-tuple-element.80, f32[16,64]{1,0:T(8,128)} %get-tuple-element.84, f32[16,64]{1,0:T(8,128)S(1)} %copy-done.88, ...), kind=kOutput, calls=%fused_computation.21 | convolution fusion | flops 7012352 | bytes 90112 | tf_op jit(solution)/shard_map/nqr,nrs->qns/dot_general | solution.py:338
  133.9 1.0 fusion.22
  134.9 0.9 fusion.20
  135.8 0.8 fusion.18
  136.7 0.9 fusion.16
  137.6 1.0 fusion.14
  138.7 0.5 fusion.13
  139.3 0.8 fusion.12
  140.3 1.6 %fusion.11 = f32[8,16,64]{2,0,1:T(8,128)S(1)} fusion(f32[8,16,64]{2,0,1:T(8,128)S(1)} %copy-done.34, f32[8,16,64]{2,0,1:T(8,128)S(1)} %bitcast.430, f32[16,64]{1,0:T(8,128)S(1)} %copy-done.80, f32[16,64]{1,0:T(8,128)S(1)} %bitcast.439, f32[16,64]{1,0:T(8,128)S(1)} %copy-done.24, f32[16,64]{1,0:T(8,128)S(1)} %bitcast.436, f32[16,64]{1,0:T(8,128)S(1)} %copy-done.26, ...), kind=kOutput, calls=%fused_computation.22 | convolution fusion | flops 7086080 | bytes 126976 | tf_op jit(solution)/shard_map/qns,nrs->qnr/dot_general | solution.py:353
  142.0 3.2 %fusion.10 = f32[8,32,64]{2,0,1:T(8,128)S(1)} fusion(f32[8,32,64]{2,0,1:T(8,128)S(1)} %copy-done.14, f32[8,32,64]{2,0,1:T(8,128)S(1)} %bitcast.416, f32[32,64]{1,0:T(8,128)S(1)} %copy-done.64, f32[32,64]{1,0:T(8,128)S(1)} %bitcast.429, f32[32,64]{1,0:T(8,128)S(1)} %copy-done.13, f32[32,64]{1,0:T(8,128)S(1)} %bitcast.426, f32[32,64]{1,0:T(8,128)S(1)} %copy-done.11, ...), kind=kOutput, calls=%fused_computation.19 | convolution fusion | flops 14172160 | bytes 253952 | tf_op jit(solution)/shard_map/qns,nrs->qnr/dot_general | solution.py:353
  145.3 2.7 %fusion.26 = f32[32,256,8]{1,2,0:T(8,128)S(1)} fusion(f32[8,32,64]{2,0,1:T(8,128)S(1)} %fusion.10, f32[32,256]{1,0:T(8,128)S(1)} %copy-done.49, f32[32,64]{1,0:T(8,128)S(1)} %copy-done.13, f32[32,256]{1,0:T(8,128)S(1)} %copy-done.20, f32[32,64]{1,0:T(8,128)S(1)} %copy-done.11, f32[32,256]{1,0:T(8,128)S(1)} %copy-done.18, f32[32,64]{1,0:T(8,128)S(1)} %sub.1263, ...), kind=kOutput, calls=%fused_computation.48 | convolution fusion | flops 56623104 | bytes 483328 | tf_op jit(solution)/shard_map/qbr,bpr->qbp/dot_general | solution.py:357
  148.0 0.7 add_add_fusion
  (417 shorter events, 6.2 us)
Async XLA Ops:
  6.5 6.1 %copy-start.3 = (f32[8,8192]{1,0:T(8,128)S(1)}, f32[8,8192]{1,0:T(8,128)}, u32[]{:S(2)}) copy-start(f32[8,8192]{1,0:T(8,128)} %param.7) | copy-start | bytes 786436
  6.5 119.7 %all-gather.3.cloned.1.call-start = ((), (), s32[]{:S(2)}) async-start(), calls=%async_computation | async-start | bytes 3170304 | tf_op jit(solution)/shard_map/all_gather | solution.py:319
  7.8 17.1 %copy-start.50 = (f32[3,8,64]{2,1,0:T(8,128)}, f32[3,8,64]{2,1,0:T(8,128)S(1)}, u32[]{:S(2)}) copy-start(f32[3,8,64]{2,1,0:T(8,128)S(1)} %slice.585) | copy-start | bytes 18436
  7.8 18.7 %copy-start.55 = (f32[3,4,64]{2,1,0:T(4,128)}, f32[3,4,64]{2,1,0:T(4,128)S(1)}, u32[]{:S(2)}) copy-start(f32[3,4,64]{2,1,0:T(4,128)S(1)} %slice.586) | copy-start | bytes 9220
  7.8 18.6 %copy-start.27 = (f32[3,32,64]{2,1,0:T(8,128)}, f32[3,32,64]{2,1,0:T(8,128)S(1)}, u32[]{:S(2)}) copy-start(f32[3,32,64]{2,1,0:T(8,128)S(1)} %slice.583) | copy-start | bytes 73732
  7.8 18.6 %copy-start.35 = (f32[3,16,64]{2,1,0:T(8,128)}, f32[3,16,64]{2,1,0:T(8,128)S(1)}, u32[]{:S(2)}) copy-start(f32[3,16,64]{2,1,0:T(8,128)S(1)} %slice.584) | copy-start | bytes 36868
  7.9 17.0 %copy-start.9 = (f32[3,128,64]{2,1,0:T(8,128)}, f32[3,128,64]{2,1,0:T(8,128)S(1)}, u32[]{:S(2)}) copy-start(f32[3,128,64]{2,1,0:T(8,128)S(1)} %slice.581) | copy-start | bytes 294916
  7.9 18.5 %copy-start.21 = (f32[3,64,64]{2,1,0:T(8,128)}, f32[3,64,64]{2,1,0:T(8,128)S(1)}, u32[]{:S(2)}) copy-start(f32[3,64,64]{2,1,0:T(8,128)S(1)} %slice.582) | copy-start | bytes 147460
  8.8 21.8 %copy-start.2 = (f32[3,30,64]{2,1,0:T(8,128)}, f32[3,30,64]{2,1,0:T(8,128)S(1)}, u32[]{:S(2)}) copy-start(f32[3,30,64]{2,1,0:T(8,128)S(1)} %reshape.3420) | copy-start | bytes 69124
  8.8 12.1 %copy-start.23 = (f32[16,64]{1,0:T(8,128)}, f32[16,64]{1,0:T(8,128)S(1)}, u32[]{:S(2)}) copy-start(f32[16,64]{1,0:T(8,128)S(1)} %get-tuple-element.77) | copy-start | bytes 12292
  8.8 12.1 %copy-start.25 = (f32[16,64]{1,0:T(8,128)}, f32[16,64]{1,0:T(8,128)S(1)}, u32[]{:S(2)}) copy-start(f32[16,64]{1,0:T(8,128)S(1)} %get-tuple-element.78) | copy-start | bytes 12292
  8.8 13.8 %copy-start.36 = (f32[8,64]{1,0:T(8,128)}, f32[8,64]{1,0:T(8,128)S(1)}, u32[]{:S(2)}) copy-start(f32[8,64]{1,0:T(8,128)S(1)} %get-tuple-element.73) | copy-start | bytes 6148
  8.8 13.8 %copy-start.38 = (f32[8,64]{1,0:T(8,128)}, f32[8,64]{1,0:T(8,128)S(1)}, u32[]{:S(2)}) copy-start(f32[8,64]{1,0:T(8,128)S(1)} %get-tuple-element.74) | copy-start | bytes 6148
  8.8 13.8 %copy-start.40 = (f32[8,64]{1,0:T(8,128)}, f32[8,64]{1,0:T(8,128)S(1)}, u32[]{:S(2)}) copy-start(f32[8,64]{1,0:T(8,128)S(1)} %get-tuple-element.75) | copy-start | bytes 6148
  8.9 15.6 %copy-start.57 = (f32[4,64]{1,0:T(4,128)}, f32[4,64]{1,0:T(4,128)S(1)}, u32[]{:S(2)}) copy-start(f32[4,64]{1,0:T(4,128)S(1)} %get-tuple-element.70) | copy-start | bytes 3076
  8.9 15.6 %copy-start.59 = (f32[4,64]{1,0:T(4,128)}, f32[4,64]{1,0:T(4,128)S(1)}, u32[]{:S(2)}) copy-start(f32[4,64]{1,0:T(4,128)S(1)} %get-tuple-element.71) | copy-start | bytes 3076
  8.9 15.6 %copy-start.61 = (f32[4,64]{1,0:T(4,128)}, f32[4,64]{1,0:T(4,128)S(1)}, u32[]{:S(2)}) copy-start(f32[4,64]{1,0:T(4,128)S(1)} %get-tuple-element.72) | copy-start | bytes 3076
  8.9 16.3 %copy-start.73 = (f32[2,64]{1,0:T(2,128)}, f32[2,64]{1,0:T(2,128)S(1)}, u32[]{:S(2)}) copy-start(f32[2,64]{1,0:T(2,128)S(1)} %get-tuple-element.67) | copy-start | bytes 1540
  8.9 16.3 %copy-start.75 = (f32[2,64]{1,0:T(2,128)}, f32[2,64]{1,0:T(2,128)S(1)}, u32[]{:S(2)}) copy-start(f32[2,64]{1,0:T(2,128)S(1)} %get-tuple-element.68) | copy-start | bytes 1540
  8.9 16.3 %copy-start.77 = (f32[2,64]{1,0:T(2,128)}, f32[2,64]{1,0:T(2,128)S(1)}, u32[]{:S(2)}) copy-start(f32[2,64]{1,0:T(2,128)S(1)} %get-tuple-element.69) | copy-start | bytes 1540
  10.1 7.4 %copy-start.10 = (f32[32,64]{1,0:T(8,128)}, f32[32,64]{1,0:T(8,128)S(1)}, u32[]{:S(2)}) copy-start(f32[32,64]{1,0:T(8,128)S(1)} %sub.1268) | copy-start | bytes 24580
  10.1 7.4 %copy-start.12 = (f32[32,64]{1,0:T(8,128)}, f32[32,64]{1,0:T(8,128)S(1)}, u32[]{:S(2)}) copy-start(f32[32,64]{1,0:T(8,128)S(1)} %sub.1273) | copy-start | bytes 24580
  24.1 5.5 %copy-start.22 = (f32[3,2048]{1,0:T(4,128)S(1)}, f32[3,2048]{1,0:T(4,128)}, u32[]{:S(2)}) copy-start(f32[3,2048]{1,0:T(4,128)} %param.10) | copy-start | bytes 73732
  24.1 5.7 %copy-start.72 = (s32[32,3]{0,1:T(4,128)S(1)}, s32[32,3]{0,1:T(4,128)}, u32[]{:S(2)}) copy-start(s32[32,3]{0,1:T(4,128)} %param.13) | copy-start | bytes 1156
  24.1 5.9 %copy-start.81 = (f32[2,2,64]{2,1,0:T(2,128)}, f32[2,2,64]{2,1,0:T(2,128)S(1)}, u32[]{:S(2)}) copy-start(f32[2,2,64]{2,1,0:T(2,128)S(1)} %broadcast_in_dim.132) | copy-start | bytes 3076
  24.1 5.9 %copy-start.83 = (f32[2,2,64]{2,1,0:T(2,128)}, f32[2,2,64]{2,1,0:T(2,128)S(1)}, u32[]{:S(2)}) copy-start(f32[2,2,64]{2,1,0:T(2,128)S(1)} %broadcast_in_dim.134) | copy-start | bytes 3076
  24.2 5.9 %copy-start.85 = (f32[2,2,64]{2,1,0:T(2,128)}, f32[2,2,64]{2,1,0:T(2,128)S(1)}, u32[]{:S(2)}) copy-start(f32[2,2,64]{2,1,0:T(2,128)S(1)} %broadcast_in_dim.136) | copy-start | bytes 3076
  26.5 6.1 %copy-start.89 = (f32[64]{0:T(128)}, f32[64]{0:T(128)S(1)}, u32[]{:S(2)}) copy-start(f32[64]{0:T(128)S(1)} %get-tuple-element.57) | copy-start | bytes 772
  26.5 6.1 %copy-start.91 = (f32[64]{0:T(128)}, f32[64]{0:T(128)S(1)}, u32[]{:S(2)}) copy-start(f32[64]{0:T(128)S(1)} %get-tuple-element.58) | copy-start | bytes 772
  26.5 6.1 %copy-start.93 = (f32[64]{0:T(128)}, f32[64]{0:T(128)S(1)}, u32[]{:S(2)}) copy-start(f32[64]{0:T(128)S(1)} %get-tuple-element.59) | copy-start | bytes 772
  27.0 5.6 %copy-start.136 = (f32[64]{0:T(128)}, f32[64]{0:T(128)S(1)}, u32[]{:S(2)}) copy-start(f32[64]{0:T(128)S(1)} %get-tuple-element.23) | copy-start | bytes 772
  27.0 5.6 %copy-start.137 = (f32[64]{0:T(128)}, f32[64]{0:T(128)S(1)}, u32[]{:S(2)}) copy-start(f32[64]{0:T(128)S(1)} %get-tuple-element.22) | copy-start | bytes 772
  27.0 5.6 %copy-start.139 = (f32[64]{0:T(128)}, f32[64]{0:T(128)S(1)}, u32[]{:S(2)}) copy-start(f32[64]{0:T(128)S(1)} %get-tuple-element.20) | copy-start | bytes 772
  27.0 5.6 %copy-start.140 = (f32[64]{0:T(128)}, f32[64]{0:T(128)S(1)}, u32[]{:S(2)}) copy-start(f32[64]{0:T(128)S(1)} %get-tuple-element.24) | copy-start | bytes 772
  33.6 21.6 %copy-start = (f32[11,8192]{1,0:T(8,128)}, f32[11,8192]{1,0:T(8,128)S(1)}, u32[]{:S(2)}) copy-start(f32[11,8192]{1,0:T(8,128)S(1)} %get-tuple-element.52) | copy-start | bytes 1081348
  69.5 5.1 %copy-start.115 = (s32[32,6]{0,1:T(8,128)S(1)}, s32[32,6]{0,1:T(8,128)}, u32[]{:S(2)}) copy-start(s32[32,6]{0,1:T(8,128)} %param.9) | copy-start | bytes 2308
  69.5 5.8 %copy-start.6 = (f32[3,8192]{1,0:T(4,128)S(1)}, f32[3,8192]{1,0:T(4,128)}, u32[]{:S(2)}) copy-start(f32[3,8192]{1,0:T(4,128)} %get-tuple-element.51) | copy-start | bytes 294916
  131.6 5.0 %copy-start.119 = (f32[64]{0:T(128)S(1)}, f32[64]{0:T(128)}, u32[]{:S(2)}) copy-start(f32[64]{0:T(128)} %copy-done.118) | copy-start | bytes 772
  131.6 5.9 %copy-start.74 = (f32[2,64]{1,0:T(2,128)S(1)}, f32[2,64]{1,0:T(2,128)}, u32[]{:S(2)}) copy-start(f32[2,64]{1,0:T(2,128)} %copy-done.73) | copy-start | bytes 1540
  131.7 6.0 %copy-start.76 = (f32[2,64]{1,0:T(2,128)S(1)}, f32[2,64]{1,0:T(2,128)}, u32[]{:S(2)}) copy-start(f32[2,64]{1,0:T(2,128)} %copy-done.75) | copy-start | bytes 1540
  131.7 6.0 %copy-start.78 = (f32[2,64]{1,0:T(2,128)S(1)}, f32[2,64]{1,0:T(2,128)}, u32[]{:S(2)}) copy-start(f32[2,64]{1,0:T(2,128)} %copy-done.77) | copy-start | bytes 1540
  131.7 6.0 %copy-start.87 = (f32[8,2,64]{2,0,1:T(8,128)S(1)}, f32[8,2,64]{2,0,1:T(8,128)}, u32[]{:S(2)}) copy-start(f32[8,2,64]{2,0,1:T(8,128)} %reduce_sum.310) | copy-start | bytes 12292
  131.7 7.0 %copy-start.58 = (f32[4,64]{1,0:T(4,128)S(1)}, f32[4,64]{1,0:T(4,128)}, u32[]{:S(2)}) copy-start(f32[4,64]{1,0:T(4,128)} %copy-done.57) | copy-start | bytes 3076
  131.7 7.0 %copy-start.60 = (f32[4,64]{1,0:T(4,128)S(1)}, f32[4,64]{1,0:T(4,128)}, u32[]{:S(2)}) copy-start(f32[4,64]{1,0:T(4,128)} %copy-done.59) | copy-start | bytes 3076
  131.7 7.0 %copy-start.62 = (f32[4,64]{1,0:T(4,128)S(1)}, f32[4,64]{1,0:T(4,128)}, u32[]{:S(2)}) copy-start(f32[4,64]{1,0:T(4,128)} %copy-done.61) | copy-start | bytes 3076
  131.7 7.0 %copy-start.71 = (f32[8,4,64]{2,0,1:T(8,128)S(1)}, f32[8,4,64]{2,0,1:T(8,128)}, u32[]{:S(2)}) copy-start(f32[8,4,64]{2,0,1:T(8,128)} %reduce_sum.311) | copy-start | bytes 24580
  131.7 7.0 %copy-start.82 = (f32[2,2,64]{2,1,0:T(2,128)S(1)}, f32[2,2,64]{2,1,0:T(2,128)}, u32[]{:S(2)}) copy-start(f32[2,2,64]{2,1,0:T(2,128)} %copy-done.81) | copy-start | bytes 3076
  131.7 7.0 %copy-start.84 = (f32[2,2,64]{2,1,0:T(2,128)S(1)}, f32[2,2,64]{2,1,0:T(2,128)}, u32[]{:S(2)}) copy-start(f32[2,2,64]{2,1,0:T(2,128)} %copy-done.83) | copy-start | bytes 3076
  131.7 7.0 %copy-start.86 = (f32[2,2,64]{2,1,0:T(2,128)S(1)}, f32[2,2,64]{2,1,0:T(2,128)}, u32[]{:S(2)}) copy-start(f32[2,2,64]{2,1,0:T(2,128)} %copy-done.85) | copy-start | bytes 3076
  131.8 7.0 %copy-start.117 = (f32[4,64]{1,0:T(4,128)S(1)}, f32[4,64]{1,0:T(4,128)}, u32[]{:S(2)}) copy-start(f32[4,64]{1,0:T(4,128)} %copy-done.116) | copy-start | bytes 3076
  133.4 5.8 %copy-start.37 = (f32[8,64]{1,0:T(8,128)S(1)}, f32[8,64]{1,0:T(8,128)}, u32[]{:S(2)}) copy-start(f32[8,64]{1,0:T(8,128)} %copy-done.36) | copy-start | bytes 6148
  133.4 5.8 %copy-start.39 = (f32[8,64]{1,0:T(8,128)S(1)}, f32[8,64]{1,0:T(8,128)}, u32[]{:S(2)}) copy-start(f32[8,64]{1,0:T(8,128)} %copy-done.38) | copy-start | bytes 6148
  133.4 5.8 %copy-start.41 = (f32[8,64]{1,0:T(8,128)S(1)}, f32[8,64]{1,0:T(8,128)}, u32[]{:S(2)}) copy-start(f32[8,64]{1,0:T(8,128)} %copy-done.40) | copy-start | bytes 6148
  133.4 5.8 %copy-start.66 = (f32[4,2,64]{2,1,0:T(2,128)S(1)}, f32[4,2,64]{2,1,0:T(2,128)}, u32[]{:S(2)}) copy-start(f32[4,2,64]{2,1,0:T(2,128)} %copy-done.65) | copy-start | bytes 6148
  133.4 5.8 %copy-start.68 = (f32[4,2,64]{2,1,0:T(2,128)S(1)}, f32[4,2,64]{2,1,0:T(2,128)}, u32[]{:S(2)}) copy-start(f32[4,2,64]{2,1,0:T(2,128)} %copy-done.67) | copy-start | bytes 6148
  133.5 5.8 %copy-start.70 = (f32[4,2,64]{2,1,0:T(2,128)S(1)}, f32[4,2,64]{2,1,0:T(2,128)}, u32[]{:S(2)}) copy-start(f32[4,2,64]{2,1,0:T(2,128)} %copy-done.69) | copy-start | bytes 6148
  133.5 5.8 %copy-start.114 = (f32[8,64]{1,0:T(8,128)S(1)}, f32[8,64]{1,0:T(8,128)}, u32[]{:S(2)}) copy-start(f32[8,64]{1,0:T(8,128)} %copy-done.113) | copy-start | bytes 6148
  133.8 6.3 %copy-start.24 = (f32[16,64]{1,0:T(8,128)S(1)}, f32[16,64]{1,0:T(8,128)}, u32[]{:S(2)}) copy-start(f32[16,64]{1,0:T(8,128)} %copy-done.23) | copy-start | bytes 12292
  133.9 6.3 %copy-start.26 = (f32[16,64]{1,0:T(8,128)S(1)}, f32[16,64]{1,0:T(8,128)}, u32[]{:S(2)}) copy-start(f32[16,64]{1,0:T(8,128)} %copy-done.25) | copy-start | bytes 12292
  133.9 6.3 %copy-start.34 = (f32[8,16,64]{2,0,1:T(8,128)S(1)}, f32[8,16,64]{2,0,1:T(8,128)}, u32[]{:S(2)}) copy-start(f32[8,16,64]{2,0,1:T(8,128)} %reduce_sum.313) | copy-start | bytes 98308
  133.9 6.3 %copy-start.43 = (f32[8,2,64]{2,1,0:T(2,128)S(1)}, f32[8,2,64]{2,1,0:T(2,128)}, u32[]{:S(2)}) copy-start(f32[8,2,64]{2,1,0:T(2,128)} %copy-done.42) | copy-start | bytes 12292
  133.9 6.3 %copy-start.45 = (f32[8,2,64]{2,1,0:T(2,128)S(1)}, f32[8,2,64]{2,1,0:T(2,128)}, u32[]{:S(2)}) copy-start(f32[8,2,64]{2,1,0:T(2,128)} %copy-done.44) | copy-start | bytes 12292
  133.9 6.3 %copy-start.47 = (f32[8,2,64]{2,1,0:T(2,128)S(1)}, f32[8,2,64]{2,1,0:T(2,128)}, u32[]{:S(2)}) copy-start(f32[8,2,64]{2,1,0:T(2,128)} %copy-done.46) | copy-start | bytes 12292
  133.9 6.3 %copy-start.80 = (f32[16,64]{1,0:T(8,128)S(1)}, f32[16,64]{1,0:T(8,128)}, u32[]{:S(2)}) copy-start(f32[16,64]{1,0:T(8,128)} %copy-done.79) | copy-start | bytes 12292
  (84 other events, 210.1 us)
Sparse Core Ops, SparseCore 0:
  29.0 87.9 all-gather.2

commit v13 on v12

--- a/solution.py
+++ b/solution.py
@@ -83,18 +83,25 @@
     return values / jnp.sum(values, axis=-1, keepdims=True)
 
 
-def near_kernel(slots, halo, source_ref, probes_ref, coords_ref, target_ref, out_ref):
+def near_kernel(slots, halo, stretch, source_ref, tiles_ref, target_ref, out_ref):
     box = pl.program_id(0)
     boxes = pl.num_programs(0)
     size = target_ref.shape[0]
-    target_x = jnp.broadcast_to(target_ref[:, 0:1], (size, size))
-    target_y = jnp.broadcast_to(target_ref[:, 1:2], (size, size))
-    target_z = jnp.broadcast_to(target_ref[:, 2:3], (size, size))
+    rows = out_ref.shape[0]
+    target_x = jnp.broadcast_to(target_ref[:, 0:1] * stretch, (size, size))
+    target_y = jnp.broadcast_to(target_ref[:, 1:2] * stretch, (size, size))
+    target_z = jnp.broadcast_to(target_ref[:, 2:3] * stretch, (size, size))
     here = box + halo
     columns = pl.ds(pl.multiple_of(box * size, size), size)
 
+    def tile_columns(tile):
+        return pl.ds(pl.multiple_of(tile * size, size), size)
+
+    def probes_of(tile):
+        return tiles_ref[0:rows, tile_columns(tile)]
+
     def block(tile):
-        near = coords_ref[tile]
+        near = tiles_ref[rows : rows + 3, tile_columns(tile)] * stretch
         distance_sq = (near[0:1, :] - target_x) ** 2
         distance_sq = distance_sq + (near[1:2, :] - target_y) ** 2
         distance_sq = distance_sq + (near[2:3, :] - target_z) ** 2
@@ -102,7 +109,7 @@
 
     def gather_into(tile, kernel_block):
         out_ref[:, columns] += lax.dot_general(
-            probes_ref[tile], kernel_block, (((1,), (1,)), ((), ())),
+            probes_of(tile), kernel_block, (((1,), (1,)), ((), ())),
             precision=lax.Precision.HIGH, preferred_element_type=jnp.float32,
         )
 
@@ -119,7 +126,7 @@
     def _():
         following = pl.ds(pl.multiple_of((box + 1) * size, size), size)
         out_ref[:, following] += jnp.dot(
-            probes_ref[here], pair_block, precision=lax.Precision.HIGH,
+            probes_of(here), pair_block, precision=lax.Precision.HIGH,
             preferred_element_type=jnp.float32,
         )
 
@@ -150,7 +157,7 @@
             gather_into(here + step, kernel_block)
             later = pl.ds(pl.multiple_of((box + step) * size, size), size)
             out_ref[:, later] += jnp.dot(
-                probes_ref[here], kernel_block, precision=lax.Precision.HIGH,
+                probes_of(here), kernel_block, precision=lax.Precision.HIGH,
                 preferred_element_type=jnp.float32,
             )
 
@@ -165,20 +172,19 @@
             gather_into(source, block(source))
 
 
-def near_field_call(slot_source, probe_tiles, coord_tiles, points, kernel_scale):
-    tiles, rows, size = probe_tiles.shape
+def near_field_call(slot_source, tiles, points, kernel_scale):
+    rows = tiles.shape[0] - 3
+    size = P_SIZE
     boxes = points.shape[1] // size
     slots = slot_source.shape[0] // boxes
-    stretch = kernel_scale**0.5
     return pl.pallas_call(
-        functools.partial(near_kernel, slots, W),
+        functools.partial(near_kernel, slots, W, kernel_scale**0.5),
         out_shape=jax.ShapeDtypeStruct((rows, boxes * size), jnp.float32),
         grid_spec=pltpu.PrefetchScalarGridSpec(
             num_scalar_prefetch=1,
             grid=(boxes,),
             in_specs=[
-                pl.BlockSpec((tiles, rows, size), lambda b, s: (0, 0, 0)),
-                pl.BlockSpec((tiles, 3, size), lambda b, s: (0, 0, 0)),
+                pl.BlockSpec(tiles.shape, lambda b, s: (0, 0)),
                 pl.BlockSpec((size, 3), lambda b, s: (b, 0)),
             ],
             out_specs=pl.BlockSpec((rows, boxes * size), lambda b, s: (0, 0)),
@@ -187,9 +193,9 @@
         cost_estimate=pl.CostEstimate(
             flops=boxes * slots * size * size * (2 * rows + 12),
             transcendentals=0,
-            bytes_accessed=4 * (probe_tiles.size + coord_tiles.size + 2 * rows * boxes * size),
+            bytes_accessed=4 * (tiles.size + 2 * rows * boxes * size),
         ),
-    )(slot_source, probe_tiles, coord_tiles * stretch, points.T * stretch)
+    )(slot_source, tiles, points.T)
 
 
 def body(probes, points, near_list, leaf_proxy, inner_proxy, top_proxy, far_list):
@@ -245,7 +251,6 @@
         jnp.concatenate([stacked[:, :width], flat_pyramid], axis=1),
     )
     extended = jnp.concatenate([from_left[:, :width], stacked, from_right[:, :width]], axis=1)
-    extended = extended.reshape(rows_here + 3, BOXES_DEV + 2 * W, P_SIZE)
     spread = jnp.concatenate(
         [
             from_left[:, width:].reshape(pyramid.shape),
@@ -257,8 +262,7 @@
     slot_source = jnp.where(live_slot, jnp.clip(where_in, 0, BOXES_DEV + 2 * W - 1), -1)
     near_field = near_field_call(
         slot_source.reshape(-1).astype(jnp.int32),
-        jnp.moveaxis(extended[:rows_here], 1, 0),
-        jnp.moveaxis(extended[rows_here:], 0, 1),
+        extended,
         points,
         kernel_scale,
     )

time: 157 us -> 155 us (0.987)
  Pallas kernels: 63.2 us -> 59.3 us
    pallas_call x1, Pallas kernels: 44.1 us -> 40.1 us  [near_field_call(): pl.pallas_call(functools.partial(near_kernel, slots, W, kernel_scale ** 0...]
    mul x1 -> x0, local copies, waits for them, and re-layouts: 2.9 us -> none  [near_field_call(): points.T * stretch]
    unnamed x303 -> x286, local copies, waits for them, and re-layouts: 5.67 us -> 8.22 us
    concatenate x1, local copies, waits for them, and re-layouts: 0.07 us -> 2.09 us  [body(): jnp.concatenate(target_parts, axis=1)]
  transfers between devices with their start and end apart: 1 -> 1, of which waited for: 0 -> 0; matrix products, arithmetic and copies ran while one was open for 20% -> 22% of each run, Pallas kernels for 41% -> 39%
where the time goes in v13:
time: 155 us; the launch traced here: 153 us
  Pallas kernels  59.3 us (38%)
  matrix products  35 us (23%)
  local copies, waits for them, and re-layouts  27.6 us (18%)
  between operations  16.7 us (11%)
  other arithmetic  13.9 us (9%)
    pallas_call x1, Pallas kernels, near_field_call(): pl.pallas_call(functools.partial(near_kernel, slots, W, kernel_scale ** 0...  40.1 us
    pallas_call x1, Pallas kernels, exchange_halo(): pl.pallas_call(halo_kernel, out_shape=(shape, shape), in_specs=[vmem, vme...  19.2 us
    dot_general x1, matrix products, body(): jnp.einsum('qnr,nrs->qns', source_moment, kernel_block, precision=PRECISE)  10 us
    unnamed x286, local copies, waits for them, and re-layouts  8.22 us
    dot_general x5, matrix products, body(): jnp.einsum('qns,nrs->qnr', jnp.repeat(descent, 2, axis=1), transfer_maps[...  7.09 us
    dot_general x5, matrix products, body(): jnp.einsum('qnr,nrs->qns', level_moments[-1], interp_map, precision=PRECISE)  5.15 us
    reduce_sum x7, other arithmetic, interpolation(): return values / jnp.sum(values, axis=-1, keepdims=True)  4.31 us
    dot_general x5, matrix products, body(): jnp.einsum('qns,nrs->qnr', descent, own_edges[height], precision=PRECISE)  3.75 us
  transfers between devices with their start and end apart: 1, of which 0 were waited for; matrix products, arithmetic and copies ran while one was open for 22% of the time, Pallas kernels for 39%

profile of v13, /device:TPU:6, one launch (start us, length us, event | category | flops | bytes accessed | tf_op | source)
XLA Modules:
  0.0 152.5 jit_solution(215793964008595758)
XLA Ops:
  6.5 1.2 reshape.3422
  7.9 0.9 reshape.3415
  9.0 0.9 slice_reduce_fusion.10
  10.1 1.3 slice_reduce_fusion.2
  11.6 1.1 divide_reduce_fusion
  12.7 3.3 %constant_dynamic-update-slice_fusion.6 = (f32[8,62,64]{2,0,1:T(8,128)S(1)}, f32[8,32,64]{2,0,1:T(8,128)S(1)}) fusion(f32[8,32,256]{2,0,1:T(8,128)S(1)} %bitcast.403, f32[32,256]{1,0:T(8,128)S(1)} %divide_reduce_fusion, f32[32,64]{1,0:T(8,128)S(1)} %sub.1273, f32[32,256]{1,0:T(8,128)S(1)} %sub.1271, f32[32,64]{1,0:T(8,128)S(1)} %sub.1268, ...), kind=kOutput, calls=%fused_computation.96 | convolution fusion | flops 56623104 | bytes 679936 | tf_op jit(solution)/shard_map/qbp,bpr->qbr/dot_general | solution.py:229
  16.1 1.4 divide_reduce_fusion.1
  17.5 2.6 %bitcast_reduce_fusion = f32[8,16,64]{2,0,1:T(8,128)S(1)} fusion(f32[8,32,64]{2,0,1:T(8,128)S(1)} %get-tuple-element.122, f32[32,64]{1,0:T(8,128)S(1)} %divide_reduce_fusion.1, f32[32,64]{1,0:T(8,128)S(1)} %bitcast.420, f32[32,64]{1,0:T(8,128)S(1)} %sub.1273, f32[32,64]{1,0:T(8,128)S(1)} %bitcast.417, f32[32,64]{1,0:T(8,128)S(1)} %sub.1268, ...), kind=kOutput, calls=%fused_computation.74 | convolution fusion | flops 14163968 | bytes 155648 | tf_op jit(solution)/shard_map/qnr,nrs->qns/dot_general | solution.py:236
  20.2 0.7 divide_reduce_fusion.2
  20.9 1.3 bitcast_reduce_fusion.1
  22.2 0.4 divide_reduce_fusion.3
  22.8 0.6 copy-done.104
  23.4 0.6 bitcast_reduce_fusion.2
  24.1 0.3 divide_reduce_fusion.4
  24.4 0.4 bitcast_reduce_fusion.3
  25.5 0.5 copy-done.126
  26.0 0.3 constant_dynamic-update-slice_fusion.11
  26.5 0.4 fusion.53
  27.4 0.2 constant_dynamic-update-slice_fusion.8
  28.1 0.6 copy-done.46
  29.8 0.6 slice.596
  30.4 0.6 slice.598
  31.0 0.6 bitcast_convert_fusion
  31.7 0.6 copy-done.5
  32.8 0.9 pad_maximum_fusion.2
  33.8 19.2 %shard_map.73 = (f32[11,4736]{1,0:T(8,128)}, f32[11,4736]{1,0:T(8,128)}) custom-call(f32[11,4736]{1,0:T(8,128)} %get-tuple-element.43.to_right, f32[11,4736]{1,0:T(8,128)} %get-tuple-element.42.to_left), custom_call_target="tpu_custom_call" | custom-call | tf_op jit(solution)/shard_map/pallas_call | solution.py:60
  53.0 1.0 slice.530
  55.1 0.6 compare_and_fusion
  55.6 1.1 pad_maximum_fusion
  56.7 0.9 gather_fusion
  57.7 1.0 select_bitcast_fusion
  59.0 2.1 %concatenate.122 = f32[3,186,64]{2,1,0:T(8,128)S(1)} concatenate(f32[3,32,64]{2,1,0:T(8,128)S(1)} %reshape.3420, f32[3,32,64]{2,1,0:T(8,128)S(1)} %reshape.3420, f32[3,32,64]{2,1,0:T(8,128)S(1)} %reshape.3420, f32[3,16,64]{2,1,0:T(8,128)S(1)} %slice-done.1, f32[3,16,64]{2,1,0:T(8,128)S(1)} %slice-done.1, f32[3,24,64]{2,1,0:T(8,128)S(1)} %slice-done, f32[3,8,64]{2,1,0:T(8,128)S(1)} %slice-done.3, ...), dimensions={1} | concatenate | bytes 285696 | tf_op jit(solution)/shard_map/concatenate | solution.py:293
  61.2 10.0 %fusion.9 = f32[8,186,64]{2,0,1:T(8,128)S(1)} fusion(f32[186,64]{1,0:T(8,128)S(1)} %get-tuple-element.40, f32[186,64]{1,0:T(8,128)S(1)} %bitcast.409, f32[186,64]{1,0:T(8,128)S(1)} %get-tuple-element.41, f32[186,64]{1,0:T(8,128)S(1)} %bitcast.410, f32[186,64]{1,0:T(8,128)S(1)} %get-tuple-element.39, f32[186,64]{1,0:T(8,128)S(1)} %bitcast.411, ...), kind=kOutput, calls=%fused_computation.16 | convolution fusion | flops 81613824 | bytes 1733632 | tf_op jit(solution)/shard_map/qnr,nrs->qns/dot_general | solution.py:295
  71.4 0.8 slice.462
  72.2 0.8 slice.463
  73.0 2.7 %copy.95 = f32[3,8192]{0,1:T(8,128)} copy(f32[3,8192]{1,0:T(4,128)S(1)} %copy-done.7) | data formatting | bytes 196608 | tf_op args[1]
  75.7 0.6 reduce_sum.310
  76.3 0.6 reduce_sum.311
  76.9 0.6 reduce_sum.313
  77.6 0.7 reduce_sum.314
  78.4 0.7 reshape.3413.source_ref
  79.1 0.9 constant_dynamic-slice_fusion.40
  80.0 0.9 constant_dynamic-slice_fusion.46
  81.0 0.9 pad_maximum_fusion.1.tiles_ref
  81.9 40.1 %shard_map.74 = f32[8,8192]{1,0:T(8,128)} custom-call(s32[192]{0:T(256)} %reshape.3413.source_ref, f32[11,9728]{1,0:T(8,128)} %pad_maximum_fusion.1.tiles_ref, f32[8192,3]{1,0:T(8,128)} %bitcast.395), custom_call_target="tpu_custom_call" | custom-call | flops 352321536 | bytes 952320 | tf_op jit(solution)/shard_map/pallas_call | solution.py:180
  122.0 0.6 slice_bitcast_fusion.8
  122.6 0.6 slice_bitcast_fusion.7
  123.2 2.0 %fusion.216 = (f32[128,8,1,64]{3,1,0,2:T(8,128)S(1)}, f32[128,8,1,64]{3,1,0,2:T(8,128)S(1)}, f32[128,8,1,64]{3,1,0,2:T(8,128)S(1)}, f32[128,8,1,64]{3,1,0,2:T(8,...) fusion(f32[128,8,6,64]{3,1,0,2:T(8,128)} %bitcast.396), kind=kLoop, calls=%fused_computation.538 | loop fusion | bytes 3145728 | tf_op jit(solution)/shard_map/slice | solution.py:328
  125.3 0.8 reduce_sum.300
  126.0 0.7 constant_dynamic-update-slice_fusion.24
  126.7 0.7 constant_dynamic-update-slice_fusion.23
  127.4 0.7 constant_dynamic-update-slice_fusion.22
  128.8 1.7 %convolution_bitcast_fusion.3 = f32[8,16,64]{2,0,1:T(8,128)S(1)} fusion(f32[16,8,64]{2,1,0:T(8,128)S(1)} %constant_dynamic-update-slice_fusion.12, f32[16,64]{1,0:T(8,128)} %get-tuple-element.81, f32[16,64]{1,0:T(8,128)} %get-tuple-element.78, f32[16,64]{1,0:T(8,128)} %get-tuple-element.82, f32[16,64]{1,0:T(8,128)} %get-tuple-element.79, ...), kind=kOutput, calls=%fused_computation.21 | convolution fusion | flops 7012352 | bytes 90112 | tf_op jit(solution)/shard_map/nqr,nrs->qns/dot_general | solution.py:342
  131.0 0.9 fusion.22
  131.9 0.9 fusion.20
  132.8 0.8 fusion.18
  133.7 0.9 fusion.16
  134.6 1.0 fusion.14
  135.7 0.5 fusion.13
  136.3 0.8 fusion.12
  137.2 1.6 %fusion.11 = f32[8,16,64]{2,0,1:T(8,128)S(1)} fusion(f32[8,16,64]{2,0,1:T(8,128)S(1)} %copy-done.30, f32[8,16,64]{2,0,1:T(8,128)S(1)} %bitcast.422, f32[16,64]{1,0:T(8,128)S(1)} %copy-done.72, f32[16,64]{1,0:T(8,128)S(1)} %bitcast.431, f32[16,64]{1,0:T(8,128)S(1)} %copy-done.20, f32[16,64]{1,0:T(8,128)S(1)} %bitcast.428, f32[16,64]{1,0:T(8,128)S(1)} %copy-done.22, ...), kind=kOutput, calls=%fused_computation.22 | convolution fusion | flops 7086080 | bytes 126976 | tf_op jit(solution)/shard_map/qns,nrs->qnr/dot_general | solution.py:357
  138.9 3.2 %fusion.10 = f32[8,32,64]{2,0,1:T(8,128)S(1)} fusion(f32[8,32,64]{2,0,1:T(8,128)S(1)} %copy-done.10, f32[8,32,64]{2,0,1:T(8,128)S(1)} %bitcast.408, f32[32,64]{1,0:T(8,128)S(1)} %copy-done.56, f32[32,64]{1,0:T(8,128)S(1)} %bitcast.421, f32[32,64]{1,0:T(8,128)S(1)} %sub.1273, f32[32,64]{1,0:T(8,128)S(1)} %bitcast.418, f32[32,64]{1,0:T(8,128)S(1)} %sub.1268, ...), kind=kOutput, calls=%fused_computation.19 | convolution fusion | flops 14172160 | bytes 253952 | tf_op jit(solution)/shard_map/qns,nrs->qnr/dot_general | solution.py:357
  142.2 2.7 %fusion.26 = f32[32,256,8]{1,2,0:T(8,128)S(1)} fusion(f32[8,32,64]{2,0,1:T(8,128)S(1)} %fusion.10, f32[32,256]{1,0:T(8,128)S(1)} %copy-done.43, f32[32,64]{1,0:T(8,128)S(1)} %sub.1273, f32[32,256]{1,0:T(8,128)S(1)} %copy-done.14, f32[32,64]{1,0:T(8,128)S(1)} %sub.1268, f32[32,256]{1,0:T(8,128)S(1)} %copy-done.12, f32[32,64]{1,0:T(8,128)S(1)} %sub.1263, ...), kind=kOutput, calls=%fused_computation.48 | convolution fusion | flops 56623104 | bytes 483328 | tf_op jit(solution)/shard_map/qbr,bpr->qbp/dot_general | solution.py:361
  144.9 0.7 add_add_fusion
  (397 shorter events, 5.6 us)
Async XLA Ops:
  6.5 6.1 %copy-start.4 = (f32[8,8192]{1,0:T(8,128)S(1)}, f32[8,8192]{1,0:T(8,128)}, u32[]{:S(2)}) copy-start(f32[8,8192]{1,0:T(8,128)} %param.7) | copy-start | bytes 786436
  6.5 116.7 %all-gather.3.cloned.1.call-start = ((), (), s32[]{:S(2)}) async-start(), calls=%async_computation | async-start | bytes 3170304 | tf_op jit(solution)/shard_map/all_gather | solution.py:323
  7.8 17.1 %copy-start.44 = (f32[3,8,64]{2,1,0:T(8,128)}, f32[3,8,64]{2,1,0:T(8,128)S(1)}, u32[]{:S(2)}) copy-start(f32[3,8,64]{2,1,0:T(8,128)S(1)} %slice.571) | copy-start | bytes 18436
  7.8 18.5 %copy-start.47 = (f32[3,4,64]{2,1,0:T(4,128)}, f32[3,4,64]{2,1,0:T(4,128)S(1)}, u32[]{:S(2)}) copy-start(f32[3,4,64]{2,1,0:T(4,128)S(1)} %slice.572) | copy-start | bytes 9220
  7.8 18.5 %copy-start.23 = (f32[3,32,64]{2,1,0:T(8,128)}, f32[3,32,64]{2,1,0:T(8,128)S(1)}, u32[]{:S(2)}) copy-start(f32[3,32,64]{2,1,0:T(8,128)S(1)} %slice.569) | copy-start | bytes 73732
  7.8 18.5 %copy-start.31 = (f32[3,16,64]{2,1,0:T(8,128)}, f32[3,16,64]{2,1,0:T(8,128)S(1)}, u32[]{:S(2)}) copy-start(f32[3,16,64]{2,1,0:T(8,128)S(1)} %slice.570) | copy-start | bytes 36868
  7.9 17.0 %copy-start.9 = (f32[3,128,64]{2,1,0:T(8,128)}, f32[3,128,64]{2,1,0:T(8,128)S(1)}, u32[]{:S(2)}) copy-start(f32[3,128,64]{2,1,0:T(8,128)S(1)} %slice.567) | copy-start | bytes 294916
  7.9 18.4 %copy-start.15 = (f32[3,64,64]{2,1,0:T(8,128)}, f32[3,64,64]{2,1,0:T(8,128)S(1)}, u32[]{:S(2)}) copy-start(f32[3,64,64]{2,1,0:T(8,128)S(1)} %slice.568) | copy-start | bytes 147460
  8.8 21.6 %copy-start.2 = (f32[3,30,64]{2,1,0:T(8,128)}, f32[3,30,64]{2,1,0:T(8,128)S(1)}, u32[]{:S(2)}) copy-start(f32[3,30,64]{2,1,0:T(8,128)S(1)} %reshape.3415) | copy-start | bytes 69124
  8.8 12.0 %copy-start.17 = (f32[16,64]{1,0:T(8,128)}, f32[16,64]{1,0:T(8,128)S(1)}, u32[]{:S(2)}) copy-start(f32[16,64]{1,0:T(8,128)S(1)} %get-tuple-element.74) | copy-start | bytes 12292
  8.8 12.0 %copy-start.19 = (f32[16,64]{1,0:T(8,128)}, f32[16,64]{1,0:T(8,128)S(1)}, u32[]{:S(2)}) copy-start(f32[16,64]{1,0:T(8,128)S(1)} %get-tuple-element.75) | copy-start | bytes 12292
  8.8 12.0 %copy-start.21 = (f32[16,64]{1,0:T(8,128)}, f32[16,64]{1,0:T(8,128)S(1)}, u32[]{:S(2)}) copy-start(f32[16,64]{1,0:T(8,128)S(1)} %get-tuple-element.76) | copy-start | bytes 12292
  8.8 13.8 %copy-start.32 = (f32[8,64]{1,0:T(8,128)}, f32[8,64]{1,0:T(8,128)S(1)}, u32[]{:S(2)}) copy-start(f32[8,64]{1,0:T(8,128)S(1)} %get-tuple-element.72) | copy-start | bytes 6148
  8.8 13.8 %copy-start.34 = (f32[8,64]{1,0:T(8,128)}, f32[8,64]{1,0:T(8,128)S(1)}, u32[]{:S(2)}) copy-start(f32[8,64]{1,0:T(8,128)S(1)} %get-tuple-element.73) | copy-start | bytes 6148
  8.9 15.5 %copy-start.49 = (f32[4,64]{1,0:T(4,128)}, f32[4,64]{1,0:T(4,128)S(1)}, u32[]{:S(2)}) copy-start(f32[4,64]{1,0:T(4,128)S(1)} %get-tuple-element.68) | copy-start | bytes 3076
  8.9 15.5 %copy-start.51 = (f32[4,64]{1,0:T(4,128)}, f32[4,64]{1,0:T(4,128)S(1)}, u32[]{:S(2)}) copy-start(f32[4,64]{1,0:T(4,128)S(1)} %get-tuple-element.69) | copy-start | bytes 3076
  8.9 15.5 %copy-start.53 = (f32[4,64]{1,0:T(4,128)}, f32[4,64]{1,0:T(4,128)S(1)}, u32[]{:S(2)}) copy-start(f32[4,64]{1,0:T(4,128)S(1)} %get-tuple-element.70) | copy-start | bytes 3076
  8.9 16.3 %copy-start.65 = (f32[2,64]{1,0:T(2,128)}, f32[2,64]{1,0:T(2,128)S(1)}, u32[]{:S(2)}) copy-start(f32[2,64]{1,0:T(2,128)S(1)} %get-tuple-element.65) | copy-start | bytes 1540
  8.9 16.3 %copy-start.67 = (f32[2,64]{1,0:T(2,128)}, f32[2,64]{1,0:T(2,128)S(1)}, u32[]{:S(2)}) copy-start(f32[2,64]{1,0:T(2,128)S(1)} %get-tuple-element.66) | copy-start | bytes 1540
  8.9 16.3 %copy-start.69 = (f32[2,64]{1,0:T(2,128)}, f32[2,64]{1,0:T(2,128)S(1)}, u32[]{:S(2)}) copy-start(f32[2,64]{1,0:T(2,128)S(1)} %get-tuple-element.67) | copy-start | bytes 1540
  24.1 5.3 %copy-start.16 = (f32[3,2048]{1,0:T(4,128)S(1)}, f32[3,2048]{1,0:T(4,128)}, u32[]{:S(2)}) copy-start(f32[3,2048]{1,0:T(4,128)} %param.10) | copy-start | bytes 73732
  24.1 5.6 %copy-start.64 = (s32[32,3]{0,1:T(4,128)S(1)}, s32[32,3]{0,1:T(4,128)}, u32[]{:S(2)}) copy-start(s32[32,3]{0,1:T(4,128)} %param.13) | copy-start | bytes 1156
  24.9 7.5 %copy-start.86 = (f32[64]{0:T(128)}, f32[64]{0:T(128)S(1)}, u32[]{:S(2)}) copy-start(f32[64]{0:T(128)S(1)} %get-tuple-element.94) | copy-start | bytes 772
  24.9 7.5 %copy-start.88 = (f32[64]{0:T(128)}, f32[64]{0:T(128)S(1)}, u32[]{:S(2)}) copy-start(f32[64]{0:T(128)S(1)} %get-tuple-element.95) | copy-start | bytes 772
  24.9 7.5 %copy-start.90 = (f32[64]{0:T(128)}, f32[64]{0:T(128)S(1)}, u32[]{:S(2)}) copy-start(f32[64]{0:T(128)S(1)} %get-tuple-element.96) | copy-start | bytes 772
  26.3 6.1 %copy-start.82 = (f32[64]{0:T(128)}, f32[64]{0:T(128)S(1)}, u32[]{:S(2)}) copy-start(f32[64]{0:T(128)S(1)} %get-tuple-element.56) | copy-start | bytes 772
  26.4 6.1 %copy-start.84 = (f32[64]{0:T(128)}, f32[64]{0:T(128)S(1)}, u32[]{:S(2)}) copy-start(f32[64]{0:T(128)S(1)} %get-tuple-element.57) | copy-start | bytes 772
  26.4 6.1 %copy-start.92 = (f32[64]{0:T(128)}, f32[64]{0:T(128)S(1)}, u32[]{:S(2)}) copy-start(f32[64]{0:T(128)S(1)} %get-tuple-element.142) | copy-start | bytes 772
  26.4 6.1 %copy-start.94 = (f32[64]{0:T(128)}, f32[64]{0:T(128)S(1)}, u32[]{:S(2)}) copy-start(f32[64]{0:T(128)S(1)} %get-tuple-element.143) | copy-start | bytes 772
  26.4 6.1 %copy-start.96 = (f32[64]{0:T(128)}, f32[64]{0:T(128)S(1)}, u32[]{:S(2)}) copy-start(f32[64]{0:T(128)S(1)} %get-tuple-element.144) | copy-start | bytes 772
  26.9 5.6 %copy-start.127 = (f32[64]{0:T(128)}, f32[64]{0:T(128)S(1)}, u32[]{:S(2)}) copy-start(f32[64]{0:T(128)S(1)} %get-tuple-element.23) | copy-start | bytes 772
  26.9 5.6 %copy-start.128 = (f32[64]{0:T(128)}, f32[64]{0:T(128)S(1)}, u32[]{:S(2)}) copy-start(f32[64]{0:T(128)S(1)} %get-tuple-element.22) | copy-start | bytes 772
  32.8 21.2 %copy-start = (f32[11,8192]{1,0:T(8,128)}, f32[11,8192]{1,0:T(8,128)S(1)}, u32[]{:S(2)}) copy-start(f32[11,8192]{1,0:T(8,128)S(1)} %constant_dynamic-update-slice_fusion) | copy-start | bytes 1081348
  61.2 11.8 %copy-start.7 = (f32[3,8192]{1,0:T(4,128)S(1)}, f32[3,8192]{1,0:T(4,128)}, u32[]{:S(2)}) copy-start(f32[3,8192]{1,0:T(4,128)} %param.8) | copy-start | bytes 294916
  73.0 5.3 %copy-start.106 = (s32[32,6]{0,1:T(8,128)S(1)}, s32[32,6]{0,1:T(8,128)}, u32[]{:S(2)}) copy-start(s32[32,6]{0,1:T(8,128)} %param.9) | copy-start | bytes 2308
  73.0 6.1 %copy-start.45 = (f32[3,8,64]{2,1,0:T(8,128)S(1)}, f32[3,8,64]{2,1,0:T(8,128)}, u32[]{:S(2)}) copy-start(f32[3,8,64]{2,1,0:T(8,128)} %copy-done.44) | copy-start | bytes 18436
  73.0 6.1 %copy-start.48 = (f32[3,4,64]{2,1,0:T(4,128)S(1)}, f32[3,4,64]{2,1,0:T(4,128)}, u32[]{:S(2)}) copy-start(f32[3,4,64]{2,1,0:T(4,128)} %copy-done.47) | copy-start | bytes 9220
  73.0 8.0 %copy-start.1 = (f32[11,8192]{1,0:T(8,128)S(1)}, f32[11,8192]{1,0:T(8,128)}, u32[]{:S(2)}) copy-start(f32[11,8192]{1,0:T(8,128)} %copy-done) | copy-start | bytes 1081348
  128.6 6.0 %copy-start.66 = (f32[2,64]{1,0:T(2,128)S(1)}, f32[2,64]{1,0:T(2,128)}, u32[]{:S(2)}) copy-start(f32[2,64]{1,0:T(2,128)} %copy-done.65) | copy-start | bytes 1540
  128.6 6.0 %copy-start.68 = (f32[2,64]{1,0:T(2,128)S(1)}, f32[2,64]{1,0:T(2,128)}, u32[]{:S(2)}) copy-start(f32[2,64]{1,0:T(2,128)} %copy-done.67) | copy-start | bytes 1540
  128.7 6.0 %copy-start.70 = (f32[2,64]{1,0:T(2,128)S(1)}, f32[2,64]{1,0:T(2,128)}, u32[]{:S(2)}) copy-start(f32[2,64]{1,0:T(2,128)} %copy-done.69) | copy-start | bytes 1540
  128.7 6.0 %copy-start.79 = (f32[8,2,64]{2,0,1:T(8,128)S(1)}, f32[8,2,64]{2,0,1:T(8,128)}, u32[]{:S(2)}) copy-start(f32[8,2,64]{2,0,1:T(8,128)} %reduce_sum.310) | copy-start | bytes 12292
  128.7 7.0 %copy-start.50 = (f32[4,64]{1,0:T(4,128)S(1)}, f32[4,64]{1,0:T(4,128)}, u32[]{:S(2)}) copy-start(f32[4,64]{1,0:T(4,128)} %copy-done.49) | copy-start | bytes 3076
  128.7 7.0 %copy-start.52 = (f32[4,64]{1,0:T(4,128)S(1)}, f32[4,64]{1,0:T(4,128)}, u32[]{:S(2)}) copy-start(f32[4,64]{1,0:T(4,128)} %copy-done.51) | copy-start | bytes 3076
  128.7 7.0 %copy-start.54 = (f32[4,64]{1,0:T(4,128)S(1)}, f32[4,64]{1,0:T(4,128)}, u32[]{:S(2)}) copy-start(f32[4,64]{1,0:T(4,128)} %copy-done.53) | copy-start | bytes 3076
  128.7 7.0 %copy-start.63 = (f32[8,4,64]{2,0,1:T(8,128)S(1)}, f32[8,4,64]{2,0,1:T(8,128)}, u32[]{:S(2)}) copy-start(f32[8,4,64]{2,0,1:T(8,128)} %reduce_sum.311) | copy-start | bytes 24580
  128.7 7.0 %copy-start.74 = (f32[2,2,64]{2,1,0:T(2,128)S(1)}, f32[2,2,64]{2,1,0:T(2,128)}, u32[]{:S(2)}) copy-start(f32[2,2,64]{2,1,0:T(2,128)} %copy-done.73) | copy-start | bytes 3076
  128.7 7.0 %copy-start.76 = (f32[2,2,64]{2,1,0:T(2,128)S(1)}, f32[2,2,64]{2,1,0:T(2,128)}, u32[]{:S(2)}) copy-start(f32[2,2,64]{2,1,0:T(2,128)} %copy-done.75) | copy-start | bytes 3076
  128.7 7.0 %copy-start.78 = (f32[2,2,64]{2,1,0:T(2,128)S(1)}, f32[2,2,64]{2,1,0:T(2,128)}, u32[]{:S(2)}) copy-start(f32[2,2,64]{2,1,0:T(2,128)} %copy-done.77) | copy-start | bytes 3076
  128.7 7.0 %copy-start.108 = (f32[4,64]{1,0:T(4,128)S(1)}, f32[4,64]{1,0:T(4,128)}, u32[]{:S(2)}) copy-start(f32[4,64]{1,0:T(4,128)} %copy-done.107) | copy-start | bytes 3076
  130.4 5.8 %copy-start.33 = (f32[8,64]{1,0:T(8,128)S(1)}, f32[8,64]{1,0:T(8,128)}, u32[]{:S(2)}) copy-start(f32[8,64]{1,0:T(8,128)} %copy-done.32) | copy-start | bytes 6148
  130.5 5.8 %copy-start.35 = (f32[8,64]{1,0:T(8,128)S(1)}, f32[8,64]{1,0:T(8,128)}, u32[]{:S(2)}) copy-start(f32[8,64]{1,0:T(8,128)} %copy-done.34) | copy-start | bytes 6148
  130.5 5.8 %copy-start.58 = (f32[4,2,64]{2,1,0:T(2,128)S(1)}, f32[4,2,64]{2,1,0:T(2,128)}, u32[]{:S(2)}) copy-start(f32[4,2,64]{2,1,0:T(2,128)} %copy-done.57) | copy-start | bytes 6148
  130.5 5.8 %copy-start.60 = (f32[4,2,64]{2,1,0:T(2,128)S(1)}, f32[4,2,64]{2,1,0:T(2,128)}, u32[]{:S(2)}) copy-start(f32[4,2,64]{2,1,0:T(2,128)} %copy-done.59) | copy-start | bytes 6148
  130.5 5.8 %copy-start.62 = (f32[4,2,64]{2,1,0:T(2,128)S(1)}, f32[4,2,64]{2,1,0:T(2,128)}, u32[]{:S(2)}) copy-start(f32[4,2,64]{2,1,0:T(2,128)} %copy-done.61) | copy-start | bytes 6148
  130.5 5.8 %copy-start.105 = (f32[8,64]{1,0:T(8,128)S(1)}, f32[8,64]{1,0:T(8,128)}, u32[]{:S(2)}) copy-start(f32[8,64]{1,0:T(8,128)} %copy-done.104) | copy-start | bytes 6148
  130.9 6.2 %copy-start.18 = (f32[16,64]{1,0:T(8,128)S(1)}, f32[16,64]{1,0:T(8,128)}, u32[]{:S(2)}) copy-start(f32[16,64]{1,0:T(8,128)} %copy-done.17) | copy-start | bytes 12292
  130.9 6.2 %copy-start.20 = (f32[16,64]{1,0:T(8,128)S(1)}, f32[16,64]{1,0:T(8,128)}, u32[]{:S(2)}) copy-start(f32[16,64]{1,0:T(8,128)} %copy-done.19) | copy-start | bytes 12292
  130.9 6.2 %copy-start.22 = (f32[16,64]{1,0:T(8,128)S(1)}, f32[16,64]{1,0:T(8,128)}, u32[]{:S(2)}) copy-start(f32[16,64]{1,0:T(8,128)} %copy-done.21) | copy-start | bytes 12292
  130.9 6.2 %copy-start.30 = (f32[8,16,64]{2,0,1:T(8,128)S(1)}, f32[8,16,64]{2,0,1:T(8,128)}, u32[]{:S(2)}) copy-start(f32[8,16,64]{2,0,1:T(8,128)} %reduce_sum.313) | copy-start | bytes 98308
  130.9 6.2 %copy-start.37 = (f32[8,2,64]{2,1,0:T(2,128)S(1)}, f32[8,2,64]{2,1,0:T(2,128)}, u32[]{:S(2)}) copy-start(f32[8,2,64]{2,1,0:T(2,128)} %copy-done.36) | copy-start | bytes 12292
  130.9 6.2 %copy-start.39 = (f32[8,2,64]{2,1,0:T(2,128)S(1)}, f32[8,2,64]{2,1,0:T(2,128)}, u32[]{:S(2)}) copy-start(f32[8,2,64]{2,1,0:T(2,128)} %copy-done.38) | copy-start | bytes 12292
  130.9 6.2 %copy-start.41 = (f32[8,2,64]{2,1,0:T(2,128)S(1)}, f32[8,2,64]{2,1,0:T(2,128)}, u32[]{:S(2)}) copy-start(f32[8,2,64]{2,1,0:T(2,128)} %copy-done.40) | copy-start | bytes 12292
  130.9 6.2 %copy-start.72 = (f32[16,64]{1,0:T(8,128)S(1)}, f32[16,64]{1,0:T(8,128)}, u32[]{:S(2)}) copy-start(f32[16,64]{1,0:T(8,128)} %copy-done.71) | copy-start | bytes 12292
  (75 other events, 185.2 us)
Sparse Core Ops, SparseCore 0:
  28.9 87.8 all-gather.2

commit v14 on v12

--- a/solution.py
+++ b/solution.py
@@ -16,7 +16,7 @@
 
 SHARPNESS = 0.05
 NUGGET = 1.0
-PRECISE = lax.Precision.HIGHEST
+PRECISE = lax.Precision.HIGH
 MESH = pl.DeviceIdType.MESH
 
 
@@ -98,7 +98,7 @@
         distance_sq = (near[0:1, :] - target_x) ** 2
         distance_sq = distance_sq + (near[1:2, :] - target_y) ** 2
         distance_sq = distance_sq + (near[2:3, :] - target_z) ** 2
-        return 1.0 / (1.0 + distance_sq)
+        return pl.reciprocal(1.0 + distance_sq, approx=False)
 
     def gather_into(tile, kernel_block):
         out_ref[:, columns] += lax.dot_general(

time: 157 us -> 155 us (0.987)
  matrix products: 35 us -> 33.4 us
    dot_general x1, matrix products: 10 us -> 12.6 us  [body(): jnp.einsum('qnr,nrs->qns', source_moment, kernel_block, precision=PRECISE)]
    dot_general x5, matrix products: 7.14 us -> 5.56 us  [body(): jnp.einsum('qns,nrs->qnr', jnp.repeat(descent, 2, axis=1), transfer_maps[...]
  transfers between devices with their start and end apart: 1 -> 1, of which waited for: 0 -> 0; matrix products, arithmetic and copies ran while one was open for 20% -> 22% of each run, Pallas kernels for 41% -> 41%
where the time goes in v14:
time: 155 us; the launch traced here: 153 us
  Pallas kernels  62.7 us (40%)
  matrix products  33.4 us (22%)
  local copies, waits for them, and re-layouts  26.8 us (17%)
  between operations  16.7 us (11%)
  other arithmetic  13.7 us (9%)
    pallas_call x1, Pallas kernels, near_field_call(): pl.pallas_call(functools.partial(near_kernel, slots, W), out_shape=jax.Sh...  43.5 us
    pallas_call x1, Pallas kernels, exchange_halo(): pl.pallas_call(halo_kernel, out_shape=(shape, shape), in_specs=[vmem, vme...  19.2 us
    dot_general x1, matrix products, body(): jnp.einsum('qnr,nrs->qns', source_moment, kernel_block, precision=PRECISE)  12.6 us
    unnamed x303, local copies, waits for them, and re-layouts  5.69 us
    dot_general x5, matrix products, body(): jnp.einsum('qns,nrs->qnr', jnp.repeat(descent, 2, axis=1), transfer_maps[...  5.56 us
    dot_general x5, matrix products, body(): jnp.einsum('qnr,nrs->qns', level_moments[-1], interp_map, precision=PRECISE)  4.34 us
    reduce_sum x7, other arithmetic, interpolation(): return values / jnp.sum(values, axis=-1, keepdims=True)  4.31 us
    dot_general x5, matrix products, body(): jnp.einsum('qns,nrs->qnr', descent, own_edges[height], precision=PRECISE)  3.68 us
  transfers between devices with their start and end apart: 1, of which 0 were waited for; matrix products, arithmetic and copies ran while one was open for 22% of the time, Pallas kernels for 41%

profile of v14, /device:TPU:6, one launch (start us, length us, event | category | flops | bytes accessed | tf_op | source)
XLA Modules:
  0.0 153.3 jit_solution(3468936641726071063)
XLA Ops:
  6.5 1.2 reshape.3427
  7.9 0.9 reshape.3420
  9.0 0.9 slice_reduce_fusion.10
  10.1 1.3 slice_reduce_fusion.2
  11.6 1.1 divide_reduce_fusion
  12.7 2.3 %constant_dynamic-update-slice_fusion.6 = (f32[8,62,64]{2,0,1:T(8,128)S(1)}, f32[8,32,64]{2,0,1:T(8,128)S(1)}) fusion(f32[8,32,256]{2,0,1:T(8,128)S(1)} %bitcast.410, f32[32,256]{1,0:T(8,128)S(1)} %divide_reduce_fusion, f32[32,64]{1,0:T(8,128)S(1)} %sub.1273, f32[32,256]{1,0:T(8,128)S(1)} %sub.1271, f32[32,64]{1,0:T(8,128)S(1)} %sub.1268, ...), kind=kOutput, calls=%fused_computation.98 | convolution fusion | flops 31457280 | bytes 679936 | tf_op jit(solution)/shard_map/qbp,bpr->qbr/dot_general | solution.py:223
  15.2 1.4 divide_reduce_fusion.1
  16.5 2.1 %bitcast_reduce_fusion = f32[8,16,64]{2,0,1:T(8,128)S(1)} fusion(f32[8,32,64]{2,0,1:T(8,128)S(1)} %get-tuple-element.124, f32[32,64]{1,0:T(8,128)S(1)} %divide_reduce_fusion.1, f32[32,64]{1,0:T(8,128)S(1)} %bitcast.428, f32[32,64]{1,0:T(8,128)S(1)} %sub.1273, f32[32,64]{1,0:T(8,128)S(1)} %bitcast.425, f32[32,64]{1,0:T(8,128)S(1)} %sub.1268, ...), kind=kOutput, calls=%fused_computation.75 | convolution fusion | flops 7872512 | bytes 155648 | tf_op jit(solution)/shard_map/qnr,nrs->qns/dot_general | solution.py:230
  18.8 0.7 divide_reduce_fusion.2
  19.5 1.1 bitcast_reduce_fusion.1
  20.7 0.4 divide_reduce_fusion.3
  21.2 0.6 copy-done.113
  21.8 0.5 bitcast_reduce_fusion.2
  22.5 0.3 divide_reduce_fusion.4
  22.8 0.4 bitcast_reduce_fusion.3
  23.5 0.3 copy-done.131
  23.8 0.6 copy-done.134
  24.8 0.4 fusion.53
  26.4 0.6 copy-done.54
  28.2 0.6 slice.610
  28.8 0.6 slice.612
  29.4 0.6 bitcast_convert_fusion
  30.1 0.6 copy-done.5
  31.1 0.7 broadcast_multiply_fusion
  31.8 0.9 pad_maximum_fusion.2
  32.8 19.2 %shard_map.73 = (f32[11,4736]{1,0:T(8,128)}, f32[11,4736]{1,0:T(8,128)}) custom-call(f32[11,4736]{1,0:T(8,128)} %get-tuple-element.43.to_right, f32[11,4736]{1,0:T(8,128)} %get-tuple-element.42.to_left), custom_call_target="tpu_custom_call" | custom-call | tf_op jit(solution)/shard_map/pallas_call | solution.py:60
  52.0 1.0 slice.543
  54.0 0.5 compare_and_fusion
  54.5 1.1 pad_maximum_fusion
  55.6 0.9 gather_fusion
  56.6 0.3 select_bitcast_fusion
  57.6 12.6 %fusion.9 = f32[8,186,64]{2,0,1:T(8,128)S(1)} fusion(f32[186,64]{1,0:T(8,128)S(1)} %get-tuple-element.40, f32[186,64]{1,0:T(8,128)S(1)} %bitcast.417, f32[186,64]{1,0:T(8,128)S(1)} %get-tuple-element.41, f32[186,64]{1,0:T(8,128)S(1)} %bitcast.418, f32[186,64]{1,0:T(8,128)S(1)} %get-tuple-element.39, f32[186,64]{1,0:T(8,128)S(1)} %bitcast.419, ...), kind=kOutput, calls=%fused_computation.16 | convolution fusion | flops 45044736 | bytes 1733632 | tf_op jit(solution)/shard_map/qnr,nrs->qns/dot_general | solution.py:291
  70.3 0.9 slice.472
  71.2 0.8 slice.473
  72.0 0.6 reduce_sum.310
  72.6 0.6 reduce_sum.311
  73.2 0.6 reduce_sum.313
  73.8 0.7 reduce_sum.314
  74.6 0.8 slice.580
  75.4 0.6 reshape.3418.source_ref
  76.1 2.7 %copy.100 = f32[3,8192]{0,1:T(8,128)} copy(f32[3,8192]{1,0:T(4,128)S(1)} %copy-done.6) | data formatting | bytes 196608 | tf_op jit(solution)/shard_map/mul | solution.py:192
  78.8 0.9 constant_dynamic-slice_fusion.40
  79.7 0.9 constant_dynamic-slice_fusion.46
  80.8 0.7 maximum_multiply_fusion
  81.5 43.5 %shard_map.74 = f32[8,8192]{1,0:T(8,128)} custom-call(s32[192]{0:T(256)} %reshape.3418.source_ref, f32[38,8,256]{2,1,0:T(8,128)} %bitcast.409, f32[38,3,256]{2,1,0:T(4,128)} %bitcast.412, f32[8192,3]{1,0:T(8,128)} %bitcast.401), custom_call_target="tpu_custom_call" | custom-call | flops 352321536 | bytes 952320 | tf_op jit(solution)/shard_map/pallas_call | solution.py:173
  125.0 0.6 slice_bitcast_fusion.8
  125.6 0.6 slice_bitcast_fusion.7
  126.2 2.0 %fusion.216 = (f32[128,8,1,64]{3,1,0,2:T(8,128)S(1)}, f32[128,8,1,64]{3,1,0,2:T(8,128)S(1)}, f32[128,8,1,64]{3,1,0,2:T(8,128)S(1)}, f32[128,8,1,64]{3,1,0,2:T(8,...) fusion(f32[128,8,6,64]{3,1,0,2:T(8,128)} %bitcast.402), kind=kLoop, calls=%fused_computation.540 | loop fusion | bytes 3145728 | tf_op jit(solution)/shard_map/slice | solution.py:324
  128.3 0.8 reduce_sum.300
  129.0 0.7 constant_dynamic-update-slice_fusion.24
  129.7 0.7 constant_dynamic-update-slice_fusion.23
  130.4 0.7 constant_dynamic-update-slice_fusion.22
  131.7 1.6 %convolution_bitcast_fusion.3 = f32[8,16,64]{2,0,1:T(8,128)S(1)} fusion(f32[16,8,64]{2,1,0:T(8,128)S(1)} %constant_dynamic-update-slice_fusion.12, f32[16,64]{1,0:T(8,128)} %get-tuple-element.83, f32[16,64]{1,0:T(8,128)S(1)} %get-tuple-element.80, f32[16,64]{1,0:T(8,128)} %get-tuple-element.84, f32[16,64]{1,0:T(8,128)S(1)} %copy-done.88, ...), kind=kOutput, calls=%fused_computation.21 | convolution fusion | flops 3866624 | bytes 90112 | tf_op jit(solution)/shard_map/nqr,nrs->qns/dot_general | solution.py:338
  133.9 0.9 fusion.22
  134.8 0.8 fusion.20
  135.7 0.8 fusion.18
  136.5 0.9 fusion.16
  137.5 1.0 fusion.14
  138.5 0.4 fusion.13
  139.0 0.6 fusion.12
  139.8 1.2 fusion.11
  141.1 2.4 %fusion.10 = f32[8,32,64]{2,0,1:T(8,128)S(1)} fusion(f32[8,32,64]{2,0,1:T(8,128)S(1)} %copy-done.14, f32[8,32,64]{2,0,1:T(8,128)S(1)} %bitcast.416, f32[32,64]{1,0:T(8,128)S(1)} %copy-done.64, f32[32,64]{1,0:T(8,128)S(1)} %bitcast.429, f32[32,64]{1,0:T(8,128)S(1)} %copy-done.13, f32[32,64]{1,0:T(8,128)S(1)} %bitcast.426, f32[32,64]{1,0:T(8,128)S(1)} %copy-done.11, ...), kind=kOutput, calls=%fused_computation.19 | convolution fusion | flops 7880704 | bytes 253952 | tf_op jit(solution)/shard_map/qns,nrs->qnr/dot_general | solution.py:353
  143.6 2.1 %fusion.26 = f32[32,256,8]{1,2,0:T(8,128)S(1)} fusion(f32[8,32,64]{2,0,1:T(8,128)S(1)} %fusion.10, f32[32,256]{1,0:T(8,128)S(1)} %copy-done.49, f32[32,64]{1,0:T(8,128)S(1)} %copy-done.13, f32[32,256]{1,0:T(8,128)S(1)} %copy-done.20, f32[32,64]{1,0:T(8,128)S(1)} %copy-done.11, f32[32,256]{1,0:T(8,128)S(1)} %copy-done.18, f32[32,64]{1,0:T(8,128)S(1)} %sub.1263, ...), kind=kOutput, calls=%fused_computation.48 | convolution fusion | flops 31457280 | bytes 483328 | tf_op jit(solution)/shard_map/qbr,bpr->qbp/dot_general | solution.py:357
  145.7 0.7 add_add_fusion
  (417 shorter events, 6.1 us)
Async XLA Ops:
  6.5 6.1 %copy-start.3 = (f32[8,8192]{1,0:T(8,128)S(1)}, f32[8,8192]{1,0:T(8,128)}, u32[]{:S(2)}) copy-start(f32[8,8192]{1,0:T(8,128)} %param.7) | copy-start | bytes 786436
  6.5 119.7 %all-gather.3.cloned.1.call-start = ((), (), s32[]{:S(2)}) async-start(), calls=%async_computation | async-start | bytes 3170304 | tf_op jit(solution)/shard_map/all_gather | solution.py:319
  7.8 15.3 %copy-start.50 = (f32[3,8,64]{2,1,0:T(8,128)}, f32[3,8,64]{2,1,0:T(8,128)S(1)}, u32[]{:S(2)}) copy-start(f32[3,8,64]{2,1,0:T(8,128)S(1)} %slice.585) | copy-start | bytes 18436
  7.8 16.9 %copy-start.55 = (f32[3,4,64]{2,1,0:T(4,128)}, f32[3,4,64]{2,1,0:T(4,128)S(1)}, u32[]{:S(2)}) copy-start(f32[3,4,64]{2,1,0:T(4,128)S(1)} %slice.586) | copy-start | bytes 9220
  7.8 16.8 %copy-start.27 = (f32[3,32,64]{2,1,0:T(8,128)}, f32[3,32,64]{2,1,0:T(8,128)S(1)}, u32[]{:S(2)}) copy-start(f32[3,32,64]{2,1,0:T(8,128)S(1)} %slice.583) | copy-start | bytes 73732
  7.8 16.8 %copy-start.35 = (f32[3,16,64]{2,1,0:T(8,128)}, f32[3,16,64]{2,1,0:T(8,128)S(1)}, u32[]{:S(2)}) copy-start(f32[3,16,64]{2,1,0:T(8,128)S(1)} %slice.584) | copy-start | bytes 36868
  7.9 15.3 %copy-start.9 = (f32[3,128,64]{2,1,0:T(8,128)}, f32[3,128,64]{2,1,0:T(8,128)S(1)}, u32[]{:S(2)}) copy-start(f32[3,128,64]{2,1,0:T(8,128)S(1)} %slice.581) | copy-start | bytes 294916
  7.9 16.7 %copy-start.21 = (f32[3,64,64]{2,1,0:T(8,128)}, f32[3,64,64]{2,1,0:T(8,128)S(1)}, u32[]{:S(2)}) copy-start(f32[3,64,64]{2,1,0:T(8,128)S(1)} %slice.582) | copy-start | bytes 147460
  8.8 20.0 %copy-start.2 = (f32[3,30,64]{2,1,0:T(8,128)}, f32[3,30,64]{2,1,0:T(8,128)S(1)}, u32[]{:S(2)}) copy-start(f32[3,30,64]{2,1,0:T(8,128)S(1)} %reshape.3420) | copy-start | bytes 69124
  8.8 10.7 %copy-start.23 = (f32[16,64]{1,0:T(8,128)}, f32[16,64]{1,0:T(8,128)S(1)}, u32[]{:S(2)}) copy-start(f32[16,64]{1,0:T(8,128)S(1)} %get-tuple-element.77) | copy-start | bytes 12292
  8.8 10.7 %copy-start.25 = (f32[16,64]{1,0:T(8,128)}, f32[16,64]{1,0:T(8,128)S(1)}, u32[]{:S(2)}) copy-start(f32[16,64]{1,0:T(8,128)S(1)} %get-tuple-element.78) | copy-start | bytes 12292
  8.8 12.2 %copy-start.36 = (f32[8,64]{1,0:T(8,128)}, f32[8,64]{1,0:T(8,128)S(1)}, u32[]{:S(2)}) copy-start(f32[8,64]{1,0:T(8,128)S(1)} %get-tuple-element.73) | copy-start | bytes 6148
  8.8 12.2 %copy-start.38 = (f32[8,64]{1,0:T(8,128)}, f32[8,64]{1,0:T(8,128)S(1)}, u32[]{:S(2)}) copy-start(f32[8,64]{1,0:T(8,128)S(1)} %get-tuple-element.74) | copy-start | bytes 6148
  8.8 12.2 %copy-start.40 = (f32[8,64]{1,0:T(8,128)}, f32[8,64]{1,0:T(8,128)S(1)}, u32[]{:S(2)}) copy-start(f32[8,64]{1,0:T(8,128)S(1)} %get-tuple-element.75) | copy-start | bytes 6148
  8.9 13.9 %copy-start.57 = (f32[4,64]{1,0:T(4,128)}, f32[4,64]{1,0:T(4,128)S(1)}, u32[]{:S(2)}) copy-start(f32[4,64]{1,0:T(4,128)S(1)} %get-tuple-element.70) | copy-start | bytes 3076
  8.9 13.9 %copy-start.59 = (f32[4,64]{1,0:T(4,128)}, f32[4,64]{1,0:T(4,128)S(1)}, u32[]{:S(2)}) copy-start(f32[4,64]{1,0:T(4,128)S(1)} %get-tuple-element.71) | copy-start | bytes 3076
  8.9 13.9 %copy-start.61 = (f32[4,64]{1,0:T(4,128)}, f32[4,64]{1,0:T(4,128)S(1)}, u32[]{:S(2)}) copy-start(f32[4,64]{1,0:T(4,128)S(1)} %get-tuple-element.72) | copy-start | bytes 3076
  8.9 14.6 %copy-start.73 = (f32[2,64]{1,0:T(2,128)}, f32[2,64]{1,0:T(2,128)S(1)}, u32[]{:S(2)}) copy-start(f32[2,64]{1,0:T(2,128)S(1)} %get-tuple-element.67) | copy-start | bytes 1540
  8.9 14.6 %copy-start.75 = (f32[2,64]{1,0:T(2,128)}, f32[2,64]{1,0:T(2,128)S(1)}, u32[]{:S(2)}) copy-start(f32[2,64]{1,0:T(2,128)S(1)} %get-tuple-element.68) | copy-start | bytes 1540
  8.9 14.6 %copy-start.77 = (f32[2,64]{1,0:T(2,128)}, f32[2,64]{1,0:T(2,128)S(1)}, u32[]{:S(2)}) copy-start(f32[2,64]{1,0:T(2,128)S(1)} %get-tuple-element.69) | copy-start | bytes 1540
  10.1 6.5 %copy-start.10 = (f32[32,64]{1,0:T(8,128)}, f32[32,64]{1,0:T(8,128)S(1)}, u32[]{:S(2)}) copy-start(f32[32,64]{1,0:T(8,128)S(1)} %sub.1268) | copy-start | bytes 24580
  10.1 6.4 %copy-start.12 = (f32[32,64]{1,0:T(8,128)}, f32[32,64]{1,0:T(8,128)S(1)}, u32[]{:S(2)}) copy-start(f32[32,64]{1,0:T(8,128)S(1)} %sub.1273) | copy-start | bytes 24580
  22.4 5.3 %copy-start.22 = (f32[3,2048]{1,0:T(4,128)S(1)}, f32[3,2048]{1,0:T(4,128)}, u32[]{:S(2)}) copy-start(f32[3,2048]{1,0:T(4,128)} %param.10) | copy-start | bytes 73732
  22.4 5.6 %copy-start.72 = (s32[32,3]{0,1:T(4,128)S(1)}, s32[32,3]{0,1:T(4,128)}, u32[]{:S(2)}) copy-start(s32[32,3]{0,1:T(4,128)} %param.13) | copy-start | bytes 1156
  22.4 5.8 %copy-start.81 = (f32[2,2,64]{2,1,0:T(2,128)}, f32[2,2,64]{2,1,0:T(2,128)S(1)}, u32[]{:S(2)}) copy-start(f32[2,2,64]{2,1,0:T(2,128)S(1)} %broadcast_in_dim.132) | copy-start | bytes 3076
  22.4 5.7 %copy-start.83 = (f32[2,2,64]{2,1,0:T(2,128)}, f32[2,2,64]{2,1,0:T(2,128)S(1)}, u32[]{:S(2)}) copy-start(f32[2,2,64]{2,1,0:T(2,128)S(1)} %broadcast_in_dim.134) | copy-start | bytes 3076
  22.5 5.7 %copy-start.85 = (f32[2,2,64]{2,1,0:T(2,128)}, f32[2,2,64]{2,1,0:T(2,128)S(1)}, u32[]{:S(2)}) copy-start(f32[2,2,64]{2,1,0:T(2,128)S(1)} %broadcast_in_dim.136) | copy-start | bytes 3076
  24.7 6.0 %copy-start.89 = (f32[64]{0:T(128)}, f32[64]{0:T(128)S(1)}, u32[]{:S(2)}) copy-start(f32[64]{0:T(128)S(1)} %get-tuple-element.57) | copy-start | bytes 772
  24.7 6.0 %copy-start.91 = (f32[64]{0:T(128)}, f32[64]{0:T(128)S(1)}, u32[]{:S(2)}) copy-start(f32[64]{0:T(128)S(1)} %get-tuple-element.58) | copy-start | bytes 772
  24.7 6.0 %copy-start.93 = (f32[64]{0:T(128)}, f32[64]{0:T(128)S(1)}, u32[]{:S(2)}) copy-start(f32[64]{0:T(128)S(1)} %get-tuple-element.59) | copy-start | bytes 772
  25.2 5.6 %copy-start.136 = (f32[64]{0:T(128)}, f32[64]{0:T(128)S(1)}, u32[]{:S(2)}) copy-start(f32[64]{0:T(128)S(1)} %get-tuple-element.23) | copy-start | bytes 772
  25.2 5.6 %copy-start.137 = (f32[64]{0:T(128)}, f32[64]{0:T(128)S(1)}, u32[]{:S(2)}) copy-start(f32[64]{0:T(128)S(1)} %get-tuple-element.22) | copy-start | bytes 772
  25.2 5.6 %copy-start.139 = (f32[64]{0:T(128)}, f32[64]{0:T(128)S(1)}, u32[]{:S(2)}) copy-start(f32[64]{0:T(128)S(1)} %get-tuple-element.20) | copy-start | bytes 772
  25.2 5.6 %copy-start.140 = (f32[64]{0:T(128)}, f32[64]{0:T(128)S(1)}, u32[]{:S(2)}) copy-start(f32[64]{0:T(128)S(1)} %get-tuple-element.24) | copy-start | bytes 772
  31.8 21.6 %copy-start = (f32[11,8192]{1,0:T(8,128)}, f32[11,8192]{1,0:T(8,128)S(1)}, u32[]{:S(2)}) copy-start(f32[11,8192]{1,0:T(8,128)S(1)} %get-tuple-element.52) | copy-start | bytes 1081348
  70.2 5.1 %copy-start.115 = (s32[32,6]{0,1:T(8,128)S(1)}, s32[32,6]{0,1:T(8,128)}, u32[]{:S(2)}) copy-start(s32[32,6]{0,1:T(8,128)} %param.9) | copy-start | bytes 2308
  70.2 5.8 %copy-start.6 = (f32[3,8192]{1,0:T(4,128)S(1)}, f32[3,8192]{1,0:T(4,128)}, u32[]{:S(2)}) copy-start(f32[3,8192]{1,0:T(4,128)} %get-tuple-element.51) | copy-start | bytes 294916
  131.6 4.9 %copy-start.119 = (f32[64]{0:T(128)S(1)}, f32[64]{0:T(128)}, u32[]{:S(2)}) copy-start(f32[64]{0:T(128)} %copy-done.118) | copy-start | bytes 772
  131.6 5.8 %copy-start.74 = (f32[2,64]{1,0:T(2,128)S(1)}, f32[2,64]{1,0:T(2,128)}, u32[]{:S(2)}) copy-start(f32[2,64]{1,0:T(2,128)} %copy-done.73) | copy-start | bytes 1540
  131.6 5.8 %copy-start.76 = (f32[2,64]{1,0:T(2,128)S(1)}, f32[2,64]{1,0:T(2,128)}, u32[]{:S(2)}) copy-start(f32[2,64]{1,0:T(2,128)} %copy-done.75) | copy-start | bytes 1540
  131.6 5.8 %copy-start.78 = (f32[2,64]{1,0:T(2,128)S(1)}, f32[2,64]{1,0:T(2,128)}, u32[]{:S(2)}) copy-start(f32[2,64]{1,0:T(2,128)} %copy-done.77) | copy-start | bytes 1540
  131.6 5.8 %copy-start.87 = (f32[8,2,64]{2,0,1:T(8,128)S(1)}, f32[8,2,64]{2,0,1:T(8,128)}, u32[]{:S(2)}) copy-start(f32[8,2,64]{2,0,1:T(8,128)} %reduce_sum.310) | copy-start | bytes 12292
  131.6 6.8 %copy-start.58 = (f32[4,64]{1,0:T(4,128)S(1)}, f32[4,64]{1,0:T(4,128)}, u32[]{:S(2)}) copy-start(f32[4,64]{1,0:T(4,128)} %copy-done.57) | copy-start | bytes 3076
  131.7 6.8 %copy-start.60 = (f32[4,64]{1,0:T(4,128)S(1)}, f32[4,64]{1,0:T(4,128)}, u32[]{:S(2)}) copy-start(f32[4,64]{1,0:T(4,128)} %copy-done.59) | copy-start | bytes 3076
  131.7 6.8 %copy-start.62 = (f32[4,64]{1,0:T(4,128)S(1)}, f32[4,64]{1,0:T(4,128)}, u32[]{:S(2)}) copy-start(f32[4,64]{1,0:T(4,128)} %copy-done.61) | copy-start | bytes 3076
  131.7 6.8 %copy-start.71 = (f32[8,4,64]{2,0,1:T(8,128)S(1)}, f32[8,4,64]{2,0,1:T(8,128)}, u32[]{:S(2)}) copy-start(f32[8,4,64]{2,0,1:T(8,128)} %reduce_sum.311) | copy-start | bytes 24580
  131.7 6.8 %copy-start.82 = (f32[2,2,64]{2,1,0:T(2,128)S(1)}, f32[2,2,64]{2,1,0:T(2,128)}, u32[]{:S(2)}) copy-start(f32[2,2,64]{2,1,0:T(2,128)} %copy-done.81) | copy-start | bytes 3076
  131.7 6.8 %copy-start.84 = (f32[2,2,64]{2,1,0:T(2,128)S(1)}, f32[2,2,64]{2,1,0:T(2,128)}, u32[]{:S(2)}) copy-start(f32[2,2,64]{2,1,0:T(2,128)} %copy-done.83) | copy-start | bytes 3076
  131.7 6.8 %copy-start.86 = (f32[2,2,64]{2,1,0:T(2,128)S(1)}, f32[2,2,64]{2,1,0:T(2,128)}, u32[]{:S(2)}) copy-start(f32[2,2,64]{2,1,0:T(2,128)} %copy-done.85) | copy-start | bytes 3076
  131.7 6.8 %copy-start.117 = (f32[4,64]{1,0:T(4,128)S(1)}, f32[4,64]{1,0:T(4,128)}, u32[]{:S(2)}) copy-start(f32[4,64]{1,0:T(4,128)} %copy-done.116) | copy-start | bytes 3076
  133.4 5.6 %copy-start.37 = (f32[8,64]{1,0:T(8,128)S(1)}, f32[8,64]{1,0:T(8,128)}, u32[]{:S(2)}) copy-start(f32[8,64]{1,0:T(8,128)} %copy-done.36) | copy-start | bytes 6148
  133.4 5.6 %copy-start.39 = (f32[8,64]{1,0:T(8,128)S(1)}, f32[8,64]{1,0:T(8,128)}, u32[]{:S(2)}) copy-start(f32[8,64]{1,0:T(8,128)} %copy-done.38) | copy-start | bytes 6148
  133.4 5.6 %copy-start.41 = (f32[8,64]{1,0:T(8,128)S(1)}, f32[8,64]{1,0:T(8,128)}, u32[]{:S(2)}) copy-start(f32[8,64]{1,0:T(8,128)} %copy-done.40) | copy-start | bytes 6148
  133.4 5.6 %copy-start.66 = (f32[4,2,64]{2,1,0:T(2,128)S(1)}, f32[4,2,64]{2,1,0:T(2,128)}, u32[]{:S(2)}) copy-start(f32[4,2,64]{2,1,0:T(2,128)} %copy-done.65) | copy-start | bytes 6148
  133.4 5.6 %copy-start.68 = (f32[4,2,64]{2,1,0:T(2,128)S(1)}, f32[4,2,64]{2,1,0:T(2,128)}, u32[]{:S(2)}) copy-start(f32[4,2,64]{2,1,0:T(2,128)} %copy-done.67) | copy-start | bytes 6148
  133.4 5.6 %copy-start.70 = (f32[4,2,64]{2,1,0:T(2,128)S(1)}, f32[4,2,64]{2,1,0:T(2,128)}, u32[]{:S(2)}) copy-start(f32[4,2,64]{2,1,0:T(2,128)} %copy-done.69) | copy-start | bytes 6148
  133.4 5.6 %copy-start.114 = (f32[8,64]{1,0:T(8,128)S(1)}, f32[8,64]{1,0:T(8,128)}, u32[]{:S(2)}) copy-start(f32[8,64]{1,0:T(8,128)} %copy-done.113) | copy-start | bytes 6148
  133.8 5.9 %copy-start.24 = (f32[16,64]{1,0:T(8,128)S(1)}, f32[16,64]{1,0:T(8,128)}, u32[]{:S(2)}) copy-start(f32[16,64]{1,0:T(8,128)} %copy-done.23) | copy-start | bytes 12292
  133.8 5.9 %copy-start.26 = (f32[16,64]{1,0:T(8,128)S(1)}, f32[16,64]{1,0:T(8,128)}, u32[]{:S(2)}) copy-start(f32[16,64]{1,0:T(8,128)} %copy-done.25) | copy-start | bytes 12292
  133.8 5.9 %copy-start.34 = (f32[8,16,64]{2,0,1:T(8,128)S(1)}, f32[8,16,64]{2,0,1:T(8,128)}, u32[]{:S(2)}) copy-start(f32[8,16,64]{2,0,1:T(8,128)} %reduce_sum.313) | copy-start | bytes 98308
  133.8 5.9 %copy-start.43 = (f32[8,2,64]{2,1,0:T(2,128)S(1)}, f32[8,2,64]{2,1,0:T(2,128)}, u32[]{:S(2)}) copy-start(f32[8,2,64]{2,1,0:T(2,128)} %copy-done.42) | copy-start | bytes 12292
  133.8 5.9 %copy-start.45 = (f32[8,2,64]{2,1,0:T(2,128)S(1)}, f32[8,2,64]{2,1,0:T(2,128)}, u32[]{:S(2)}) copy-start(f32[8,2,64]{2,1,0:T(2,128)} %copy-done.44) | copy-start | bytes 12292
  133.8 5.9 %copy-start.47 = (f32[8,2,64]{2,1,0:T(2,128)S(1)}, f32[8,2,64]{2,1,0:T(2,128)}, u32[]{:S(2)}) copy-start(f32[8,2,64]{2,1,0:T(2,128)} %copy-done.46) | copy-start | bytes 12292
  133.9 5.9 %copy-start.80 = (f32[16,64]{1,0:T(8,128)S(1)}, f32[16,64]{1,0:T(8,128)}, u32[]{:S(2)}) copy-start(f32[16,64]{1,0:T(8,128)} %copy-done.79) | copy-start | bytes 12292
  (84 other events, 194.8 us)
Sparse Core Ops, SparseCore 0:
  27.2 87.8 all-gather.2

commit v15 on v12

--- a/solution.py
+++ b/solution.py
@@ -111,7 +111,34 @@
         out_ref[...] = jnp.zeros_like(out_ref)
         gather_into(here - 1, block(here - 1))
 
-    gather_into(here, block(here))
+    half = size // 2
+    own = coords_ref[here]
+    own_probes = probes_ref[here]
+
+    def quarter(rows, cols):
+        distance_sq = (own[0:1, cols] - target_x[rows, cols]) ** 2
+        distance_sq = distance_sq + (own[1:2, cols] - target_y[rows, cols]) ** 2
+        distance_sq = distance_sq + (own[2:3, cols] - target_z[rows, cols]) ** 2
+        return 1.0 / (1.0 + distance_sq)
+
+    low, high = slice(0, half), slice(half, size)
+    upper_left = quarter(low, low)
+    upper_right = quarter(low, high)
+    lower_right = quarter(high, high)
+
+    def side(probe_part, kernel_part):
+        return lax.dot_general(
+            probe_part, kernel_part, (((1,), (1,)), ((), ())),
+            precision=lax.Precision.HIGH, preferred_element_type=jnp.float32,
+        )
+
+    first = pl.ds(pl.multiple_of(box * size, size), half)
+    second = pl.ds(pl.multiple_of(box * size + half, half), half)
+    out_ref[:, first] += side(own_probes[:, low], upper_left) + side(own_probes[:, high], upper_right)
+    out_ref[:, second] += jnp.dot(
+        own_probes[:, low], upper_right, precision=lax.Precision.HIGH,
+        preferred_element_type=jnp.float32,
+    ) + side(own_probes[:, high], lower_right)
     pair_block = block(here + 1)
     gather_into(here + 1, pair_block)
 

time: 157 us -> 154 us (0.981)
  the two profiles are of different devices: /device:TPU:6 before, /device:TPU:62 now
where the time goes in v15:
time: 154 us; the launch traced here: 153 us
  Pallas kernels  60.5 us (39%)
  matrix products  35 us (23%)
  local copies, waits for them, and re-layouts  27 us (18%)
  between operations  16.7 us (11%)
  other arithmetic  13.7 us (9%)
    pallas_call x1, Pallas kernels, near_field_call(): pl.pallas_call(functools.partial(near_kernel, slots, W), out_shape=jax.Sh...  43.5 us
    pallas_call x1, Pallas kernels, exchange_halo(): pl.pallas_call(halo_kernel, out_shape=(shape, shape), in_specs=[vmem, vme...  17.1 us
    dot_general x1, matrix products, body(): jnp.einsum('qnr,nrs->qns', source_moment, kernel_block, precision=PRECISE)  10 us
    dot_general x5, matrix products, body(): jnp.einsum('qns,nrs->qnr', jnp.repeat(descent, 2, axis=1), transfer_maps[...  7.14 us
    unnamed x303, local copies, waits for them, and re-layouts  5.68 us
    dot_general x5, matrix products, body(): jnp.einsum('qnr,nrs->qns', level_moments[-1], interp_map, precision=PRECISE)  5.15 us
    reduce_sum x7, other arithmetic, interpolation(): return values / jnp.sum(values, axis=-1, keepdims=True)  4.31 us
    dot_general x5, matrix products, body(): jnp.einsum('qns,nrs->qnr', descent, own_edges[height], precision=PRECISE)  3.82 us
  transfers between devices with their start and end apart: 1, of which 0 were waited for; matrix products, arithmetic and copies ran while one was open for 21% of the time, Pallas kernels for 40%

profile of v15, /device:TPU:62, one launch (start us, length us, event | category | flops | bytes accessed | tf_op | source)
XLA Modules:
  0.0 152.9 jit_solution(6899753234905082993)
XLA Ops:
  6.5 1.2 reshape.3427
  7.9 0.9 reshape.3420
  9.0 0.9 slice_reduce_fusion.10
  10.1 1.3 slice_reduce_fusion.2
  11.6 1.1 divide_reduce_fusion
  12.7 3.3 %constant_dynamic-update-slice_fusion.6 = (f32[8,62,64]{2,0,1:T(8,128)S(1)}, f32[8,32,64]{2,0,1:T(8,128)S(1)}) fusion(f32[8,32,256]{2,0,1:T(8,128)S(1)} %bitcast.410, f32[32,256]{1,0:T(8,128)S(1)} %divide_reduce_fusion, f32[32,64]{1,0:T(8,128)S(1)} %sub.1273, f32[32,256]{1,0:T(8,128)S(1)} %sub.1271, f32[32,64]{1,0:T(8,128)S(1)} %sub.1268, ...), kind=kOutput, calls=%fused_computation.98 | convolution fusion | flops 56623104 | bytes 679936 | tf_op jit(solution)/shard_map/qbp,bpr->qbr/dot_general | solution.py:250
  16.1 1.4 divide_reduce_fusion.1
  17.5 2.6 %bitcast_reduce_fusion = f32[8,16,64]{2,0,1:T(8,128)S(1)} fusion(f32[8,32,64]{2,0,1:T(8,128)S(1)} %get-tuple-element.124, f32[32,64]{1,0:T(8,128)S(1)} %divide_reduce_fusion.1, f32[32,64]{1,0:T(8,128)S(1)} %bitcast.428, f32[32,64]{1,0:T(8,128)S(1)} %sub.1273, f32[32,64]{1,0:T(8,128)S(1)} %bitcast.425, f32[32,64]{1,0:T(8,128)S(1)} %sub.1268, ...), kind=kOutput, calls=%fused_computation.75 | convolution fusion | flops 14163968 | bytes 155648 | tf_op jit(solution)/shard_map/qnr,nrs->qns/dot_general | solution.py:257
  20.2 0.7 divide_reduce_fusion.2
  20.9 1.3 bitcast_reduce_fusion.1
  22.3 0.4 divide_reduce_fusion.3
  22.8 0.6 copy-done.113
  23.4 0.6 bitcast_reduce_fusion.2
  24.5 0.4 bitcast_reduce_fusion.3
  25.3 0.3 copy-done.131
  25.6 0.6 copy-done.134
  26.1 0.3 constant_dynamic-update-slice_fusion.11
  26.6 0.4 fusion.53
  28.3 0.6 copy-done.54
  30.0 0.6 slice.610
  30.6 0.6 slice.612
  31.2 0.6 bitcast_convert_fusion
  31.9 0.6 copy-done.5
  32.9 0.7 broadcast_multiply_fusion
  33.6 0.9 pad_maximum_fusion.2
  34.6 17.1 %shard_map.73 = (f32[11,4736]{1,0:T(8,128)}, f32[11,4736]{1,0:T(8,128)}) custom-call(f32[11,4736]{1,0:T(8,128)} %get-tuple-element.43.to_right, f32[11,4736]{1,0:T(8,128)} %get-tuple-element.42.to_left), custom_call_target="tpu_custom_call" | custom-call | tf_op jit(solution)/shard_map/pallas_call | solution.py:60
  51.7 1.0 slice.543
  53.7 0.5 compare_and_fusion
  54.2 1.1 pad_maximum_fusion
  55.3 0.9 gather_fusion
  56.3 0.3 select_bitcast_fusion
  57.3 10.0 %fusion.9 = f32[8,186,64]{2,0,1:T(8,128)S(1)} fusion(f32[186,64]{1,0:T(8,128)S(1)} %get-tuple-element.40, f32[186,64]{1,0:T(8,128)S(1)} %bitcast.417, f32[186,64]{1,0:T(8,128)S(1)} %get-tuple-element.41, f32[186,64]{1,0:T(8,128)S(1)} %bitcast.418, f32[186,64]{1,0:T(8,128)S(1)} %get-tuple-element.39, f32[186,64]{1,0:T(8,128)S(1)} %bitcast.419, ...), kind=kOutput, calls=%fused_computation.16 | convolution fusion | flops 81613824 | bytes 1733632 | tf_op jit(solution)/shard_map/qnr,nrs->qns/dot_general | solution.py:318
  67.5 0.9 slice.472
  68.4 0.8 slice.473
  69.2 0.6 reduce_sum.310
  69.8 0.6 reduce_sum.311
  70.4 0.6 reduce_sum.313
  71.0 0.7 reduce_sum.314
  71.8 0.8 slice.580
  72.6 0.6 reshape.3418.source_ref
  73.3 2.9 %copy.100 = f32[3,8192]{0,1:T(8,128)} copy(f32[3,8192]{1,0:T(4,128)S(1)} %copy-done.6) | data formatting | bytes 196608 | tf_op jit(solution)/shard_map/mul | solution.py:219
  76.2 0.9 constant_dynamic-slice_fusion.40
  77.1 0.9 constant_dynamic-slice_fusion.46
  78.2 0.7 maximum_multiply_fusion
  78.9 43.5 %shard_map.74 = f32[8,8192]{1,0:T(8,128)} custom-call(s32[192]{0:T(256)} %reshape.3418.source_ref, f32[38,8,256]{2,1,0:T(8,128)} %bitcast.409, f32[38,3,256]{2,1,0:T(4,128)} %bitcast.412, f32[8192,3]{1,0:T(8,128)} %bitcast.401), custom_call_target="tpu_custom_call" | custom-call | flops 352321536 | bytes 952320 | tf_op jit(solution)/shard_map/pallas_call | solution.py:200
  122.3 0.6 slice_bitcast_fusion.8
  122.9 0.6 slice_bitcast_fusion.7
  123.6 2.0 %fusion.216 = (f32[128,8,1,64]{3,1,0,2:T(8,128)S(1)}, f32[128,8,1,64]{3,1,0,2:T(8,128)S(1)}, f32[128,8,1,64]{3,1,0,2:T(8,128)S(1)}, f32[128,8,1,64]{3,1,0,2:T(8,...) fusion(f32[128,8,6,64]{3,1,0,2:T(8,128)} %bitcast.402), kind=kLoop, calls=%fused_computation.540 | loop fusion | bytes 3145728 | tf_op jit(solution)/shard_map/slice | solution.py:351
  125.6 0.8 reduce_sum.300
  126.4 0.7 constant_dynamic-update-slice_fusion.24
  127.0 0.7 constant_dynamic-update-slice_fusion.23
  127.7 0.7 constant_dynamic-update-slice_fusion.22
  129.1 1.6 %convolution_bitcast_fusion.3 = f32[8,16,64]{2,0,1:T(8,128)S(1)} fusion(f32[16,8,64]{2,1,0:T(8,128)S(1)} %constant_dynamic-update-slice_fusion.12, f32[16,64]{1,0:T(8,128)} %get-tuple-element.83, f32[16,64]{1,0:T(8,128)S(1)} %get-tuple-element.80, f32[16,64]{1,0:T(8,128)} %get-tuple-element.84, f32[16,64]{1,0:T(8,128)S(1)} %copy-done.88, ...), kind=kOutput, calls=%fused_computation.21 | convolution fusion | flops 7012352 | bytes 90112 | tf_op jit(solution)/shard_map/nqr,nrs->qns/dot_general | solution.py:365
  131.2 1.0 fusion.22
  132.2 0.9 fusion.20
  133.2 0.8 fusion.18
  134.0 0.9 fusion.16
  135.0 1.0 fusion.14
  136.1 0.5 fusion.13
  136.6 0.8 fusion.12
  137.6 1.6 %fusion.11 = f32[8,16,64]{2,0,1:T(8,128)S(1)} fusion(f32[8,16,64]{2,0,1:T(8,128)S(1)} %copy-done.34, f32[8,16,64]{2,0,1:T(8,128)S(1)} %bitcast.430, f32[16,64]{1,0:T(8,128)S(1)} %copy-done.80, f32[16,64]{1,0:T(8,128)S(1)} %bitcast.439, f32[16,64]{1,0:T(8,128)S(1)} %copy-done.24, f32[16,64]{1,0:T(8,128)S(1)} %bitcast.436, f32[16,64]{1,0:T(8,128)S(1)} %copy-done.26, ...), kind=kOutput, calls=%fused_computation.22 | convolution fusion | flops 7086080 | bytes 126976 | tf_op jit(solution)/shard_map/qns,nrs->qnr/dot_general | solution.py:380
  139.3 3.2 %fusion.10 = f32[8,32,64]{2,0,1:T(8,128)S(1)} fusion(f32[8,32,64]{2,0,1:T(8,128)S(1)} %copy-done.14, f32[8,32,64]{2,0,1:T(8,128)S(1)} %bitcast.416, f32[32,64]{1,0:T(8,128)S(1)} %copy-done.64, f32[32,64]{1,0:T(8,128)S(1)} %bitcast.429, f32[32,64]{1,0:T(8,128)S(1)} %copy-done.13, f32[32,64]{1,0:T(8,128)S(1)} %bitcast.426, f32[32,64]{1,0:T(8,128)S(1)} %copy-done.11, ...), kind=kOutput, calls=%fused_computation.19 | convolution fusion | flops 14172160 | bytes 253952 | tf_op jit(solution)/shard_map/qns,nrs->qnr/dot_general | solution.py:380
  142.6 2.7 %fusion.26 = f32[32,256,8]{1,2,0:T(8,128)S(1)} fusion(f32[8,32,64]{2,0,1:T(8,128)S(1)} %fusion.10, f32[32,256]{1,0:T(8,128)S(1)} %copy-done.49, f32[32,64]{1,0:T(8,128)S(1)} %copy-done.13, f32[32,256]{1,0:T(8,128)S(1)} %copy-done.20, f32[32,64]{1,0:T(8,128)S(1)} %copy-done.11, f32[32,256]{1,0:T(8,128)S(1)} %copy-done.18, f32[32,64]{1,0:T(8,128)S(1)} %sub.1263, ...), kind=kOutput, calls=%fused_computation.48 | convolution fusion | flops 56623104 | bytes 483328 | tf_op jit(solution)/shard_map/qbr,bpr->qbp/dot_general | solution.py:384
  145.3 0.7 add_add_fusion
  (417 shorter events, 6.2 us)
Async XLA Ops:
  6.5 6.1 %copy-start.3 = (f32[8,8192]{1,0:T(8,128)S(1)}, f32[8,8192]{1,0:T(8,128)}, u32[]{:S(2)}) copy-start(f32[8,8192]{1,0:T(8,128)} %param.7) | copy-start | bytes 786436
  6.5 117.0 %all-gather.3.cloned.1.call-start = ((), (), s32[]{:S(2)}) async-start(), calls=%async_computation | async-start | bytes 3170304 | tf_op jit(solution)/shard_map/all_gather | solution.py:346
  7.8 17.1 %copy-start.50 = (f32[3,8,64]{2,1,0:T(8,128)}, f32[3,8,64]{2,1,0:T(8,128)S(1)}, u32[]{:S(2)}) copy-start(f32[3,8,64]{2,1,0:T(8,128)S(1)} %slice.585) | copy-start | bytes 18436
  7.8 18.7 %copy-start.55 = (f32[3,4,64]{2,1,0:T(4,128)}, f32[3,4,64]{2,1,0:T(4,128)S(1)}, u32[]{:S(2)}) copy-start(f32[3,4,64]{2,1,0:T(4,128)S(1)} %slice.586) | copy-start | bytes 9220
  7.8 18.6 %copy-start.27 = (f32[3,32,64]{2,1,0:T(8,128)}, f32[3,32,64]{2,1,0:T(8,128)S(1)}, u32[]{:S(2)}) copy-start(f32[3,32,64]{2,1,0:T(8,128)S(1)} %slice.583) | copy-start | bytes 73732
  7.8 18.6 %copy-start.35 = (f32[3,16,64]{2,1,0:T(8,128)}, f32[3,16,64]{2,1,0:T(8,128)S(1)}, u32[]{:S(2)}) copy-start(f32[3,16,64]{2,1,0:T(8,128)S(1)} %slice.584) | copy-start | bytes 36868
  7.9 17.0 %copy-start.9 = (f32[3,128,64]{2,1,0:T(8,128)}, f32[3,128,64]{2,1,0:T(8,128)S(1)}, u32[]{:S(2)}) copy-start(f32[3,128,64]{2,1,0:T(8,128)S(1)} %slice.581) | copy-start | bytes 294916
  7.9 18.5 %copy-start.21 = (f32[3,64,64]{2,1,0:T(8,128)}, f32[3,64,64]{2,1,0:T(8,128)S(1)}, u32[]{:S(2)}) copy-start(f32[3,64,64]{2,1,0:T(8,128)S(1)} %slice.582) | copy-start | bytes 147460
  8.8 21.8 %copy-start.2 = (f32[3,30,64]{2,1,0:T(8,128)}, f32[3,30,64]{2,1,0:T(8,128)S(1)}, u32[]{:S(2)}) copy-start(f32[3,30,64]{2,1,0:T(8,128)S(1)} %reshape.3420) | copy-start | bytes 69124
  8.8 12.1 %copy-start.23 = (f32[16,64]{1,0:T(8,128)}, f32[16,64]{1,0:T(8,128)S(1)}, u32[]{:S(2)}) copy-start(f32[16,64]{1,0:T(8,128)S(1)} %get-tuple-element.77) | copy-start | bytes 12292
  8.8 12.1 %copy-start.25 = (f32[16,64]{1,0:T(8,128)}, f32[16,64]{1,0:T(8,128)S(1)}, u32[]{:S(2)}) copy-start(f32[16,64]{1,0:T(8,128)S(1)} %get-tuple-element.78) | copy-start | bytes 12292
  8.8 13.8 %copy-start.36 = (f32[8,64]{1,0:T(8,128)}, f32[8,64]{1,0:T(8,128)S(1)}, u32[]{:S(2)}) copy-start(f32[8,64]{1,0:T(8,128)S(1)} %get-tuple-element.73) | copy-start | bytes 6148
  8.8 13.8 %copy-start.38 = (f32[8,64]{1,0:T(8,128)}, f32[8,64]{1,0:T(8,128)S(1)}, u32[]{:S(2)}) copy-start(f32[8,64]{1,0:T(8,128)S(1)} %get-tuple-element.74) | copy-start | bytes 6148
  8.8 13.8 %copy-start.40 = (f32[8,64]{1,0:T(8,128)}, f32[8,64]{1,0:T(8,128)S(1)}, u32[]{:S(2)}) copy-start(f32[8,64]{1,0:T(8,128)S(1)} %get-tuple-element.75) | copy-start | bytes 6148
  8.9 15.6 %copy-start.57 = (f32[4,64]{1,0:T(4,128)}, f32[4,64]{1,0:T(4,128)S(1)}, u32[]{:S(2)}) copy-start(f32[4,64]{1,0:T(4,128)S(1)} %get-tuple-element.70) | copy-start | bytes 3076
  8.9 15.6 %copy-start.59 = (f32[4,64]{1,0:T(4,128)}, f32[4,64]{1,0:T(4,128)S(1)}, u32[]{:S(2)}) copy-start(f32[4,64]{1,0:T(4,128)S(1)} %get-tuple-element.71) | copy-start | bytes 3076
  8.9 15.6 %copy-start.61 = (f32[4,64]{1,0:T(4,128)}, f32[4,64]{1,0:T(4,128)S(1)}, u32[]{:S(2)}) copy-start(f32[4,64]{1,0:T(4,128)S(1)} %get-tuple-element.72) | copy-start | bytes 3076
  8.9 16.3 %copy-start.73 = (f32[2,64]{1,0:T(2,128)}, f32[2,64]{1,0:T(2,128)S(1)}, u32[]{:S(2)}) copy-start(f32[2,64]{1,0:T(2,128)S(1)} %get-tuple-element.67) | copy-start | bytes 1540
  8.9 16.3 %copy-start.75 = (f32[2,64]{1,0:T(2,128)}, f32[2,64]{1,0:T(2,128)S(1)}, u32[]{:S(2)}) copy-start(f32[2,64]{1,0:T(2,128)S(1)} %get-tuple-element.68) | copy-start | bytes 1540
  8.9 16.3 %copy-start.77 = (f32[2,64]{1,0:T(2,128)}, f32[2,64]{1,0:T(2,128)S(1)}, u32[]{:S(2)}) copy-start(f32[2,64]{1,0:T(2,128)S(1)} %get-tuple-element.69) | copy-start | bytes 1540
  10.1 7.4 %copy-start.10 = (f32[32,64]{1,0:T(8,128)}, f32[32,64]{1,0:T(8,128)S(1)}, u32[]{:S(2)}) copy-start(f32[32,64]{1,0:T(8,128)S(1)} %sub.1268) | copy-start | bytes 24580
  10.1 7.4 %copy-start.12 = (f32[32,64]{1,0:T(8,128)}, f32[32,64]{1,0:T(8,128)S(1)}, u32[]{:S(2)}) copy-start(f32[32,64]{1,0:T(8,128)S(1)} %sub.1273) | copy-start | bytes 24580
  24.1 5.5 %copy-start.22 = (f32[3,2048]{1,0:T(4,128)S(1)}, f32[3,2048]{1,0:T(4,128)}, u32[]{:S(2)}) copy-start(f32[3,2048]{1,0:T(4,128)} %param.10) | copy-start | bytes 73732
  24.1 5.7 %copy-start.72 = (s32[32,3]{0,1:T(4,128)S(1)}, s32[32,3]{0,1:T(4,128)}, u32[]{:S(2)}) copy-start(s32[32,3]{0,1:T(4,128)} %param.13) | copy-start | bytes 1156
  24.1 5.9 %copy-start.81 = (f32[2,2,64]{2,1,0:T(2,128)}, f32[2,2,64]{2,1,0:T(2,128)S(1)}, u32[]{:S(2)}) copy-start(f32[2,2,64]{2,1,0:T(2,128)S(1)} %broadcast_in_dim.132) | copy-start | bytes 3076
  24.1 5.9 %copy-start.83 = (f32[2,2,64]{2,1,0:T(2,128)}, f32[2,2,64]{2,1,0:T(2,128)S(1)}, u32[]{:S(2)}) copy-start(f32[2,2,64]{2,1,0:T(2,128)S(1)} %broadcast_in_dim.134) | copy-start | bytes 3076
  24.2 5.9 %copy-start.85 = (f32[2,2,64]{2,1,0:T(2,128)}, f32[2,2,64]{2,1,0:T(2,128)S(1)}, u32[]{:S(2)}) copy-start(f32[2,2,64]{2,1,0:T(2,128)S(1)} %broadcast_in_dim.136) | copy-start | bytes 3076
  26.5 6.1 %copy-start.89 = (f32[64]{0:T(128)}, f32[64]{0:T(128)S(1)}, u32[]{:S(2)}) copy-start(f32[64]{0:T(128)S(1)} %get-tuple-element.57) | copy-start | bytes 772
  26.5 6.1 %copy-start.91 = (f32[64]{0:T(128)}, f32[64]{0:T(128)S(1)}, u32[]{:S(2)}) copy-start(f32[64]{0:T(128)S(1)} %get-tuple-element.58) | copy-start | bytes 772
  26.5 6.1 %copy-start.93 = (f32[64]{0:T(128)}, f32[64]{0:T(128)S(1)}, u32[]{:S(2)}) copy-start(f32[64]{0:T(128)S(1)} %get-tuple-element.59) | copy-start | bytes 772
  27.0 5.6 %copy-start.136 = (f32[64]{0:T(128)}, f32[64]{0:T(128)S(1)}, u32[]{:S(2)}) copy-start(f32[64]{0:T(128)S(1)} %get-tuple-element.23) | copy-start | bytes 772
  27.0 5.6 %copy-start.137 = (f32[64]{0:T(128)}, f32[64]{0:T(128)S(1)}, u32[]{:S(2)}) copy-start(f32[64]{0:T(128)S(1)} %get-tuple-element.22) | copy-start | bytes 772
  27.0 5.6 %copy-start.139 = (f32[64]{0:T(128)}, f32[64]{0:T(128)S(1)}, u32[]{:S(2)}) copy-start(f32[64]{0:T(128)S(1)} %get-tuple-element.20) | copy-start | bytes 772
  27.0 5.6 %copy-start.140 = (f32[64]{0:T(128)}, f32[64]{0:T(128)S(1)}, u32[]{:S(2)}) copy-start(f32[64]{0:T(128)S(1)} %get-tuple-element.24) | copy-start | bytes 772
  33.6 19.5 %copy-start = (f32[11,8192]{1,0:T(8,128)}, f32[11,8192]{1,0:T(8,128)S(1)}, u32[]{:S(2)}) copy-start(f32[11,8192]{1,0:T(8,128)S(1)} %get-tuple-element.52) | copy-start | bytes 1081348
  67.4 5.1 %copy-start.115 = (s32[32,6]{0,1:T(8,128)S(1)}, s32[32,6]{0,1:T(8,128)}, u32[]{:S(2)}) copy-start(s32[32,6]{0,1:T(8,128)} %param.9) | copy-start | bytes 2308
  67.4 5.8 %copy-start.6 = (f32[3,8192]{1,0:T(4,128)S(1)}, f32[3,8192]{1,0:T(4,128)}, u32[]{:S(2)}) copy-start(f32[3,8192]{1,0:T(4,128)} %get-tuple-element.51) | copy-start | bytes 294916
  128.9 5.0 %copy-start.119 = (f32[64]{0:T(128)S(1)}, f32[64]{0:T(128)}, u32[]{:S(2)}) copy-start(f32[64]{0:T(128)} %copy-done.118) | copy-start | bytes 772
  129.0 5.9 %copy-start.74 = (f32[2,64]{1,0:T(2,128)S(1)}, f32[2,64]{1,0:T(2,128)}, u32[]{:S(2)}) copy-start(f32[2,64]{1,0:T(2,128)} %copy-done.73) | copy-start | bytes 1540
  129.0 6.0 %copy-start.76 = (f32[2,64]{1,0:T(2,128)S(1)}, f32[2,64]{1,0:T(2,128)}, u32[]{:S(2)}) copy-start(f32[2,64]{1,0:T(2,128)} %copy-done.75) | copy-start | bytes 1540
  129.0 6.0 %copy-start.78 = (f32[2,64]{1,0:T(2,128)S(1)}, f32[2,64]{1,0:T(2,128)}, u32[]{:S(2)}) copy-start(f32[2,64]{1,0:T(2,128)} %copy-done.77) | copy-start | bytes 1540
  129.0 6.0 %copy-start.87 = (f32[8,2,64]{2,0,1:T(8,128)S(1)}, f32[8,2,64]{2,0,1:T(8,128)}, u32[]{:S(2)}) copy-start(f32[8,2,64]{2,0,1:T(8,128)} %reduce_sum.310) | copy-start | bytes 12292
  129.0 7.0 %copy-start.58 = (f32[4,64]{1,0:T(4,128)S(1)}, f32[4,64]{1,0:T(4,128)}, u32[]{:S(2)}) copy-start(f32[4,64]{1,0:T(4,128)} %copy-done.57) | copy-start | bytes 3076
  129.0 7.0 %copy-start.60 = (f32[4,64]{1,0:T(4,128)S(1)}, f32[4,64]{1,0:T(4,128)}, u32[]{:S(2)}) copy-start(f32[4,64]{1,0:T(4,128)} %copy-done.59) | copy-start | bytes 3076
  129.0 7.0 %copy-start.62 = (f32[4,64]{1,0:T(4,128)S(1)}, f32[4,64]{1,0:T(4,128)}, u32[]{:S(2)}) copy-start(f32[4,64]{1,0:T(4,128)} %copy-done.61) | copy-start | bytes 3076
  129.0 7.0 %copy-start.71 = (f32[8,4,64]{2,0,1:T(8,128)S(1)}, f32[8,4,64]{2,0,1:T(8,128)}, u32[]{:S(2)}) copy-start(f32[8,4,64]{2,0,1:T(8,128)} %reduce_sum.311) | copy-start | bytes 24580
  129.0 7.0 %copy-start.82 = (f32[2,2,64]{2,1,0:T(2,128)S(1)}, f32[2,2,64]{2,1,0:T(2,128)}, u32[]{:S(2)}) copy-start(f32[2,2,64]{2,1,0:T(2,128)} %copy-done.81) | copy-start | bytes 3076
  129.0 7.0 %copy-start.84 = (f32[2,2,64]{2,1,0:T(2,128)S(1)}, f32[2,2,64]{2,1,0:T(2,128)}, u32[]{:S(2)}) copy-start(f32[2,2,64]{2,1,0:T(2,128)} %copy-done.83) | copy-start | bytes 3076
  129.1 7.0 %copy-start.86 = (f32[2,2,64]{2,1,0:T(2,128)S(1)}, f32[2,2,64]{2,1,0:T(2,128)}, u32[]{:S(2)}) copy-start(f32[2,2,64]{2,1,0:T(2,128)} %copy-done.85) | copy-start | bytes 3076
  129.1 7.0 %copy-start.117 = (f32[4,64]{1,0:T(4,128)S(1)}, f32[4,64]{1,0:T(4,128)}, u32[]{:S(2)}) copy-start(f32[4,64]{1,0:T(4,128)} %copy-done.116) | copy-start | bytes 3076
  130.7 5.8 %copy-start.37 = (f32[8,64]{1,0:T(8,128)S(1)}, f32[8,64]{1,0:T(8,128)}, u32[]{:S(2)}) copy-start(f32[8,64]{1,0:T(8,128)} %copy-done.36) | copy-start | bytes 6148
  130.7 5.8 %copy-start.39 = (f32[8,64]{1,0:T(8,128)S(1)}, f32[8,64]{1,0:T(8,128)}, u32[]{:S(2)}) copy-start(f32[8,64]{1,0:T(8,128)} %copy-done.38) | copy-start | bytes 6148
  130.7 5.8 %copy-start.41 = (f32[8,64]{1,0:T(8,128)S(1)}, f32[8,64]{1,0:T(8,128)}, u32[]{:S(2)}) copy-start(f32[8,64]{1,0:T(8,128)} %copy-done.40) | copy-start | bytes 6148
  130.8 5.8 %copy-start.66 = (f32[4,2,64]{2,1,0:T(2,128)S(1)}, f32[4,2,64]{2,1,0:T(2,128)}, u32[]{:S(2)}) copy-start(f32[4,2,64]{2,1,0:T(2,128)} %copy-done.65) | copy-start | bytes 6148
  130.8 5.8 %copy-start.68 = (f32[4,2,64]{2,1,0:T(2,128)S(1)}, f32[4,2,64]{2,1,0:T(2,128)}, u32[]{:S(2)}) copy-start(f32[4,2,64]{2,1,0:T(2,128)} %copy-done.67) | copy-start | bytes 6148
  130.8 5.8 %copy-start.70 = (f32[4,2,64]{2,1,0:T(2,128)S(1)}, f32[4,2,64]{2,1,0:T(2,128)}, u32[]{:S(2)}) copy-start(f32[4,2,64]{2,1,0:T(2,128)} %copy-done.69) | copy-start | bytes 6148
  130.8 5.8 %copy-start.114 = (f32[8,64]{1,0:T(8,128)S(1)}, f32[8,64]{1,0:T(8,128)}, u32[]{:S(2)}) copy-start(f32[8,64]{1,0:T(8,128)} %copy-done.113) | copy-start | bytes 6148
  131.2 6.3 %copy-start.24 = (f32[16,64]{1,0:T(8,128)S(1)}, f32[16,64]{1,0:T(8,128)}, u32[]{:S(2)}) copy-start(f32[16,64]{1,0:T(8,128)} %copy-done.23) | copy-start | bytes 12292
  131.2 6.3 %copy-start.26 = (f32[16,64]{1,0:T(8,128)S(1)}, f32[16,64]{1,0:T(8,128)}, u32[]{:S(2)}) copy-start(f32[16,64]{1,0:T(8,128)} %copy-done.25) | copy-start | bytes 12292
  131.2 6.3 %copy-start.34 = (f32[8,16,64]{2,0,1:T(8,128)S(1)}, f32[8,16,64]{2,0,1:T(8,128)}, u32[]{:S(2)}) copy-start(f32[8,16,64]{2,0,1:T(8,128)} %reduce_sum.313) | copy-start | bytes 98308
  131.2 6.3 %copy-start.43 = (f32[8,2,64]{2,1,0:T(2,128)S(1)}, f32[8,2,64]{2,1,0:T(2,128)}, u32[]{:S(2)}) copy-start(f32[8,2,64]{2,1,0:T(2,128)} %copy-done.42) | copy-start | bytes 12292
  131.2 6.3 %copy-start.45 = (f32[8,2,64]{2,1,0:T(2,128)S(1)}, f32[8,2,64]{2,1,0:T(2,128)}, u32[]{:S(2)}) copy-start(f32[8,2,64]{2,1,0:T(2,128)} %copy-done.44) | copy-start | bytes 12292
  131.2 6.3 %copy-start.47 = (f32[8,2,64]{2,1,0:T(2,128)S(1)}, f32[8,2,64]{2,1,0:T(2,128)}, u32[]{:S(2)}) copy-start(f32[8,2,64]{2,1,0:T(2,128)} %copy-done.46) | copy-start | bytes 12292
  131.2 6.3 %copy-start.80 = (f32[16,64]{1,0:T(8,128)S(1)}, f32[16,64]{1,0:T(8,128)}, u32[]{:S(2)}) copy-start(f32[16,64]{1,0:T(8,128)} %copy-done.79) | copy-start | bytes 12292
  (84 other events, 210.1 us)
Sparse Core Ops, SparseCore 0:
  29.0 86.1 all-gather.2

commit v16 on v12

--- a/solution.py
+++ b/solution.py
@@ -17,6 +17,7 @@
 SHARPNESS = 0.05
 NUGGET = 1.0
 PRECISE = lax.Precision.HIGHEST
+TAIL_PRECISION = lax.Precision.HIGH
 MESH = pl.DeviceIdType.MESH
 
 
@@ -336,7 +337,7 @@
         jnp.concatenate(top_sources, axis=1), jnp.concatenate(top_targets, axis=1), kernel_scale
     )
     contributions = jnp.einsum(
-        "nqr,nrs->qns", jnp.concatenate(top_moments, axis=0), kernel_block, precision=PRECISE
+        "nqr,nrs->qns", jnp.concatenate(top_moments, axis=0), kernel_block, precision=TAIL_PRECISION
     )
     top_couplings = []
     first = 0
@@ -346,15 +347,15 @@
     descent = top_couplings[-1]
     for height in range(top_levels - 2, -1, -1):
         descent = (
-            jnp.einsum("qns,nrs->qnr", descent, own_edges[height], precision=PRECISE)
+            jnp.einsum("qns,nrs->qnr", descent, own_edges[height], precision=TAIL_PRECISION)
             + top_couplings[height]
         )
     for height in range(local_depth - 1, -1, -1):
         descent = jnp.einsum(
-            "qns,nrs->qnr", jnp.repeat(descent, 2, axis=1), transfer_maps[height], precision=PRECISE
+            "qns,nrs->qnr", jnp.repeat(descent, 2, axis=1), transfer_maps[height], precision=TAIL_PRECISION
         )
         descent = descent + local_couplings[height]
-    far_field = jnp.einsum("qbr,bpr->qbp", descent, leaf_basis, precision=PRECISE).reshape(
+    far_field = jnp.einsum("qbr,bpr->qbp", descent, leaf_basis, precision=TAIL_PRECISION).reshape(
         rows_here, BOXES_DEV * P_SIZE
     )
     return near_field + far_field + NUGGET * probes

time: 157 us -> 153 us (0.975)
  matrix products: 35 us -> 32.7 us
    dot_general x5, matrix products: 7.14 us -> 5.56 us  [body(): jnp.einsum('qns,nrs->qnr', jnp.repeat(descent, 2, axis=1), transfer_maps[...]
  transfers between devices with their start and end apart: 1 -> 1, of which waited for: 0 -> 0; matrix products, arithmetic and copies ran while one was open for 20% -> 21% of each run, Pallas kernels for 41% -> 41%
where the time goes in v16:
time: 153 us; the launch traced here: 152 us
  Pallas kernels  62.1 us (41%)
  matrix products  32.7 us (21%)
  local copies, waits for them, and re-layouts  26.9 us (18%)
  between operations  16.8 us (11%)
  other arithmetic  13.7 us (9%)
    pallas_call x1, Pallas kernels, near_field_call(): pl.pallas_call(functools.partial(near_kernel, slots, W), out_shape=jax.Sh...  42.9 us
    pallas_call x1, Pallas kernels, exchange_halo(): pl.pallas_call(halo_kernel, out_shape=(shape, shape), in_specs=[vmem, vme...  19.2 us
    dot_general x1, matrix products, body(): jnp.einsum('qnr,nrs->qns', source_moment, kernel_block, precision=PRECISE)  10 us
    unnamed x303, local copies, waits for them, and re-layouts  5.68 us
    dot_general x5, matrix products, body(): jnp.einsum('qns,nrs->qnr', jnp.repeat(descent, 2, axis=1), transfer_maps[...  5.56 us
    dot_general x5, matrix products, body(): jnp.einsum('qnr,nrs->qns', level_moments[-1], interp_map, precision=PRECISE)  5.15 us
    reduce_sum x7, other arithmetic, interpolation(): return values / jnp.sum(values, axis=-1, keepdims=True)  4.31 us
    dot_general x5, matrix products, body(): jnp.einsum('qns,nrs->qnr', descent, own_edges[height], precision=TAIL_PRE...  3.68 us
  transfers between devices with their start and end apart: 1, of which 0 were waited for; matrix products, arithmetic and copies ran while one was open for 21% of the time, Pallas kernels for 41%

profile of v16, /device:TPU:6, one launch (start us, length us, event | category | flops | bytes accessed | tf_op | source)
XLA Modules:
  0.0 152.1 jit_solution(9732836128191428942)
XLA Ops:
  6.5 1.2 reshape.3427
  7.9 0.9 reshape.3420
  9.0 0.9 slice_reduce_fusion.10
  10.1 1.3 slice_reduce_fusion.2
  11.6 1.1 divide_reduce_fusion
  12.7 3.3 %constant_dynamic-update-slice_fusion.6 = (f32[8,62,64]{2,0,1:T(8,128)S(1)}, f32[8,32,64]{2,0,1:T(8,128)S(1)}) fusion(f32[8,32,256]{2,0,1:T(8,128)S(1)} %bitcast.410, f32[32,256]{1,0:T(8,128)S(1)} %divide_reduce_fusion, f32[32,64]{1,0:T(8,128)S(1)} %sub.1273, f32[32,256]{1,0:T(8,128)S(1)} %sub.1271, f32[32,64]{1,0:T(8,128)S(1)} %sub.1268, ...), kind=kOutput, calls=%fused_computation.98 | convolution fusion | flops 56623104 | bytes 679936 | tf_op jit(solution)/shard_map/qbp,bpr->qbr/dot_general | solution.py:224
  16.1 1.4 divide_reduce_fusion.1
  17.5 2.6 %bitcast_reduce_fusion = f32[8,16,64]{2,0,1:T(8,128)S(1)} fusion(f32[8,32,64]{2,0,1:T(8,128)S(1)} %get-tuple-element.124, f32[32,64]{1,0:T(8,128)S(1)} %divide_reduce_fusion.1, f32[32,64]{1,0:T(8,128)S(1)} %bitcast.428, f32[32,64]{1,0:T(8,128)S(1)} %sub.1273, f32[32,64]{1,0:T(8,128)S(1)} %bitcast.425, f32[32,64]{1,0:T(8,128)S(1)} %sub.1268, ...), kind=kOutput, calls=%fused_computation.75 | convolution fusion | flops 14163968 | bytes 155648 | tf_op jit(solution)/shard_map/qnr,nrs->qns/dot_general | solution.py:231
  20.2 0.7 divide_reduce_fusion.2
  20.9 1.3 bitcast_reduce_fusion.1
  22.3 0.4 divide_reduce_fusion.3
  22.8 0.6 copy-done.113
  23.4 0.6 bitcast_reduce_fusion.2
  24.5 0.4 bitcast_reduce_fusion.3
  25.3 0.3 copy-done.131
  25.6 0.6 copy-done.134
  26.1 0.3 constant_dynamic-update-slice_fusion.11
  26.6 0.4 fusion.53
  28.3 0.6 copy-done.54
  30.0 0.6 slice.610
  30.6 0.6 slice.612
  31.2 0.6 bitcast_convert_fusion
  31.9 0.6 copy-done.5
  32.9 0.7 broadcast_multiply_fusion
  33.6 0.9 pad_maximum_fusion.2
  34.6 19.2 %shard_map.73 = (f32[11,4736]{1,0:T(8,128)}, f32[11,4736]{1,0:T(8,128)}) custom-call(f32[11,4736]{1,0:T(8,128)} %get-tuple-element.43.to_right, f32[11,4736]{1,0:T(8,128)} %get-tuple-element.42.to_left), custom_call_target="tpu_custom_call" | custom-call | tf_op jit(solution)/shard_map/pallas_call | solution.py:61
  53.8 1.0 slice.543
  55.8 0.5 compare_and_fusion
  56.4 1.1 pad_maximum_fusion
  57.4 0.9 gather_fusion
  58.4 0.3 select_bitcast_fusion
  59.4 10.0 %fusion.9 = f32[8,186,64]{2,0,1:T(8,128)S(1)} fusion(f32[186,64]{1,0:T(8,128)S(1)} %get-tuple-element.40, f32[186,64]{1,0:T(8,128)S(1)} %bitcast.417, f32[186,64]{1,0:T(8,128)S(1)} %get-tuple-element.41, f32[186,64]{1,0:T(8,128)S(1)} %bitcast.418, f32[186,64]{1,0:T(8,128)S(1)} %get-tuple-element.39, f32[186,64]{1,0:T(8,128)S(1)} %bitcast.419, ...), kind=kOutput, calls=%fused_computation.16 | convolution fusion | flops 81613824 | bytes 1733632 | tf_op jit(solution)/shard_map/qnr,nrs->qns/dot_general | solution.py:292
  69.6 0.9 slice.472
  70.5 0.8 slice.473
  71.3 0.6 reduce_sum.310
  71.9 0.6 reduce_sum.311
  72.5 0.6 reduce_sum.313
  73.2 0.7 reduce_sum.314
  73.9 0.8 slice.580
  74.8 0.6 reshape.3418.source_ref
  75.4 2.9 %copy.100 = f32[3,8192]{0,1:T(8,128)} copy(f32[3,8192]{1,0:T(4,128)S(1)} %copy-done.6) | data formatting | bytes 196608 | tf_op jit(solution)/shard_map/mul | solution.py:193
  78.3 0.9 constant_dynamic-slice_fusion.40
  79.2 0.9 constant_dynamic-slice_fusion.46
  80.3 0.7 maximum_multiply_fusion
  81.0 42.9 %shard_map.74 = f32[8,8192]{1,0:T(8,128)} custom-call(s32[192]{0:T(256)} %reshape.3418.source_ref, f32[38,8,256]{2,1,0:T(8,128)} %bitcast.409, f32[38,3,256]{2,1,0:T(4,128)} %bitcast.412, f32[8192,3]{1,0:T(8,128)} %bitcast.401), custom_call_target="tpu_custom_call" | custom-call | flops 352321536 | bytes 952320 | tf_op jit(solution)/shard_map/pallas_call | solution.py:174
  123.9 0.6 slice_bitcast_fusion.8
  124.5 0.6 slice_bitcast_fusion.7
  125.1 2.0 %fusion.216 = (f32[128,8,1,64]{3,1,0,2:T(8,128)S(1)}, f32[128,8,1,64]{3,1,0,2:T(8,128)S(1)}, f32[128,8,1,64]{3,1,0,2:T(8,128)S(1)}, f32[128,8,1,64]{3,1,0,2:T(8,...) fusion(f32[128,8,6,64]{3,1,0,2:T(8,128)} %bitcast.402), kind=kLoop, calls=%fused_computation.540 | loop fusion | bytes 3145728 | tf_op jit(solution)/shard_map/slice | solution.py:325
  127.1 0.8 reduce_sum.300
  127.9 0.7 constant_dynamic-update-slice_fusion.24
  128.6 0.7 constant_dynamic-update-slice_fusion.23
  129.3 0.7 constant_dynamic-update-slice_fusion.22
  130.6 1.6 %convolution_bitcast_fusion.3 = f32[8,16,64]{2,0,1:T(8,128)S(1)} fusion(f32[16,8,64]{2,1,0:T(8,128)S(1)} %constant_dynamic-update-slice_fusion.12, f32[16,64]{1,0:T(8,128)} %get-tuple-element.83, f32[16,64]{1,0:T(8,128)S(1)} %get-tuple-element.80, f32[16,64]{1,0:T(8,128)} %get-tuple-element.84, f32[16,64]{1,0:T(8,128)S(1)} %copy-done.88, ...), kind=kOutput, calls=%fused_computation.21 | convolution fusion | flops 3866624 | bytes 90112 | tf_op jit(solution)/shard_map/nqr,nrs->qns/dot_general | solution.py:339
  132.7 0.9 fusion.22
  133.7 0.8 fusion.20
  134.6 0.8 fusion.18
  135.4 0.9 fusion.16
  136.4 1.0 fusion.14
  137.4 0.4 fusion.13
  137.9 0.6 fusion.12
  138.6 1.2 fusion.11
  140.0 2.4 %fusion.10 = f32[8,32,64]{2,0,1:T(8,128)S(1)} fusion(f32[8,32,64]{2,0,1:T(8,128)S(1)} %copy-done.14, f32[8,32,64]{2,0,1:T(8,128)S(1)} %bitcast.416, f32[32,64]{1,0:T(8,128)S(1)} %copy-done.64, f32[32,64]{1,0:T(8,128)S(1)} %bitcast.429, f32[32,64]{1,0:T(8,128)S(1)} %copy-done.13, f32[32,64]{1,0:T(8,128)S(1)} %bitcast.426, f32[32,64]{1,0:T(8,128)S(1)} %copy-done.11, ...), kind=kOutput, calls=%fused_computation.19 | convolution fusion | flops 7880704 | bytes 253952 | tf_op jit(solution)/shard_map/qns,nrs->qnr/dot_general | solution.py:354
  142.4 2.1 %fusion.26 = f32[32,256,8]{1,2,0:T(8,128)S(1)} fusion(f32[8,32,64]{2,0,1:T(8,128)S(1)} %fusion.10, f32[32,256]{1,0:T(8,128)S(1)} %copy-done.49, f32[32,64]{1,0:T(8,128)S(1)} %copy-done.13, f32[32,256]{1,0:T(8,128)S(1)} %copy-done.20, f32[32,64]{1,0:T(8,128)S(1)} %copy-done.11, f32[32,256]{1,0:T(8,128)S(1)} %copy-done.18, f32[32,64]{1,0:T(8,128)S(1)} %sub.1263, ...), kind=kOutput, calls=%fused_computation.48 | convolution fusion | flops 31457280 | bytes 483328 | tf_op jit(solution)/shard_map/qbr,bpr->qbp/dot_general | solution.py:358
  144.5 0.7 add_add_fusion
  (417 shorter events, 6.2 us)
Async XLA Ops:
  6.5 6.1 %copy-start.3 = (f32[8,8192]{1,0:T(8,128)S(1)}, f32[8,8192]{1,0:T(8,128)}, u32[]{:S(2)}) copy-start(f32[8,8192]{1,0:T(8,128)} %param.7) | copy-start | bytes 786436
  6.5 118.6 %all-gather.3.cloned.1.call-start = ((), (), s32[]{:S(2)}) async-start(), calls=%async_computation | async-start | bytes 3170304 | tf_op jit(solution)/shard_map/all_gather | solution.py:320
  7.8 17.1 %copy-start.50 = (f32[3,8,64]{2,1,0:T(8,128)}, f32[3,8,64]{2,1,0:T(8,128)S(1)}, u32[]{:S(2)}) copy-start(f32[3,8,64]{2,1,0:T(8,128)S(1)} %slice.585) | copy-start | bytes 18436
  7.8 18.7 %copy-start.55 = (f32[3,4,64]{2,1,0:T(4,128)}, f32[3,4,64]{2,1,0:T(4,128)S(1)}, u32[]{:S(2)}) copy-start(f32[3,4,64]{2,1,0:T(4,128)S(1)} %slice.586) | copy-start | bytes 9220
  7.8 18.6 %copy-start.27 = (f32[3,32,64]{2,1,0:T(8,128)}, f32[3,32,64]{2,1,0:T(8,128)S(1)}, u32[]{:S(2)}) copy-start(f32[3,32,64]{2,1,0:T(8,128)S(1)} %slice.583) | copy-start | bytes 73732
  7.8 18.6 %copy-start.35 = (f32[3,16,64]{2,1,0:T(8,128)}, f32[3,16,64]{2,1,0:T(8,128)S(1)}, u32[]{:S(2)}) copy-start(f32[3,16,64]{2,1,0:T(8,128)S(1)} %slice.584) | copy-start | bytes 36868
  7.9 17.0 %copy-start.9 = (f32[3,128,64]{2,1,0:T(8,128)}, f32[3,128,64]{2,1,0:T(8,128)S(1)}, u32[]{:S(2)}) copy-start(f32[3,128,64]{2,1,0:T(8,128)S(1)} %slice.581) | copy-start | bytes 294916
  7.9 18.5 %copy-start.21 = (f32[3,64,64]{2,1,0:T(8,128)}, f32[3,64,64]{2,1,0:T(8,128)S(1)}, u32[]{:S(2)}) copy-start(f32[3,64,64]{2,1,0:T(8,128)S(1)} %slice.582) | copy-start | bytes 147460
  8.8 21.8 %copy-start.2 = (f32[3,30,64]{2,1,0:T(8,128)}, f32[3,30,64]{2,1,0:T(8,128)S(1)}, u32[]{:S(2)}) copy-start(f32[3,30,64]{2,1,0:T(8,128)S(1)} %reshape.3420) | copy-start | bytes 69124
  8.8 12.1 %copy-start.23 = (f32[16,64]{1,0:T(8,128)}, f32[16,64]{1,0:T(8,128)S(1)}, u32[]{:S(2)}) copy-start(f32[16,64]{1,0:T(8,128)S(1)} %get-tuple-element.77) | copy-start | bytes 12292
  8.8 12.1 %copy-start.25 = (f32[16,64]{1,0:T(8,128)}, f32[16,64]{1,0:T(8,128)S(1)}, u32[]{:S(2)}) copy-start(f32[16,64]{1,0:T(8,128)S(1)} %get-tuple-element.78) | copy-start | bytes 12292
  8.8 13.8 %copy-start.36 = (f32[8,64]{1,0:T(8,128)}, f32[8,64]{1,0:T(8,128)S(1)}, u32[]{:S(2)}) copy-start(f32[8,64]{1,0:T(8,128)S(1)} %get-tuple-element.73) | copy-start | bytes 6148
  8.8 13.8 %copy-start.38 = (f32[8,64]{1,0:T(8,128)}, f32[8,64]{1,0:T(8,128)S(1)}, u32[]{:S(2)}) copy-start(f32[8,64]{1,0:T(8,128)S(1)} %get-tuple-element.74) | copy-start | bytes 6148
  8.8 13.8 %copy-start.40 = (f32[8,64]{1,0:T(8,128)}, f32[8,64]{1,0:T(8,128)S(1)}, u32[]{:S(2)}) copy-start(f32[8,64]{1,0:T(8,128)S(1)} %get-tuple-element.75) | copy-start | bytes 6148
  8.9 15.6 %copy-start.57 = (f32[4,64]{1,0:T(4,128)}, f32[4,64]{1,0:T(4,128)S(1)}, u32[]{:S(2)}) copy-start(f32[4,64]{1,0:T(4,128)S(1)} %get-tuple-element.70) | copy-start | bytes 3076
  8.9 15.6 %copy-start.59 = (f32[4,64]{1,0:T(4,128)}, f32[4,64]{1,0:T(4,128)S(1)}, u32[]{:S(2)}) copy-start(f32[4,64]{1,0:T(4,128)S(1)} %get-tuple-element.71) | copy-start | bytes 3076
  8.9 15.6 %copy-start.61 = (f32[4,64]{1,0:T(4,128)}, f32[4,64]{1,0:T(4,128)S(1)}, u32[]{:S(2)}) copy-start(f32[4,64]{1,0:T(4,128)S(1)} %get-tuple-element.72) | copy-start | bytes 3076
  8.9 16.3 %copy-start.73 = (f32[2,64]{1,0:T(2,128)}, f32[2,64]{1,0:T(2,128)S(1)}, u32[]{:S(2)}) copy-start(f32[2,64]{1,0:T(2,128)S(1)} %get-tuple-element.67) | copy-start | bytes 1540
  8.9 16.3 %copy-start.75 = (f32[2,64]{1,0:T(2,128)}, f32[2,64]{1,0:T(2,128)S(1)}, u32[]{:S(2)}) copy-start(f32[2,64]{1,0:T(2,128)S(1)} %get-tuple-element.68) | copy-start | bytes 1540
  8.9 16.3 %copy-start.77 = (f32[2,64]{1,0:T(2,128)}, f32[2,64]{1,0:T(2,128)S(1)}, u32[]{:S(2)}) copy-start(f32[2,64]{1,0:T(2,128)S(1)} %get-tuple-element.69) | copy-start | bytes 1540
  10.1 7.4 %copy-start.10 = (f32[32,64]{1,0:T(8,128)}, f32[32,64]{1,0:T(8,128)S(1)}, u32[]{:S(2)}) copy-start(f32[32,64]{1,0:T(8,128)S(1)} %sub.1268) | copy-start | bytes 24580
  10.1 7.4 %copy-start.12 = (f32[32,64]{1,0:T(8,128)}, f32[32,64]{1,0:T(8,128)S(1)}, u32[]{:S(2)}) copy-start(f32[32,64]{1,0:T(8,128)S(1)} %sub.1273) | copy-start | bytes 24580
  24.1 5.5 %copy-start.22 = (f32[3,2048]{1,0:T(4,128)S(1)}, f32[3,2048]{1,0:T(4,128)}, u32[]{:S(2)}) copy-start(f32[3,2048]{1,0:T(4,128)} %param.10) | copy-start | bytes 73732
  24.1 5.7 %copy-start.72 = (s32[32,3]{0,1:T(4,128)S(1)}, s32[32,3]{0,1:T(4,128)}, u32[]{:S(2)}) copy-start(s32[32,3]{0,1:T(4,128)} %param.13) | copy-start | bytes 1156
  24.1 5.9 %copy-start.81 = (f32[2,2,64]{2,1,0:T(2,128)}, f32[2,2,64]{2,1,0:T(2,128)S(1)}, u32[]{:S(2)}) copy-start(f32[2,2,64]{2,1,0:T(2,128)S(1)} %broadcast_in_dim.132) | copy-start | bytes 3076
  24.1 5.9 %copy-start.83 = (f32[2,2,64]{2,1,0:T(2,128)}, f32[2,2,64]{2,1,0:T(2,128)S(1)}, u32[]{:S(2)}) copy-start(f32[2,2,64]{2,1,0:T(2,128)S(1)} %broadcast_in_dim.134) | copy-start | bytes 3076
  24.2 5.9 %copy-start.85 = (f32[2,2,64]{2,1,0:T(2,128)}, f32[2,2,64]{2,1,0:T(2,128)S(1)}, u32[]{:S(2)}) copy-start(f32[2,2,64]{2,1,0:T(2,128)S(1)} %broadcast_in_dim.136) | copy-start | bytes 3076
  24.5 5.0 %copy-start.116 = (f32[4,64]{1,0:T(4,128)}, f32[4,64]{1,0:T(4,128)S(1)}, u32[]{:S(2)}) copy-start(f32[4,64]{1,0:T(4,128)S(1)} %divide_reduce_fusion.4) | copy-start | bytes 3076
  26.5 6.1 %copy-start.89 = (f32[64]{0:T(128)}, f32[64]{0:T(128)S(1)}, u32[]{:S(2)}) copy-start(f32[64]{0:T(128)S(1)} %get-tuple-element.57) | copy-start | bytes 772
  26.5 6.1 %copy-start.91 = (f32[64]{0:T(128)}, f32[64]{0:T(128)S(1)}, u32[]{:S(2)}) copy-start(f32[64]{0:T(128)S(1)} %get-tuple-element.58) | copy-start | bytes 772
  26.5 6.1 %copy-start.93 = (f32[64]{0:T(128)}, f32[64]{0:T(128)S(1)}, u32[]{:S(2)}) copy-start(f32[64]{0:T(128)S(1)} %get-tuple-element.59) | copy-start | bytes 772
  27.0 5.6 %copy-start.136 = (f32[64]{0:T(128)}, f32[64]{0:T(128)S(1)}, u32[]{:S(2)}) copy-start(f32[64]{0:T(128)S(1)} %get-tuple-element.23) | copy-start | bytes 772
  27.0 5.6 %copy-start.137 = (f32[64]{0:T(128)}, f32[64]{0:T(128)S(1)}, u32[]{:S(2)}) copy-start(f32[64]{0:T(128)S(1)} %get-tuple-element.22) | copy-start | bytes 772
  27.0 5.6 %copy-start.139 = (f32[64]{0:T(128)}, f32[64]{0:T(128)S(1)}, u32[]{:S(2)}) copy-start(f32[64]{0:T(128)S(1)} %get-tuple-element.20) | copy-start | bytes 772
  27.0 5.6 %copy-start.140 = (f32[64]{0:T(128)}, f32[64]{0:T(128)S(1)}, u32[]{:S(2)}) copy-start(f32[64]{0:T(128)S(1)} %get-tuple-element.24) | copy-start | bytes 772
  33.6 21.6 %copy-start = (f32[11,8192]{1,0:T(8,128)}, f32[11,8192]{1,0:T(8,128)S(1)}, u32[]{:S(2)}) copy-start(f32[11,8192]{1,0:T(8,128)S(1)} %get-tuple-element.52) | copy-start | bytes 1081348
  69.5 5.1 %copy-start.115 = (s32[32,6]{0,1:T(8,128)S(1)}, s32[32,6]{0,1:T(8,128)}, u32[]{:S(2)}) copy-start(s32[32,6]{0,1:T(8,128)} %param.9) | copy-start | bytes 2308
  69.5 5.8 %copy-start.6 = (f32[3,8192]{1,0:T(4,128)S(1)}, f32[3,8192]{1,0:T(4,128)}, u32[]{:S(2)}) copy-start(f32[3,8192]{1,0:T(4,128)} %get-tuple-element.51) | copy-start | bytes 294916
  130.5 5.8 %copy-start.74 = (f32[2,64]{1,0:T(2,128)S(1)}, f32[2,64]{1,0:T(2,128)}, u32[]{:S(2)}) copy-start(f32[2,64]{1,0:T(2,128)} %copy-done.73) | copy-start | bytes 1540
  130.5 5.8 %copy-start.76 = (f32[2,64]{1,0:T(2,128)S(1)}, f32[2,64]{1,0:T(2,128)}, u32[]{:S(2)}) copy-start(f32[2,64]{1,0:T(2,128)} %copy-done.75) | copy-start | bytes 1540
  130.5 5.8 %copy-start.78 = (f32[2,64]{1,0:T(2,128)S(1)}, f32[2,64]{1,0:T(2,128)}, u32[]{:S(2)}) copy-start(f32[2,64]{1,0:T(2,128)} %copy-done.77) | copy-start | bytes 1540
  130.5 5.8 %copy-start.87 = (f32[8,2,64]{2,0,1:T(8,128)S(1)}, f32[8,2,64]{2,0,1:T(8,128)}, u32[]{:S(2)}) copy-start(f32[8,2,64]{2,0,1:T(8,128)} %reduce_sum.310) | copy-start | bytes 12292
  130.5 6.8 %copy-start.58 = (f32[4,64]{1,0:T(4,128)S(1)}, f32[4,64]{1,0:T(4,128)}, u32[]{:S(2)}) copy-start(f32[4,64]{1,0:T(4,128)} %copy-done.57) | copy-start | bytes 3076
  130.5 6.8 %copy-start.60 = (f32[4,64]{1,0:T(4,128)S(1)}, f32[4,64]{1,0:T(4,128)}, u32[]{:S(2)}) copy-start(f32[4,64]{1,0:T(4,128)} %copy-done.59) | copy-start | bytes 3076
  130.5 6.8 %copy-start.62 = (f32[4,64]{1,0:T(4,128)S(1)}, f32[4,64]{1,0:T(4,128)}, u32[]{:S(2)}) copy-start(f32[4,64]{1,0:T(4,128)} %copy-done.61) | copy-start | bytes 3076
  130.5 6.8 %copy-start.71 = (f32[8,4,64]{2,0,1:T(8,128)S(1)}, f32[8,4,64]{2,0,1:T(8,128)}, u32[]{:S(2)}) copy-start(f32[8,4,64]{2,0,1:T(8,128)} %reduce_sum.311) | copy-start | bytes 24580
  130.6 6.8 %copy-start.82 = (f32[2,2,64]{2,1,0:T(2,128)S(1)}, f32[2,2,64]{2,1,0:T(2,128)}, u32[]{:S(2)}) copy-start(f32[2,2,64]{2,1,0:T(2,128)} %copy-done.81) | copy-start | bytes 3076
  130.6 6.8 %copy-start.84 = (f32[2,2,64]{2,1,0:T(2,128)S(1)}, f32[2,2,64]{2,1,0:T(2,128)}, u32[]{:S(2)}) copy-start(f32[2,2,64]{2,1,0:T(2,128)} %copy-done.83) | copy-start | bytes 3076
  130.6 6.8 %copy-start.86 = (f32[2,2,64]{2,1,0:T(2,128)S(1)}, f32[2,2,64]{2,1,0:T(2,128)}, u32[]{:S(2)}) copy-start(f32[2,2,64]{2,1,0:T(2,128)} %copy-done.85) | copy-start | bytes 3076
  130.6 6.8 %copy-start.117 = (f32[4,64]{1,0:T(4,128)S(1)}, f32[4,64]{1,0:T(4,128)}, u32[]{:S(2)}) copy-start(f32[4,64]{1,0:T(4,128)} %copy-done.116) | copy-start | bytes 3076
  132.2 5.6 %copy-start.37 = (f32[8,64]{1,0:T(8,128)S(1)}, f32[8,64]{1,0:T(8,128)}, u32[]{:S(2)}) copy-start(f32[8,64]{1,0:T(8,128)} %copy-done.36) | copy-start | bytes 6148
  132.3 5.6 %copy-start.39 = (f32[8,64]{1,0:T(8,128)S(1)}, f32[8,64]{1,0:T(8,128)}, u32[]{:S(2)}) copy-start(f32[8,64]{1,0:T(8,128)} %copy-done.38) | copy-start | bytes 6148
  132.3 5.6 %copy-start.41 = (f32[8,64]{1,0:T(8,128)S(1)}, f32[8,64]{1,0:T(8,128)}, u32[]{:S(2)}) copy-start(f32[8,64]{1,0:T(8,128)} %copy-done.40) | copy-start | bytes 6148
  132.3 5.6 %copy-start.66 = (f32[4,2,64]{2,1,0:T(2,128)S(1)}, f32[4,2,64]{2,1,0:T(2,128)}, u32[]{:S(2)}) copy-start(f32[4,2,64]{2,1,0:T(2,128)} %copy-done.65) | copy-start | bytes 6148
  132.3 5.6 %copy-start.68 = (f32[4,2,64]{2,1,0:T(2,128)S(1)}, f32[4,2,64]{2,1,0:T(2,128)}, u32[]{:S(2)}) copy-start(f32[4,2,64]{2,1,0:T(2,128)} %copy-done.67) | copy-start | bytes 6148
  132.3 5.6 %copy-start.70 = (f32[4,2,64]{2,1,0:T(2,128)S(1)}, f32[4,2,64]{2,1,0:T(2,128)}, u32[]{:S(2)}) copy-start(f32[4,2,64]{2,1,0:T(2,128)} %copy-done.69) | copy-start | bytes 6148
  132.3 5.6 %copy-start.114 = (f32[8,64]{1,0:T(8,128)S(1)}, f32[8,64]{1,0:T(8,128)}, u32[]{:S(2)}) copy-start(f32[8,64]{1,0:T(8,128)} %copy-done.113) | copy-start | bytes 6148
  132.7 5.9 %copy-start.24 = (f32[16,64]{1,0:T(8,128)S(1)}, f32[16,64]{1,0:T(8,128)}, u32[]{:S(2)}) copy-start(f32[16,64]{1,0:T(8,128)} %copy-done.23) | copy-start | bytes 12292
  132.7 5.9 %copy-start.26 = (f32[16,64]{1,0:T(8,128)S(1)}, f32[16,64]{1,0:T(8,128)}, u32[]{:S(2)}) copy-start(f32[16,64]{1,0:T(8,128)} %copy-done.25) | copy-start | bytes 12292
  132.7 5.9 %copy-start.34 = (f32[8,16,64]{2,0,1:T(8,128)S(1)}, f32[8,16,64]{2,0,1:T(8,128)}, u32[]{:S(2)}) copy-start(f32[8,16,64]{2,0,1:T(8,128)} %reduce_sum.313) | copy-start | bytes 98308
  132.7 5.9 %copy-start.43 = (f32[8,2,64]{2,1,0:T(2,128)S(1)}, f32[8,2,64]{2,1,0:T(2,128)}, u32[]{:S(2)}) copy-start(f32[8,2,64]{2,1,0:T(2,128)} %copy-done.42) | copy-start | bytes 12292
  132.7 5.9 %copy-start.45 = (f32[8,2,64]{2,1,0:T(2,128)S(1)}, f32[8,2,64]{2,1,0:T(2,128)}, u32[]{:S(2)}) copy-start(f32[8,2,64]{2,1,0:T(2,128)} %copy-done.44) | copy-start | bytes 12292
  132.7 5.9 %copy-start.47 = (f32[8,2,64]{2,1,0:T(2,128)S(1)}, f32[8,2,64]{2,1,0:T(2,128)}, u32[]{:S(2)}) copy-start(f32[8,2,64]{2,1,0:T(2,128)} %copy-done.46) | copy-start | bytes 12292
  132.7 5.9 %copy-start.80 = (f32[16,64]{1,0:T(8,128)S(1)}, f32[16,64]{1,0:T(8,128)}, u32[]{:S(2)}) copy-start(f32[16,64]{1,0:T(8,128)} %copy-done.79) | copy-start | bytes 12292
  (84 other events, 202.8 us)
Sparse Core Ops, SparseCore 0:
  29.0 87.8 all-gather.2
